TPU v7x, 32 devices: a whole 2x2x4 slice. The times are simulated.
32 devices in a mesh: dp: 8 (over z, y), tensor: 4 (over x, core).
Axes of the slice: x: 2, y: 2, z: 4, core: 2. Of those that a mesh axis runs over, the one named last changes fastest.
Arguments:
- image_tokens: bfloat16 [16, 1024, 1536], P('dp', 'tensor'), may hold values from -6 to 6
- text_tokens: bfloat16 [16, 160, 1536], P('dp', 'tensor'), may hold values from -6 to 6
- conditioning: bfloat16 [16, 1536], P('dp'), may hold values from -6 to 6
- group_seqs: int32 [8], P('dp'), may hold values from 0 to 2, as said below
- ada_weight: bfloat16 [2, 6, 1536, 1536], P(None, None, 'dp', 'tensor'), may hold values from -0.15625 to 0.15625
- ada_bias: bfloat16 [2, 6, 1536], replicated, may hold values from -3 to 3
- qkv_weight: bfloat16 [2, 3, 1536, 1536], P(None, None, 'dp', 'tensor'), may hold values from -0.15625 to 0.15625
- qv_bias: bfloat16 [2, 2, 1536], replicated, may hold values from -3 to 3
- proj_weight: bfloat16 [2, 1536, 1536], P(None, 'tensor', 'dp'), may hold values from -2.5 to 2.5
- proj_bias: bfloat16 [2, 1536], replicated, may hold values from -3 to 3
- fc1_weight: bfloat16 [2, 1536, 6144], P(None, 'dp', 'tensor'), may hold values from -0.15625 to 0.15625
- fc1_bias: bfloat16 [2, 6144], replicated, may hold values from -3 to 3
- fc2_weight: bfloat16 [2, 6144, 1536], P(None, 'tensor', 'dp'), may hold values from -0.078125 to 0.078125
- fc2_bias: bfloat16 [2, 1536], replicated, may hold values from -3 to 3
- image_cot: bfloat16 [16, 1024, 1536], P('dp', 'tensor'), may hold values from -6 to 6
- text_cot: bfloat16 [16, 160, 1536], P('dp', 'tensor'), may hold values from -6 to 6
Outputs:
- image_out: bfloat16 [16, 1024, 1536], P('dp', 'tensor')
- text_out: bfloat16 [16, 160, 1536], P('dp', 'tensor')
- image_grad: float32 [16, 1024, 1536], P('dp', 'tensor')
- text_grad: float32 [16, 160, 1536], P('dp', 'tensor')
- cond_grad: float32 [16, 1536], P('dp', 'tensor')
- ada_weight_grad: float32 [2, 6, 1536, 1536], P(None, None, 'dp', 'tensor')
- ada_bias_grad: float32 [2, 6, 1536], replicated
- qkv_weight_grad: float32 [2, 3, 1536, 1536], P(None, None, 'dp', 'tensor')
- qv_bias_grad: float32 [2, 2, 1536], replicated
- proj_weight_grad: float32 [2, 1536, 1536], P(None, 'tensor', 'dp')
- proj_bias_grad: float32 [2, 1536], replicated
- fc1_weight_grad: float32 [2, 1536, 6144], P(None, 'dp', 'tensor')
- fc1_bias_grad: float32 [2, 6144], replicated
- fc2_weight_grad: float32 [2, 6144, 1536], P(None, 'tensor', 'dp')
- fc2_bias_grad: float32 [2, 1536], replicated
Inputs may be any that keep to these rules, and one draw needn't show every extreme that they name: A data group's sequences fill its first group_seqs[g] slots; its other slots of 2 are empty. The counts sum to 8; in every draw some group holds 2 sequences and some none.
All inputs are finite; a program needn't handle non-finite values.
Results may differ from a plain program's by a relative error of at most 0.02.
Values may be sent and summed in bfloat16 or wider, within the bound.
No kernel may reach another device: no remote copies, remote signals or barrier semaphores. Data moves between devices by JAX's collectives and lax.ppermute only.
A program may use at most 512 MiB of HBM per device.

v0:
```python
import math

import jax
import jax.numpy as jnp
from jax import lax
from jax.sharding import PartitionSpec as P

HEAD_DIM = 64


epsilon = 1e-06


def modulate_norm(values, shift_vec, scale_vec):
    average = jnp.mean(values, -1, keepdims=True)
    centred = values - average
    spread = jnp.mean(centred * centred, -1, keepdims=True)
    return (
        centred * lax.rsqrt(spread + epsilon) * (1.0 + scale_vec[:, None, :])
        + shift_vec[:, None, :]
    )


def gelu_tanh(values):
    return jax.nn.gelu(values, approximate=True)


def gather_tokens(image_part, text_part):
    return (
        lax.all_gather(image_part, "tensor", axis=1, tiled=True),
        lax.all_gather(text_part, "tensor", axis=1, tiled=True),
    )


def scatter_tokens(image_part, text_part):
    return (
        lax.psum_scatter(
            image_part.astype(jnp.bfloat16), "tensor", scatter_dimension=1, tiled=True
        ).astype(jnp.float32),
        lax.psum_scatter(
            text_part.astype(jnp.bfloat16), "tensor", scatter_dimension=1, tiled=True
        ).astype(jnp.float32),
    )


def split_heads(matrix):
    return matrix.reshape(matrix.shape[0], matrix.shape[1] // HEAD_DIM, HEAD_DIM)


def attend(query_block, key_block, value_block):
    factor = 1.0 / math.sqrt(HEAD_DIM)
    query_heads = split_heads(query_block)
    key_heads = split_heads(key_block)
    value_heads = split_heads(value_block)
    scores = (
        jnp.einsum("qhe,khe->hqk", query_heads, key_heads, preferred_element_type=jnp.float32)
        * factor
    )
    row_top = jnp.max(scores, -1, keepdims=True)
    total_log = row_top + jnp.log(jnp.sum(jnp.exp(scores - row_top), -1, keepdims=True))
    attn_probs = jnp.exp(scores - total_log).astype(jnp.bfloat16)
    output = jnp.einsum("hqk,khe->qhe", attn_probs, value_heads, preferred_element_type=jnp.float32)
    return (output.reshape(query_block.shape).astype(jnp.bfloat16), total_log)


def attend_back(query_block, key_block, value_block, total_log, out_grad):
    factor = 1.0 / math.sqrt(HEAD_DIM)
    query_heads = split_heads(query_block)
    key_heads = split_heads(key_block)
    value_heads = split_heads(value_block)
    grad_heads = split_heads(out_grad)
    scores = (
        jnp.einsum("qhe,khe->hqk", query_heads, key_heads, preferred_element_type=jnp.float32)
        * factor
    )
    attn_probs = jnp.exp(scores - total_log)
    prob_grad = jnp.einsum(
        "qhe,khe->hqk", grad_heads, value_heads, preferred_element_type=jnp.float32
    )
    row_inner = jnp.sum(attn_probs * prob_grad, -1, keepdims=True)
    score_grad = (attn_probs * (prob_grad - row_inner)).astype(jnp.bfloat16)
    query_grad = (
        jnp.einsum("hqk,khe->qhe", score_grad, key_heads, preferred_element_type=jnp.float32)
        * factor
    )
    key_grad = (
        jnp.einsum("hqk,qhe->khe", score_grad, query_heads, preferred_element_type=jnp.float32)
        * factor
    )
    value_grad = jnp.einsum(
        "hqk,qhe->khe",
        attn_probs.astype(jnp.bfloat16),
        grad_heads,
        preferred_element_type=jnp.float32,
    )
    flat_shape = query_block.shape
    return jnp.stack(
        [
            query_grad.reshape(flat_shape),
            key_grad.reshape(flat_shape),
            value_grad.reshape(flat_shape),
        ]
    ).astype(jnp.bfloat16)


def forward(streams, cond_low, weights, biases):
    ada_full, qkv_full, proj_full, fc1_full, fc2_full = weights
    ada_part, qv_part, proj_add, fc1_part, fc2_add = biases
    modul_local = (
        jnp.einsum("cd,sjdn->csjn", cond_low, ada_full, preferred_element_type=jnp.float32)
        + ada_part[None]
    )
    modulation = lax.all_gather(modul_local, "tensor", axis=3, tiled=True)
    first_low = [
        modulate_norm(streams[stream], modulation[:, stream, 0], modulation[:, stream, 1]).astype(
            jnp.bfloat16
        )
        for stream in range(2)
    ]
    first_full = gather_tokens(first_low[0], first_low[1])
    joined_list = []
    for stream in range(2):
        projected = jnp.einsum(
            "cld,jdn->jcln",
            first_full[stream],
            qkv_full[stream],
            preferred_element_type=jnp.float32,
        )
        offsets = jnp.stack(
            [qv_part[stream, 0], jnp.zeros_like(qv_part[stream, 0]), qv_part[stream, 1]]
        )
        joined_list.append((projected + offsets[:, None, None, :]).astype(jnp.bfloat16))
    joined = jnp.concatenate(joined_list, 2)
    attended_rows = []
    totals = []
    for slot_index in range(joined.shape[1]):
        attended_slot, total_log = attend(
            joined[0, slot_index], joined[1, slot_index], joined[2, slot_index]
        )
        attended_rows.append(attended_slot)
        totals.append(total_log)
    attended = jnp.stack(attended_rows)
    split_at = first_full[0].shape[1]
    pieces = (attended[:, :split_at], attended[:, split_at:])
    branch_sums = scatter_tokens(
        jnp.einsum("cln,nd->cld", pieces[0], proj_full[0], preferred_element_type=jnp.float32),
        jnp.einsum("cln,nd->cld", pieces[1], proj_full[1], preferred_element_type=jnp.float32),
    )
    branches = [branch_sums[stream] + proj_add[stream] for stream in range(2)]
    after_attn = [
        streams[stream] + modulation[:, stream, 2][:, None, :] * branches[stream]
        for stream in range(2)
    ]
    second = [
        modulate_norm(
            after_attn[stream], modulation[:, stream, 3], modulation[:, stream, 4]
        ).astype(jnp.bfloat16)
        for stream in range(2)
    ]
    second_full = gather_tokens(second[0], second[1])
    pre_act = [
        jnp.einsum(
            "cld,df->clf", second_full[stream], fc1_full[stream], preferred_element_type=jnp.float32
        )
        + fc1_part[stream]
        for stream in range(2)
    ]
    activated = [gelu_tanh(pre_act[stream]).astype(jnp.bfloat16) for stream in range(2)]
    mlp_sums = scatter_tokens(
        jnp.einsum("clf,fd->cld", activated[0], fc2_full[0], preferred_element_type=jnp.float32),
        jnp.einsum("clf,fd->cld", activated[1], fc2_full[1], preferred_element_type=jnp.float32),
    )
    mlp_out = [mlp_sums[stream] + fc2_add[stream] for stream in range(2)]
    results = [
        after_attn[stream] + modulation[:, stream, 5][:, None, :] * mlp_out[stream]
        for stream in range(2)
    ]
    return dict(
        modulation=modulation,
        first_full=first_full,
        joined=joined,
        totals=totals,
        pieces=pieces,
        branches=branches,
        after_attn=after_attn,
        second_full=second_full,
        pre_act=pre_act,
        activated=activated,
        mlp_out=mlp_out,
        results=results,
        streams=streams,
    )


def on_device(
    image_tokens,
    text_tokens,
    conditioning,
    group_seqs,
    ada_weight,
    ada_bias,
    qkv_weight,
    qv_bias,
    proj_weight,
    proj_bias,
    fc1_weight,
    fc1_bias,
    fc2_weight,
    fc2_bias,
    image_cot,
    text_cot,
):
    column = lax.axis_index("tensor")
    col_width = qkv_weight.shape[-1]
    hidden = fc1_weight.shape[-1]
    ada_part = lax.dynamic_slice_in_dim(
        ada_bias.astype(jnp.float32), column * col_width, col_width, 2
    )
    qv_part = lax.dynamic_slice_in_dim(
        qv_bias.astype(jnp.float32), column * col_width, col_width, 2
    )
    fc1_part = lax.dynamic_slice_in_dim(fc1_bias.astype(jnp.float32), column * hidden, hidden, 1)
    biases = (
        ada_part,
        qv_part,
        proj_bias.astype(jnp.float32),
        fc1_part,
        fc2_bias.astype(jnp.float32),
    )
    live_mask = (jnp.arange(image_tokens.shape[0], dtype=jnp.int32) < group_seqs[0]).astype(
        jnp.float32
    )[:, None, None]
    cond_act, silu_back = jax.vjp(jax.nn.silu, conditioning.astype(jnp.float32))
    cond_low = cond_act.astype(jnp.bfloat16)
    ada_full, qkv_full = (
        lax.all_gather(ada_weight, "dp", axis=2, tiled=True),
        lax.all_gather(qkv_weight, "dp", axis=2, tiled=True),
    )
    proj_full, fc1_full, fc2_full = (
        lax.all_gather(proj_weight, "dp", axis=2, tiled=True),
        lax.all_gather(fc1_weight, "dp", axis=1, tiled=True),
        lax.all_gather(fc2_weight, "dp", axis=2, tiled=True),
    )
    weights = (ada_full, qkv_full, proj_full, fc1_full, fc2_full)
    streams = (image_tokens.astype(jnp.float32), text_tokens.astype(jnp.float32))
    kept_vals = forward(streams, cond_low, weights, biases)
    image_out = (kept_vals["results"][0] * live_mask).astype(jnp.bfloat16)
    text_out = (kept_vals["results"][1] * live_mask).astype(jnp.bfloat16)
    modulation = kept_vals["modulation"]
    streams = kept_vals["streams"]
    out_grad = [image_cot.astype(jnp.float32) * live_mask, text_cot.astype(jnp.float32) * live_mask]
    mlp_round = [
        (out_grad[stream] * modulation[:, stream, 5][:, None, :]).astype(jnp.bfloat16)
        for stream in range(2)
    ]
    gate_two = [jnp.sum(out_grad[stream] * kept_vals["mlp_out"][stream], 1) for stream in range(2)]
    mlp_full = gather_tokens(mlp_round[0], mlp_round[1])
    activated = kept_vals["activated"]
    fc2_grad = jnp.stack(
        [
            jnp.einsum(
                "clf,cld->fd",
                activated[stream],
                mlp_full[stream],
                preferred_element_type=jnp.float32,
            )
            for stream in range(2)
        ]
    )
    fc2_bias_local = jnp.stack(
        [jnp.sum(mlp_round[stream].astype(jnp.float32), (0, 1)) for stream in range(2)]
    )
    pre_round = []
    for stream in range(2):
        act_grad = jnp.einsum(
            "cld,fd->clf", mlp_full[stream], fc2_full[stream], preferred_element_type=jnp.float32
        )
        _, gelu_back = jax.vjp(gelu_tanh, kept_vals["pre_act"][stream])
        pre_round.append(gelu_back(act_grad)[0].astype(jnp.bfloat16))
    second_full = kept_vals["second_full"]
    fc1_grad = jnp.stack(
        [
            jnp.einsum(
                "cld,clf->df",
                second_full[stream],
                pre_round[stream],
                preferred_element_type=jnp.float32,
            )
            for stream in range(2)
        ]
    )
    fc1_bias_local = jnp.stack(
        [jnp.sum(pre_round[stream].astype(jnp.float32), (0, 1)) for stream in range(2)]
    )
    norm_two = scatter_tokens(
        jnp.einsum("clf,df->cld", pre_round[0], fc1_full[0], preferred_element_type=jnp.float32),
        jnp.einsum("clf,df->cld", pre_round[1], fc1_full[1], preferred_element_type=jnp.float32),
    )
    residual_grads, shift_two, scale_two, gate_one, branch_round = ([], [], [], [], [])
    for stream in range(2):
        _, norm_back = jax.vjp(
            modulate_norm,
            kept_vals["after_attn"][stream],
            modulation[:, stream, 3],
            modulation[:, stream, 4],
        )
        input_part, shift_part, scale_part = norm_back(norm_two[stream])
        residual_grad = out_grad[stream] + input_part
        residual_grads.append(residual_grad)
        shift_two.append(shift_part)
        scale_two.append(scale_part)
        gate_one.append(jnp.sum(residual_grad * kept_vals["branches"][stream], 1))
        branch_round.append(
            (residual_grad * modulation[:, stream, 2][:, None, :]).astype(jnp.bfloat16)
        )
    branch_full = gather_tokens(branch_round[0], branch_round[1])
    pieces = kept_vals["pieces"]
    proj_grad = jnp.stack(
        [
            jnp.einsum(
                "cln,cld->nd",
                pieces[stream],
                branch_full[stream],
                preferred_element_type=jnp.float32,
            )
            for stream in range(2)
        ]
    )
    proj_bias_local = jnp.stack(
        [jnp.sum(branch_round[stream].astype(jnp.float32), (0, 1)) for stream in range(2)]
    )
    attended_grad = jnp.concatenate(
        [
            jnp.einsum(
                "cld,nd->cln",
                branch_full[stream],
                proj_full[stream],
                preferred_element_type=jnp.float32,
            )
            for stream in range(2)
        ],
        1,
    ).astype(jnp.bfloat16)
    second_sums = None
    joined = kept_vals["joined"]
    totals = kept_vals["totals"]
    qkv_rows = []
    for slot_index in range(joined.shape[1]):
        qkv_rows.append(
            attend_back(
                joined[0, slot_index],
                joined[1, slot_index],
                joined[2, slot_index],
                totals[slot_index],
                attended_grad[slot_index],
            )
        )
    qkv_round = jnp.stack(qkv_rows, 1)
    first_full = kept_vals["first_full"]
    split_at = first_full[0].shape[1]
    qkv_parts = (qkv_round[:, :, :split_at], qkv_round[:, :, split_at:])
    qkv_grad = jnp.stack(
        [
            jnp.einsum(
                "cld,jcln->jdn",
                first_full[stream],
                qkv_parts[stream],
                preferred_element_type=jnp.float32,
            )
            for stream in range(2)
        ]
    )
    qv_bias_local = jnp.stack(
        [jnp.sum(qkv_parts[stream][0::2].astype(jnp.float32), (1, 2)) for stream in range(2)]
    )
    norm_one = scatter_tokens(
        jnp.einsum("jcln,jdn->cld", qkv_parts[0], qkv_full[0], preferred_element_type=jnp.float32),
        jnp.einsum("jcln,jdn->cld", qkv_parts[1], qkv_full[1], preferred_element_type=jnp.float32),
    )
    input_grads, modul_grads = ([], [])
    for stream in range(2):
        _, norm_back = jax.vjp(
            modulate_norm, streams[stream], modulation[:, stream, 0], modulation[:, stream, 1]
        )
        input_part, shift_part, scale_part = norm_back(norm_one[stream])
        input_grads.append(residual_grads[stream] + input_part)
        modul_grads.append(
            jnp.stack(
                [
                    shift_part,
                    scale_part,
                    gate_one[stream],
                    shift_two[stream],
                    scale_two[stream],
                    gate_two[stream],
                ],
                1,
            )
        )
    modul_grad = jnp.stack(modul_grads, 1)
    modul_round = lax.psum_scatter(
        modul_grad.astype(jnp.bfloat16), "tensor", scatter_dimension=3, tiled=True
    )
    ada_grad = jnp.einsum(
        "cd,csjn->sjdn", cond_low, modul_round, preferred_element_type=jnp.float32
    )
    ada_bias_local = jnp.sum(modul_round.astype(jnp.float32), 0)
    cond_term = jnp.einsum(
        "csjn,sjdn->cd", modul_round, ada_full, preferred_element_type=jnp.float32
    )
    cond_grad = lax.psum_scatter(silu_back(cond_term)[0], "tensor", scatter_dimension=1, tiled=True)
    ada_bias_grad = lax.dynamic_update_slice_in_dim(
        jnp.zeros(ada_bias.shape, jnp.float32), ada_bias_local, column * col_width, 2
    )
    qv_bias_grad = lax.dynamic_update_slice_in_dim(
        jnp.zeros(qv_bias.shape, jnp.float32), qv_bias_local, column * col_width, 2
    )
    fc1_bias_grad = lax.dynamic_update_slice_in_dim(
        jnp.zeros(fc1_bias.shape, jnp.float32), fc1_bias_local, column * hidden, 1
    )
    bias_sums = lax.psum(
        (ada_bias_grad, qv_bias_grad, proj_bias_local, fc1_bias_grad, fc2_bias_local),
        ("dp", "tensor"),
    )
    first_sums = (
        lax.psum_scatter(
            ada_grad.astype(jnp.bfloat16), "dp", scatter_dimension=2, tiled=True
        ).astype(jnp.float32),
        lax.psum_scatter(
            qkv_grad.astype(jnp.bfloat16), "dp", scatter_dimension=2, tiled=True
        ).astype(jnp.float32),
    )
    second_sums = (
        lax.psum_scatter(
            proj_grad.astype(jnp.bfloat16), "dp", scatter_dimension=2, tiled=True
        ).astype(jnp.float32),
        lax.psum_scatter(
            fc1_grad.astype(jnp.bfloat16), "dp", scatter_dimension=1, tiled=True
        ).astype(jnp.float32),
        lax.psum_scatter(
            fc2_grad.astype(jnp.bfloat16), "dp", scatter_dimension=2, tiled=True
        ).astype(jnp.float32),
    )
    return (
        image_out,
        text_out,
        input_grads[0],
        input_grads[1],
        cond_grad,
        first_sums[0],
        bias_sums[0],
        first_sums[1],
        bias_sums[1],
        second_sums[0],
        bias_sums[2],
        second_sums[1],
        bias_sums[3],
        second_sums[2],
        bias_sums[4],
    )


def solution(mesh):
    in_specs = (
        P("dp", "tensor", None),
        P("dp", "tensor", None),
        P("dp", None),
        P("dp"),
        P(None, None, "dp", "tensor"),
        P(),
        P(None, None, "dp", "tensor"),
        P(),
        P(None, "tensor", "dp"),
        P(),
        P(None, "dp", "tensor"),
        P(),
        P(None, "tensor", "dp"),
        P(),
        P("dp", "tensor", None),
        P("dp", "tensor", None),
    )
    out_specs = (
        P("dp", "tensor", None),
        P("dp", "tensor", None),
        P("dp", "tensor", None),
        P("dp", "tensor", None),
        P("dp", "tensor"),
        P(None, None, "dp", "tensor"),
        P(),
        P(None, None, "dp", "tensor"),
        P(),
        P(None, "tensor", "dp"),
        P(),
        P(None, "dp", "tensor"),
        P(),
        P(None, "tensor", "dp"),
        P(),
    )
    return jax.shard_map(
        on_device, mesh=mesh, in_specs=in_specs, out_specs=out_specs, check_vma=False
    )
```

profile of v0, /device:TPU:0, one launch (start us, length us, event | category | flops | bytes accessed | tf_op | source)
XLA Modules:
  0.0 3074.3 jit_solution(6352690388552557443)
XLA Ops:
  12.4 196.2 %all-gather.10.cloned.1.call-done = bf16[2,6,1536,384]{3,2,1,0:T(8,128)(2,1)} async-done(((bf16[2,6,192,384]{3,2,1,0:T(8,128)(2,1)}), bf16[2,6,1536,384]{3,2,1,0:T(8,128)(2,1)}) %all-gather.10.cloned.1.call-update) | async-done | bytes 14155792 | tf_op jit(solution)/shard_map/all_gather | solution.py:236
  224.9 36.7 %all-gather.16.cloned.1.call-done = bf16[2,384,1536]{1,0,2:T(2,128)(2,1)} async-done(((bf16[2,384,192]{1,0,2:T(2,128)(2,1)}), bf16[2,384,1536]{1,0,2:T(2,128)(2,1)}) %all-gather.16.cloned.1.call-update) | async-done | bytes 2359312 | tf_op jit(solution)/shard_map/all_gather | solution.py:240
  285.8 85.4 %all-gather.14.cloned.1.call-done = bf16[2,3,1536,384]{3,2,1,0:T(8,128)(2,1)} async-done(((bf16[2,3,192,384]{3,2,1,0:T(8,128)(2,1)}), bf16[2,3,1536,384]{3,2,1,0:T(8,128)(2,1)}) %all-gather.14.cloned.1.call-update) | async-done | bytes 7077904 | tf_op jit(solution)/shard_map/all_gather | solution.py:237
  375.5 42.3 %all-gather.12.cloned.1.call-done = bf16[2,1024,1536]{2,1,0:T(8,128)(2,1)} async-done(((bf16[2,256,1536]{2,1,0:T(8,128)(2,1)}), bf16[2,1024,1536]{2,1,0:T(8,128)(2,1)}) %all-gather.12.cloned.1.call-update) | async-done | bytes 6291472 | tf_op jit(solution)/shard_map/all_gather | solution.py:30
  550.5 53.6 %reduce-scatter.24.cloned.1.call-done = bf16[2,256,1536]{2,1,0:T(8,128)(2,1)} async-done(((bf16[2,1024,1536]{2,1,0:T(8,128)(2,1)}), bf16[2,256,1536]{2,1,0:T(8,128)(2,1)}) %reduce-scatter.24.cloned.1.call-update) | async-done | bytes 1572880 | tf_op jit(solution)/shard_map/reduce_scatter | solution.py:37
  620.2 124.8 %all-gather.22.cloned.1.call-done = bf16[2,1536,1536]{1,0,2:T(2,128)(2,1)} async-done(((bf16[2,1536,192]{1,0,2:T(2,128)(2,1)}), bf16[2,1536,1536]{1,0,2:T(2,128)(2,1)}) %all-gather.22.cloned.1.call-update) | async-done | bytes 9437200 | tf_op jit(solution)/shard_map/all_gather | solution.py:242
  745.1 19.1 fusion.164
  764.1 22.5 copy.195
  790.5 93.3 %all-gather.20.cloned.1.call-done = bf16[2,1536,1536]{2,1,0:T(8,128)(2,1)} async-done(((bf16[2,192,1536]{2,1,0:T(8,128)(2,1)}), bf16[2,1536,1536]{2,1,0:T(8,128)(2,1)}) %all-gather.20.cloned.1.call-update) | async-done | bytes 9437200 | tf_op jit(solution)/shard_map/all_gather | solution.py:241
  883.8 46.8 %all-gather.18.cloned.1.call-done = bf16[2,1024,1536]{2,1,0:T(8,128)(2,1)} async-done(((bf16[2,256,1536]{2,1,0:T(8,128)(2,1)}), bf16[2,1024,1536]{2,1,0:T(8,128)(2,1)}) %all-gather.18.cloned.1.call-update) | async-done | bytes 6291472 | tf_op jit(solution)/shard_map/all_gather | solution.py:30
  946.7 32.5 %all-gather.24.cloned.1.call-done = bf16[2,1024,1536]{2,1,0:T(8,128)(2,1)} async-done(((bf16[2,256,1536]{2,1,0:T(8,128)(2,1)}), bf16[2,1024,1536]{2,1,0:T(8,128)(2,1)}) %all-gather.24.cloned.1.call-update) | async-done | bytes 6291472 | tf_op jit(solution)/shard_map/all_gather | solution.py:30
  979.2 25.4 convert_reduce_fusion
  1018.9 17.1 convolution_convert_fusion.1
  1036.8 22.6 copy.197
  1112.9 30.8 %reduce-scatter.26.cloned.1.call-done = bf16[2,256,1536]{2,1,0:T(8,128)(2,1)} async-done(((bf16[2,1024,1536]{2,1,0:T(8,128)(2,1)}), bf16[2,256,1536]{2,1,0:T(8,128)(2,1)}) %reduce-scatter.26.cloned.1.call-update) | async-done | bytes 1572880 | tf_op jit(solution)/shard_map/reduce_scatter | solution.py:37
  1149.9 20.9 reduce-scatter.36.cloned.1.call-done
  1172.6 25.9 reduce-scatter.38.cloned.1.call-done
  1218.9 29.9 all-gather.26.cloned.1.call-done
  1271.9 26.6 multiply_reduce_fusion
  1298.5 29.9 multiply_convert_fusion
  1367.9 26.6 multiply_reduce_fusion.1
  1394.5 29.9 multiply_convert_fusion.1
  1490.1 18.1 fusion.12
  1513.3 38.4 %reduce-scatter.30.cloned.1.call-done = bf16[2,256,1536]{2,1,0:T(8,128)(2,1)} async-done(((bf16[2,1024,1536]{2,1,0:T(8,128)(2,1)}), bf16[2,256,1536]{2,1,0:T(8,128)(2,1)}) %reduce-scatter.30.cloned.1.call-update) | async-done | bytes 1572880 | tf_op jit(solution)/shard_map/reduce_scatter | solution.py:37
  1586.2 24.1 copy.156
  1677.1 18.3 copy.151
  1718.7 35.4 %copy.148 = bf16[2,6,1536,384]{3,0,1,2:T(2,128)(2,1)} copy(bf16[2,6,1536,384]{2,3,1,0:T(8,128)(2,1)} %convert_bitcast_fusion) | data formatting | bytes 28311552 | tf_op jit(solution)/shard_map/convert_element_type | solution.py:427
  1756.1 152.5 %all-reduce.13.cloned.1.call-done = bf16[2,1536,1536]{1,0,2:T(2,128)(2,1)} async-done(((bf16[2,1536,1536]{1,0,2:T(2,128)(2,1)}), bf16[2,1536,1536]{1,0,2:T(2,128)(2,1)}) %all-reduce.13.cloned.1.call-update) | async-done | bytes 9437200
  1913.2 161.3 %reduce-scatter.32.cloned.1.call-done = bf16[2,192,1536]{2,1,0:T(8,128)(2,1)} async-done(((bf16[2,1536,1536]{2,1,0:T(8,128)(2,1)}), bf16[2,192,1536]{2,1,0:T(8,128)(2,1)}) %reduce-scatter.32.cloned.1.call-update) | async-done | bytes 1179664 | tf_op jit(solution)/shard_map/reduce_scatter | solution.py:437
  2101.7 703.4 %all-reduce.17.cloned.1.call-done = (bf16[2,6,1536,384]{3,0,1,2:T(2,128)(2,1)}, bf16[2,3,1536,384]{3,0,1,2:T(2,128)(2,1)}, bf16[2,384,1536]{1,0,2:T(2,128)(2,1)}) async-done(((bf16[2,6,1536,384]{3,0,1,2:T(2,128)(2,1)}, bf16[2,3,1536,384]{3,0,1,2:T(2,128)(2,1)}, bf16[2,384,1536]{1,0,2:T(2,128)(2,1)}), (bf16[2,6,1536,384]{3,0,1,2:T(2,128)(2,1)}, bf16[2,3,1536,384]{3,0,1,2:T(2,128)(2,1)}, ...) | async-done | bytes 23592976
  2815.1 119.0 %all-reduce.15.cloned.1.call-done = (f32[2,2,1536]{2,1,0:T(2,128)}, f32[2,1536]{1,0:T(2,128)}, f32[2,6144]{1,0:T(2,128)}, f32[2,1536]{1,0:T(2,128)}) async-done(((f32[2,2,1536]{2,1,0:T(2,128)}, f32[2,1536]{1,0:T(2,128)}, f32[2,6144]{1,0:T(2,128)}, f32[2,1536]{1,0:T(2,128)}), (f32[2,2,1536]{2,1,0:T(2,128)}, f32[2,1536]{1,0:T(2,128)}, f32[2,6144]{1,0:T(2,128)}, ...) | async-done | bytes 98320 | tf_op jit(solution)/shard_map/psum | solution.py:421
  2934.1 126.3 %all-reduce.11.cloned.1.call-done = f32[2,6,1536]{2,0,1:T(2,128)} async-done(((f32[2,6,1536]{2,0,1:T(2,128)}), f32[2,6,1536]{2,0,1:T(2,128)}) %all-reduce.11.cloned.1.call-update) | async-done | bytes 73744 | tf_op jit(solution)/shard_map/psum | solution.py:421
  (524 shorter events, 621.0 us)
Async XLA Ops:
  7.2 201.4 %copy-start.87 = (bf16[2,1536]{1,0:T(2,128)(2,1)S(1)}, bf16[2,1536]{1,0:T(2,128)(2,1)}, u32[]{:S(2)}) copy-start(bf16[2,1536]{1,0:T(2,128)(2,1)} %param.18) | copy-start | bytes 18436
  7.2 201.4 %all-gather.10.cloned.1.call-start = ((), (), s32[]{:S(2)}) async-start(), calls=%async_computation.11 | async-start | bytes 15925248 | tf_op jit(solution)/shard_map/all_gather | solution.py:236
  7.9 253.7 %all-gather.16.cloned.1.call-start = ((), (), s32[]{:S(2)}) async-start(), calls=%async_computation.14 | async-start | bytes 2654208 | tf_op jit(solution)/shard_map/all_gather | solution.py:240
  10.0 361.2 %all-gather.14.cloned.1.call-start = ((), (), s32[]{:S(2)}) async-start(), calls=%async_computation.13 | async-start | bytes 7962624 | tf_op jit(solution)/shard_map/all_gather | solution.py:237
  10.7 407.1 %all-gather.12.cloned.1.call-start = ((), (), s32[]{:S(2)}) async-start(), calls=%async_computation.12 | async-start | bytes 7864320 | tf_op jit(solution)/shard_map/all_gather | solution.py:30
  11.8 210.0 %copy-start.80 = (f32[2,256]{1,0:T(2,128)}, f32[2,256]{1,0:T(2,128)S(1)}, u32[]{:S(2)}) copy-start(f32[2,256]{1,0:T(2,128)S(1)} %broadcast_multiply_fusion.1) | copy-start | bytes 6148
  12.4 203.2 %copy-start.105 = (f32[2,256]{1,0:T(2,128)}, f32[2,256]{1,0:T(2,128)S(1)}, u32[]{:S(2)}) copy-start(f32[2,256]{1,0:T(2,128)S(1)} %fusion.56) | copy-start | bytes 6148
  12.4 209.4 %copy-start.95 = (f32[2,256]{1,0:T(2,128)}, f32[2,256]{1,0:T(2,128)S(1)}, u32[]{:S(2)}) copy-start(f32[2,256]{1,0:T(2,128)S(1)} %fusion.150) | copy-start | bytes 6148
  221.8 386.0 %copy-start.45 = (f32[2,1536]{1,0:T(2,128)}, f32[2,1536]{1,0:T(2,128)S(1)}, u32[]{:S(2)}) copy-start(f32[2,1536]{1,0:T(2,128)S(1)} %get-tuple-element.121) | copy-start | bytes 36868
  223.6 380.5 %reduce-scatter.24.cloned.1.call-start = ((), (), s32[]{:S(2)}) async-start(), calls=%async_computation.15 | async-start | bytes 7864320 | tf_op jit(solution)/shard_map/reduce_scatter | solution.py:37
  545.6 199.4 %all-gather.22.cloned.1.call-start = ((), (), s32[]{:S(2)}) async-start(), calls=%async_computation.18 | async-start | bytes 10616832 | tf_op jit(solution)/shard_map/all_gather | solution.py:242
  549.1 334.7 %all-gather.20.cloned.1.call-start = ((), (), s32[]{:S(2)}) async-start(), calls=%async_computation.17 | async-start | bytes 10616832 | tf_op jit(solution)/shard_map/all_gather | solution.py:241
  549.8 380.7 %all-gather.18.cloned.1.call-start = ((), (), s32[]{:S(2)}) async-start(), calls=%async_computation.16 | async-start | bytes 7864320 | tf_op jit(solution)/shard_map/all_gather | solution.py:30
  610.2 369.0 %all-gather.24.cloned.1.call-start = ((), (), s32[]{:S(2)}) async-start(), calls=%async_computation.20 | async-start | bytes 7864320 | tf_op jit(solution)/shard_map/all_gather | solution.py:30
  613.2 446.1 %reduce-scatter.34.cloned.1.call-start = ((), (), s32[]{:S(2)}) async-start(), calls=%async_computation.26 | async-start | bytes 1228800
  614.6 404.2 %copy-start.116 = (f32[1536]{0:T(1024)}, f32[1536]{0:T(1024)S(1)}, u32[]{:S(2)}) copy-start(f32[1536]{0:T(1024)S(1)} %get-tuple-element.72) | copy-start | bytes 18436
  620.2 166.5 %copy-start.33 = (bf16[1,384,1536]{2,1,0:T(8,128)(2,1)}, bf16[1,384,1536]{2,1,0:T(8,128)(2,1)S(1)}, u32[]{:S(2)}) copy-start(bf16[1,384,1536]{2,1,0:T(8,128)(2,1)S(1)} %copy.196) | copy-start | bytes 3538948
  790.2 317.8 %reduce-scatter.28.cloned.1.call-start = ((), (), s32[]{:S(2)}) async-start(), calls=%async_computation.21 | async-start | bytes 7864320 | tf_op jit(solution)/shard_map/reduce_scatter | solution.py:37
  1018.8 124.8 %reduce-scatter.26.cloned.1.call-start = ((), (), s32[]{:S(2)}) async-start(), calls=%async_computation.19 | async-start | bytes 7864320 | tf_op jit(solution)/shard_map/reduce_scatter | solution.py:37
  1036.0 134.7 %reduce-scatter.36.cloned.1.call-start = ((), (), s32[]{:S(2)}) async-start(), calls=%async_computation.27 | async-start | bytes 1228800
  1085.1 113.3 %reduce-scatter.38.cloned.1.call-start = ((), (), s32[]{:S(2)}) async-start(), calls=%async_computation.28 | async-start | bytes 1228800
  1108.0 140.8 %all-gather.26.cloned.1.call-start = ((), (), s32[]{:S(2)}) async-start(), calls=%async_computation.22 | async-start | bytes 7864320 | tf_op jit(solution)/shard_map/all_gather | solution.py:30
  1149.8 358.7 %reduce-scatter.40.cloned.1.call-start = ((), (), s32[]{:S(2)}) async-start(), calls=%async_computation.29 | async-start | bytes 1228800
  1465.8 85.9 %reduce-scatter.30.cloned.1.call-start = ((), (), s32[]{:S(2)}) async-start(), calls=%async_computation.23 | async-start | bytes 7864320 | tf_op jit(solution)/shard_map/reduce_scatter | solution.py:37
  1483.5 211.8 %reduce-scatter.42.cloned.1.call-start = ((), (), s32[]{:S(2)}) async-start(), calls=%async_computation.30 | async-start | bytes 491520
  1577.9 330.7 %all-reduce.13.cloned.1.call-start = ((), (), s32[]{:S(2)}) async-start(), calls=%async_computation.32 | async-start | bytes 18874368
  1610.3 464.2 %reduce-scatter.32.cloned.1.call-start = ((), (), s32[]{:S(2)}) async-start(), calls=%async_computation.25 | async-start | bytes 10616832 | tf_op jit(solution)/shard_map/reduce_scatter | solution.py:437
  1641.2 458.9 %reduce-scatter.44.cloned.1.call-start = ((), (), s32[]{:S(2)}) async-start(), calls=%async_computation.31 | async-start | bytes 983040
  1711.2 1093.9 %all-reduce.17.cloned.1.call-start = ((), (), s32[]{:S(2)}) async-start(), calls=%async_computation.34 | async-start | bytes 47185920
  1754.1 1180.0 %all-reduce.15.cloned.1.call-start = ((), (), s32[]{:S(2)}) async-start(), calls=%async_computation.33 | async-start | bytes 196608 | tf_op jit(solution)/shard_map/psum | solution.py:421
  1756.1 156.4 %copy-start.72 = (f32[2,6144]{1,0:T(2,128)}, f32[2,6144]{1,0:T(2,128)S(1)}, u32[]{:S(2)}) copy-start(f32[2,6144]{1,0:T(2,128)S(1)} %maximum_dynamic-update-slice_fusion) | copy-start | bytes 147460
  2081.2 979.1 %all-reduce.11.cloned.1.call-start = ((), (), s32[]{:S(2)}) async-start(), calls=%async_computation.24 | async-start | bytes 147456 | tf_op jit(solution)/shard_map/psum | solution.py:421
  (128 other events, 2401.6 us)
Sparse Core Ops, SparseCore 0:
  10.2 198.3 all-gather.9
  211.3 50.2 all-gather.15
  263.8 107.3 all-gather.13
  373.2 44.5 all-gather.11
  545.7 58.3 reduce-scatter.23
  606.9 138.0 all-gather.21
  747.5 136.2 all-gather.19
  886.0 44.5 all-gather.17
  932.8 46.3 all-gather.23
  982.4 24.4 reduce-scatter.33
  1018.9 63.6 reduce-scatter.27
  1085.1 58.4 reduce-scatter.25
  1146.2 24.4 reduce-scatter.35
  1174.0 24.4 reduce-scatter.37
  1200.5 48.3 all-gather.25
  1465.9 24.8 reduce-scatter.39
  1493.3 58.3 reduce-scatter.29
  1578.0 20.7 reduce-scatter.41
  1610.4 298.1 all-reduce.12
  1912.1 162.4 reduce-scatter.31
  2077.7 22.3 reduce-scatter.43
  2105.9 699.1 all-reduce.16
  2812.9 121.1 all-reduce.14
  2941.0 119.2 all-reduce.10
where the time goes:
time: 3090 us; the launch traced here: 3070 us
  waiting for transfers between devices  2130 us (69%)
  matrix products  416 us (13%)
  local copies, waits for them, and re-layouts  268 us (9%)
  other arithmetic  183 us (6%)
  blocking collectives  52.9 us (2%)
    unnamed x32, waiting for transfers between devices  917 us
    psum x2, waiting for transfers between devices, on_device(): lax.psum((ada_bias_grad, qv_bias_grad, proj_bias_local, fc1_bias_grad, fc...  245 us
    all_gather x1, waiting for transfers between devices, on_device(): lax.all_gather(ada_weight, 'dp', axis=2, tiled=True)  196 us
    reduce_scatter x1, waiting for transfers between devices, on_device(): lax.psum_scatter(fc1_grad.astype(jnp.bfloat16), 'dp', scatter_dimension=1...  161 us
    all_gather x4, waiting for transfers between devices, gather_tokens(): lax.all_gather(image_part, 'tensor', axis=1, tiled=True)  151 us
    unnamed x314, local copies, waits for them, and re-layouts  126 us
    all_gather x1, waiting for transfers between devices, on_device(): lax.all_gather(fc2_weight, 'dp', axis=2, tiled=True)  125 us
    reduce_scatter x4, waiting for transfers between devices, scatter_tokens(): lax.psum_scatter(image_part.astype(jnp.bfloat16), 'tensor', scatter_dimen...  123 us
  transfers between devices with their start and end apart: 24, of which 20 were waited for; matrix products, arithmetic and copies ran while one was open for 15% of the time, Pallas kernels for 0%

commit v1 on v0

v1 whole, which is shorter than its diff:
```python
import math

import jax
import jax.numpy as jnp
from jax import lax
from jax.sharding import PartitionSpec as P

HEAD_DIM = 64
EPSILON = 1e-06
F32 = jnp.float32
BF16 = jnp.bfloat16


def hop(value, axis, mask, size):
    return lax.ppermute(value, axis, [(i, i ^ mask) for i in range(size)])


def spread_rows(rows, axis, size):
    mask = 1
    while mask < size:
        rows = jnp.concatenate([rows, hop(rows, axis, mask, size)], 0)
        mask *= 2
    return rows


def collect_rows(parts, axis, size):
    mask = size // 2
    while mask >= 1:
        half = parts.shape[0] // 2
        parts = parts[:half] + hop(parts[half:], axis, mask, size)
        mask //= 2
    return parts


def add_all(value, axis, size):
    mask = 1
    while mask < size:
        value = value + hop(value, axis, mask, size)
        mask *= 2
    return value


class Ring:
    def __init__(self, size):
        self.size = size
        self.order = list(range(0, size, 2)) + list(range(size - 1, 0, -2))
        self.ahead = [(self.order[i], self.order[(i + 1) % size]) for i in range(size)]
        self.back = [(b, a) for a, b in self.ahead]
        place = [0] * size
        for position, device in enumerate(self.order):
            place[device] = position
        self.mine = jnp.asarray(place, jnp.int32)[lax.axis_index("dp")]
        self.table = jnp.asarray(self.order, jnp.int32)

    def device(self, distance):
        return self.table[(self.mine + distance) % self.size]

    def forward(self, value):
        return lax.ppermute(value, "dp", self.ahead)

    def backward(self, value):
        return lax.ppermute(value, "dp", self.back)

    def gather(self, shard):
        half = self.size // 2
        pieces = [(self.device(0), 0, shard)]
        ahead = back = shard
        for step in range(1, half):
            ahead, back = self.forward(ahead), self.backward(back)
            pieces.append((self.device(-step), 0, ahead))
            pieces.append((self.device(step), 0, back))
        pieces.append((self.device(half), 0, self.forward(ahead[:1])))
        pieces.append((self.device(half), 1, self.backward(back[1:])))
        return pieces

    def scatter(self, chunk):
        half = self.size // 2
        far = chunk(self.device(half))
        ahead, back = self.forward(far[:1]), self.backward(far[1:])
        for step in range(half - 1, 0, -1):
            mine_a, mine_b = chunk(self.device(step)), chunk(self.device(-step))
            if step == half - 1:
                sum_a = jnp.concatenate(
                    [mine_a[:1].astype(F32) + ahead.astype(F32), mine_a[1:].astype(F32)], 0
                )
                sum_b = jnp.concatenate(
                    [mine_b[:1].astype(F32), mine_b[1:].astype(F32) + back.astype(F32)], 0
                )
            else:
                sum_a = mine_a.astype(F32) + ahead.astype(F32)
                sum_b = mine_b.astype(F32) + back.astype(F32)
            ahead, back = self.forward(sum_a.astype(BF16)), self.backward(sum_b.astype(BF16))
        return chunk(self.device(0)).astype(F32) + ahead.astype(F32) + back.astype(F32)


def assemble(pieces, axis, size):
    shape = list(pieces[0][2].shape)
    shape.insert(axis, size)
    full = jnp.zeros(shape, pieces[0][2].dtype)
    for device, stream, piece in pieces:
        starts = [jnp.int32(0)] * len(shape)
        starts[0] = jnp.int32(stream)
        starts[axis] = device
        full = lax.dynamic_update_slice(full, jnp.expand_dims(piece, axis), starts)
    return full


def gather_tokens(part):
    across = hop(part, "tensor", 2, 4)
    beside = hop(part, "tensor", 1, 4)
    corner = hop(across, "tensor", 1, 4)
    full = jnp.stack([part, beside, across, corner], 1)
    return full.reshape(part.shape[0], -1, part.shape[2])


def scatter_tokens(partial):
    blocks = partial.reshape(partial.shape[0], 4, -1, partial.shape[2])
    corner = hop(blocks[:, 3], "tensor", 1, 4)
    beside = hop(blocks[:, 1], "tensor", 1, 4)
    send = (blocks[:, 2].astype(F32) + corner.astype(F32)).astype(BF16)
    across = hop(send, "tensor", 2, 4)
    return blocks[:, 0].astype(F32) + beside.astype(F32) + across.astype(F32)


def normalize(values):
    average = jnp.mean(values, -1, keepdims=True)
    centred = values - average
    spread = jnp.mean(centred * centred, -1, keepdims=True)
    inverse = lax.rsqrt(spread + EPSILON)
    return centred * inverse, inverse


def norm_back(grad, normed, inverse, scale_vec):
    scaled = grad * (1.0 + scale_vec[:, None, :])
    input_grad = inverse * (
        scaled
        - jnp.mean(scaled, -1, keepdims=True)
        - normed * jnp.mean(scaled * normed, -1, keepdims=True)
    )
    return input_grad, jnp.sum(grad, 1), jnp.sum(grad * normed, 1)


def gelu_tanh(values):
    return jax.nn.gelu(values, approximate=True)


def split_heads(matrix):
    return matrix.reshape(matrix.shape[0], matrix.shape[1] // HEAD_DIM, HEAD_DIM)


def dot(spec, a, b):
    return jnp.einsum(spec, a, b, preferred_element_type=F32)


def attend(query_block, key_block, value_block):
    factor = 1.0 / math.sqrt(HEAD_DIM)
    query_heads = split_heads(query_block)
    key_heads = split_heads(key_block)
    value_heads = split_heads(value_block)
    scores = dot("qhe,khe->hqk", query_heads, key_heads) * factor
    row_top = jnp.max(scores, -1, keepdims=True)
    total_log = row_top + jnp.log(jnp.sum(jnp.exp(scores - row_top), -1, keepdims=True))
    attn_probs = jnp.exp(scores - total_log).astype(BF16)
    output = dot("hqk,khe->qhe", attn_probs, value_heads)
    return (output.reshape(query_block.shape).astype(BF16), total_log)


def attend_back(query_block, key_block, value_block, total_log, out_grad):
    factor = 1.0 / math.sqrt(HEAD_DIM)
    query_heads = split_heads(query_block)
    key_heads = split_heads(key_block)
    value_heads = split_heads(value_block)
    grad_heads = split_heads(out_grad)
    scores = dot("qhe,khe->hqk", query_heads, key_heads) * factor
    attn_probs = jnp.exp(scores - total_log)
    prob_grad = dot("qhe,khe->hqk", grad_heads, value_heads)
    row_inner = jnp.sum(attn_probs * prob_grad, -1, keepdims=True)
    score_grad = (attn_probs * (prob_grad - row_inner)).astype(BF16)
    query_grad = dot("hqk,khe->qhe", score_grad, key_heads) * factor
    key_grad = dot("hqk,qhe->khe", score_grad, query_heads) * factor
    value_grad = dot("hqk,qhe->khe", attn_probs.astype(BF16), grad_heads)
    flat_shape = query_block.shape
    return jnp.stack(
        [
            query_grad.reshape(flat_shape),
            key_grad.reshape(flat_shape),
            value_grad.reshape(flat_shape),
        ]
    ).astype(BF16)


def on_device(
    groups,
    image_tokens,
    text_tokens,
    conditioning,
    group_seqs,
    ada_weight,
    ada_bias,
    qkv_weight,
    qv_bias,
    proj_weight,
    proj_bias,
    fc1_weight,
    fc1_bias,
    fc2_weight,
    fc2_bias,
    image_cot,
    text_cot,
):
    column = lax.axis_index("tensor")
    group = lax.axis_index("dp")
    ring = Ring(groups)
    slots = image_tokens.shape[0]
    width = image_tokens.shape[2]
    rows = qkv_weight.shape[2]
    col_width = qkv_weight.shape[-1]
    hidden = fc1_weight.shape[-1]

    qkv_pieces = ring.gather(qkv_weight)
    proj_turned = jnp.swapaxes(proj_weight, 1, 2)
    fc2_turned = jnp.swapaxes(fc2_weight, 1, 2)
    _, _, proj_turned, fc1_shard = lax.optimization_barrier(
        (qkv_pieces[-1][2], qkv_pieces[-2][2], proj_turned, fc1_weight)
    )
    proj_pieces = ring.gather(proj_turned)
    fc1_pieces = ring.gather(fc1_shard)
    _, _, fc2_turned = lax.optimization_barrier(
        (fc1_pieces[-4][2], fc1_pieces[-3][2], fc2_turned)
    )
    fc2_pieces = ring.gather(fc2_turned)
    qkv_full = assemble(qkv_pieces, 2, groups).reshape(2, 3, width, col_width)
    proj_full = assemble(proj_pieces, 1, groups).reshape(2, width, col_width)
    fc1_full = assemble(fc1_pieces, 1, groups).reshape(2, width, hidden)
    fc2_full = assemble(fc2_pieces, 1, groups).reshape(2, width, hidden)

    ada_part = lax.dynamic_slice_in_dim(ada_bias.astype(F32), column * col_width, col_width, 2)
    qv_part = lax.dynamic_slice_in_dim(qv_bias.astype(F32), column * col_width, col_width, 2)
    fc1_part = lax.dynamic_slice_in_dim(fc1_bias.astype(F32), column * hidden, hidden, 1)
    proj_add = proj_bias.astype(F32)
    fc2_add = fc2_bias.astype(F32)
    live_mask = (jnp.arange(slots, dtype=jnp.int32) < group_seqs[0]).astype(F32)[:, None, None]

    cond_act, silu_back = jax.vjp(jax.nn.silu, conditioning.astype(F32))
    cond_all = spread_rows(cond_act.astype(BF16), "dp", groups)
    cond_rows = lax.dynamic_index_in_dim(
        cond_all.reshape(-1, groups, rows), group, 1, keepdims=False
    )
    modul_parts = dot("cd,sjdn->csjn", cond_rows, ada_weight)
    modul_local = collect_rows(modul_parts, "dp", groups) + ada_part[None]
    modulation = lax.all_gather(modul_local, "tensor", axis=3, tiled=True)

    streams = (image_tokens.astype(F32), text_tokens.astype(F32))
    out_grad = [image_cot.astype(F32) * live_mask, text_cot.astype(F32) * live_mask]
    first_normed = [normalize(streams[s]) for s in range(2)]
    first_full = [
        gather_tokens(
            (
                first_normed[s][0] * (1.0 + modulation[:, s, 1][:, None, :])
                + modulation[:, s, 0][:, None, :]
            ).astype(BF16)
        )
        for s in range(2)
    ]
    mlp_round = [
        (out_grad[s] * modulation[:, s, 5][:, None, :]).astype(BF16) for s in range(2)
    ]
    mlp_full = [gather_tokens(mlp_round[s]) for s in range(2)]
    joined_list = []
    for s in range(2):
        projected = dot("cld,jdn->jcln", first_full[s], qkv_full[s])
        offsets = jnp.stack([qv_part[s, 0], jnp.zeros_like(qv_part[s, 0]), qv_part[s, 1]])
        joined_list.append((projected + offsets[:, None, None, :]).astype(BF16))
    joined = jnp.concatenate(joined_list, 2)
    attended_rows, totals = [], []
    for slot in range(slots):
        attended_slot, total_log = attend(joined[0, slot], joined[1, slot], joined[2, slot])
        attended_rows.append(attended_slot)
        totals.append(total_log)
    attended = jnp.stack(attended_rows)
    split_at = first_full[0].shape[1]
    pieces = (attended[:, :split_at], attended[:, split_at:])
    branches = [
        scatter_tokens(dot("cln,dn->cld", pieces[s], proj_full[s]).astype(BF16)) + proj_add[s]
        for s in range(2)
    ]
    after_attn = [
        streams[s] + modulation[:, s, 2][:, None, :] * branches[s] for s in range(2)
    ]
    second_normed = [normalize(after_attn[s]) for s in range(2)]
    second_full = [
        gather_tokens(
            (
                second_normed[s][0] * (1.0 + modulation[:, s, 4][:, None, :])
                + modulation[:, s, 3][:, None, :]
            ).astype(BF16)
        )
        for s in range(2)
    ]
    activated, pre_round, fc1_grad, fc2_grad = [], [], [], []
    for s in range(2):
        pre_act = dot("cld,df->clf", second_full[s], fc1_full[s]) + fc1_part[s]
        act, gelu_back = jax.vjp(gelu_tanh, pre_act)
        activated.append(act.astype(BF16))
        act_grad = dot("cld,df->clf", mlp_full[s], fc2_full[s])
        pre_round.append(gelu_back(act_grad)[0].astype(BF16))
    fc2_grad = jnp.stack(
        [dot("cld,clf->df", mlp_full[s], activated[s]).astype(BF16) for s in range(2)]
    ).reshape(2, groups, rows, hidden)
    fc2_sum = ring.scatter(lambda d: lax.dynamic_index_in_dim(fc2_grad, d, 1, keepdims=False))
    fc1_grad = jnp.stack(
        [dot("cld,clf->df", second_full[s], pre_round[s]).astype(BF16) for s in range(2)]
    ).reshape(2, groups, rows, hidden)
    fc1_sum = ring.scatter(lambda d: lax.dynamic_index_in_dim(fc1_grad, d, 1, keepdims=False))
    second_grad = [
        scatter_tokens(dot("clf,df->cld", pre_round[s], fc1_full[s]).astype(BF16))
        for s in range(2)
    ]
    mlp_out = [
        scatter_tokens(dot("clf,df->cld", activated[s], fc2_full[s]).astype(BF16)) + fc2_add[s]
        for s in range(2)
    ]
    outs = [
        (
            (after_attn[s] + modulation[:, s, 5][:, None, :] * mlp_out[s]) * live_mask
        ).astype(BF16)
        for s in range(2)
    ]
    gate_two = [jnp.sum(out_grad[s] * mlp_out[s], 1) for s in range(2)]
    fc2_bias_local = jnp.stack([jnp.sum(mlp_round[s].astype(F32), (0, 1)) for s in range(2)])
    fc1_bias_local = jnp.stack([jnp.sum(pre_round[s].astype(F32), (0, 1)) for s in range(2)])

    residual_grads, shift_two, scale_two, gate_one, branch_round = [], [], [], [], []
    for s in range(2):
        input_part, shift_part, scale_part = norm_back(
            second_grad[s], second_normed[s][0], second_normed[s][1], modulation[:, s, 4]
        )
        residual = out_grad[s] + input_part
        residual_grads.append(residual)
        shift_two.append(shift_part)
        scale_two.append(scale_part)
        gate_one.append(jnp.sum(residual * branches[s], 1))
        branch_round.append((residual * modulation[:, s, 2][:, None, :]).astype(BF16))
    branch_full = [gather_tokens(branch_round[s]) for s in range(2)]
    proj_bias_local = jnp.stack([jnp.sum(branch_round[s].astype(F32), (0, 1)) for s in range(2)])
    attended_grad = jnp.concatenate(
        [dot("cld,dn->cln", branch_full[s], proj_full[s]) for s in range(2)], 1
    ).astype(BF16)
    proj_grad = jnp.stack(
        [dot("cld,cln->dn", branch_full[s], pieces[s]).astype(BF16) for s in range(2)]
    ).reshape(2, groups, rows, col_width)
    proj_sum = ring.scatter(lambda d: lax.dynamic_index_in_dim(proj_grad, d, 1, keepdims=False))
    qkv_rows = [
        attend_back(
            joined[0, slot], joined[1, slot], joined[2, slot], totals[slot], attended_grad[slot]
        )
        for slot in range(slots)
    ]
    qkv_round = jnp.stack(qkv_rows, 1)
    qkv_parts = (qkv_round[:, :, :split_at], qkv_round[:, :, split_at:])
    first_grad = [
        scatter_tokens(dot("jcln,jdn->cld", qkv_parts[s], qkv_full[s]).astype(BF16))
        for s in range(2)
    ]
    qkv_grad = jnp.stack(
        [dot("cld,jcln->jdn", first_full[s], qkv_parts[s]).astype(BF16) for s in range(2)]
    ).reshape(2, 3, groups, rows, col_width)
    qkv_sum = ring.scatter(lambda d: lax.dynamic_index_in_dim(qkv_grad, d, 2, keepdims=False))
    qv_bias_local = jnp.stack(
        [jnp.sum(qkv_parts[s][0::2].astype(F32), (1, 2)) for s in range(2)]
    )
    input_grads, modul_grads = [], []
    for s in range(2):
        input_part, shift_part, scale_part = norm_back(
            first_grad[s], first_normed[s][0], first_normed[s][1], modulation[:, s, 1]
        )
        input_grads.append(residual_grads[s] + input_part)
        modul_grads.append(
            jnp.stack(
                [
                    shift_part,
                    scale_part,
                    gate_one[s],
                    shift_two[s],
                    scale_two[s],
                    gate_two[s],
                ],
                1,
            )
        )
    modul_grad = jnp.stack(modul_grads, 1).reshape(slots, 2, 6, 4, col_width)
    modul_blocks = jnp.stack(
        [
            lax.dynamic_index_in_dim(modul_grad, column ^ mask, 3, keepdims=False)
            for mask in range(4)
        ]
    )
    modul_round = collect_rows(modul_blocks, "tensor", 4)[0].astype(BF16)
    modul_all = spread_rows(modul_round, "dp", groups)
    ada_grad = dot("cd,csjn->sjdn", cond_rows, modul_all)
    ada_bias_part = jnp.sum(modul_all.astype(F32), 0)
    cond_part = add_all(dot("csjn,sjdn->cd", modul_all, ada_weight), "tensor", 4)
    cond_blocks = cond_part.reshape(groups, slots, rows)
    cond_terms = spread_rows(cond_blocks[None], "dp", groups)
    masks = jnp.arange(groups, dtype=jnp.int32)
    cond_term = jnp.stack(
        [
            lax.dynamic_index_in_dim(
                lax.dynamic_index_in_dim(cond_terms, group ^ d, 0, keepdims=False),
                group ^ d,
                0,
                keepdims=False,
            )
            for d in range(groups)
        ],
        1,
    ).reshape(slots, width)
    del masks
    cond_grad = lax.dynamic_slice_in_dim(
        silu_back(cond_term)[0], column * col_width, col_width, 1
    )

    split_sums = jnp.concatenate([qv_bias_local.reshape(-1), fc1_bias_local.reshape(-1)])
    token_sums = jnp.concatenate([proj_bias_local.reshape(-1), fc2_bias_local.reshape(-1)])
    bias_local = add_all(jnp.concatenate([split_sums, token_sums]), "dp", groups)
    bias_local = jnp.concatenate([bias_local, ada_bias_part.reshape(-1)])
    bias_all = lax.all_gather(bias_local, "tensor")
    cut_a = qv_bias_local.size
    cut_b = cut_a + fc1_bias_local.size
    cut_c = cut_b + proj_bias_local.size
    cut_d = cut_c + fc2_bias_local.size

    def by_column(block, shape):
        return jnp.moveaxis(block.reshape((4,) + shape), 0, -2).reshape(
            shape[:-1] + (4 * shape[-1],)
        )

    qv_bias_grad = by_column(bias_all[:, :cut_a], qv_bias_local.shape)
    fc1_bias_grad = by_column(bias_all[:, cut_a:cut_b], fc1_bias_local.shape)
    proj_bias_grad = jnp.sum(bias_all[:, cut_b:cut_c], 0).reshape(proj_bias_local.shape)
    fc2_bias_grad = jnp.sum(bias_all[:, cut_c:cut_d], 0).reshape(fc2_bias_local.shape)
    ada_bias_grad = by_column(bias_all[:, cut_d:], ada_bias_part.shape)
    return (
        outs[0],
        outs[1],
        input_grads[0],
        input_grads[1],
        cond_grad,
        ada_grad,
        ada_bias_grad,
        qkv_sum,
        qv_bias_grad,
        jnp.swapaxes(proj_sum, 1, 2),
        proj_bias_grad,
        fc1_sum,
        fc1_bias_grad,
        jnp.swapaxes(fc2_sum, 1, 2),
        fc2_bias_grad,
    )


def solution(mesh):
    groups = mesh.shape["dp"]
    in_specs = (
        P("dp", "tensor", None),
        P("dp", "tensor", None),
        P("dp", None),
        P("dp"),
        P(None, None, "dp", "tensor"),
        P(),
        P(None, None, "dp", "tensor"),
        P(),
        P(None, "tensor", "dp"),
        P(),
        P(None, "dp", "tensor"),
        P(),
        P(None, "tensor", "dp"),
        P(),
        P("dp", "tensor", None),
        P("dp", "tensor", None),
    )
    out_specs = (
        P("dp", "tensor", None),
        P("dp", "tensor", None),
        P("dp", "tensor", None),
        P("dp", "tensor", None),
        P("dp", "tensor"),
        P(None, None, "dp", "tensor"),
        P(),
        P(None, None, "dp", "tensor"),
        P(),
        P(None, "tensor", "dp"),
        P(),
        P(None, "dp", "tensor"),
        P(),
        P(None, "tensor", "dp"),
        P(),
    )

    def step(*args):
        return on_device(groups, *args)

    return jax.shard_map(
        step, mesh=mesh, in_specs=in_specs, out_specs=out_specs, check_vma=False
    )
```

time: 3090 us -> 1270 us (0.41)
  waiting for transfers between devices: 2130 us -> 344 us
  starting transfers between devices: 1.17 us -> 128 us
  local copies, waits for them, and re-layouts: 268 us -> 160 us
  blocking collectives: 52.9 us -> 11.4 us
  matrix products: 416 us -> 384 us
    unnamed x32 -> x0, waiting for transfers between devices: 917 us -> none
    all_gather x9 -> x0, waiting for transfers between devices: 688 us -> none  [the longest x1 196 us: on_device(): lax.all_gather(ada_weight, 'dp', axis=2, tiled=True)]
    ppermute x0 -> x131, waiting for transfers between devices: none -> 344 us  [the longest x32 150 us: backward(): return lax.ppermute(value, 'dp', self.back)]
    reduce_scatter x5 -> x0, waiting for transfers between devices: 284 us -> none  [the longest x1 161 us: on_device(): lax.psum_scatter(fc1_grad.astype(jnp.bfloat16), 'dp', scatter_dimension=1...]
    psum x2 -> x0, waiting for transfers between devices: 245 us -> none  [on_device(): lax.psum((ada_bias_grad, qv_bias_grad, proj_bias_local, fc1_bias_grad, fc...]
    ppermute x0 -> x131, starting transfers between devices: none -> 128 us  [the longest x67 56.3 us: hop(): return lax.ppermute(value, axis, [(i, i ^ mask) for i in range(size)])]
    unnamed x314 -> x391, local copies, waits for them, and re-layouts: 126 us -> 14 us
    dynamic_update_slice x1 -> x36, local copies, waits for them, and re-layouts: 0.02 us -> 46 us  [assemble(): full = lax.dynamic_update_slice(full, jnp.expand_dims(piece, axis), starts)]
  transfers between devices with their start and end apart: 24 -> 131, of which waited for: 20 -> 56; matrix products, arithmetic and copies ran while one was open for 15% -> 50% of each run, Pallas kernels for 0% -> 0%
where the time goes in v1:
time: 1270 us; the launch traced here: 1260 us
  matrix products  384 us (30%)
  waiting for transfers between devices  344 us (27%)
  other arithmetic  203 us (16%)
  local copies, waits for them, and re-layouts  160 us (13%)
  starting transfers between devices  128 us (10%)
  between operations  26.9 us (2%)
    dot_general x39, matrix products, dot(): return jnp.einsum(spec, a, b, preferred_element_type=F32)  384 us
    ppermute x32, waiting for transfers between devices, backward(): return lax.ppermute(value, 'dp', self.back)  150 us
    ppermute x67, waiting for transfers between devices, hop(): return lax.ppermute(value, axis, [(i, i ^ mask) for i in range(size)])  132 us
    ppermute x32, waiting for transfers between devices, forward(): return lax.ppermute(value, 'dp', self.ahead)  61.8 us
    convert_element_type x2, other arithmetic, attend_back(): score_grad = (attn_probs * (prob_grad - row_inner)).astype(BF16)  60.2 us
    ppermute x67, starting transfers between devices, hop(): return lax.ppermute(value, axis, [(i, i ^ mask) for i in range(size)])  56.3 us
    dynamic_update_slice x36, local copies, waits for them, and re-layouts, assemble(): full = lax.dynamic_update_slice(full, jnp.expand_dims(piece, axis), starts)  46 us
    ppermute x32, starting transfers between devices, backward(): return lax.ppermute(value, 'dp', self.back)  45.4 us
  transfers between devices with their start and end apart: 131, of which 56 were waited for; matrix products, arithmetic and copies ran while one was open for 50% of the time, Pallas kernels for 0%

profile of v1, /device:TPU:0, one launch (start us, length us, event | category | flops | bytes accessed | tf_op | source)
XLA Modules:
  0.0 1256.7 jit_solution(9807688208767369121)
XLA Ops:
  93.7 12.3 collective-permute-done.9
  114.4 10.7 collective-permute-done.15
  181.1 14.3 %fusion.208 = (f32[6,1184]{1,0:T(8,128)S(1)}, f32[6,1184,1184]{1,2,0:T(8,128)}) fusion(bf16[1184,6,64]{0,2,1:T(8,128)(2,1)S(1)} %bitcast.912, bf16[1184,6,64]{0,2,1:T(8,128)(2,1)S(1)} %bitcast.924), kind=kOutput, calls=%fused_computation.623 | convolution fusion | flops 1093440512 | bytes 35491584 | tf_op jit(solution)/shard_map/qhe,khe->hqk/dot_general | solution.py:152
  195.4 14.5 %exponential_reduce_fusion = f32[6,1184]{1,0:T(8,128)S(1)} fusion(f32[6,1184,1184]{1,2,0:T(8,128)} %get-tuple-element.187, f32[6,1184]{1,0:T(8,128)S(1)} %get-tuple-element.186), kind=kLoop, calls=%fused_computation.7 | loop fusion | flops 16815168 | bytes 33701376 | tf_op jit(solution)/shard_map/reduce_sum | solution.py:162
  209.9 14.2 %fusion.207 = (f32[6,1184]{1,0:T(8,128)S(1)}, f32[6,1184,1184]{1,2,0:T(8,128)}) fusion(bf16[1184,6,64]{0,2,1:T(8,128)(2,1)S(1)} %bitcast.910, bf16[1184,6,64]{0,2,1:T(8,128)(2,1)S(1)} %bitcast.922), kind=kOutput, calls=%fused_computation.622 | convolution fusion | flops 1093440512 | bytes 35491584 | tf_op jit(solution)/shard_map/qhe,khe->hqk/dot_general | solution.py:152
  224.1 14.5 %exponential_reduce_fusion.1 = f32[6,1184]{1,0:T(8,128)S(1)} fusion(f32[6,1184,1184]{1,2,0:T(8,128)} %get-tuple-element.185, f32[6,1184]{1,0:T(8,128)S(1)} %get-tuple-element.184), kind=kLoop, calls=%fused_computation.9 | loop fusion | flops 16815168 | bytes 33701376 | tf_op jit(solution)/shard_map/reduce_sum | solution.py:162
  238.6 22.9 %fusion.56 = bf16[6,64,1184]{2,1,0:T(8,128)(2,1)S(1)} fusion(bf16[1184,6,64]{0,2,1:T(8,128)(2,1)S(1)} %bitcast.916, f32[6,1184,1184]{1,2,0:T(8,128)} %get-tuple-element.187, f32[6,1184]{1,0:T(8,128)S(1)} %log_add_fusion), kind=kOutput, calls=%fused_computation.188 | convolution fusion | flops 1093902336 | bytes 35491584 | tf_op jit(solution)/shard_map/hqk,khe->qhe/dot_general | solution.py:152
  261.6 15.1 %fusion.50 = bf16[6,64,1184]{2,1,0:T(8,128)(2,1)} fusion(bf16[1184,6,64]{0,2,1:T(8,128)(2,1)S(1)} %bitcast.914, f32[6,1184,1184]{1,2,0:T(8,128)} %get-tuple-element.185, f32[6,1184]{1,0:T(8,128)S(1)} %log_add_fusion.1), kind=kOutput, calls=%fused_computation.186 | convolution fusion | flops 1093902336 | bytes 35491584 | tf_op jit(solution)/shard_map/hqk,khe->qhe/dot_general | solution.py:152
  349.4 20.0 %collective-permute-done.39 = bf16[2,192,1536]{2,1,0:T(8,128)(2,1)S(1)} collective-permute-done((bf16[2,192,1536]{2,1,0:T(8,128)(2,1)S(1)}, bf16[2,192,1536]{2,1,0:T(8,128)(2,1)S(1)}, u32[]{:S(2)}, u32[]{:S(2)}) %collective-permute-start.39) | collective-permute-done | bytes 1179680 | tf_op jit(solution)/shard_map/ppermute | solution.py:62
  416.8 18.6 %collective-permute-done.45 = bf16[2,192,1536]{2,1,0:T(8,128)(2,1)S(1)} collective-permute-done((bf16[2,192,1536]{2,1,0:T(8,128)(2,1)}, bf16[2,192,1536]{2,1,0:T(8,128)(2,1)S(1)}, u32[]{:S(2)}, u32[]{:S(2)}) %collective-permute-start.45) | collective-permute-done | bytes 1179680 | tf_op jit(solution)/shard_map/ppermute | solution.py:62
  467.6 17.0 %fusion.209 = f32[2,1024,1536]{2,1,0:T(8,128)} fusion(bf16[2,1024,1536]{2,1,0:T(8,128)(2,1)S(1)} %bitcast.956, bf16[1536,1536,1]{1,0,2:T(8,128)(2,1)} %bitcast.970), kind=kOutput, calls=%fused_computation.624 | convolution fusion | flops 9663676416 | bytes 23592960 | tf_op jit(solution)/shard_map/cld,df->clf/dot_general | solution.py:152
  484.6 13.6 %bitcast_convert_fusion.2 = bf16[1536,1536]{1,0:T(8,128)(2,1)S(1)} fusion(bf16[2,1024,1536]{2,1,0:T(8,128)(2,1)S(1)} %bitcast.955, f32[2,1024,1536]{2,1,0:T(8,128)} %fusion.209, f32[1536]{0:T(1024)S(1)} %copy-done.153), kind=kOutput, calls=%fused_computation.78 | convolution fusion | flops 9697492992 | bytes 23599104 | tf_op jit(solution)/shard_map/cld,clf->df/dot_general | solution.py:152
  521.3 26.5 %convert_reduce_fusion = (f32[1536]{0:T(1024)S(1)}, bf16[2,1024,1536]{2,1,0:T(8,128)(2,1)}) fusion(f32[2,1024,1536]{2,1,0:T(8,128)} %fusion.209, f32[1536]{0:T(1024)S(1)} %copy-done.153, bf16[2,1024,1536]{2,1,0:T(8,128)(2,1)} %bitcast.952, bf16[1536,1536,1]{1,0,2:T(8,128)(2,1)} %bitcast.976), kind=kOutput, calls=%fused_computation.70 | convolution fusion | flops 9736026112 | bytes 29896704 | tf_op jit(solution)/shard_map/cld,df->clf/dot_general | solution.py:152
  547.8 17.5 %convolution_convert_fusion.1 = bf16[2,1024,1536]{2,1,0:T(8,128)(2,1)} fusion(bf16[1536,1536,1]{1,0,2:T(8,128)(2,1)} %bitcast.977, f32[2,1024,1536]{2,1,0:T(8,128)} %fusion.209, f32[1536]{0:T(1024)S(1)} %copy-done.153), kind=kOutput, calls=%fused_computation.96 | convolution fusion | flops 9698279424 | bytes 23599104 | tf_op jit(solution)/shard_map/clf,df->cld/dot_general | solution.py:152
  565.4 15.6 %bitcast_convert_fusion.4 = bf16[1536,1536]{1,0:T(8,128)(2,1)} fusion(bf16[2,1024,1536]{2,1,0:T(8,128)(2,1)} %bitcast.957, bf16[2,1024,1536]{2,1,0:T(8,128)(2,1)} %get-tuple-element.195), kind=kOutput, calls=%fused_computation.80 | convolution fusion | flops 9666035712 | bytes 17301504 | tf_op jit(solution)/shard_map/cld,clf->df/dot_general | solution.py:152
  581.0 15.6 %convolution_convert_fusion = bf16[2,1024,1536]{2,1,0:T(8,128)(2,1)} fusion(bf16[2,1024,1536]{2,1,0:T(8,128)(2,1)} %get-tuple-element.195, bf16[1536,1536,1]{1,0,2:T(8,128)(2,1)} %bitcast.971), kind=kOutput, calls=%fused_computation.95 | convolution fusion | flops 9666822144 | bytes 17301504 | tf_op jit(solution)/shard_map/clf,df->cld/dot_general | solution.py:152
  658.5 14.2 %collective-permute-done.120 = bf16[2,192,1536]{2,1,0:T(8,128)(2,1)S(1)} collective-permute-done((bf16[2,192,1536]{2,1,0:T(8,128)(2,1)}, bf16[2,192,1536]{2,1,0:T(8,128)(2,1)S(1)}, u32[]{:S(2)}, u32[]{:S(2)}) %collective-permute-start.120) | collective-permute-done | bytes 1179680 | tf_op jit(solution)/shard_map/ppermute | solution.py:62
  695.0 25.0 %collective-permute-done.52 = bf16[2,256,1536]{2,1,0:T(8,128)(2,1)} collective-permute-done((bf16[2,256,1536]{2,1,0:T(8,128)(2,1)}, bf16[2,256,1536]{2,1,0:T(8,128)(2,1)}, u32[]{:S(2)}, u32[]{:S(2)}) %collective-permute-start.52) | collective-permute-done | bytes 1572896 | tf_op jit(solution)/shard_map/ppermute | solution.py:15
  748.6 14.3 %collective-permute-done.125 = bf16[2,192,1536]{2,1,0:T(8,128)(2,1)} collective-permute-done((bf16[2,192,1536]{2,1,0:T(8,128)(2,1)}, bf16[2,192,1536]{2,1,0:T(8,128)(2,1)}, u32[]{:S(2)}, u32[]{:S(2)}) %collective-permute-start.125) | collective-permute-done | bytes 1179680 | tf_op jit(solution)/shard_map/ppermute | solution.py:59
  772.4 15.8 %collective-permute-done.118 = bf16[2,192,1536]{2,1,0:T(8,128)(2,1)} collective-permute-done((bf16[2,192,1536]{2,1,0:T(8,128)(2,1)}, bf16[2,192,1536]{2,1,0:T(8,128)(2,1)}, u32[]{:S(2)}, u32[]{:S(2)}) %collective-permute-start.118) | collective-permute-done | bytes 1179680 | tf_op jit(solution)/shard_map/ppermute | solution.py:59
  808.8 15.7 %fusion.59 = bf16[6,64,1184]{2,1,0:T(8,128)(2,1)} fusion(bf16[1184,6,64]{0,2,1:T(8,128)(2,1)} %bitcast.918, f32[6,1184,1184]{1,2,0:T(8,128)} %get-tuple-element.187, f32[6,1184]{1,0:T(8,128)S(1)} %copy-done.41), kind=kOutput, calls=%fused_computation.189 | convolution fusion | flops 1093902336 | bytes 35491584 | tf_op jit(solution)/shard_map/hqk,qhe->khe/dot_general | solution.py:152
  824.5 26.8 %multiply_reduce_fusion = (f32[6,1184]{1,0:T(8,128)S(1)}, f32[6,1184,1184]{1,2,0:T(8,128)}) fusion(f32[6,1184,1184]{1,2,0:T(8,128)} %get-tuple-element.187, f32[6,1184]{1,0:T(8,128)S(1)} %copy-done.41, bf16[1184,6,64]{0,2,1:T(8,128)(2,1)} %bitcast.919, bf16[1184,6,64]{0,2,1:T(8,128)(2,1)S(1)} %bitcast.917), kind=kOutput, calls=%fused_computation.3 | convolution fusion | flops 1101851648 | bytes 69164544 | tf_op jit(solution)/shard_map/qhe,khe->hqk/dot_general | solution.py:152
  851.4 30.2 %multiply_convert_fusion = bf16[6,1184,1184]{1,2,0:T(8,128)(2,1)} fusion(f32[6,1184,1184]{1,2,0:T(8,128)} %get-tuple-element.189, f32[6,1184,1184]{1,2,0:T(8,128)} %get-tuple-element.187, f32[6,1184]{1,0:T(8,128)S(1)} %get-tuple-element.188, f32[6,1184]{1,0:T(8,128)S(1)} %copy-done.41), kind=kLoop, calls=%fused_computation.2 | loop fusion | flops 33644544 | bytes 84168192 | tf_op jit(solution)/shard_map/convert_element_type | solution.py:178
  881.5 12.6 %fusion.49 = bf16[6,64,1184]{2,1,0:T(8,128)(2,1)} fusion(bf16[1184,6,64]{0,2,1:T(8,128)(2,1)S(1)} %bitcast.913, bf16[6,1184,1184]{1,2,0:T(8,128)(2,1)} %multiply_convert_fusion), kind=kOutput, calls=%fused_computation.185 | convolution fusion | flops 1077534720 | bytes 18640896 | tf_op jit(solution)/shard_map/hqk,qhe->khe/dot_general | solution.py:152
  894.2 10.7 fusion.48
  906.5 15.7 %fusion.53 = bf16[6,64,1184]{2,1,0:T(8,128)(2,1)} fusion(bf16[1184,6,64]{0,2,1:T(8,128)(2,1)} %bitcast.920, f32[6,1184,1184]{1,2,0:T(8,128)} %get-tuple-element.185, f32[6,1184]{1,0:T(8,128)S(1)} %copy-done.39), kind=kOutput, calls=%fused_computation.187 | convolution fusion | flops 1093902336 | bytes 35491584 | tf_op jit(solution)/shard_map/hqk,qhe->khe/dot_general | solution.py:152
  922.2 26.9 %multiply_reduce_fusion.1 = (f32[6,1184]{1,0:T(8,128)S(1)}, f32[6,1184,1184]{1,2,0:T(8,128)}) fusion(f32[6,1184,1184]{1,2,0:T(8,128)} %get-tuple-element.185, f32[6,1184]{1,0:T(8,128)S(1)} %copy-done.39, bf16[1184,6,64]{0,2,1:T(8,128)(2,1)} %bitcast.921, bf16[1184,6,64]{0,2,1:T(8,128)(2,1)S(1)} %bitcast.915), kind=kOutput, calls=%fused_computation.5 | convolution fusion | flops 1101851648 | bytes 69164544 | tf_op jit(solution)/shard_map/qhe,khe->hqk/dot_general | solution.py:152
  949.1 30.0 %multiply_convert_fusion.1 = bf16[6,1184,1184]{1,2,0:T(8,128)(2,1)} fusion(f32[6,1184,1184]{1,2,0:T(8,128)} %get-tuple-element.191, f32[6,1184,1184]{1,2,0:T(8,128)} %get-tuple-element.185, f32[6,1184]{1,0:T(8,128)S(1)} %get-tuple-element.190, f32[6,1184]{1,0:T(8,128)S(1)} %copy-done.39), kind=kLoop, calls=%fused_computation.4 | loop fusion | flops 33644544 | bytes 84168192 | tf_op jit(solution)/shard_map/convert_element_type | solution.py:178
  979.2 12.6 %fusion.47 = bf16[6,64,1184]{2,1,0:T(8,128)(2,1)} fusion(bf16[1184,6,64]{0,2,1:T(8,128)(2,1)S(1)} %bitcast.911, bf16[6,1184,1184]{1,2,0:T(8,128)(2,1)} %multiply_convert_fusion.1), kind=kOutput, calls=%fused_computation.183 | convolution fusion | flops 1077534720 | bytes 18640896 | tf_op jit(solution)/shard_map/hqk,qhe->khe/dot_general | solution.py:152
  1137.0 11.8 collective-permute-done.82
  1174.9 22.4 %collective-permute-done.130 = bf16[2,192,1536]{2,1,0:T(8,128)(2,1)S(1)} collective-permute-done((bf16[2,192,1536]{2,1,0:T(8,128)(2,1)S(1)}, bf16[2,192,1536]{2,1,0:T(8,128)(2,1)S(1)}, u32[]{:S(2)}, u32[]{:S(2)}) %collective-permute-start.130) | collective-permute-done | bytes 1179680 | tf_op jit(solution)/shard_map/ppermute | solution.py:62
  1203.4 12.1 collective-permute-done.88
  (957 shorter events, 669.9 us)
Async XLA Ops:
  0.7 83.2 %collective-permute-start.7 = (bf16[2,3,192,384]{3,2,1,0:T(8,128)(2,1)}, bf16[2,3,192,384]{3,2,1,0:T(8,128)(2,1)}, u32[]{:S(2)}, u32[]{:S(2)}) collective-permute-start(bf16[2,3,192,384]{3,2,1,0:T(8,128)(2,1)} %param.24), channel_id=1, source_target_pairs={{8,0},{16,8},{24,16},{28,24},{20,28},{12,20},{4,12},{0,4},{9,1},{1... | collective-permute-start | bytes 2654216 | tf_op jit(solution)/shard_map/ppermute | solution.py:62
  3.7 82.0 %collective-permute-start.6 = (bf16[2,3,192,384]{3,2,1,0:T(8,128)(2,1)}, bf16[2,3,192,384]{3,2,1,0:T(8,128)(2,1)}, u32[]{:S(2)}, u32[]{:S(2)}) collective-permute-start(bf16[2,3,192,384]{3,2,1,0:T(8,128)(2,1)} %param.24), channel_id=1, source_target_pairs={{0,8},{8,16},{16,24},{24,28},{28,20},{20,12},{12,4},{4,0},{1,9},{9... | collective-permute-start | bytes 2654216 | tf_op jit(solution)/shard_map/ppermute | solution.py:59
  91.7 72.3 %collective-permute-start.14 = (bf16[2,256,1536]{2,1,0:T(8,128)(2,1)S(1)}, bf16[2,256,1536]{2,1,0:T(8,128)(2,1)S(1)}, u32[]{:S(2)}, u32[]{:S(2)}) collective-permute-start(bf16[2,256,1536]{2,1,0:T(8,128)(2,1)S(1)} %copy-done.66), channel_id=1, source_target_pairs={{0,1},{1,0},{2,3},{3,2},{4,5},{5,4},{6,7},{7,6},{8,9},{9,8},{10,11... | collective-permute-start | bytes 4718600 | tf_op jit(solution)/shard_map/ppermute | solution.py:15
  92.2 68.5 %collective-permute-start.63 = (bf16[2,256,1536]{2,1,0:T(8,128)(2,1)}, bf16[2,256,1536]{2,1,0:T(8,128)(2,1)}, u32[]{:S(2)}, u32[]{:S(2)}) collective-permute-start(bf16[2,256,1536]{2,1,0:T(8,128)(2,1)} %get-tuple-element.46), channel_id=1, source_target_pairs={{0,2},{1,3},{2,0},{3,1},{4,6},{5,7},{6,4},{7,5},{8,10},{9,11},{10,... | collective-permute-start | bytes 4718600 | tf_op jit(solution)/shard_map/ppermute | solution.py:15
  125.1 39.4 %collective-permute-start.16 = (bf16[2,256,1536]{2,1,0:T(8,128)(2,1)S(1)}, bf16[2,256,1536]{2,1,0:T(8,128)(2,1)S(1)}, u32[]{:S(2)}, u32[]{:S(2)}) collective-permute-start(bf16[2,256,1536]{2,1,0:T(8,128)(2,1)S(1)} %collective-permute-done.15), channel_id=1, source_target_pairs={{0,1},{1,0},{2,3},{3,2},{4,5},{5,4},{6,7},{7,6},{8,9},{9,8},{10,11... | collective-permute-start | bytes 4718600 | tf_op jit(solution)/shard_map/ppermute | solution.py:15
  160.7 116.0 %collective-permute-start.62 = (bf16[2,256,1536]{2,1,0:T(8,128)(2,1)}, bf16[2,256,1536]{2,1,0:T(8,128)(2,1)}, u32[]{:S(2)}, u32[]{:S(2)}) collective-permute-start(bf16[2,256,1536]{2,1,0:T(8,128)(2,1)} %get-tuple-element.46), channel_id=1, source_target_pairs={{0,1},{1,0},{2,3},{3,2},{4,5},{5,4},{6,7},{7,6},{8,9},{9,8},{10,11... | collective-permute-start | bytes 4718600 | tf_op jit(solution)/shard_map/ppermute | solution.py:15
  160.8 116.4 %collective-permute-start.64 = (bf16[2,256,1536]{2,1,0:T(8,128)(2,1)}, bf16[2,256,1536]{2,1,0:T(8,128)(2,1)}, u32[]{:S(2)}, u32[]{:S(2)}) collective-permute-start(bf16[2,256,1536]{2,1,0:T(8,128)(2,1)} %collective-permute-done.63), channel_id=1, source_target_pairs={{0,1},{1,0},{2,3},{3,2},{4,5},{5,4},{6,7},{7,6},{8,9},{9,8},{10,11... | collective-permute-start | bytes 4718600 | tf_op jit(solution)/shard_map/ppermute | solution.py:15
  161.4 152.0 %collective-permute-start.35 = (bf16[2,192,1536]{2,1,0:T(8,128)(2,1)}, bf16[2,192,1536]{2,1,0:T(8,128)(2,1)}, u32[]{:S(2)}, u32[]{:S(2)}) collective-permute-start(bf16[2,192,1536]{2,1,0:T(8,128)(2,1)} %param.28), channel_id=1, source_target_pairs={{8,0},{16,8},{24,16},{28,24},{20,28},{12,20},{4,12},{0,4},{9,1},{1... | collective-permute-start | bytes 3538952 | tf_op jit(solution)/shard_map/ppermute | solution.py:62
  164.0 151.1 %collective-permute-start.34 = (bf16[2,192,1536]{2,1,0:T(8,128)(2,1)}, bf16[2,192,1536]{2,1,0:T(8,128)(2,1)}, u32[]{:S(2)}, u32[]{:S(2)}) collective-permute-start(bf16[2,192,1536]{2,1,0:T(8,128)(2,1)} %param.28), channel_id=1, source_target_pairs={{0,8},{8,16},{16,24},{24,28},{28,20},{20,12},{12,4},{4,0},{1,9},{9... | collective-permute-start | bytes 3538952 | tf_op jit(solution)/shard_map/ppermute | solution.py:59
  164.5 123.9 %collective-permute-start.23 = (bf16[2,192,384]{2,1,0:T(8,128)(2,1)}, bf16[2,192,384]{2,1,0:T(8,128)(2,1)}, u32[]{:S(2)}, u32[]{:S(2)}) collective-permute-start(bf16[2,192,384]{2,1,0:T(8,128)(2,1)} %collective-permute-done.21), channel_id=1, source_target_pairs={{8,0},{16,8},{24,16},{28,24},{20,28},{12,20},{4,12},{0,4},{9,1},{1... | collective-permute-start | bytes 884744 | tf_op jit(solution)/shard_map/ppermute | solution.py:62
  331.1 73.3 %collective-permute-start.28 = (bf16[2,256,1536]{2,1,0:T(8,128)(2,1)}, bf16[2,256,1536]{2,1,0:T(8,128)(2,1)S(1)}, u32[]{:S(2)}, u32[]{:S(2)}) collective-permute-start(bf16[2,256,1536]{2,1,0:T(8,128)(2,1)} %get-tuple-element.98), channel_id=1, source_target_pairs={{0,1},{1,0},{2,3},{3,2},{4,5},{5,4},{6,7},{7,6},{8,9},{9,8},{10,11... | collective-permute-start | bytes 4718600 | tf_op jit(solution)/shard_map/ppermute | solution.py:15
  347.9 56.5 %collective-permute-start.30 = (bf16[2,256,1536]{2,1,0:T(8,128)(2,1)}, bf16[2,256,1536]{2,1,0:T(8,128)(2,1)}, u32[]{:S(2)}, u32[]{:S(2)}) collective-permute-start(bf16[2,256,1536]{2,1,0:T(8,128)(2,1)} %fusion.41), channel_id=1, source_target_pairs={{0,2},{1,3},{2,0},{3,1},{4,6},{5,7},{6,4},{7,5},{8,10},{9,11},{10,... | collective-permute-start | bytes 4718600 | tf_op jit(solution)/shard_map/ppermute | solution.py:15
  412.1 54.2 %collective-permute-start.31 = (bf16[2,256,1536]{2,1,0:T(8,128)(2,1)S(1)}, bf16[2,256,1536]{2,1,0:T(8,128)(2,1)S(1)}, u32[]{:S(2)}, u32[]{:S(2)}) collective-permute-start(bf16[2,256,1536]{2,1,0:T(8,128)(2,1)S(1)} %add_convert_fusion.1), channel_id=1, source_target_pairs={{0,1},{1,0},{2,3},{3,2},{4,5},{5,4},{6,7},{7,6},{8,9},{9,8},{10,11... | collective-permute-start | bytes 4718600 | tf_op jit(solution)/shard_map/ppermute | solution.py:15
  602.1 79.0 %collective-permute-start.65 = (bf16[2,256,1536]{2,1,0:T(8,128)(2,1)}, bf16[2,256,1536]{2,1,0:T(8,128)(2,1)S(1)}, u32[]{:S(2)}, u32[]{:S(2)}) collective-permute-start(bf16[2,256,1536]{2,1,0:T(8,128)(2,1)} %get-tuple-element.94), channel_id=1, source_target_pairs={{0,1},{1,0},{2,3},{3,2},{4,5},{5,4},{6,7},{7,6},{8,9},{9,8},{10,11... | collective-permute-start | bytes 4718600 | tf_op jit(solution)/shard_map/ppermute | solution.py:15
  605.0 46.4 %collective-permute-start.66 = (bf16[2,256,1536]{2,1,0:T(8,128)(2,1)S(1)}, bf16[2,256,1536]{2,1,0:T(8,128)(2,1)S(1)}, u32[]{:S(2)}, u32[]{:S(2)}) collective-permute-start(bf16[2,256,1536]{2,1,0:T(8,128)(2,1)S(1)} %copy-done.67), channel_id=1, source_target_pairs={{0,1},{1,0},{2,3},{3,2},{4,5},{5,4},{6,7},{7,6},{8,9},{9,8},{10,11... | collective-permute-start | bytes 4718600 | tf_op jit(solution)/shard_map/ppermute | solution.py:15
  616.2 39.4 %collective-permute-start.51 = (bf16[2,256,1536]{2,1,0:T(8,128)(2,1)S(1)}, bf16[2,256,1536]{2,1,0:T(8,128)(2,1)S(1)}, u32[]{:S(2)}, u32[]{:S(2)}) collective-permute-start(bf16[2,256,1536]{2,1,0:T(8,128)(2,1)S(1)} %get-tuple-element.97), channel_id=1, source_target_pairs={{0,1},{1,0},{2,3},{3,2},{4,5},{5,4},{6,7},{7,6},{8,9},{9,8},{10,11... | collective-permute-start | bytes 4718600 | tf_op jit(solution)/shard_map/ppermute | solution.py:15
  655.6 37.9 %collective-permute-start.50 = (bf16[2,256,1536]{2,1,0:T(8,128)(2,1)S(1)}, bf16[2,256,1536]{2,1,0:T(8,128)(2,1)}, u32[]{:S(2)}, u32[]{:S(2)}) collective-permute-start(bf16[2,256,1536]{2,1,0:T(8,128)(2,1)S(1)} %get-tuple-element.96), channel_id=1, source_target_pairs={{0,1},{1,0},{2,3},{3,2},{4,5},{5,4},{6,7},{7,6},{8,9},{9,8},{10,11... | collective-permute-start | bytes 4718600 | tf_op jit(solution)/shard_map/ppermute | solution.py:15
  672.7 47.3 %collective-permute-start.52 = (bf16[2,256,1536]{2,1,0:T(8,128)(2,1)}, bf16[2,256,1536]{2,1,0:T(8,128)(2,1)}, u32[]{:S(2)}, u32[]{:S(2)}) collective-permute-start(bf16[2,256,1536]{2,1,0:T(8,128)(2,1)} %fusion.38), channel_id=1, source_target_pairs={{0,2},{1,3},{2,0},{3,1},{4,6},{5,7},{6,4},{7,5},{8,10},{9,11},{10,... | collective-permute-start | bytes 4718600 | tf_op jit(solution)/shard_map/ppermute | solution.py:15
  676.4 52.5 %collective-permute-start.78 = (bf16[2,40,1536]{2,1,0:T(8,128)(2,1)S(1)}, bf16[2,40,1536]{2,1,0:T(8,128)(2,1)}, u32[]{:S(2)}, u32[]{:S(2)}) collective-permute-start(bf16[2,40,1536]{2,1,0:T(8,128)(2,1)S(1)} %get-tuple-element.139), channel_id=1, source_target_pairs={{0,2},{1,3},{2,0},{3,1},{4,6},{5,7},{6,4},{7,5},{8,10},{9,11},{10,... | collective-permute-start | bytes 737288 | tf_op jit(solution)/shard_map/ppermute | solution.py:15
  681.0 47.9 %collective-permute-start.128 = (bf16[2,192,1536]{2,1,0:T(8,128)(2,1)}, bf16[2,192,1536]{2,1,0:T(8,128)(2,1)S(1)}, u32[]{:S(2)}, u32[]{:S(2)}) collective-permute-start(bf16[2,192,1536]{2,1,0:T(8,128)(2,1)} %pad_maximum_fusion.7), channel_id=1, source_target_pairs={{8,0},{16,8},{24,16},{28,24},{20,28},{12,20},{4,12},{0,4},{9,1},{1... | collective-permute-start | bytes 3538952 | tf_op jit(solution)/shard_map/ppermute | solution.py:62
  690.5 39.0 %collective-permute-start.124 = (bf16[2,192,1536]{2,1,0:T(8,128)(2,1)}, bf16[2,192,1536]{2,1,0:T(8,128)(2,1)S(1)}, u32[]{:S(2)}, u32[]{:S(2)}) collective-permute-start(bf16[2,192,1536]{2,1,0:T(8,128)(2,1)} %pad_maximum_fusion.6), channel_id=1, source_target_pairs={{0,8},{8,16},{16,24},{24,28},{28,20},{20,12},{12,4},{4,0},{1,9},{9... | collective-permute-start | bytes 3538952 | tf_op jit(solution)/shard_map/ppermute | solution.py:59
  693.5 44.6 %collective-permute-start.117 = (bf16[2,192,1536]{2,1,0:T(8,128)(2,1)}, bf16[2,192,1536]{2,1,0:T(8,128)(2,1)}, u32[]{:S(2)}, u32[]{:S(2)}) collective-permute-start(bf16[2,192,1536]{2,1,0:T(8,128)(2,1)} %get-tuple-element.74), channel_id=1, source_target_pairs={{0,8},{8,16},{16,24},{24,28},{28,20},{20,12},{12,4},{4,0},{1,9},{9... | collective-permute-start | bytes 3538952 | tf_op jit(solution)/shard_map/ppermute | solution.py:59
  745.2 43.0 %collective-permute-start.118 = (bf16[2,192,1536]{2,1,0:T(8,128)(2,1)}, bf16[2,192,1536]{2,1,0:T(8,128)(2,1)}, u32[]{:S(2)}, u32[]{:S(2)}) collective-permute-start(bf16[2,192,1536]{2,1,0:T(8,128)(2,1)} %get-tuple-element.72), channel_id=1, source_target_pairs={{0,8},{8,16},{16,24},{24,28},{28,20},{20,12},{12,4},{4,0},{1,9},{9... | collective-permute-start | bytes 3538952 | tf_op jit(solution)/shard_map/ppermute | solution.py:59
  746.9 42.4 %collective-permute-start.122 = (bf16[2,192,1536]{2,1,0:T(8,128)(2,1)}, bf16[2,192,1536]{2,1,0:T(8,128)(2,1)}, u32[]{:S(2)}, u32[]{:S(2)}) collective-permute-start(bf16[2,192,1536]{2,1,0:T(8,128)(2,1)} %get-tuple-element.73), channel_id=1, source_target_pairs={{8,0},{16,8},{24,16},{28,24},{20,28},{12,20},{4,12},{0,4},{9,1},{1... | collective-permute-start | bytes 3538952 | tf_op jit(solution)/shard_map/ppermute | solution.py:62
  771.3 401.8 %collective-permute-start.126 = (bf16[2,192,1536]{2,1,0:T(8,128)(2,1)}, bf16[2,192,1536]{2,1,0:T(8,128)(2,1)}, u32[]{:S(2)}, u32[]{:S(2)}) collective-permute-start(bf16[2,192,1536]{2,1,0:T(8,128)(2,1)} %get-tuple-element.65), channel_id=1, source_target_pairs={{0,8},{8,16},{16,24},{24,28},{28,20},{20,12},{12,4},{4,0},{1,9},{9... | collective-permute-start | bytes 3538952 | tf_op jit(solution)/shard_map/ppermute | solution.py:59
  1021.9 59.3 %collective-permute-start.107 = (bf16[1,192,384]{2,1,0:T(8,128)(2,1)}, bf16[1,192,384]{2,1,0:T(8,128)(2,1)}, u32[]{:S(2)}, u32[]{:S(2)}) collective-permute-start(bf16[1,192,384]{2,1,0:T(8,128)(2,1)} %get-tuple-element.143), channel_id=1, source_target_pairs={{0,8},{8,16},{16,24},{24,28},{28,20},{20,12},{12,4},{4,0},{1,9},{9... | collective-permute-start | bytes 442376 | tf_op jit(solution)/shard_map/ppermute | solution.py:59
  1023.7 60.5 %collective-permute-start.111 = (bf16[1,192,384]{2,1,0:T(8,128)(2,1)}, bf16[1,192,384]{2,1,0:T(8,128)(2,1)}, u32[]{:S(2)}, u32[]{:S(2)}) collective-permute-start(bf16[1,192,384]{2,1,0:T(8,128)(2,1)} %get-tuple-element.144), channel_id=1, source_target_pairs={{8,0},{16,8},{24,16},{28,24},{20,28},{12,20},{4,12},{0,4},{9,1},{1... | collective-permute-start | bytes 442376 | tf_op jit(solution)/shard_map/ppermute | solution.py:62
  1045.6 61.6 %collective-permute-start.83 = (bf16[2,40,1536]{2,1,0:T(8,128)(2,1)}, bf16[2,40,1536]{2,1,0:T(8,128)(2,1)}, u32[]{:S(2)}, u32[]{:S(2)}) collective-permute-start(bf16[2,40,1536]{2,1,0:T(8,128)(2,1)} %get-tuple-element.128), channel_id=1, source_target_pairs={{0,1},{1,0},{2,3},{3,2},{4,5},{5,4},{6,7},{7,6},{8,9},{9,8},{10,11... | collective-permute-start | bytes 737288 | tf_op jit(solution)/shard_map/ppermute | solution.py:15
  1156.6 40.7 %collective-permute-start.130 = (bf16[2,192,1536]{2,1,0:T(8,128)(2,1)S(1)}, bf16[2,192,1536]{2,1,0:T(8,128)(2,1)S(1)}, u32[]{:S(2)}, u32[]{:S(2)}) collective-permute-start(bf16[2,192,1536]{2,1,0:T(8,128)(2,1)S(1)} %copy-done.71), channel_id=1, source_target_pairs={{8,0},{16,8},{24,16},{28,24},{20,28},{12,20},{4,12},{0,4},{9,1},{1... | collective-permute-start | bytes 3538952 | tf_op jit(solution)/shard_map/ppermute | solution.py:62
  1165.0 50.6 %collective-permute-start.110 = (bf16[2,192,384]{2,1,0:T(8,128)(2,1)S(1)}, bf16[2,192,384]{2,1,0:T(8,128)(2,1)S(1)}, u32[]{:S(2)}, u32[]{:S(2)}) collective-permute-start(bf16[2,192,384]{2,1,0:T(8,128)(2,1)S(1)} %get-tuple-element.111), channel_id=1, source_target_pairs={{0,8},{8,16},{16,24},{24,28},{28,20},{20,12},{12,4},{4,0},{1,9},{9... | collective-permute-start | bytes 884744 | tf_op jit(solution)/shard_map/ppermute | solution.py:59
  1172.8 42.9 %collective-permute-start.114 = (bf16[2,192,384]{2,1,0:T(8,128)(2,1)S(1)}, bf16[2,192,384]{2,1,0:T(8,128)(2,1)S(1)}, u32[]{:S(2)}, u32[]{:S(2)}) collective-permute-start(bf16[2,192,384]{2,1,0:T(8,128)(2,1)S(1)} %get-tuple-element.112), channel_id=1, source_target_pairs={{8,0},{16,8},{24,16},{28,24},{20,28},{12,20},{4,12},{0,4},{9,1},{1... | collective-permute-start | bytes 884744 | tf_op jit(solution)/shard_map/ppermute | solution.py:62
  1173.0 51.8 %collective-permute-start.102 = (bf16[2,3,192,384]{3,2,1,0:T(8,128)(2,1)S(1)}, bf16[2,3,192,384]{3,2,1,0:T(8,128)(2,1)S(1)}, u32[]{:S(2)}, u32[]{:S(2)}) collective-permute-start(bf16[2,3,192,384]{3,2,1,0:T(8,128)(2,1)S(1)} %get-tuple-element.83), channel_id=1, source_target_pairs={{0,8},{8,16},{16,24},{24,28},{28,20},{20,12},{12,4},{4,0},{1,9},{9... | collective-permute-start | bytes 2654216 | tf_op jit(solution)/shard_map/ppermute | solution.py:59
  (287 other events, 5238.0 us)

commit v2 on v1

--- a/solution.py
+++ b/solution.py
@@ -3,9 +3,14 @@
 import jax
 import jax.numpy as jnp
 from jax import lax
+from jax.experimental import pallas as pl
+from jax.experimental.pallas import tpu as pltpu
 from jax.sharding import PartitionSpec as P
 
 HEAD_DIM = 64
+PAIR = 2 * HEAD_DIM
+FACTOR = 1.0 / math.sqrt(HEAD_DIM)
+BLOCK = 512
 EPSILON = 1e-06
 F32 = jnp.float32
 BF16 = jnp.bfloat16
@@ -144,49 +149,112 @@
     return jax.nn.gelu(values, approximate=True)
 
 
-def split_heads(matrix):
-    return matrix.reshape(matrix.shape[0], matrix.shape[1] // HEAD_DIM, HEAD_DIM)
-
-
 def dot(spec, a, b):
     return jnp.einsum(spec, a, b, preferred_element_type=F32)
 
 
-def attend(query_block, key_block, value_block):
-    factor = 1.0 / math.sqrt(HEAD_DIM)
-    query_heads = split_heads(query_block)
-    key_heads = split_heads(key_block)
-    value_heads = split_heads(value_block)
-    scores = dot("qhe,khe->hqk", query_heads, key_heads) * factor
-    row_top = jnp.max(scores, -1, keepdims=True)
-    total_log = row_top + jnp.log(jnp.sum(jnp.exp(scores - row_top), -1, keepdims=True))
-    attn_probs = jnp.exp(scores - total_log).astype(BF16)
-    output = dot("hqk,khe->qhe", attn_probs, value_heads)
-    return (output.reshape(query_block.shape).astype(BF16), total_log)
-
-
-def attend_back(query_block, key_block, value_block, total_log, out_grad):
-    factor = 1.0 / math.sqrt(HEAD_DIM)
-    query_heads = split_heads(query_block)
-    key_heads = split_heads(key_block)
-    value_heads = split_heads(value_block)
-    grad_heads = split_heads(out_grad)
-    scores = dot("qhe,khe->hqk", query_heads, key_heads) * factor
-    attn_probs = jnp.exp(scores - total_log)
-    prob_grad = dot("qhe,khe->hqk", grad_heads, value_heads)
-    row_inner = jnp.sum(attn_probs * prob_grad, -1, keepdims=True)
-    score_grad = (attn_probs * (prob_grad - row_inner)).astype(BF16)
-    query_grad = dot("hqk,khe->qhe", score_grad, key_heads) * factor
-    key_grad = dot("hqk,qhe->khe", score_grad, query_heads) * factor
-    value_grad = dot("hqk,qhe->khe", attn_probs.astype(BF16), grad_heads)
-    flat_shape = query_block.shape
-    return jnp.stack(
-        [
-            query_grad.reshape(flat_shape),
-            key_grad.reshape(flat_shape),
-            value_grad.reshape(flat_shape),
-        ]
-    ).astype(BF16)
+def lane_masks(dtype):
+    lane = lax.broadcasted_iota(jnp.int32, (1, PAIR), 1)
+    low = (lane < HEAD_DIM).astype(F32)
+    return [low.astype(dtype), (1.0 - low).astype(dtype)]
+
+def dot_nt(a,b): return lax.dot_general(a,b,(((1,),(1,)),((),())),preferred_element_type=F32)
+def dot_nn(a,b): return lax.dot_general(a,b,(((1,),(0,)),((),())),preferred_element_type=F32)
+def dot_tn(a,b): return lax.dot_general(a,b,(((0,),(0,)),((),())),preferred_element_type=F32)
+
+def row_blocks(image_rows, text_rows, block):
+    blocks=[(0,i,min(block,image_rows-i),i) for i in range(0,image_rows,block)]
+    blocks.append((1,0,text_rows,image_rows))
+    return blocks
+
+def attend_kernel(img, txt, out_img, out_txt, lse):
+    refs, outs = (img, txt), (out_img, out_txt)
+    keys=[r[0,:,PAIR:2*PAIR] for r in refs]
+    values=[r[0,:,2*PAIR:3*PAIR] for r in refs]
+    masks=lane_masks(F32)
+    low=[m.astype(BF16) for m in masks]
+    for part,start,size,place in row_blocks(img.shape[1],txt.shape[1],BLOCK):
+        query=refs[part][0,pl.ds(start,size),0:PAIR]*jnp.asarray(FACTOR,BF16)
+        total=None; logs=None
+        for head in range(2):
+            masked=query*low[head]
+            scores=[dot_nt(masked,k) for k in keys]
+            top=jnp.maximum(jnp.max(scores[0],-1,keepdims=True),jnp.max(scores[1],-1,keepdims=True))
+            probs=[jnp.exp(s-top) for s in scores]
+            denom=jnp.sum(probs[0],-1,keepdims=True)+jnp.sum(probs[1],-1,keepdims=True)
+            mixed=dot_nn(probs[0].astype(BF16),values[0])+dot_nn(probs[1].astype(BF16),values[1])
+            mixed=mixed*(masks[head]/denom)
+            log=(top+jnp.log(denom))*masks[head]
+            total=mixed if total is None else total+mixed
+            logs=log if logs is None else logs+log
+        outs[part][0,pl.ds(start,size),:]=total.astype(BF16)
+        turned=jnp.transpose(logs)
+        lse[0,0,0:1,pl.ds(place,size)]=turned[0:1]
+        lse[0,0,1:2,pl.ds(place,size)]=turned[HEAD_DIM:HEAD_DIM+1]
+
+def attend(img, txt, slots, pairs):
+    ni,nt=img.shape[1],txt.shape[1]
+    spec=lambda n,w: pl.BlockSpec((1,n,w),lambda c,p:(c,0,p))
+    flops=slots*pairs*2*2*2*(ni+nt)**2*PAIR
+    return pl.pallas_call(
+        attend_kernel, grid=(slots,pairs),
+        in_specs=[spec(ni,3*PAIR),spec(nt,3*PAIR)],
+        out_specs=[spec(ni,PAIR),spec(nt,PAIR),pl.BlockSpec((1,1,2,ni+nt),lambda c,p:(c,p,0,0))],
+        out_shape=[jax.ShapeDtypeStruct((slots,ni,pairs*PAIR),BF16),jax.ShapeDtypeStruct((slots,nt,pairs*PAIR),BF16),
+                   jax.ShapeDtypeStruct((slots,pairs,2,ni+nt),F32)],
+        compiler_params=pltpu.CompilerParams(vmem_limit_bytes=48<<20),
+        cost_estimate=pl.CostEstimate(flops=flops,bytes_accessed=slots*pairs*(ni+nt)*PAIR*8,transcendentals=slots*pairs*2*(ni+nt)**2),
+        name="attend")(img,txt)
+
+def attend_back_kernel(img, txt, o_img, o_txt, g_img, g_txt, lse, d_img, d_txt, dk_img, dk_txt, dv_img, dv_txt):
+    refs,o_refs,g_refs,d_refs=(img,txt),(o_img,o_txt),(g_img,g_txt),(d_img,d_txt)
+    dk,dv=(dk_img,dk_txt),(dv_img,dv_txt)
+    keys=[r[0,:,PAIR:2*PAIR] for r in refs]
+    values=[r[0,:,2*PAIR:3*PAIR] for r in refs]
+    low=lane_masks(BF16)
+    first=True
+    for part,start,size,place in row_blocks(img.shape[1],txt.shape[1],BLOCK):
+        rows=pl.ds(start,size)
+        query=refs[part][0,rows,0:PAIR]*jnp.asarray(FACTOR,BF16)
+        grad=g_refs[part][0,rows,:]
+        inner=jnp.transpose(grad.astype(F32)*o_refs[part][0,rows,:].astype(F32))
+        query_grad=None
+        for head in range(2):
+            q=query*low[head]; g=grad*low[head]
+            delta=jnp.sum(inner[head*HEAD_DIM:(head+1)*HEAD_DIM],0,keepdims=True)
+            log=lse[0,0,head:head+1,pl.ds(place,size)]
+            for kp in range(2):
+                probs=jnp.exp(dot_nt(keys[kp],q)-log)
+                prob_grad=dot_nt(values[kp],g)
+                score_grad=(probs*(prob_grad-delta)).astype(BF16)
+                v_part=dot_nn(probs.astype(BF16),g)
+                k_part=dot_nn(score_grad,q)
+                q_part=dot_tn(score_grad,keys[kp]*low[head])
+                query_grad=q_part if query_grad is None else query_grad+q_part
+                if first:
+                    dv[kp][...]=v_part; dk[kp][...]=k_part
+                else:
+                    dv[kp][...]+=v_part; dk[kp][...]+=k_part
+            first=False
+        d_refs[part][0,rows,0:PAIR]=(query_grad*FACTOR).astype(BF16)
+    for kp in range(2):
+        d_refs[kp][0,:,PAIR:2*PAIR]=dk[kp][...].astype(BF16)
+        d_refs[kp][0,:,2*PAIR:3*PAIR]=dv[kp][...].astype(BF16)
+
+def attend_back(img, txt, o_img, o_txt, g_img, g_txt, lse):
+    slots,ni=img.shape[:2]; nt=txt.shape[1]; pairs=lse.shape[1]
+    spec=lambda n,w: pl.BlockSpec((1,n,w),lambda c,p:(c,0,p))
+    flops=slots*pairs*2*5*2*(ni+nt)**2*PAIR
+    return pl.pallas_call(
+        attend_back_kernel, grid=(slots,pairs),
+        in_specs=[spec(ni,3*PAIR),spec(nt,3*PAIR),spec(ni,PAIR),spec(nt,PAIR),spec(ni,PAIR),spec(nt,PAIR),
+                  pl.BlockSpec((1,1,2,ni+nt),lambda c,p:(c,p,0,0))],
+        out_specs=[spec(ni,3*PAIR),spec(nt,3*PAIR)],
+        out_shape=[jax.ShapeDtypeStruct(img.shape,BF16),jax.ShapeDtypeStruct(txt.shape,BF16)],
+        scratch_shapes=[pltpu.VMEM((ni,PAIR),F32),pltpu.VMEM((nt,PAIR),F32)]*2,
+        compiler_params=pltpu.CompilerParams(vmem_limit_bytes=48<<20),
+        cost_estimate=pl.CostEstimate(flops=flops,bytes_accessed=slots*pairs*(ni+nt)*PAIR*16,transcendentals=slots*pairs*2*(ni+nt)**2),
+        name="attend_back")(img,txt,o_img,o_txt,g_img,g_txt,lse)
 
 
 def on_device(
@@ -217,7 +285,11 @@
     col_width = qkv_weight.shape[-1]
     hidden = fc1_weight.shape[-1]
 
-    qkv_pieces = ring.gather(qkv_weight)
+    pairs = col_width // PAIR
+    qkv_turned = jnp.transpose(
+        qkv_weight.reshape(2, 3, rows, pairs, PAIR), (0, 2, 3, 1, 4)
+    ).reshape(2, rows, 3 * col_width)
+    qkv_pieces = ring.gather(qkv_turned)
     proj_turned = jnp.swapaxes(proj_weight, 1, 2)
     fc2_turned = jnp.swapaxes(fc2_weight, 1, 2)
     _, _, proj_turned, fc1_shard = lax.optimization_barrier(
@@ -229,7 +301,7 @@
         (fc1_pieces[-4][2], fc1_pieces[-3][2], fc2_turned)
     )
     fc2_pieces = ring.gather(fc2_turned)
-    qkv_full = assemble(qkv_pieces, 2, groups).reshape(2, 3, width, col_width)
+    qkv_full = assemble(qkv_pieces, 1, groups).reshape(2, width, 3 * col_width)
     proj_full = assemble(proj_pieces, 1, groups).reshape(2, width, col_width)
     fc1_full = assemble(fc1_pieces, 1, groups).reshape(2, width, hidden)
     fc2_full = assemble(fc2_pieces, 1, groups).reshape(2, width, hidden)
@@ -266,20 +338,13 @@
         (out_grad[s] * modulation[:, s, 5][:, None, :]).astype(BF16) for s in range(2)
     ]
     mlp_full = [gather_tokens(mlp_round[s]) for s in range(2)]
-    joined_list = []
-    for s in range(2):
-        projected = dot("cld,jdn->jcln", first_full[s], qkv_full[s])
-        offsets = jnp.stack([qv_part[s, 0], jnp.zeros_like(qv_part[s, 0]), qv_part[s, 1]])
-        joined_list.append((projected + offsets[:, None, None, :]).astype(BF16))
-    joined = jnp.concatenate(joined_list, 2)
-    attended_rows, totals = [], []
-    for slot in range(slots):
-        attended_slot, total_log = attend(joined[0, slot], joined[1, slot], joined[2, slot])
-        attended_rows.append(attended_slot)
-        totals.append(total_log)
-    attended = jnp.stack(attended_rows)
-    split_at = first_full[0].shape[1]
-    pieces = (attended[:, :split_at], attended[:, split_at:])
+    offsets = jnp.stack([qv_part[:, 0], jnp.zeros_like(qv_part[:, 0]), qv_part[:, 1]], 1)
+    offsets = jnp.swapaxes(offsets.reshape(2, 3, pairs, PAIR), 1, 2).reshape(2, 3 * col_width)
+    qkv = [
+        (dot("cld,dn->cln", first_full[s], qkv_full[s]) + offsets[s]).astype(BF16)
+        for s in range(2)
+    ]
+    *pieces, total_log = attend(qkv[0], qkv[1], slots, pairs)
     branches = [
         scatter_tokens(dot("cln,dn->cld", pieces[s], proj_full[s]).astype(BF16)) + proj_add[s]
         for s in range(2)
@@ -343,32 +408,29 @@
         branch_round.append((residual * modulation[:, s, 2][:, None, :]).astype(BF16))
     branch_full = [gather_tokens(branch_round[s]) for s in range(2)]
     proj_bias_local = jnp.stack([jnp.sum(branch_round[s].astype(F32), (0, 1)) for s in range(2)])
-    attended_grad = jnp.concatenate(
-        [dot("cld,dn->cln", branch_full[s], proj_full[s]) for s in range(2)], 1
-    ).astype(BF16)
+    attended_grad = [
+        dot("cld,dn->cln", branch_full[s], proj_full[s]).astype(BF16) for s in range(2)
+    ]
     proj_grad = jnp.stack(
         [dot("cld,cln->dn", branch_full[s], pieces[s]).astype(BF16) for s in range(2)]
     ).reshape(2, groups, rows, col_width)
     proj_sum = ring.scatter(lambda d: lax.dynamic_index_in_dim(proj_grad, d, 1, keepdims=False))
-    qkv_rows = [
-        attend_back(
-            joined[0, slot], joined[1, slot], joined[2, slot], totals[slot], attended_grad[slot]
-        )
-        for slot in range(slots)
-    ]
-    qkv_round = jnp.stack(qkv_rows, 1)
-    qkv_parts = (qkv_round[:, :, :split_at], qkv_round[:, :, split_at:])
+    qkv_parts = attend_back(qkv[0], qkv[1], *pieces, *attended_grad, total_log)
     first_grad = [
-        scatter_tokens(dot("jcln,jdn->cld", qkv_parts[s], qkv_full[s]).astype(BF16))
+        scatter_tokens(dot("cln,dn->cld", qkv_parts[s], qkv_full[s]).astype(BF16))
         for s in range(2)
     ]
     qkv_grad = jnp.stack(
-        [dot("cld,jcln->jdn", first_full[s], qkv_parts[s]).astype(BF16) for s in range(2)]
-    ).reshape(2, 3, groups, rows, col_width)
-    qkv_sum = ring.scatter(lambda d: lax.dynamic_index_in_dim(qkv_grad, d, 2, keepdims=False))
-    qv_bias_local = jnp.stack(
-        [jnp.sum(qkv_parts[s][0::2].astype(F32), (1, 2)) for s in range(2)]
-    )
+        [dot("cld,cln->dn", first_full[s], qkv_parts[s]).astype(BF16) for s in range(2)]
+    ).reshape(2, groups, rows, 3 * col_width)
+    qkv_sum = ring.scatter(lambda d: lax.dynamic_index_in_dim(qkv_grad, d, 1, keepdims=False))
+    qkv_sum = jnp.transpose(
+        qkv_sum.reshape(2, rows, pairs, 3, PAIR), (0, 3, 1, 2, 4)
+    ).reshape(qkv_weight.shape)
+    qv_bias_local = jnp.stack([jnp.sum(qkv_parts[s].astype(F32), (0, 1)) for s in range(2)])
+    qv_bias_local = jnp.swapaxes(
+        qv_bias_local.reshape(2, pairs, 3, PAIR)[:, :, 0::2], 1, 2
+    ).reshape(2, 2, col_width)
     input_grads, modul_grads = [], []
     for s in range(2):
         input_part, shift_part, scale_part = norm_back(

time: 1270 us -> 1050 us (0.83)
  matrix products: 384 us -> 190 us
  other arithmetic: 203 us -> 104 us
  Pallas kernels: 0 us -> 82.8 us
  waiting for transfers between devices: 344 us -> 375 us
  local copies, waits for them, and re-layouts: 160 us -> 136 us
  starting transfers between devices: 128 us -> 109 us
    dot_general x39 -> x27, matrix products: 384 us -> 190 us  [dot(): return jnp.einsum(spec, a, b, preferred_element_type=F32)]
    pallas_call x0 -> x2, Pallas kernels: none -> 82.8 us  [the longest x1 54.7 us: attend_back(): pl.pallas_call(attend_back_kernel, grid=(slots, pairs), in_specs=[spec(ni...]
    convert_element_type x2 -> x0, other arithmetic: 60.2 us -> none  [attend_back(): score_grad = (attn_probs * (prob_grad - row_inner)).astype(BF16)]
    reduce_sum x4 -> x2, other arithmetic: 29.5 us -> 0.84 us  [on_device(): jnp.sum(qkv_parts[s].astype(F32), (0, 1))]
    ppermute x32, waiting for transfers between devices: 150 us -> 177 us  [backward(): return lax.ppermute(value, 'dp', self.back)]
    ppermute x67, starting transfers between devices: 56.3 us -> 37.1 us  [hop(): return lax.ppermute(value, axis, [(i, i ^ mask) for i in range(size)])]
    convert_element_type x4 -> x0, local copies, waits for them, and re-layouts: 15.2 us -> none  [the longest x2 12.2 us: on_device(): dot('cld,jcln->jdn', first_full[s], qkv_parts[s]).astype(BF16)]
    reshape x1 -> x5, local copies, waits for them, and re-layouts: 0.01 us -> 13.3 us  [the longest x1 4.19 us: on_device(): qkv_sum = jnp.transpose(qkv_sum.reshape(2, rows, pairs, 3, PAIR), (0, 3,...]
  transfers between devices with their start and end apart: 131 -> 131, of which waited for: 56 -> 58; matrix products, arithmetic and copies ran while one was open for 50% -> 30% of each run, Pallas kernels for 0% -> 8%
where the time goes in v2:
time: 1050 us; the launch traced here: 1040 us
  waiting for transfers between devices  375 us (36%)
  matrix products  190 us (18%)
  local copies, waits for them, and re-layouts  136 us (13%)
  starting transfers between devices  109 us (10%)
  other arithmetic  104 us (10%)
  Pallas kernels  82.8 us (8%)
  between operations  26.8 us (3%)
  blocking collectives  11.4 us (1%)
    dot_general x27, matrix products, dot(): return jnp.einsum(spec, a, b, preferred_element_type=F32)  190 us
    ppermute x32, waiting for transfers between devices, backward(): return lax.ppermute(value, 'dp', self.back)  177 us
    ppermute x67, waiting for transfers between devices, hop(): return lax.ppermute(value, axis, [(i, i ^ mask) for i in range(size)])  143 us
    ppermute x32, waiting for transfers between devices, forward(): return lax.ppermute(value, 'dp', self.ahead)  55.7 us
    pallas_call x1, Pallas kernels, attend_back(): pl.pallas_call(attend_back_kernel, grid=(slots, pairs), in_specs=[spec(ni...  54.7 us
    ppermute x32, starting transfers between devices, backward(): return lax.ppermute(value, 'dp', self.back)  40.8 us
    dynamic_update_slice x36, local copies, waits for them, and re-layouts, assemble(): full = lax.dynamic_update_slice(full, jnp.expand_dims(piece, axis), starts)  39.5 us
    ppermute x67, starting transfers between devices, hop(): return lax.ppermute(value, axis, [(i, i ^ mask) for i in range(size)])  37.1 us
  transfers between devices with their start and end apart: 131, of which 58 were waited for; matrix products, arithmetic and copies ran while one was open for 30% of the time, Pallas kernels for 8%

profile of v2, /device:TPU:0, one launch (start us, length us, event | category | flops | bytes accessed | tf_op | source)
XLA Modules:
  0.0 1035.1 jit_solution(6242204275976089601)
XLA Ops:
  109.3 15.2 %collective-permute-done.12 = bf16[2,192,1152]{2,1,0:T(8,128)(2,1)S(1)} collective-permute-done((bf16[2,192,1152]{2,1,0:T(8,128)(2,1)}, bf16[2,192,1152]{2,1,0:T(8,128)(2,1)S(1)}, u32[]{:S(2)}, u32[]{:S(2)}) %collective-permute-start.12) | collective-permute-done | bytes 884768 | tf_op jit(solution)/shard_map/ppermute | solution.py:67
  128.7 9.1 collective-permute-done.7
  185.6 11.7 %add_convert_fusion.img = bf16[2,1024,1152]{2,1,0:T(8,128)(2,1)} fusion(bf16[2,1024,1536]{2,1,0:T(8,128)(2,1)} %bitcast.834, bf16[1536,1152,1]{1,0,2:T(8,128)(2,1)S(1)} %bitcast.869, f32[1152]{0:T(1024)S(1)} %add.913), kind=kOutput, calls=%fused_computation.64 | convolution fusion | flops 7252475904 | bytes 14553600 | tf_op jit(solution)/shard_map/cld,dn->cln/dot_general | solution.py:153
  197.3 28.1 %attend.1 = (bf16[2,1024,384]{2,1,0:T(8,128)(2,1)S(1)}, bf16[2,160,384]{2,1,0:T(8,128)(2,1)S(1)}, f32[2,3,2,1184]{3,2,1,0:T(2,128)S(1)}) custom-call(bf16[2,1024,1152]{2,1,0:T(8,128)(2,1)} %add_convert_fusion.img, bf16[2,160,1152]{2,1,0:T(8,128)(2,1)S(1)} %fusion.35.txt), custom_call_target="tpu_custom_call" | custom-call | flops 8613003264 | bytes 7274496 | tf_op jit(solution)/shard_map/attend/pallas_call | solution.py:199
  275.3 8.3 collective-permute-done.37
  289.5 21.6 %collective-permute-done.39 = bf16[2,192,1536]{2,1,0:T(8,128)(2,1)S(1)} collective-permute-done((bf16[2,192,1536]{2,1,0:T(8,128)(2,1)S(1)}, bf16[2,192,1536]{2,1,0:T(8,128)(2,1)S(1)}, u32[]{:S(2)}, u32[]{:S(2)}) %collective-permute-start.39) | collective-permute-done | bytes 1179680 | tf_op jit(solution)/shard_map/ppermute | solution.py:67
  329.1 8.2 fusion.163
  357.3 19.7 %collective-permute-done.45 = bf16[2,192,1536]{2,1,0:T(8,128)(2,1)S(1)} collective-permute-done((bf16[2,192,1536]{2,1,0:T(8,128)(2,1)}, bf16[2,192,1536]{2,1,0:T(8,128)(2,1)S(1)}, u32[]{:S(2)}, u32[]{:S(2)}) %collective-permute-start.45) | collective-permute-done | bytes 1179680 | tf_op jit(solution)/shard_map/ppermute | solution.py:67
  381.4 9.4 collective-permute-done.32
  393.0 10.0 collective-permute-done.47
  409.0 17.0 %fusion.170 = f32[2,1024,1536]{2,1,0:T(8,128)} fusion(bf16[2,1024,1536]{2,1,0:T(8,128)(2,1)S(1)} %bitcast.842, bf16[1536,1536,1]{1,0,2:T(8,128)(2,1)} %bitcast.857), kind=kOutput, calls=%fused_computation.559 | convolution fusion | flops 9663676416 | bytes 23592960 | tf_op jit(solution)/shard_map/cld,df->clf/dot_general | solution.py:153
  426.1 13.7 %bitcast_convert_fusion.1 = bf16[1536,1536]{1,0:T(8,128)(2,1)S(1)} fusion(bf16[2,1024,1536]{2,1,0:T(8,128)(2,1)S(1)} %bitcast.841, f32[2,1024,1536]{2,1,0:T(8,128)} %fusion.170, f32[1536]{0:T(1024)S(1)} %copy-done.130), kind=kOutput, calls=%fused_computation.60 | convolution fusion | flops 9697492992 | bytes 23599104 | tf_op jit(solution)/shard_map/cld,clf->df/dot_general | solution.py:153
  442.1 8.1 fusion.164
  462.8 26.5 %convert_reduce_fusion = (f32[1536]{0:T(1024)S(1)}, bf16[2,1024,1536]{2,1,0:T(8,128)(2,1)}) fusion(f32[2,1024,1536]{2,1,0:T(8,128)} %fusion.170, f32[1536]{0:T(1024)S(1)} %copy-done.130, bf16[2,1024,1536]{2,1,0:T(8,128)(2,1)} %bitcast.838, bf16[1536,1536,1]{1,0,2:T(8,128)(2,1)} %bitcast.863), kind=kOutput, calls=%fused_computation.57 | convolution fusion | flops 9736026112 | bytes 29896704 | tf_op jit(solution)/shard_map/cld,df->clf/dot_general | solution.py:153
  489.3 17.4 %convolution_convert_fusion.2 = bf16[2,1024,1536]{2,1,0:T(8,128)(2,1)} fusion(bf16[1536,1536,1]{1,0,2:T(8,128)(2,1)} %bitcast.864, f32[2,1024,1536]{2,1,0:T(8,128)} %fusion.170, f32[1536]{0:T(1024)S(1)} %copy-done.130), kind=kOutput, calls=%fused_computation.75 | convolution fusion | flops 9698279424 | bytes 23599104 | tf_op jit(solution)/shard_map/clf,df->cld/dot_general | solution.py:153
  506.6 15.6 %bitcast_convert_fusion.3 = bf16[1536,1536]{1,0:T(8,128)(2,1)} fusion(bf16[2,1024,1536]{2,1,0:T(8,128)(2,1)} %bitcast.843, bf16[2,1024,1536]{2,1,0:T(8,128)(2,1)} %get-tuple-element.187), kind=kOutput, calls=%fused_computation.62 | convolution fusion | flops 9666035712 | bytes 17301504 | tf_op jit(solution)/shard_map/cld,clf->df/dot_general | solution.py:153
  522.2 15.3 %convolution_convert_fusion.1 = bf16[2,1024,1536]{2,1,0:T(8,128)(2,1)} fusion(bf16[2,1024,1536]{2,1,0:T(8,128)(2,1)} %get-tuple-element.187, bf16[1536,1536,1]{1,0,2:T(8,128)(2,1)} %bitcast.858), kind=kOutput, calls=%fused_computation.74 | convolution fusion | flops 9666822144 | bytes 17301504 | tf_op jit(solution)/shard_map/clf,df->cld/dot_general | solution.py:153
  568.6 11.0 %collective-permute-done.119 = bf16[1,192,1536]{2,1,0:T(8,128)(2,1)S(1)} collective-permute-done((bf16[1,192,1536]{2,1,0:T(8,128)(2,1)S(1)}, bf16[1,192,1536]{2,1,0:T(8,128)(2,1)S(1)}, u32[]{:S(2)}, u32[]{:S(2)}) %collective-permute-start.119) | collective-permute-done | bytes 589856 | tf_op jit(solution)/shard_map/ppermute | solution.py:67
  581.8 8.9 collective-permute-done.115
  601.8 13.6 %collective-permute-done.120 = bf16[2,192,1536]{2,1,0:T(8,128)(2,1)S(1)} collective-permute-done((bf16[2,192,1536]{2,1,0:T(8,128)(2,1)}, bf16[2,192,1536]{2,1,0:T(8,128)(2,1)S(1)}, u32[]{:S(2)}, u32[]{:S(2)}) %collective-permute-start.120) | collective-permute-done | bytes 1179680 | tf_op jit(solution)/shard_map/ppermute | solution.py:67
  625.2 9.6 collective-permute-done.67
  640.8 23.8 %collective-permute-done.52 = bf16[2,256,1536]{2,1,0:T(8,128)(2,1)} collective-permute-done((bf16[2,256,1536]{2,1,0:T(8,128)(2,1)}, bf16[2,256,1536]{2,1,0:T(8,128)(2,1)}, u32[]{:S(2)}, u32[]{:S(2)}) %collective-permute-start.52) | collective-permute-done | bytes 1572896 | tf_op jit(solution)/shard_map/ppermute | solution.py:20
  666.1 7.7 multiply_reduce_fusion
  695.4 10.9 %collective-permute-done.125 = bf16[2,192,1536]{2,1,0:T(8,128)(2,1)} collective-permute-done((bf16[2,192,1536]{2,1,0:T(8,128)(2,1)}, bf16[2,192,1536]{2,1,0:T(8,128)(2,1)}, u32[]{:S(2)}, u32[]{:S(2)}) %collective-permute-start.125) | collective-permute-done | bytes 1179680 | tf_op jit(solution)/shard_map/ppermute | solution.py:64
  720.6 10.9 %collective-permute-done.118 = bf16[2,192,1536]{2,1,0:T(8,128)(2,1)} collective-permute-done((bf16[2,192,1536]{2,1,0:T(8,128)(2,1)}, bf16[2,192,1536]{2,1,0:T(8,128)(2,1)}, u32[]{:S(2)}, u32[]{:S(2)}) %collective-permute-start.118) | collective-permute-done | bytes 1179680 | tf_op jit(solution)/shard_map/ppermute | solution.py:64
  757.4 54.7 %attend_back.1 = (bf16[2,1024,1152]{2,1,0:T(8,128)(2,1)}, bf16[2,160,1152]{2,1,0:T(8,128)(2,1)S(1)}) custom-call(bf16[2,1024,1152]{2,1,0:T(8,128)(2,1)} %add_convert_fusion.img, bf16[2,160,1152]{2,1,0:T(8,128)(2,1)S(1)} %copy-done.6, bf16[2,1024,384]{2,1,0:T(8,128)(2,1)S(1)} %copy-done.4, bf16[2,160,384]{2,1,0:T(8,128)(2,1)S(1)} %copy-done.2, ...), custom_call_target="tpu_custom_call" | custom-call | flops 21532508160 | bytes 14548992 | tf_op jit(solution)/shard_map/attend_back/pallas_call | solution.py:248
  812.1 12.7 %fusion.7 = bf16[1536,1152]{1,0:T(8,128)(2,1)} fusion(bf16[2,1024,1536]{2,1,0:T(8,128)(2,1)S(1)} %bitcast.837, bf16[2,1024,1152]{2,1,0:T(8,128)(2,1)} %get-tuple-element.29), kind=kOutput, calls=%fused_computation.67 | convolution fusion | flops 7249526784 | bytes 14548992 | tf_op jit(solution)/shard_map/cld,cln->dn/dot_general | solution.py:153
  826.8 10.5 %convolution_convert_fusion = bf16[2,1024,1536]{2,1,0:T(8,128)(2,1)} fusion(bf16[2,1024,1152]{2,1,0:T(8,128)(2,1)S(1)} %copy-done.35, bf16[1536,1152,1]{1,0,2:T(8,128)(2,1)S(1)} %bitcast.870), kind=kOutput, calls=%fused_computation.73 | convolution fusion | flops 7250903040 | bytes 14548992 | tf_op jit(solution)/shard_map/cln,dn->cld/dot_general | solution.py:153
  902.6 8.1 collective-permute-done.100
  913.3 9.3 collective-permute-done.82
  948.6 22.4 %collective-permute-done.130 = bf16[2,192,1536]{2,1,0:T(8,128)(2,1)S(1)} collective-permute-done((bf16[2,192,1536]{2,1,0:T(8,128)(2,1)S(1)}, bf16[2,192,1536]{2,1,0:T(8,128)(2,1)S(1)}, u32[]{:S(2)}, u32[]{:S(2)}) %collective-permute-start.130) | collective-permute-done | bytes 1179680 | tf_op jit(solution)/shard_map/ppermute | solution.py:67
  977.4 10.2 collective-permute-done.88
  (885 shorter events, 528.8 us)
Async XLA Ops:
  11.2 91.6 %collective-permute-start.10 = (bf16[2,192,1152]{2,1,0:T(8,128)(2,1)}, bf16[2,192,1152]{2,1,0:T(8,128)(2,1)}, u32[]{:S(2)}, u32[]{:S(2)}) collective-permute-start(bf16[2,192,1152]{2,1,0:T(8,128)(2,1)} %reshape.704), channel_id=1, source_target_pairs={{8,0},{16,8},{24,16},{28,24},{20,28},{12,20},{4,12},{0,4},{9,1},{1... | collective-permute-start | bytes 2654216 | tf_op jit(solution)/shard_map/ppermute | solution.py:67
  14.1 90.3 %collective-permute-start.9 = (bf16[2,192,1152]{2,1,0:T(8,128)(2,1)}, bf16[2,192,1152]{2,1,0:T(8,128)(2,1)}, u32[]{:S(2)}, u32[]{:S(2)}) collective-permute-start(bf16[2,192,1152]{2,1,0:T(8,128)(2,1)} %reshape.704), channel_id=1, source_target_pairs={{0,8},{8,16},{16,24},{24,28},{28,20},{20,12},{12,4},{4,0},{1,9},{9... | collective-permute-start | bytes 2654216 | tf_op jit(solution)/shard_map/ppermute | solution.py:64
  97.6 79.3 %collective-permute-start.6 = (bf16[2,256,1536]{2,1,0:T(8,128)(2,1)}, bf16[2,256,1536]{2,1,0:T(8,128)(2,1)S(1)}, u32[]{:S(2)}, u32[]{:S(2)}) collective-permute-start(bf16[2,256,1536]{2,1,0:T(8,128)(2,1)} %fusion.16), channel_id=1, source_target_pairs={{0,1},{1,0},{2,3},{3,2},{4,5},{5,4},{6,7},{7,6},{8,9},{9,8},{10,11... | collective-permute-start | bytes 4718600 | tf_op jit(solution)/shard_map/ppermute | solution.py:20
  102.0 71.8 %collective-permute-start.63 = (bf16[2,256,1536]{2,1,0:T(8,128)(2,1)S(1)}, bf16[2,256,1536]{2,1,0:T(8,128)(2,1)}, u32[]{:S(2)}, u32[]{:S(2)}) collective-permute-start(bf16[2,256,1536]{2,1,0:T(8,128)(2,1)S(1)} %copy-done.27), channel_id=1, source_target_pairs={{0,2},{1,3},{2,0},{3,1},{4,6},{5,7},{6,4},{7,5},{8,10},{9,11},{10,... | collective-permute-start | bytes 4718600 | tf_op jit(solution)/shard_map/ppermute | solution.py:20
  137.8 39.7 %collective-permute-start.8 = (bf16[2,256,1536]{2,1,0:T(8,128)(2,1)S(1)}, bf16[2,256,1536]{2,1,0:T(8,128)(2,1)S(1)}, u32[]{:S(2)}, u32[]{:S(2)}) collective-permute-start(bf16[2,256,1536]{2,1,0:T(8,128)(2,1)S(1)} %collective-permute-done.7), channel_id=1, source_target_pairs={{0,1},{1,0},{2,3},{3,2},{4,5},{5,4},{6,7},{7,6},{8,9},{9,8},{10,11... | collective-permute-start | bytes 4718600 | tf_op jit(solution)/shard_map/ppermute | solution.py:20
  173.7 51.7 %collective-permute-start.62 = (bf16[2,256,1536]{2,1,0:T(8,128)(2,1)S(1)}, bf16[2,256,1536]{2,1,0:T(8,128)(2,1)}, u32[]{:S(2)}, u32[]{:S(2)}) collective-permute-start(bf16[2,256,1536]{2,1,0:T(8,128)(2,1)S(1)} %copy-done.27), channel_id=1, source_target_pairs={{0,1},{1,0},{2,3},{3,2},{4,5},{5,4},{6,7},{7,6},{8,9},{9,8},{10,11... | collective-permute-start | bytes 4718600 | tf_op jit(solution)/shard_map/ppermute | solution.py:20
  173.8 52.7 %collective-permute-start.64 = (bf16[2,256,1536]{2,1,0:T(8,128)(2,1)}, bf16[2,256,1536]{2,1,0:T(8,128)(2,1)}, u32[]{:S(2)}, u32[]{:S(2)}) collective-permute-start(bf16[2,256,1536]{2,1,0:T(8,128)(2,1)} %collective-permute-done.63), channel_id=1, source_target_pairs={{0,1},{1,0},{2,3},{3,2},{4,5},{5,4},{6,7},{7,6},{8,9},{9,8},{10,11... | collective-permute-start | bytes 4718600 | tf_op jit(solution)/shard_map/ppermute | solution.py:20
  174.4 80.7 %collective-permute-start.35 = (bf16[2,192,1536]{2,1,0:T(8,128)(2,1)S(1)}, bf16[2,192,1536]{2,1,0:T(8,128)(2,1)}, u32[]{:S(2)}, u32[]{:S(2)}) collective-permute-start(bf16[2,192,1536]{2,1,0:T(8,128)(2,1)S(1)} %copy-done.56), channel_id=1, source_target_pairs={{8,0},{16,8},{24,16},{28,24},{20,28},{12,20},{4,12},{0,4},{9,1},{1... | collective-permute-start | bytes 3538952 | tf_op jit(solution)/shard_map/ppermute | solution.py:67
  176.9 79.9 %collective-permute-start.34 = (bf16[2,192,1536]{2,1,0:T(8,128)(2,1)S(1)}, bf16[2,192,1536]{2,1,0:T(8,128)(2,1)}, u32[]{:S(2)}, u32[]{:S(2)}) collective-permute-start(bf16[2,192,1536]{2,1,0:T(8,128)(2,1)S(1)} %copy-done.56), channel_id=1, source_target_pairs={{0,8},{8,16},{16,24},{24,28},{28,20},{20,12},{12,4},{4,0},{1,9},{9... | collective-permute-start | bytes 3538952 | tf_op jit(solution)/shard_map/ppermute | solution.py:64
  177.6 55.6 %collective-permute-start.23 = (bf16[2,192,384]{2,1,0:T(8,128)(2,1)}, bf16[2,192,384]{2,1,0:T(8,128)(2,1)}, u32[]{:S(2)}, u32[]{:S(2)}) collective-permute-start(bf16[2,192,384]{2,1,0:T(8,128)(2,1)} %collective-permute-done.21), channel_id=1, source_target_pairs={{8,0},{16,8},{24,16},{28,24},{20,28},{12,20},{4,12},{0,4},{9,1},{1... | collective-permute-start | bytes 884744 | tf_op jit(solution)/shard_map/ppermute | solution.py:67
  272.8 73.6 %collective-permute-start.28 = (bf16[2,256,1536]{2,1,0:T(8,128)(2,1)}, bf16[2,256,1536]{2,1,0:T(8,128)(2,1)S(1)}, u32[]{:S(2)}, u32[]{:S(2)}) collective-permute-start(bf16[2,256,1536]{2,1,0:T(8,128)(2,1)} %get-tuple-element.108), channel_id=1, source_target_pairs={{0,1},{1,0},{2,3},{3,2},{4,5},{5,4},{6,7},{7,6},{8,9},{9,8},{10,11... | collective-permute-start | bytes 4718600 | tf_op jit(solution)/shard_map/ppermute | solution.py:20
  289.4 57.0 %collective-permute-start.30 = (bf16[2,256,1536]{2,1,0:T(8,128)(2,1)}, bf16[2,256,1536]{2,1,0:T(8,128)(2,1)}, u32[]{:S(2)}, u32[]{:S(2)}) collective-permute-start(bf16[2,256,1536]{2,1,0:T(8,128)(2,1)} %fusion.30), channel_id=1, source_target_pairs={{0,2},{1,3},{2,0},{3,1},{4,6},{5,7},{6,4},{7,5},{8,10},{9,11},{10,... | collective-permute-start | bytes 4718600 | tf_op jit(solution)/shard_map/ppermute | solution.py:20
  353.9 53.8 %collective-permute-start.31 = (bf16[2,256,1536]{2,1,0:T(8,128)(2,1)S(1)}, bf16[2,256,1536]{2,1,0:T(8,128)(2,1)S(1)}, u32[]{:S(2)}, u32[]{:S(2)}) collective-permute-start(bf16[2,256,1536]{2,1,0:T(8,128)(2,1)S(1)} %add_convert_fusion.1), channel_id=1, source_target_pairs={{0,1},{1,0},{2,3},{3,2},{4,5},{5,4},{6,7},{7,6},{8,9},{9,8},{10,11... | collective-permute-start | bytes 4718600 | tf_op jit(solution)/shard_map/ppermute | solution.py:20
  403.1 37.6 %collective-permute-start.49 = (bf16[1,192,1536]{2,1,0:T(8,128)(2,1)S(1)}, bf16[1,192,1536]{2,1,0:T(8,128)(2,1)S(1)}, u32[]{:S(2)}, u32[]{:S(2)}) collective-permute-start(bf16[1,192,1536]{2,1,0:T(8,128)(2,1)S(1)} %slice.545), channel_id=1, source_target_pairs={{8,0},{16,8},{24,16},{28,24},{20,28},{12,20},{4,12},{0,4},{9,1},{1... | collective-permute-start | bytes 1769480 | tf_op jit(solution)/shard_map/ppermute | solution.py:67
  543.1 80.2 %collective-permute-start.65 = (bf16[2,256,1536]{2,1,0:T(8,128)(2,1)}, bf16[2,256,1536]{2,1,0:T(8,128)(2,1)S(1)}, u32[]{:S(2)}, u32[]{:S(2)}) collective-permute-start(bf16[2,256,1536]{2,1,0:T(8,128)(2,1)} %get-tuple-element.104), channel_id=1, source_target_pairs={{0,1},{1,0},{2,3},{3,2},{4,5},{5,4},{6,7},{7,6},{8,9},{9,8},{10,11... | collective-permute-start | bytes 4718600 | tf_op jit(solution)/shard_map/ppermute | solution.py:20
  546.4 47.7 %collective-permute-start.66 = (bf16[2,256,1536]{2,1,0:T(8,128)(2,1)}, bf16[2,256,1536]{2,1,0:T(8,128)(2,1)}, u32[]{:S(2)}, u32[]{:S(2)}) collective-permute-start(bf16[2,256,1536]{2,1,0:T(8,128)(2,1)} %get-tuple-element.105), channel_id=1, source_target_pairs={{0,1},{1,0},{2,3},{3,2},{4,5},{5,4},{6,7},{7,6},{8,9},{9,8},{10,11... | collective-permute-start | bytes 4718600 | tf_op jit(solution)/shard_map/ppermute | solution.py:20
  556.5 42.4 %collective-permute-start.51 = (bf16[2,256,1536]{2,1,0:T(8,128)(2,1)}, bf16[2,256,1536]{2,1,0:T(8,128)(2,1)}, u32[]{:S(2)}, u32[]{:S(2)}) collective-permute-start(bf16[2,256,1536]{2,1,0:T(8,128)(2,1)} %get-tuple-element.107), channel_id=1, source_target_pairs={{0,1},{1,0},{2,3},{3,2},{4,5},{5,4},{6,7},{7,6},{8,9},{9,8},{10,11... | collective-permute-start | bytes 4718600 | tf_op jit(solution)/shard_map/ppermute | solution.py:20
  597.1 37.6 %collective-permute-start.67 = (bf16[2,256,1536]{2,1,0:T(8,128)(2,1)}, bf16[2,256,1536]{2,1,0:T(8,128)(2,1)}, u32[]{:S(2)}, u32[]{:S(2)}) collective-permute-start(bf16[2,256,1536]{2,1,0:T(8,128)(2,1)} %fusion.25), channel_id=1, source_target_pairs={{0,2},{1,3},{2,0},{3,1},{4,6},{5,7},{6,4},{7,5},{8,10},{9,11},{10,... | collective-permute-start | bytes 4718600 | tf_op jit(solution)/shard_map/ppermute | solution.py:20
  598.8 40.3 %collective-permute-start.50 = (bf16[2,256,1536]{2,1,0:T(8,128)(2,1)}, bf16[2,256,1536]{2,1,0:T(8,128)(2,1)}, u32[]{:S(2)}, u32[]{:S(2)}) collective-permute-start(bf16[2,256,1536]{2,1,0:T(8,128)(2,1)} %get-tuple-element.106), channel_id=1, source_target_pairs={{0,1},{1,0},{2,3},{3,2},{4,5},{5,4},{6,7},{7,6},{8,9},{9,8},{10,11... | collective-permute-start | bytes 4718600 | tf_op jit(solution)/shard_map/ppermute | solution.py:20
  615.3 49.3 %collective-permute-start.52 = (bf16[2,256,1536]{2,1,0:T(8,128)(2,1)}, bf16[2,256,1536]{2,1,0:T(8,128)(2,1)}, u32[]{:S(2)}, u32[]{:S(2)}) collective-permute-start(bf16[2,256,1536]{2,1,0:T(8,128)(2,1)} %fusion.27), channel_id=1, source_target_pairs={{0,2},{1,3},{2,0},{3,1},{4,6},{5,7},{6,4},{7,5},{8,10},{9,11},{10,... | collective-permute-start | bytes 4718600 | tf_op jit(solution)/shard_map/ppermute | solution.py:20
  618.0 55.8 %collective-permute-start.78 = (bf16[2,40,1536]{2,1,0:T(8,128)(2,1)}, bf16[2,40,1536]{2,1,0:T(8,128)(2,1)}, u32[]{:S(2)}, u32[]{:S(2)}) collective-permute-start(bf16[2,40,1536]{2,1,0:T(8,128)(2,1)} %get-tuple-element.141), channel_id=1, source_target_pairs={{0,2},{1,3},{2,0},{3,1},{4,6},{5,7},{6,4},{7,5},{8,10},{9,11},{10,... | collective-permute-start | bytes 737288 | tf_op jit(solution)/shard_map/ppermute | solution.py:20
  623.3 50.5 %collective-permute-start.128 = (bf16[2,192,1536]{2,1,0:T(8,128)(2,1)}, bf16[2,192,1536]{2,1,0:T(8,128)(2,1)S(1)}, u32[]{:S(2)}, u32[]{:S(2)}) collective-permute-start(bf16[2,192,1536]{2,1,0:T(8,128)(2,1)} %pad_maximum_fusion.7), channel_id=1, source_target_pairs={{8,0},{16,8},{24,16},{28,24},{20,28},{12,20},{4,12},{0,4},{9,1},{1... | collective-permute-start | bytes 3538952 | tf_op jit(solution)/shard_map/ppermute | solution.py:67
  634.8 39.5 %collective-permute-start.124 = (bf16[2,192,1536]{2,1,0:T(8,128)(2,1)}, bf16[2,192,1536]{2,1,0:T(8,128)(2,1)S(1)}, u32[]{:S(2)}, u32[]{:S(2)}) collective-permute-start(bf16[2,192,1536]{2,1,0:T(8,128)(2,1)} %pad_maximum_fusion.6), channel_id=1, source_target_pairs={{0,8},{8,16},{16,24},{24,28},{28,20},{20,12},{12,4},{4,0},{1,9},{9... | collective-permute-start | bytes 3538952 | tf_op jit(solution)/shard_map/ppermute | solution.py:64
  639.2 41.9 %collective-permute-start.117 = (bf16[2,192,1536]{2,1,0:T(8,128)(2,1)}, bf16[2,192,1536]{2,1,0:T(8,128)(2,1)}, u32[]{:S(2)}, u32[]{:S(2)}) collective-permute-start(bf16[2,192,1536]{2,1,0:T(8,128)(2,1)} %get-tuple-element.84), channel_id=1, source_target_pairs={{0,8},{8,16},{16,24},{24,28},{28,20},{20,12},{12,4},{4,0},{1,9},{9... | collective-permute-start | bytes 3538952 | tf_op jit(solution)/shard_map/ppermute | solution.py:64
  692.6 38.8 %collective-permute-start.118 = (bf16[2,192,1536]{2,1,0:T(8,128)(2,1)}, bf16[2,192,1536]{2,1,0:T(8,128)(2,1)}, u32[]{:S(2)}, u32[]{:S(2)}) collective-permute-start(bf16[2,192,1536]{2,1,0:T(8,128)(2,1)} %get-tuple-element.82), channel_id=1, source_target_pairs={{0,8},{8,16},{16,24},{24,28},{28,20},{20,12},{12,4},{4,0},{1,9},{9... | collective-permute-start | bytes 3538952 | tf_op jit(solution)/shard_map/ppermute | solution.py:64
  694.4 40.8 %collective-permute-start.122 = (bf16[2,192,1536]{2,1,0:T(8,128)(2,1)}, bf16[2,192,1536]{2,1,0:T(8,128)(2,1)}, u32[]{:S(2)}, u32[]{:S(2)}) collective-permute-start(bf16[2,192,1536]{2,1,0:T(8,128)(2,1)} %get-tuple-element.83), channel_id=1, source_target_pairs={{8,0},{16,8},{24,16},{28,24},{20,28},{12,20},{4,12},{0,4},{9,1},{1... | collective-permute-start | bytes 3538952 | tf_op jit(solution)/shard_map/ppermute | solution.py:67
  716.8 229.9 %collective-permute-start.126 = (bf16[2,192,1536]{2,1,0:T(8,128)(2,1)}, bf16[2,192,1536]{2,1,0:T(8,128)(2,1)}, u32[]{:S(2)}, u32[]{:S(2)}) collective-permute-start(bf16[2,192,1536]{2,1,0:T(8,128)(2,1)} %get-tuple-element.75), channel_id=1, source_target_pairs={{0,8},{8,16},{16,24},{24,28},{28,20},{20,12},{12,4},{4,0},{1,9},{9... | collective-permute-start | bytes 3538952 | tf_op jit(solution)/shard_map/ppermute | solution.py:64
  930.6 40.4 %collective-permute-start.130 = (bf16[2,192,1536]{2,1,0:T(8,128)(2,1)S(1)}, bf16[2,192,1536]{2,1,0:T(8,128)(2,1)S(1)}, u32[]{:S(2)}, u32[]{:S(2)}) collective-permute-start(bf16[2,192,1536]{2,1,0:T(8,128)(2,1)S(1)} %copy-done.53), channel_id=1, source_target_pairs={{8,0},{16,8},{24,16},{28,24},{20,28},{12,20},{4,12},{0,4},{9,1},{1... | collective-permute-start | bytes 3538952 | tf_op jit(solution)/shard_map/ppermute | solution.py:67
  935.3 38.3 %collective-permute-start.98 = (f32[10752]{0:T(1024)S(1)}, f32[10752]{0:T(1024)S(1)}, u32[]{:S(2)}, u32[]{:S(2)}) collective-permute-start(f32[10752]{0:T(1024)S(1)} %add.1008), channel_id=1, source_target_pairs={{0,16},{4,20},{8,24},{12,28},{16,0},{20,4},{24,8},{28,12},{1,17},{... | collective-permute-start | bytes 129032 | tf_op jit(solution)/shard_map/ppermute | solution.py:20
  938.3 49.4 %collective-permute-start.110 = (bf16[2,192,384]{2,1,0:T(8,128)(2,1)S(1)}, bf16[2,192,384]{2,1,0:T(8,128)(2,1)S(1)}, u32[]{:S(2)}, u32[]{:S(2)}) collective-permute-start(bf16[2,192,384]{2,1,0:T(8,128)(2,1)S(1)} %get-tuple-element.115), channel_id=1, source_target_pairs={{0,8},{8,16},{16,24},{24,28},{28,20},{20,12},{12,4},{4,0},{1,9},{9... | collective-permute-start | bytes 884744 | tf_op jit(solution)/shard_map/ppermute | solution.py:64
  946.4 41.4 %collective-permute-start.114 = (bf16[2,192,384]{2,1,0:T(8,128)(2,1)S(1)}, bf16[2,192,384]{2,1,0:T(8,128)(2,1)S(1)}, u32[]{:S(2)}, u32[]{:S(2)}) collective-permute-start(bf16[2,192,384]{2,1,0:T(8,128)(2,1)S(1)} %get-tuple-element.116), channel_id=1, source_target_pairs={{8,0},{16,8},{24,16},{28,24},{20,28},{12,20},{4,12},{0,4},{9,1},{1... | collective-permute-start | bytes 884744 | tf_op jit(solution)/shard_map/ppermute | solution.py:67
  946.8 48.6 %collective-permute-start.102 = (bf16[2,192,1152]{2,1,0:T(8,128)(2,1)S(1)}, bf16[2,192,1152]{2,1,0:T(8,128)(2,1)S(1)}, u32[]{:S(2)}, u32[]{:S(2)}) collective-permute-start(bf16[2,192,1152]{2,1,0:T(8,128)(2,1)S(1)} %get-tuple-element.93), channel_id=1, source_target_pairs={{0,8},{8,16},{16,24},{24,28},{28,20},{20,12},{12,4},{4,0},{1,9},{9... | collective-permute-start | bytes 2654216 | tf_op jit(solution)/shard_map/ppermute | solution.py:64
  (259 other events, 5927.8 us)

commit v3 on v1

v3 whole, which is shorter than its diff:
```python
import math

import jax
import jax.numpy as jnp
from jax import lax
from jax.experimental import pallas as pl
from jax.experimental.pallas import tpu as pltpu
from jax.sharding import PartitionSpec as P

HEAD_DIM = 64
PAIR = 2 * HEAD_DIM
FACTOR = 1.0 / math.sqrt(HEAD_DIM)
VMEM = 60 << 20
FLOPS_PER_US = 460000000
EPSILON = 1e-06
F32 = jnp.float32
BF16 = jnp.bfloat16


def hop(value, axis, mask, size):
    return lax.ppermute(value, axis, [(i, i ^ mask) for i in range(size)])


def halves(size):
    low = 1
    while low * low < size:
        low *= 2
    return low, size // low


def spread(value, axis, size):
    low, high = halves(size)
    held = jnp.stack(
        [value] + [hop(value, axis, low * step, size) for step in range(1, high)]
    )
    full = [held] + [hop(held, axis, mask, size) for mask in range(1, low)]
    return jnp.stack(full, 1).reshape((size,) + value.shape)


def exchange(blocks, axis, size):
    low, high = halves(size)
    blocks = blocks.reshape((high, low) + blocks.shape[1:])
    held = jnp.stack(
        [blocks[0]] + [hop(blocks[step], axis, low * step, size) for step in range(1, high)]
    )
    full = [held[:, 0]] + [hop(held[:, mask], axis, mask, size) for mask in range(1, low)]
    return jnp.stack(full, 1).reshape((size,) + blocks.shape[2:])


def collect(blocks, axis, size):
    low, high = halves(size)
    blocks = blocks.reshape((high, low) + blocks.shape[1:])
    held = blocks[0] + sum(
        hop(blocks[step], axis, low * step, size) for step in range(1, high)
    )
    return held[0] + sum(hop(held[mask], axis, mask, size) for mask in range(1, low))


def add_all(value, axis, size):
    mask = 1
    while mask < size:
        value = value + hop(value, axis, mask, size)
        mask *= 2
    return value


class Order:
    def __init__(self, seed):
        self.token = seed

    def __call__(self, *values):
        self.token, *values = lax.optimization_barrier((self.token, *values))
        return values[0] if len(values) == 1 else values

    def run(self, function, *values):
        results = function(*self(*values)) if len(values) > 1 else function(self(*values))
        return self(*results) if isinstance(results, (tuple, list)) else self(results)


class Ring:
    def __init__(self, size):
        self.size = size
        self.order = list(range(0, size, 2)) + list(range(size - 1, 0, -2))
        self.ahead = [(self.order[i], self.order[(i + 1) % size]) for i in range(size)]
        self.back = [(b, a) for a, b in self.ahead]
        place = [0] * size
        for position, device in enumerate(self.order):
            place[device] = position
        self.mine = jnp.asarray(place, jnp.int32)[lax.axis_index("dp")]
        self.table = jnp.asarray(self.order, jnp.int32)

    def devices(self, distances):
        return self.table[(self.mine + jnp.asarray(distances, jnp.int32)) % self.size]

    def forward(self, value):
        return lax.ppermute(value, "dp", self.ahead)

    def backward(self, value):
        return lax.ppermute(value, "dp", self.back)


class Gather:
    def __init__(self, ring, shard):
        self.ring, self.step = ring, 0
        self.pieces, self.distances, self.streams = [shard], [0], [0]
        self.send(shard, shard)

    def send(self, ahead, back):
        self.step += 1
        if self.step == self.ring.size // 2:
            ahead, back = ahead[:1], back[1:]
        self.moving = (self.ring.forward(ahead), self.ring.backward(back))

    def arrive(self, order):
        ahead, back = order(*self.moving)
        last = self.step == self.ring.size // 2
        self.pieces += [ahead, back]
        self.distances += [-self.step, self.step]
        self.streams += [0, 1 if last else 0]
        if not last:
            self.send(ahead, back)
        return last

    def finish(self, order):
        while len(self.pieces) < self.ring.size + 1:
            self.arrive(order)
        return assemble(
            self.pieces, self.streams, self.ring.devices(self.distances), self.ring.size
        )


class Scatter:
    def __init__(self, ring, image, text, form="plain"):
        self.ring, self.image, self.text, self.form = ring, image, text, form
        self.left = ring.size // 2
        far = ring.devices([self.left])[0]
        chunk = [lax.dynamic_index_in_dim(g, far, 0) for g in (image, text)]
        self.moving = (ring.forward(chunk[0]), ring.backward(chunk[1]))

    def arrive(self, order):
        ahead, back = order(*self.moving)
        self.left -= 1
        places = self.ring.devices([self.left, -self.left])
        if self.left == 0:
            self.total = ring_total(self.image, self.text, ahead, back, places, self.form)
            return True
        ahead, back = order(*ring_add(self.image, self.text, ahead, back, places))
        self.moving = (self.ring.forward(ahead), self.ring.backward(back))
        return False

    def finish(self, order):
        while self.left:
            self.arrive(order)
        return self.total


def kernel_call(kernel, name, cost_us, grid, in_specs, out_specs, out_shape, scalars=0, **more):
    return pl.pallas_call(
        kernel,
        grid_spec=pltpu.PrefetchScalarGridSpec(
            num_scalar_prefetch=scalars,
            grid=grid,
            in_specs=in_specs,
            out_specs=out_specs,
            scratch_shapes=more.pop("scratch", ()),
        ),
        out_shape=out_shape,
        compiler_params=pltpu.CompilerParams(vmem_limit_bytes=VMEM),
        cost_estimate=pl.CostEstimate(
            flops=int(cost_us * FLOPS_PER_US), bytes_accessed=1, transcendentals=0
        ),
        name=name,
        **more,
    )


def assemble(pieces, streams, places, size):
    count = len(pieces)
    parts, rows, width = pieces[0].shape[1:]
    moves = [
        (i, streams[i] + s, s, part)
        for i in range(count)
        for s in range(pieces[i].shape[0])
        for part in range(parts)
    ]

    def kernel(place, *refs):
        shards, full = refs[:count], refs[count : count + 2]
        held, sems_in, sems_out = refs[count + 2 : -2], refs[-2], refs[-1]
        ins = [pltpu.make_async_copy(shards[i], held[i], sems_in.at[i]) for i in range(count)]
        for copy in ins:
            copy.start()
        outs, last = [], -1
        for m, (i, stream, s, part) in enumerate(moves):
            if i != last:
                ins[i].wait()
                last = i
            spot = full[stream].at[place[i], :, pl.ds(part * width, width)]
            outs.append(pltpu.make_async_copy(held[i].at[s, part], spot, sems_out.at[m]))
            outs[-1].start()
        for copy in outs:
            copy.wait()

    whole = pl.BlockSpec(memory_space=pltpu.HBM)
    out = jax.ShapeDtypeStruct((size, rows, parts * width), BF16)
    full = kernel_call(
        kernel,
        "assemble",
        5e-7 * math.prod(out.shape) * 2.5 + 1,
        (1,),
        [whole] * count,
        [whole] * 2,
        [out] * 2,
        scalars=1,
        scratch=[pltpu.VMEM(p.shape, p.dtype) for p in pieces]
        + [pltpu.SemaphoreType.DMA((count,)), pltpu.SemaphoreType.DMA((len(moves),))],
    )(places, *pieces)
    return [f.reshape(size * rows, parts * width) for f in full]


def ring_specs(image, ahead, back, block):
    width = image.shape[2]

    def local(which):
        return pl.BlockSpec((1, block, width), lambda i, place: (place[which], i, 0))

    def moved(value):
        return pl.BlockSpec((value.shape[0], block, width), lambda i, place: (0, i, 0))

    return [local(0), local(0), local(1), local(1), moved(ahead), moved(back)]


def ring_add(image, text, ahead, back, places):
    size, rows, width = image.shape
    block = rows // 4 if rows % 64 == 0 else rows
    whole = ahead.shape[0] == 2

    def kernel(place, image_a, text_a, image_b, text_b, ahead, back, send_a, send_b):
        send_a[0] = (image_a[0].astype(F32) + ahead[0].astype(F32)).astype(BF16)
        send_b[1] = (text_b[0].astype(F32) + back[back.shape[0] - 1].astype(F32)).astype(BF16)
        if whole:
            send_a[1] = (text_a[0].astype(F32) + ahead[1].astype(F32)).astype(BF16)
            send_b[0] = (image_b[0].astype(F32) + back[0].astype(F32)).astype(BF16)
        else:
            send_a[1] = text_a[0]
            send_b[0] = image_b[0]

    out = pl.BlockSpec((2, block, width), lambda i, place: (0, i, 0))
    return kernel_call(
        kernel,
        "ring_add",
        1 + 7e-6 * image.shape[1] * image.shape[2] * 2,
        (rows // block,),
        ring_specs(image, ahead, back, block),
        [out] * 2,
        [jax.ShapeDtypeStruct((2, rows, width), BF16)] * 2,
        scalars=1,
    )(places, image, text, image, text, ahead, back)


def ring_total(image, text, ahead, back, places, form):
    size, rows, width = image.shape
    turned = form == "turned"
    block = rows if turned or rows % 64 else rows // 4
    part = width // 3

    def kernel(place, image_a, text_a, image_b, text_b, ahead, back, total):
        for s, mine in enumerate((image_a, text_a)):
            value = mine[0].astype(F32) + ahead[s].astype(F32) + back[s].astype(F32)
            if form == "parts":
                for j in range(3):
                    total[s, j] = value[:, j * part : (j + 1) * part]
            else:
                total[s] = jnp.transpose(value) if turned else value

    if form == "parts":
        out = pl.BlockSpec((2, 3, block, part), lambda i, place: (0, 0, i, 0))
        shape = (2, 3, rows, part)
    elif turned:
        out = pl.BlockSpec((2, width, rows), lambda i, place: (0, 0, 0))
        shape = (2, width, rows)
    else:
        out = pl.BlockSpec((2, block, width), lambda i, place: (0, i, 0))
        shape = (2, rows, width)
    return kernel_call(
        kernel,
        "ring_total",
        1 + 7e-6 * image.shape[1] * image.shape[2] * 2,
        (rows // block,),
        ring_specs(image, ahead, back, block),
        out,
        jax.ShapeDtypeStruct(shape, F32),
        scalars=1,
    )(places, image, text, image, text, ahead, back)


class Spread:
    def __init__(self, part):
        self.part = part
        self.across = hop(part, "tensor", 2, 4)
        self.beside = hop(part, "tensor", 1, 4)

    def arrive(self, order):
        self.across = order(self.across)
        self.corner = hop(self.across, "tensor", 1, 4)

    def finish(self, order):
        beside, corner = order(self.beside, self.corner)
        return [self.part, beside, self.across, corner]


class Collect:
    def __init__(self, own, beside, across, corner):
        self.own, self.kept = own, across
        self.corner = hop(corner, "tensor", 1, 4)
        self.beside = hop(beside, "tensor", 1, 4)

    def arrive(self, order):
        corner = order(self.corner)
        send = (self.kept.astype(F32) + corner.astype(F32)).astype(BF16)
        self.across = hop(order(send), "tensor", 2, 4)

    def finish(self, order):
        return [self.own, *order(self.beside, self.across)]


def piece_specs(pieces, block=None):
    if isinstance(pieces, (list, tuple)):
        shape = pieces[0].shape
        spec = pl.BlockSpec(shape, lambda j: (0, 0, 0), pipeline_mode=pl.Buffered(1))
        return [spec] * 4, list(pieces), shape
    shape = pieces.shape[1:]
    specs = [
        pl.BlockSpec(
            (None,) + shape, lambda j, k=k: (k, 0, 0, 0), pipeline_mode=pl.Buffered(1)
        )
        for k in range(4)
    ]
    return specs, [pieces] * 4, shape


def column_block(width):
    for block in (512, 384, 256, 128):
        if width % block == 0:
            return block
    return width


def rows_times(
    pieces, weights, image, turned, outputs, finish=None, extras=(), extra_specs=(), columns=None
):
    specs, arrays, (slots, tokens, depth) = piece_specs(pieces)
    start, count = columns or (0, weights[0].shape[1])
    width = weights[0].shape[0] if turned else count
    block = column_block(math.gcd(start, width))
    text = tokens - image
    spots = [(k, c) for k in range(4) for c in range(slots)]
    dims = DOT_NT if turned else DOT_NN
    split = outputs == "split"
    count = 4 if split else outputs

    def kernel(*refs):
        rows, (image_w, text_w) = refs[:4], refs[4:6]
        more, outs = refs[6 : 6 + len(extras)], refs[6 + len(extras) :]

        def store(stream, spot, sums):
            k, c = spot
            cut = slice(0, image) if stream == 0 else slice(image, tokens)
            values = [sums] if finish is None else finish(stream, spot, cut, sums, *more)
            for which, value in enumerate(values):
                if split:
                    outs[k][c, cut] = value.astype(BF16)
                else:
                    outs[which][k, c, cut] = value.astype(BF16)

        for spot in spots:
            store(0, spot, mul(rows[spot[0]][spot[1], :image], image_w[...], dims))
        joined = jnp.concatenate([rows[k][c, image:] for k, c in spots], 0)
        sums = mul(joined, text_w[...], dims)
        for i, spot in enumerate(spots):
            store(1, spot, sums[i * text : (i + 1) * text])

    if turned:
        weight = pl.BlockSpec((block, depth), lambda j: (j, start // depth))
    else:
        weight = pl.BlockSpec((depth, block), lambda j: (0, start // block + j))
    if split:
        out = pl.BlockSpec((slots, tokens, block), lambda j: (0, 0, j))
        shape = jax.ShapeDtypeStruct((slots, tokens, width), BF16)
    else:
        out = pl.BlockSpec((4, slots, tokens, block), lambda j: (0, 0, 0, j))
        shape = jax.ShapeDtypeStruct((4, slots, tokens, width), BF16)
    return kernel_call(
        kernel,
        "rows_times",
        1 + 3e-9 * 4 * slots * tokens * depth * width,
        (width // block,),
        specs + [weight, weight] + [make(block) for make in extra_specs],
        [out] * count,
        [shape] * count,
    )(*arrays, *weights, *extras)


def weight_grad(pieces, grads, image, size):
    specs, arrays, (slots, tokens, depth) = piece_specs(pieces)
    width = grads.shape[3]
    block = column_block(width)
    text = tokens - image
    spots = [(k, c) for k in range(4) for c in range(slots)]

    def kernel(a, b, c, d, grad, image_out, text_out, sums, image_turned, text_turned):
        rows = (a, b, c, d)

        @pl.when(pl.program_id(0) == 0)
        def _():
            for i, (k, s) in enumerate(spots):
                image_turned[:, pl.ds(i * image, image)] = jnp.transpose(rows[k][s, :image])
            text_turned[...] = jnp.transpose(
                jnp.concatenate([rows[k][s, image:] for k, s in spots], 0)
            )

        image_grads = jnp.concatenate([grad[k, s, :image] for k, s in spots], 0)
        text_grads = jnp.concatenate([grad[k, s, image:] for k, s in spots], 0)
        image_out[...] = (
            mul(image_turned[...], image_grads, DOT_NN).astype(BF16).reshape(image_out.shape)
        )
        text_out[...] = (
            mul(text_turned[...], text_grads, DOT_NN).astype(BF16).reshape(text_out.shape)
        )
        sums[0:1] = jnp.sum(image_grads.astype(F32), 0, keepdims=True)
        sums[1:2] = jnp.sum(text_grads.astype(F32), 0, keepdims=True)

    out = pl.BlockSpec((size, depth // size, block), lambda j: (0, 0, j))
    shape = jax.ShapeDtypeStruct((size, depth // size, width), BF16)
    return kernel_call(
        kernel,
        "weight_grad",
        1 + 3.4e-9 * 4 * slots * tokens * depth * width,
        (width // block,),
        specs + [pl.BlockSpec((4, slots, tokens, block), lambda j: (0, 0, 0, j))],
        [out, out, pl.BlockSpec((2, block), lambda j: (0, j))],
        [shape, shape, jax.ShapeDtypeStruct((2, width), F32)],
        scratch=[
            pltpu.VMEM((depth, len(spots) * image), BF16),
            pltpu.VMEM((depth, len(spots) * text), BF16),
        ],
    )(*arrays, grads)


def mul(a, b, dims):
    return lax.dot_general(a, b, dims, preferred_element_type=F32)


DOT_NN = (((1,), (0,)), ((), ()))
DOT_NT = (((1,), (1,)), ((), ()))
DOT_TN = (((0,), (0,)), ((), ()))


def lane_masks(dtype):
    lane = lax.broadcasted_iota(jnp.int32, (1, PAIR), 1)
    low = (lane < HEAD_DIM).astype(F32)
    return [low.astype(dtype), (1.0 - low).astype(dtype)]


def stream_rows(ref, image, stream):
    cut = slice(0, image) if stream == 0 else slice(image, ref.shape[2])
    return jnp.concatenate([ref[k, 0, cut] for k in range(4)], 0)


def query_blocks(image, text):
    return [(0, (0, 1), 0), (0, (2, 3), 2 * image), (1, (0, 1, 2, 3), 4 * image)]


def attend(qkv, image, slot, earlier):
    _, slots, tokens, width = qkv.shape
    text, pairs = tokens - image, width // (3 * PAIR)

    def kernel(q, k, v, *refs):
        out, logs_out = refs[-2:]
        keys = [stream_rows(k, image, s) for s in range(2)]
        values = [stream_rows(v, image, s) for s in range(2)]
        masks = lane_masks(F32)
        low = [m.astype(BF16) for m in masks]
        for stream, members, place in query_blocks(image, text):
            cut = slice(0, image) if stream == 0 else slice(image, tokens)
            size = image if stream == 0 else text
            query = jnp.concatenate([q[m, 0, cut] for m in members], 0)
            query = query * jnp.asarray(FACTOR, BF16)
            total = logs = None
            for head in range(2):
                scores = [mul(query * low[head], key, DOT_NT) for key in keys]
                top = jnp.maximum(
                    jnp.max(scores[0], -1, keepdims=True), jnp.max(scores[1], -1, keepdims=True)
                )
                probs = [jnp.exp(s - top) for s in scores]
                denom = jnp.sum(probs[0], -1, keepdims=True) + jnp.sum(
                    probs[1], -1, keepdims=True
                )
                mixed = mul(probs[0].astype(BF16), values[0], DOT_NN) + mul(
                    probs[1].astype(BF16), values[1], DOT_NN
                )
                mixed = mixed * (masks[head] / denom)
                log = (top + jnp.log(denom)) * masks[head]
                total = mixed if total is None else total + mixed
                logs = log if logs is None else logs + log
            for i, m in enumerate(members):
                out[m, 0, cut] = total[i * size : (i + 1) * size].astype(BF16)
            turned = jnp.transpose(logs)
            span = pl.ds(place, size * len(members))
            logs_out[0, 0, 0:1, span] = turned[0:1]
            logs_out[0, 0, 1:2, span] = turned[HEAD_DIM : HEAD_DIM + 1]

    def spec(which):
        return pl.BlockSpec((4, 1, tokens, PAIR), lambda p: (0, slot, 0, which * pairs + p))

    total = 4 * tokens
    return kernel_call(
        kernel,
        "attend",
        15,
        (pairs,),
        [spec(0), spec(1), spec(2)] + [pl.BlockSpec(memory_space=pl.ANY)] * len(earlier),
        [spec(0), pl.BlockSpec((1, 1, 2, total), lambda p: (slot, p, 0, 0))],
        [
            jax.ShapeDtypeStruct((4, slots, tokens, pairs * PAIR), BF16),
            jax.ShapeDtypeStruct((slots, pairs, 2, total), F32),
        ],
        input_output_aliases={3: 0, 4: 1} if earlier else {},
    )(qkv, qkv, qkv, *earlier)


def attend_back(qkv, mixed, grads, logs, image, slot, earlier):
    _, slots, tokens, width = qkv.shape
    text, pairs = tokens - image, width // (3 * PAIR)

    def kernel(q, k, v, mixed, grads, logs, *refs):
        out, key_image, key_text, value_image, value_text = refs[-5:]
        key_sums, value_sums = (key_image, key_text), (value_image, value_text)
        keys = [stream_rows(k, image, s) for s in range(2)]
        values = [stream_rows(v, image, s) for s in range(2)]
        low = lane_masks(BF16)
        pair = pl.program_id(0)

        def lanes(which):
            return pl.ds(pl.multiple_of((which * pairs + pair) * PAIR, PAIR), PAIR)

        first = True
        for stream, members, place in query_blocks(image, text):
            cut = slice(0, image) if stream == 0 else slice(image, tokens)
            size = image if stream == 0 else text
            query = jnp.concatenate([q[m, 0, cut] for m in members], 0)
            query = query * jnp.asarray(FACTOR, BF16)
            grad = jnp.concatenate([grads[m, 0, cut] for m in members], 0)
            output = jnp.concatenate([mixed[m, 0, cut] for m in members], 0)
            inner = jnp.transpose(grad.astype(F32) * output.astype(F32))
            query_grad = None
            for head in range(2):
                head_q, head_g = query * low[head], grad * low[head]
                half = slice(head * HEAD_DIM, (head + 1) * HEAD_DIM)
                delta = jnp.sum(inner[half], 0, keepdims=True)
                log = logs[0, 0, head : head + 1, pl.ds(place, size * len(members))]
                for part in range(2):
                    probs = jnp.exp(mul(keys[part], head_q, DOT_NT) - log)
                    prob_grad = mul(values[part], head_g, DOT_NT)
                    score_grad = (probs * (prob_grad - delta)).astype(BF16)
                    value_part = mul(probs.astype(BF16), head_g, DOT_NN)
                    key_part = mul(score_grad, head_q, DOT_NN)
                    query_part = mul(score_grad, keys[part] * low[head], DOT_TN)
                    query_grad = query_part if query_grad is None else query_grad + query_part
                    if first:
                        value_sums[part][...] = value_part
                        key_sums[part][...] = key_part
                    else:
                        value_sums[part][...] += value_part
                        key_sums[part][...] += key_part
                first = False
            query_grad = query_grad * FACTOR
            for i, m in enumerate(members):
                out[m, 0, cut, lanes(0)] = query_grad[i * size : (i + 1) * size].astype(BF16)
        for which, sums in ((1, key_sums), (2, value_sums)):
            for m in range(4):
                out[m, 0, :image, lanes(which)] = sums[0][
                    m * image : (m + 1) * image
                ].astype(BF16)
                out[m, 0, image:, lanes(which)] = sums[1][m * text : (m + 1) * text].astype(BF16)

    def spec(which):
        return pl.BlockSpec((4, 1, tokens, PAIR), lambda p: (0, slot, 0, which * pairs + p))

    before = [] if earlier is None else [earlier]
    return kernel_call(
        kernel,
        "attend_back",
        29,
        (pairs,),
        [
            spec(0),
            spec(1),
            spec(2),
            spec(0),
            spec(0),
            pl.BlockSpec((1, 1, 2, 4 * tokens), lambda p: (slot, p, 0, 0)),
        ]
        + [pl.BlockSpec(memory_space=pl.ANY)] * len(before),
        pl.BlockSpec((4, 1, tokens, width), lambda p: (0, slot, 0, 0)),
        jax.ShapeDtypeStruct(qkv.shape, BF16),
        scratch=[pltpu.VMEM((4 * image, PAIR), F32), pltpu.VMEM((4 * text, PAIR), F32)] * 2,
        input_output_aliases={6: 0} if before else {},
    )(qkv, qkv, qkv, mixed, grads, logs, *before)


def normalize(values):
    average = jnp.mean(values, -1, keepdims=True)
    centred = values - average
    spread = jnp.mean(centred * centred, -1, keepdims=True)
    inverse = lax.rsqrt(spread + EPSILON)
    return centred * inverse, inverse


def norm_back(grad, normed, inverse, scale):
    scaled = grad * (1.0 + scale)
    return inverse * (
        scaled
        - jnp.mean(scaled, -1, keepdims=True)
        - normed * jnp.mean(scaled * normed, -1, keepdims=True)
    )


def add_up(values):
    return jnp.sum(values, 0, keepdims=True)


def per_slot(function, name, seqs, ins, outs):
    slots = ins[0].shape[0]

    def spec(shape, whole):
        rest = (0,) * (len(shape) - 1)
        if whole:
            return pl.BlockSpec(shape, lambda c, seqs: (0,) + rest)
        return pl.BlockSpec((1,) + tuple(shape[1:]), lambda c, seqs: (c,) + rest)

    def kernel(seqs, *refs):
        function((pl.program_id(0) < seqs[0]).astype(F32), *refs)

    return kernel_call(
        kernel,
        name,
        6,
        (slots,),
        [spec(value.shape, value.ndim == 2) for value in ins],
        [spec(shape, False) for shape, _ in outs],
        [jax.ShapeDtypeStruct(shape, dtype) for shape, dtype in outs],
        scalars=1,
    )(seqs, *ins)


def enter(live, image, text, image_cot, text_cot, vecs, first, mlp_round, sums):
    cut = image.shape[1]
    for s, (tokens, cot, rows) in enumerate(
        ((image, image_cot, slice(0, cut)), (text, text_cot, slice(cut, None)))
    ):
        normed, _ = normalize(tokens[0].astype(F32))
        first[0, rows] = (normed * (1.0 + vecs[0, s, 1:2]) + vecs[0, s, 0:1]).astype(BF16)
        rounded = (cot[0].astype(F32) * live * vecs[0, s, 5:6]).astype(BF16)
        mlp_round[0, rows] = rounded
        sums[0, s : s + 1] = add_up(rounded.astype(F32))


def middle(live, image, text, own, beside, across, vecs, bias, after, branch, second):
    cut = image.shape[1]
    for s, (tokens, rows) in enumerate(((image, slice(0, cut)), (text, slice(cut, None)))):
        value = own[0, rows].astype(F32) + beside[0, rows].astype(F32)
        value = value + across[0, rows].astype(F32) + bias[s : s + 1]
        result = tokens[0].astype(F32) + vecs[0, s, 2:3] * value
        normed, _ = normalize(result)
        branch[0, rows] = value
        after[0, rows] = result
        second[0, rows] = (normed * (1.0 + vecs[0, s, 4:5]) + vecs[0, s, 3:4]).astype(BF16)


def middle_back(
    live, image_cot, text_cot, own, beside, across, vecs, after, branch, residual, rounded, sums
):
    cut = image_cot.shape[1]
    for s, (cot, rows) in enumerate(((image_cot, slice(0, cut)), (text_cot, slice(cut, None)))):
        grad = own[0, rows].astype(F32) + beside[0, rows].astype(F32)
        grad = grad + across[0, rows].astype(F32)
        normed, inverse = normalize(after[0, rows])
        value = cot[0].astype(F32) * live + norm_back(grad, normed, inverse, vecs[0, s, 4:5])
        residual[0, rows] = value
        low = (value * vecs[0, s, 2:3]).astype(BF16)
        rounded[0, rows] = low
        sums[0, s, 0:1] = add_up(value * branch[0, rows])
        sums[0, s, 1:2] = add_up(grad)
        sums[0, s, 2:3] = add_up(grad * normed)
        sums[0, s, 3:4] = add_up(low.astype(F32))


def leave(
    live, image_cot, text_cot, own, beside, across, vecs, after, bias, image_out, text_out, sums
):
    cut = image_cot.shape[1]
    for s, (cot, rows, out) in enumerate(
        ((image_cot, slice(0, cut), image_out), (text_cot, slice(cut, None), text_out))
    ):
        value = own[0, rows].astype(F32) + beside[0, rows].astype(F32)
        value = value + across[0, rows].astype(F32) + bias[s : s + 1]
        out[0] = ((after[0, rows] + vecs[0, s, 5:6] * value) * live).astype(BF16)
        sums[0, s : s + 1] = add_up(cot[0].astype(F32) * live * value)


def enter_back(
    live, image, text, own, beside, across, vecs, residual, image_grad, text_grad, sums
):
    cut = image.shape[1]
    for s, (tokens, rows, out) in enumerate(
        ((image, slice(0, cut), image_grad), (text, slice(cut, None), text_grad))
    ):
        grad = own[0, rows].astype(F32) + beside[0, rows].astype(F32)
        grad = grad + across[0, rows].astype(F32)
        normed, inverse = normalize(tokens[0].astype(F32))
        out[0] = residual[0, rows] + norm_back(grad, normed, inverse, vecs[0, s, 1:2])
        sums[0, s, 0:1] = add_up(grad)
        sums[0, s, 1:2] = add_up(grad * normed)


def bias_spec(block):
    return pl.BlockSpec((2, block), lambda j: (0, j))


def add_bias(stream, spot, cut, sums, bias):
    return [sums + bias[stream : stream + 1]]


def gelu_both(stream, spot, cut, sums, bias):
    value = sums + bias[stream : stream + 1]
    factor = math.sqrt(2.0 / math.pi)
    square = value * value
    bend = jnp.tanh(factor * (value + 0.044715 * value * square))
    half = 0.5 * (1.0 + bend)
    slope = half + 0.5 * value * (1.0 - bend * bend) * factor * (1.0 + 0.134145 * square)
    return [value * half, slope]


def times_slope(stream, spot, cut, sums, slope):
    return [sums * slope[spot[0], spot[1], cut].astype(F32)]


def dot(spec, a, b):
    return jnp.einsum(spec, a, b, preferred_element_type=F32)


def on_device(
    groups,
    image_tokens,
    text_tokens,
    conditioning,
    group_seqs,
    ada_weight,
    ada_bias,
    qkv_weight,
    qv_bias,
    proj_weight,
    proj_bias,
    fc1_weight,
    fc1_bias,
    fc2_weight,
    fc2_bias,
    image_cot,
    text_cot,
):
    column = lax.axis_index("tensor")
    group = lax.axis_index("dp")
    ring = Ring(groups)
    order = Order(group_seqs)
    slots, image, width = image_tokens.shape
    text = text_tokens.shape[1]
    tokens = image + text
    rows = qkv_weight.shape[2]
    col_width = qkv_weight.shape[-1]
    hidden = fc1_weight.shape[-1]
    both = range(2)

    proj_turned = jnp.swapaxes(proj_weight, 1, 2)[:, None]
    fc1_shard = fc1_weight[:, None]
    fc2_turned = jnp.swapaxes(fc2_weight, 1, 2)[:, None]

    ada_part = lax.dynamic_slice_in_dim(ada_bias.astype(F32), column * col_width, col_width, 2)
    qv_part = lax.dynamic_slice_in_dim(qv_bias.astype(F32), column * col_width, col_width, 2)
    fc1_part = lax.dynamic_slice_in_dim(fc1_bias.astype(F32), column * hidden, hidden, 1)
    offsets = jnp.stack([qv_part[:, 0], jnp.zeros_like(qv_part[:, 0]), qv_part[:, 1]], 1)
    offsets = offsets.reshape(2, 3 * col_width)
    proj_add = proj_bias.astype(F32)
    fc2_add = fc2_bias.astype(F32)

    cond_act, silu_back = jax.vjp(jax.nn.silu, conditioning.astype(F32))
    cond_low = cond_act.astype(BF16).reshape(slots, groups, rows)
    cond_sends = jnp.stack(
        [
            lax.dynamic_index_in_dim(cond_low, group ^ mask, 1, keepdims=False)
            for mask in range(groups)
        ]
    )
    cond_rows = order(exchange(cond_sends, "dp", groups)).reshape(groups * slots, rows)
    modul_parts = order(dot("cd,sjdn->csjn", cond_rows, ada_weight))
    modul_parts = modul_parts.reshape((groups, slots) + modul_parts.shape[1:])
    modul_local = order(collect(modul_parts, "dp", groups) + ada_part[None])
    qkv_ring = Gather(ring, order(jnp.concatenate([qkv_weight, proj_turned], 1)))
    qkv_part = (0, 3 * col_width)
    proj_part = (3 * col_width, col_width)
    vecs = order(lax.all_gather(modul_local, "tensor", axis=3, tiled=True))

    first, mlp_round, fc2_bias_local = order.run(
        lambda *a: per_slot(
            enter,
            "enter",
            group_seqs,
            a,
            [
                ((slots, tokens, width), BF16),
                ((slots, tokens, width), BF16),
                ((slots, 2, width), F32),
            ],
        ),
        image_tokens,
        text_tokens,
        image_cot,
        text_cot,
        vecs,
    )
    qkv_ring.arrive(order)
    first_move = Spread(order(first))
    qkv_ring.arrive(order)
    qkv_ring.arrive(order)
    first_move.arrive(order)
    first_full = first_move.finish(order)
    qkv_ring.arrive(order)
    fc1_ring = Gather(ring, order(fc1_shard))
    mlp_move = Spread(order(mlp_round))
    qkv_full = order(*qkv_ring.finish(order))

    qkv = order.run(
        lambda *a: rows_times(
            a[:4], a[4:], image, False, 1, add_bias, (offsets,), (bias_spec,), qkv_part
        ),
        *first_full,
        *qkv_full,
    )
    fc1_ring.arrive(order)
    mixed = ()
    for slot in range(slots):
        mixed = order.run(
            lambda *a, slot=slot: attend(a[0], image, slot, a[1:]), *((qkv,) + tuple(mixed))
        )
    mixed, logs = mixed
    fc1_ring.arrive(order)
    mlp_move.arrive(order)
    branch_parts = order.run(
        lambda *a: rows_times(a[0], a[1:], image, True, "split", columns=proj_part),
        mixed,
        *qkv_full,
    )
    branch_move = Collect(*order(*branch_parts))
    mlp_full = mlp_move.finish(order)
    branch_move.arrive(order)
    fc1_ring.arrive(order)
    fc1_ring.arrive(order)
    fc2_ring = Gather(ring, order(fc2_turned))
    branch_terms = branch_move.finish(order)
    after, branch, second = order.run(
        lambda *a: per_slot(
            middle,
            "middle",
            group_seqs,
            a,
            [
                ((slots, tokens, width), F32),
                ((slots, tokens, width), F32),
                ((slots, tokens, width), BF16),
            ],
        ),
        image_tokens,
        text_tokens,
        *branch_terms,
        vecs,
        proj_add,
    )
    second_move = Spread(second)
    fc1_full = order(*fc1_ring.finish(order))
    fc2_ring.arrive(order)
    fc2_ring.arrive(order)
    second_move.arrive(order)
    second_full = second_move.finish(order)
    activated, slope = order.run(
        lambda *a: rows_times(
            a[:4], a[4:], image, False, 2, gelu_both, (fc1_part,), (bias_spec,)
        ),
        *second_full,
        *fc1_full,
    )
    fc2_ring.arrive(order)
    *fc2_grad, _ = order.run(
        lambda *a: weight_grad(a[:4], a[4], image, groups), *mlp_full, activated
    )
    fc2_ring.arrive(order)
    fc2_sums = Scatter(ring, *order(*fc2_grad), "turned")
    fc2_full = order(*fc2_ring.finish(order))
    pre_round = order.run(
        lambda *a: rows_times(
            a[:4],
            a[4:],
            image,
            False,
            1,
            times_slope,
            (slope,),
            (
                lambda block: pl.BlockSpec(
                    (4, slots, tokens, block), lambda j: (0, 0, 0, j)
                ),
            ),
        ),
        *mlp_full,
        *fc2_full,
    )
    fc2_sums.arrive(order)
    second_parts = order.run(
        lambda *a: rows_times(a[0], a[1:], image, True, "split"), pre_round, *fc1_full
    )
    second_back = Collect(*second_parts)
    second_back.arrive(order)
    *fc1_grad, fc1_bias_local = order.run(
        lambda *a: weight_grad(a[:4], a[4], image, groups), *second_full, pre_round
    )
    fc1_sums = Scatter(ring, *order(*fc1_grad))
    mlp_parts = order.run(
        lambda *a: rows_times(a[0], a[1:], image, True, "split"), activated, *fc2_full
    )
    fc2_sums.arrive(order)
    second_terms = second_back.finish(order)
    residual, branch_round, middle_vecs = order.run(
        lambda *a: per_slot(
            middle_back,
            "middle_back",
            group_seqs,
            a,
            [
                ((slots, tokens, width), F32),
                ((slots, tokens, width), BF16),
                ((slots, 2, 4, width), F32),
            ],
        ),
        image_cot,
        text_cot,
        *second_terms,
        vecs,
        after,
        branch,
    )
    branch_back = Spread(branch_round)
    fc2_sums.arrive(order)
    fc1_sums.arrive(order)
    branch_back.arrive(order)
    branch_full = branch_back.finish(order)
    mixed_grad = order.run(
        lambda *a: rows_times(a[:4], a[4:], image, False, 1, columns=proj_part),
        *branch_full,
        *qkv_full,
    )
    mlp_back = Collect(*order(*mlp_parts))
    mlp_back.arrive(order)
    *proj_grad, _ = order.run(
        lambda *a: weight_grad(a[:4], a[4], image, groups), *branch_full, mixed
    )
    fc2_sums.arrive(order)
    proj_sum = lax.psum_scatter(
        jnp.stack(order(*proj_grad), 1), "dp", scatter_dimension=0, tiled=False
    )
    qkv_grads = None
    for slot in range(slots):
        given = (qkv, mixed, mixed_grad, logs) + (() if slot == 0 else (qkv_grads,))
        qkv_grads = order.run(
            lambda *a, slot=slot: attend_back(
                *a[:4], image, slot, a[4] if len(a) > 4 else None
            ),
            *given,
        )
        if slot == 0:
            fc1_sums.arrive(order)
    mlp_terms = mlp_back.finish(order)
    fc1_sums.arrive(order)
    *qkv_grad, qv_sums = order.run(
        lambda *a: weight_grad(a[:4], a[4], image, groups), *first_full, qkv_grads
    )
    qkv_sums = Scatter(ring, *order(*qkv_grad), "parts")
    first_parts = order.run(
        lambda *a: rows_times(a[0], a[1:], image, True, "split", columns=qkv_part),
        qkv_grads,
        *qkv_full,
    )
    fc1_sums.arrive(order)
    first_back = Collect(*first_parts)
    first_back.arrive(order)
    qkv_sums.arrive(order)
    qv_bias_local = qv_sums.reshape(2, 3, col_width)[:, 0::2]
    proj_bias_local = jnp.sum(middle_vecs[:, :, 3], 0)
    fc2_bias_local = jnp.sum(fc2_bias_local, 0)
    split_sums = jnp.concatenate([qv_bias_local.reshape(-1), fc1_bias_local.reshape(-1)])
    token_sums = jnp.concatenate([proj_bias_local.reshape(-1), fc2_bias_local.reshape(-1)])
    bias_local = add_all(jnp.concatenate([split_sums, token_sums]), "dp", groups)
    bias_all = order(lax.all_gather(order(bias_local), "tensor"))
    cut_a = qv_bias_local.size
    cut_b = cut_a + fc1_bias_local.size
    cut_c = cut_b + proj_bias_local.size
    cut_d = cut_c + fc2_bias_local.size

    def by_column(block, shape):
        return jnp.moveaxis(block.reshape((4,) + shape), 0, -2).reshape(
            shape[:-1] + (4 * shape[-1],)
        )

    qv_bias_grad = by_column(bias_all[:, :cut_a], qv_bias_local.shape)
    fc1_bias_grad = by_column(bias_all[:, cut_a:cut_b], fc1_bias_local.shape)
    proj_bias_grad = jnp.sum(bias_all[:, cut_b:cut_c], 0).reshape(proj_bias_local.shape)
    fc2_bias_grad = jnp.sum(bias_all[:, cut_c:cut_d], 0).reshape(fc2_bias_local.shape)
    image_out, text_out, gate_two = order.run(
        lambda *a: per_slot(
            leave,
            "leave",
            group_seqs,
            a,
            [
                (image_tokens.shape, BF16),
                (text_tokens.shape, BF16),
                ((slots, 2, width), F32),
            ],
        ),
        image_cot,
        text_cot,
        *mlp_terms,
        vecs,
        after,
        fc2_add,
    )
    qkv_sums.arrive(order)
    first_terms = first_back.finish(order)
    image_grad, text_grad, enter_vecs = order.run(
        lambda *a: per_slot(
            enter_back,
            "enter_back",
            group_seqs,
            a,
            [
                (image_tokens.shape, F32),
                (text_tokens.shape, F32),
                ((slots, 2, 2, width), F32),
            ],
        ),
        image_tokens,
        text_tokens,
        *first_terms,
        vecs,
        residual,
    )
    qkv_sums.arrive(order)
    modul_grad = jnp.concatenate(
        [
            enter_vecs,
            middle_vecs[:, :, 0:3],
            gate_two[:, :, None],
        ],
        2,
    ).reshape(slots, 2, 6, 4, col_width)
    modul_blocks = jnp.stack(
        [
            lax.dynamic_index_in_dim(modul_grad, column ^ mask, 3, keepdims=False)
            for mask in range(4)
        ]
    )
    modul_round = order(collect(modul_blocks, "tensor", 4).astype(BF16))
    modul_all = order(spread(modul_round, "dp", groups))
    modul_all = modul_all.reshape((groups * slots,) + modul_round.shape[1:])
    cond_part = dot("csjn,sjdn->cd", modul_all, ada_weight)
    ada_bias_part = jnp.sum(modul_all.astype(F32), 0)
    last = jnp.concatenate([cond_part.reshape(-1), ada_bias_part.reshape(-1)])
    last = order(spread(order(last), "tensor", 4))
    cond_part = jnp.sum(last[:, : cond_part.size], 0).reshape(groups, slots, rows)
    cond_terms = order(exchange(cond_part, "dp", groups))
    cond_term = jnp.stack(
        [
            lax.dynamic_index_in_dim(cond_terms, group ^ place, 0, keepdims=False)
            for place in range(groups)
        ],
        1,
    ).reshape(slots, width)
    cond_grad = lax.dynamic_slice_in_dim(
        silu_back(cond_term)[0], column * col_width, col_width, 1
    )
    ada_bias_grad = jnp.stack(
        [
            lax.dynamic_index_in_dim(
                last[:, cond_part.size :], column ^ place, 0, keepdims=False
            ).reshape(ada_bias_part.shape)
            for place in range(4)
        ],
        2,
    ).reshape(ada_bias.shape)
    ada_grad = dot("cd,csjn->sjdn", cond_rows, modul_all)
    fc2_sum, fc1_sum = fc2_sums.finish(order), fc1_sums.finish(order)
    proj_sum = jnp.swapaxes(order(proj_sum).astype(F32), 1, 2)
    qkv_sum = qkv_sums.finish(order)
    cond_grad = order(cond_grad)
    live = jnp.arange(slots, dtype=jnp.int32) < order.token[0]
    cond_grad = jnp.where(live[:, None], cond_grad, 0.0)
    return (
        image_out,
        text_out,
        image_grad,
        text_grad,
        cond_grad,
        ada_grad,
        ada_bias_grad,
        qkv_sum,
        qv_bias_grad,
        proj_sum,
        proj_bias_grad,
        fc1_sum,
        fc1_bias_grad,
        fc2_sum,
        fc2_bias_grad,
    )


def solution(mesh):
    groups = mesh.shape["dp"]
    in_specs = (
        P("dp", "tensor", None),
        P("dp", "tensor", None),
        P("dp", None),
        P("dp"),
        P(None, None, "dp", "tensor"),
        P(),
        P(None, None, "dp", "tensor"),
        P(),
        P(None, "tensor", "dp"),
        P(),
        P(None, "dp", "tensor"),
        P(),
        P(None, "tensor", "dp"),
        P(),
        P("dp", "tensor", None),
        P("dp", "tensor", None),
    )
    out_specs = (
        P("dp", "tensor", None),
        P("dp", "tensor", None),
        P("dp", "tensor", None),
        P("dp", "tensor", None),
        P("dp", "tensor"),
        P(None, None, "dp", "tensor"),
        P(),
        P(None, None, "dp", "tensor"),
        P(),
        P(None, "tensor", "dp"),
        P(),
        P(None, "dp", "tensor"),
        P(),
        P(None, "tensor", "dp"),
        P(),
    )

    def step(*args):
        return on_device(groups, *args)

    return jax.shard_map(
        step, mesh=mesh, in_specs=in_specs, out_specs=out_specs, check_vma=False
    )
```

time: 1270 us -> 930 us (0.73)
  Pallas kernels: 0 us -> 406 us
  matrix products: 384 us -> 3.34 us
  other arithmetic: 203 us -> 33 us
  local copies, waits for them, and re-layouts: 160 us -> 49.3 us
  starting transfers between devices: 128 us -> 89.8 us
  waiting for transfers between devices: 344 us -> 306 us
    pallas_call x0 -> x36, Pallas kernels: none -> 406 us  [the longest x8 129 us: rows_times(): kernel_call(kernel, 'rows_times', 1 + 3e-09 * 4 * slots * tokens * depth...]
    dot_general x39 -> x3, matrix products: 384 us -> 3.34 us  [dot(): return jnp.einsum(spec, a, b, preferred_element_type=F32)]
    ppermute x32 -> x24, waiting for transfers between devices: 150 us -> 12.4 us  [backward(): return lax.ppermute(value, 'dp', self.back)]
    ppermute x32 -> x24, waiting for transfers between devices: 61.8 us -> 190 us  [forward(): return lax.ppermute(value, 'dp', self.ahead)]
    convert_element_type x25 -> x6, other arithmetic: 88.4 us -> 14.2 us  [the longest x4 12.7 us: arrive(): send = (self.kept.astype(F32) + corner.astype(F32)).astype(BF16)]
    reduce_sum x22 -> x3, other arithmetic: 65 us -> 1 us  [the longest x1 0.95 us: on_device(): proj_bias_local = jnp.sum(middle_vecs[:, :, 3], 0)]
    ppermute x67 -> x47, waiting for transfers between devices: 132 us -> 71.2 us  [hop(): return lax.ppermute(value, axis, [(i, i ^ mask) for i in range(size)])]
    dynamic_update_slice x36 -> x0, local copies, waits for them, and re-layouts: 46 us -> none  [assemble(): full = lax.dynamic_update_slice(full, jnp.expand_dims(piece, axis), starts)]
  transfers between devices with their start and end apart: 131 -> 96, of which waited for: 56 -> 43; matrix products, arithmetic and copies ran while one was open for 50% -> 8% of each run, Pallas kernels for 0% -> 34%
where the time goes in v3:
time: 930 us; the launch traced here: 921 us
  Pallas kernels  406 us (44%)
  waiting for transfers between devices  306 us (33%)
  starting transfers between devices  89.8 us (10%)
  local copies, waits for them, and re-layouts  49.3 us (5%)
  other arithmetic  33 us (4%)
  between operations  20.8 us (2%)
  blocking collectives  11.6 us (1%)
    ppermute x24, waiting for transfers between devices, forward(): return lax.ppermute(value, 'dp', self.ahead)  190 us
    pallas_call x8, Pallas kernels, rows_times(): kernel_call(kernel, 'rows_times', 1 + 3e-09 * 4 * slots * tokens * depth...  129 us
    ppermute x47, waiting for transfers between devices, hop(): return lax.ppermute(value, axis, [(i, i ^ mask) for i in range(size)])  71.2 us
    pallas_call x4, Pallas kernels, weight_grad(): kernel_call(kernel, 'weight_grad', 1 + 3.4e-09 * 4 * slots * tokens * dep...  68.6 us
    pallas_call x2, Pallas kernels, attend_back(): kernel_call(kernel, 'attend_back', 29, (pairs,), [spec(0), spec(1), spec(...  58.9 us
    pallas_call x9, Pallas kernels, ring_add(): kernel_call(kernel, 'ring_add', 1 + 7e-06 * image.shape[1] * image.shape[...  45.9 us
    ppermute x47, starting transfers between devices, hop(): return lax.ppermute(value, axis, [(i, i ^ mask) for i in range(size)])  38.8 us
    pallas_call x5, Pallas kernels, per_slot(): kernel_call(kernel, name, 6, (slots,), [spec(value.shape, value.ndim == 2...  33.6 us
  transfers between devices with their start and end apart: 96, of which 43 were waited for; matrix products, arithmetic and copies ran while one was open for 8% of the time, Pallas kernels for 34%

profile of v3, /device:TPU:0, one launch (start us, length us, event | category | flops | bytes accessed | tf_op | source)
XLA Modules:
  0.0 920.5 jit_solution(4058334638612997963)
XLA Ops:
  53.1 9.7 %collective-permute-done.8.refs_1_ = bf16[2,4,192,384]{3,2,1,0:T(8,128)(2,1)} collective-permute-done((bf16[2,4,192,384]{3,2,1,0:T(8,128)(2,1)S(1)}, bf16[2,4,192,384]{3,2,1,0:T(8,128)(2,1)}, u32[]{:S(2)}, u32[]{:S(2)}) %collective-permute-start.8) | collective-permute-done | bytes 1179680 | tf_op jit(solution)/shard_map/ppermute | solution.py:96
  70.2 22.3 %collective-permute-done.10.refs_3_ = bf16[2,4,192,384]{3,2,1,0:T(8,128)(2,1)S(1)} collective-permute-done((bf16[2,4,192,384]{3,2,1,0:T(8,128)(2,1)}, bf16[2,4,192,384]{3,2,1,0:T(8,128)(2,1)S(1)}, u32[]{:S(2)}, u32[]{:S(2)}) %collective-permute-start.10) | collective-permute-done | bytes 1179680 | tf_op jit(solution)/shard_map/ppermute | solution.py:96
  95.1 20.4 %collective-permute-done.12.refs_5_ = bf16[2,4,192,384]{3,2,1,0:T(8,128)(2,1)S(1)} collective-permute-done((bf16[2,4,192,384]{3,2,1,0:T(8,128)(2,1)S(1)}, bf16[2,4,192,384]{3,2,1,0:T(8,128)(2,1)S(1)}, u32[]{:S(2)}, u32[]{:S(2)}) %collective-permute-start.12) | collective-permute-done | bytes 1179680 | tf_op jit(solution)/shard_map/ppermute | solution.py:96
  120.6 12.1 %collective-permute-done.17.refs_7_ = bf16[1,4,192,384]{3,2,1,0:T(8,128)(2,1)S(1)} collective-permute-done((bf16[1,4,192,384]{3,2,1,0:T(8,128)(2,1)S(1)}, bf16[1,4,192,384]{3,2,1,0:T(8,128)(2,1)S(1)}, u32[]{:S(2)}, u32[]{:S(2)}) %collective-permute-start.17) | collective-permute-done | bytes 589856 | tf_op jit(solution)/shard_map/ppermute | solution.py:96
  149.3 17.4 %rows_times.8.q.k.v = bf16[4,2,296,1152]{3,2,1,0:T(8,128)(2,1)} custom-call(bf16[2,296,1536]{2,1,0:T(8,128)(2,1)} %get-tuple-element.844.refs_0_.a, bf16[2,296,1536]{2,1,0:T(8,128)(2,1)} %copy-done.42, bf16[2,296,1536]{2,1,0:T(8,128)(2,1)} %copy-done.41, bf16[2,296,1536]{2,1,0:T(8,128)(2,1)} %copy-done.43, bf16[1536,1536]{1,0:T(8,128)(2,1)} %bitcast.168, ...), custom_call_target="tpu_custom_call" | custom-call | flops 6242351616 | bytes 1 | tf_op jit(solution)/shard_map/rows_times/pallas_call | solution.py:393
  169.0 15.3 %attend.2 = (bf16[4,2,296,384]{3,2,1,0:T(8,128)(2,1)}, f32[2,3,2,1184]{3,2,1,0:T(2,128)}) custom-call(bf16[4,2,296,1152]{3,2,1,0:T(8,128)(2,1)} %rows_times.8.q.k.v, bf16[4,2,296,1152]{3,2,1,0:T(8,128)(2,1)} %rows_times.8.q.k.v, bf16[4,2,296,1152]{3,2,1,0:T(8,128)(2,1)} %rows_times.8.q.k.v), custom_call_target="tpu_custom_call" | custom-call | flops 6899999744 | bytes 1 | tf_op jit(solution)/shard_map/attend/pallas_call | solution.py:517
  184.3 15.3 %attend.3 = (bf16[4,2,296,384]{3,2,1,0:T(8,128)(2,1)}, f32[2,3,2,1184]{3,2,1,0:T(2,128)}) custom-call(bf16[4,2,296,1152]{3,2,1,0:T(8,128)(2,1)} %rows_times.8.q.k.v, bf16[4,2,296,1152]{3,2,1,0:T(8,128)(2,1)} %rows_times.8.q.k.v, bf16[4,2,296,1152]{3,2,1,0:T(8,128)(2,1)} %rows_times.8.q.k.v, ...), custom_call_target="tpu_custom_call", output_to_operand_aliasing={{0}: (3, {}), {1}: (4, {})} | custom-call | flops 6899999744 | bytes 1 | tf_op jit(solution)/shard_map/attend/pallas_call | solution.py:517
  199.8 8.9 rows_times.9
  215.2 22.1 %collective-permute-done.27.refs_5_ = bf16[2,1,192,1536]{3,2,1,0:T(8,128)(2,1)S(1)} collective-permute-done((bf16[2,1,192,1536]{3,2,1,0:T(8,128)(2,1)}, bf16[2,1,192,1536]{3,2,1,0:T(8,128)(2,1)S(1)}, u32[]{:S(2)}, u32[]{:S(2)}) %collective-permute-start.27) | collective-permute-done | bytes 1179680 | tf_op jit(solution)/shard_map/ppermute | solution.py:96
  240.3 12.0 %collective-permute-done.29.refs_7_ = bf16[1,1,192,1536]{3,2,1,0:T(8,128)(2,1)S(1)} collective-permute-done((bf16[1,1,192,1536]{3,2,1,0:T(8,128)(2,1)S(1)}, bf16[1,1,192,1536]{3,2,1,0:T(8,128)(2,1)S(1)}, u32[]{:S(2)}, u32[]{:S(2)}) %collective-permute-start.29) | collective-permute-done | bytes 589856 | tf_op jit(solution)/shard_map/ppermute | solution.py:96
  271.3 8.8 collective-permute-done.33.refs_1_
  282.5 23.2 %collective-permute-done.35.refs_3_ = bf16[2,1,192,1536]{3,2,1,0:T(8,128)(2,1)} collective-permute-done((bf16[2,1,192,1536]{3,2,1,0:T(8,128)(2,1)}, bf16[2,1,192,1536]{3,2,1,0:T(8,128)(2,1)}, u32[]{:S(2)}, u32[]{:S(2)}) %collective-permute-start.35) | collective-permute-done | bytes 1179680 | tf_op jit(solution)/shard_map/ppermute | solution.py:96
  315.4 25.5 %rows_times.10 = (bf16[4,2,296,1536]{3,2,1,0:T(8,128)(2,1)}, bf16[4,2,296,1536]{3,2,1,0:T(8,128)(2,1)}) custom-call(bf16[2,296,1536]{2,1,0:T(8,128)(2,1)} %get-tuple-element.702.refs_0_.a, bf16[2,296,1536]{2,1,0:T(8,128)(2,1)} %collective-permute-done.38.refs_1_.b, bf16[2,296,1536]{2,1,0:T(8,128)(2,1)} %collective-permute-done.37.refs_2_.c, ...), custom_call_target="tpu_custom_call" | custom-call | flops 8169801728 | bytes 1 | tf_op jit(solution)/shard_map/rows_times/pallas_call | solution.py:393
  346.3 20.0 %weight_grad.4 = (bf16[8,192,1536]{2,1,0:T(8,128)(2,1)}, bf16[8,192,1536]{2,1,0:T(8,128)(2,1)}, f32[2,1536]{1,0:T(2,128)}) custom-call(bf16[2,296,1536]{2,1,0:T(8,128)(2,1)} %get-tuple-element.670.a.refs_0_, bf16[2,296,1536]{2,1,0:T(8,128)(2,1)} %collective-permute-done.24.b.refs_1_, bf16[2,296,1536]{2,1,0:T(8,128)(2,1)} %collective-permute-done.23.c.refs_2_, ...), custom_call_target="tpu_custom_call" | custom-call | flops 9197775872 | bytes 1 | tf_op jit(solution)/shard_map/weight_grad/pallas_call | solution.py:435
  380.1 18.6 %rows_times.11.refs_0_.refs_1_.refs_2_.refs_3_.grad = bf16[4,2,296,1536]{3,2,1,0:T(8,128)(2,1)} custom-call(bf16[2,296,1536]{2,1,0:T(8,128)(2,1)} %get-tuple-element.670.a.refs_0_, bf16[2,296,1536]{2,1,0:T(8,128)(2,1)} %collective-permute-done.24.b.refs_1_, bf16[2,296,1536]{2,1,0:T(8,128)(2,1)} %collective-permute-done.23.c.refs_2_, ...), custom_call_target="tpu_custom_call" | custom-call | flops 8169801728 | bytes 1 | tf_op jit(solution)/shard_map/rows_times/pallas_call | solution.py:393
  405.2 17.4 %rows_times.12 = (bf16[2,296,1536]{2,1,0:T(8,128)(2,1)}, bf16[2,296,1536]{2,1,0:T(8,128)(2,1)}, bf16[2,296,1536]{2,1,0:T(8,128)(2,1)}, bf16[2,296,1536]{2,1,0:T(8,128)(2,1)}) custom-call(bf16[4,2,296,1536]{3,2,1,0:T(8,128)(2,1)} %rows_times.11.refs_0_.refs_1_.refs_2_.refs_3_.grad, bf16[4,2,296,1536]{3,2,1,0:T(8,128)(2,1)} %rows_times.11.refs_0_.refs_1_.refs_2_.refs_3_.grad, ...), custom_call_target="tpu_custom_call" | custom-call | flops 8169801728 | bytes 1 | tf_op jit(solution)/shard_map/rows_times/pallas_call | solution.py:393
  431.0 20.0 %weight_grad.5 = (bf16[8,192,1536]{2,1,0:T(8,128)(2,1)}, bf16[8,192,1536]{2,1,0:T(8,128)(2,1)}, f32[2,1536]{1,0:T(2,128)}) custom-call(bf16[2,296,1536]{2,1,0:T(8,128)(2,1)} %get-tuple-element.702.refs_0_.a, bf16[2,296,1536]{2,1,0:T(8,128)(2,1)} %collective-permute-done.38.refs_1_.b, bf16[2,296,1536]{2,1,0:T(8,128)(2,1)} %collective-permute-done.37.refs_2_.c, ...), custom_call_target="tpu_custom_call" | custom-call | flops 9197775872 | bytes 1 | tf_op jit(solution)/shard_map/weight_grad/pallas_call | solution.py:435
  451.1 17.4 %rows_times.13 = (bf16[2,296,1536]{2,1,0:T(8,128)(2,1)}, bf16[2,296,1536]{2,1,0:T(8,128)(2,1)}, bf16[2,296,1536]{2,1,0:T(8,128)(2,1)}, bf16[2,296,1536]{2,1,0:T(8,128)(2,1)}) custom-call(bf16[4,2,296,1536]{3,2,1,0:T(8,128)(2,1)} %get-tuple-element.715.grad.refs_0_.refs_1_.refs_2_.refs_3_, ...), custom_call_target="tpu_custom_call" | custom-call | flops 8169801728 | bytes 1 | tf_op jit(solution)/shard_map/rows_times/pallas_call | solution.py:393
  475.0 9.1 middle_back.1
  494.9 19.9 %collective-permute-done.51.ahead = bf16[2,192,1536]{2,1,0:T(8,128)(2,1)} collective-permute-done((bf16[2,192,1536]{2,1,0:T(8,128)(2,1)}, bf16[2,192,1536]{2,1,0:T(8,128)(2,1)}, u32[]{:S(2)}, u32[]{:S(2)}) %collective-permute-start.51) | collective-permute-done | bytes 1179680 | tf_op jit(solution)/shard_map/ppermute | solution.py:96
  535.9 8.9 rows_times.14.grads
  552.3 8.9 weight_grad.6
  561.2 12.9 %collective-permute-done.59.ahead = bf16[2,192,1536]{2,1,0:T(8,128)(2,1)} collective-permute-done((bf16[2,192,1536]{2,1,0:T(8,128)(2,1)}, bf16[2,192,1536]{2,1,0:T(8,128)(2,1)}, u32[]{:S(2)}, u32[]{:S(2)}) %collective-permute-start.59) | collective-permute-done | bytes 1179680 | tf_op jit(solution)/shard_map/ppermute | solution.py:96
  575.2 29.6 %attend_back.2.refs_0_ = bf16[4,2,296,1152]{3,2,1,0:T(8,128)(2,1)} custom-call(bf16[4,2,296,1152]{3,2,1,0:T(8,128)(2,1)} %rows_times.8.q.k.v, bf16[4,2,296,1152]{3,2,1,0:T(8,128)(2,1)} %rows_times.8.q.k.v, bf16[4,2,296,1152]{3,2,1,0:T(8,128)(2,1)} %rows_times.8.q.k.v, bf16[4,2,296,384]{3,2,1,0:T(8,128)(2,1)} %get-tuple-element.826.refs_0_.refs_1_.refs_2_.refs_3_.grad.mixed, ...), custom_call_target="tpu_custom_call" | custom-call | flops 13340000256 | bytes 1 | tf_op jit(solution)/shard_map/attend_back/pallas_call | solution.py:591
  612.1 29.3 %attend_back.3.grad.refs_0_.refs_1_.refs_2_.refs_3_ = bf16[4,2,296,1152]{3,2,1,0:T(8,128)(2,1)} custom-call(bf16[4,2,296,1152]{3,2,1,0:T(8,128)(2,1)} %rows_times.8.q.k.v, bf16[4,2,296,1152]{3,2,1,0:T(8,128)(2,1)} %rows_times.8.q.k.v, bf16[4,2,296,1152]{3,2,1,0:T(8,128)(2,1)} %rows_times.8.q.k.v, ...), custom_call_target="tpu_custom_call", output_to_operand_aliasing={{}: (6, {})} | custom-call | flops 13340000256 | bytes 1 | tf_op jit(solution)/shard_map/attend_back/pallas_call | solution.py:591
  646.8 19.7 %weight_grad.7 = (bf16[8,192,1152]{2,1,0:T(8,128)(2,1)}, bf16[8,192,1152]{2,1,0:T(8,128)(2,1)}, f32[2,1152]{1,0:T(2,128)}) custom-call(bf16[2,296,1536]{2,1,0:T(8,128)(2,1)} %get-tuple-element.844.refs_0_.a, bf16[2,296,1536]{2,1,0:T(8,128)(2,1)} %copy-done.42, bf16[2,296,1536]{2,1,0:T(8,128)(2,1)} %copy-done.41, bf16[2,296,1536]{2,1,0:T(8,128)(2,1)} %copy-done.43, ...), custom_call_target="tpu_custom_call" | custom-call | flops 7013331456 | bytes 1 | tf_op jit(solution)/shard_map/weight_grad/pallas_call | solution.py:435
  666.5 14.7 %rows_times.15 = (bf16[2,296,1536]{2,1,0:T(8,128)(2,1)}, bf16[2,296,1536]{2,1,0:T(8,128)(2,1)}, bf16[2,296,1536]{2,1,0:T(8,128)(2,1)}, bf16[2,296,1536]{2,1,0:T(8,128)(2,1)}) custom-call(bf16[4,2,296,1152]{3,2,1,0:T(8,128)(2,1)} %attend_back.3.grad.refs_0_.refs_1_.refs_2_.refs_3_, bf16[4,2,296,1152]{3,2,1,0:T(8,128)(2,1)} %attend_back.3.grad.refs_0_.refs_1_.refs_2_.refs_3_, ...), custom_call_target="tpu_custom_call" | custom-call | flops 6242351616 | bytes 1 | tf_op jit(solution)/shard_map/rows_times/pallas_call | solution.py:393
  688.9 21.3 %collective-permute-done.67.ahead = bf16[2,192,1536]{2,1,0:T(8,128)(2,1)S(1)} collective-permute-done((bf16[2,192,1536]{2,1,0:T(8,128)(2,1)}, bf16[2,192,1536]{2,1,0:T(8,128)(2,1)S(1)}, u32[]{:S(2)}, u32[]{:S(2)}) %collective-permute-start.67) | collective-permute-done | bytes 1179680 | tf_op jit(solution)/shard_map/ppermute | solution.py:96
  734.9 18.1 %collective-permute-done.72 = f32[10752]{0:T(1024)} collective-permute-done((f32[10752]{0:T(1024)}, f32[10752]{0:T(1024)}, u32[]{:S(2)}, u32[]{:S(2)}) %collective-permute-start.72) | collective-permute-done | bytes 43040 | tf_op jit(solution)/shard_map/ppermute | solution.py:21
  754.5 15.3 %collective-permute-done.73 = f32[10752]{0:T(1024)S(1)} collective-permute-done((f32[10752]{0:T(1024)S(1)}, f32[10752]{0:T(1024)S(1)}, u32[]{:S(2)}, u32[]{:S(2)}) %collective-permute-start.73) | collective-permute-done | bytes 43040 | tf_op jit(solution)/shard_map/ppermute | solution.py:21
  820.1 32.5 %all-reduce.3.cloned.1.call-done = bf16[8,2,192,384]{3,2,0,1:T(8,128)(2,1)} async-done(((bf16[8,2,192,384]{3,2,0,1:T(8,128)(2,1)}), bf16[8,2,192,384]{3,2,0,1:T(8,128)(2,1)}) %all-reduce.3.cloned.1.call-update) | async-done | bytes 2359312
  886.1 14.5 %collective-permute-done.89 = f32[4,2,192]{2,1,0:T(2,128)S(1)} collective-permute-done((f32[4,2,192]{2,1,0:T(2,128)S(1)}, f32[4,2,192]{2,1,0:T(2,128)S(1)}, u32[]{:S(2)}, u32[]{:S(2)}) %collective-permute-start.89) | collective-permute-done | bytes 6176 | tf_op jit(solution)/shard_map/ppermute | solution.py:21
  (445 shorter events, 338.3 us)
Async XLA Ops:
  7.2 845.4 %all-reduce.3.cloned.1.call-start = ((), (), s32[]{:S(2)}) async-start(), calls=%async_computation | async-start | bytes 4718592
  68.7 48.0 %collective-permute-start.14 = (bf16[2,296,1536]{2,1,0:T(8,128)(2,1)}, bf16[2,296,1536]{2,1,0:T(8,128)(2,1)S(1)}, u32[]{:S(2)}, u32[]{:S(2)}) collective-permute-start(bf16[2,296,1536]{2,1,0:T(8,128)(2,1)} %get-tuple-element.844.refs_0_.a), channel_id=1, source_target_pairs={{0,2},{1,3},{2,0},{3,1},{4,6},{5,7},{6,4},{7,5},{8,10},{9,11},{10,... | collective-permute-start | bytes 5455880 | tf_op jit(solution)/shard_map/ppermute | solution.py:21
  134.4 32.4 %collective-permute-start.19 = (bf16[2,1,192,1536]{3,2,1,0:T(8,128)(2,1)}, bf16[2,1,192,1536]{3,2,1,0:T(8,128)(2,1)}, u32[]{:S(2)}, u32[]{:S(2)}) collective-permute-start(bf16[2,1,192,1536]{3,2,1,0:T(8,128)(2,1)} %bitcast.26.refs_0_), channel_id=1, source_target_pairs={{0,8},{8,16},{16,24},{24,28},{28,20},{20,12},{12,4},{4,0},{1,9},{9... | collective-permute-start | bytes 3538952 | tf_op jit(solution)/shard_map/ppermute | solution.py:96
  139.5 60.2 %collective-permute-start.23 = (bf16[2,296,1536]{2,1,0:T(8,128)(2,1)}, bf16[2,296,1536]{2,1,0:T(8,128)(2,1)}, u32[]{:S(2)}, u32[]{:S(2)}) collective-permute-start(bf16[2,296,1536]{2,1,0:T(8,128)(2,1)} %get-tuple-element.670.a.refs_0_), channel_id=1, source_target_pairs={{0,2},{1,3},{2,0},{3,1},{4,6},{5,7},{6,4},{7,5},{8,10},{9,11},{10,... | collective-permute-start | bytes 5455880 | tf_op jit(solution)/shard_map/ppermute | solution.py:21
  141.0 69.9 %collective-permute-start.24 = (bf16[2,296,1536]{2,1,0:T(8,128)(2,1)}, bf16[2,296,1536]{2,1,0:T(8,128)(2,1)}, u32[]{:S(2)}, u32[]{:S(2)}) collective-permute-start(bf16[2,296,1536]{2,1,0:T(8,128)(2,1)} %get-tuple-element.670.a.refs_0_), channel_id=1, source_target_pairs={{0,1},{1,0},{2,3},{3,2},{4,5},{5,4},{6,7},{7,6},{8,9},{9,8},{10,11... | collective-permute-start | bytes 5455880 | tf_op jit(solution)/shard_map/ppermute | solution.py:21
  166.8 32.9 %collective-permute-start.21 = (bf16[2,1,192,1536]{3,2,1,0:T(8,128)(2,1)}, bf16[2,1,192,1536]{3,2,1,0:T(8,128)(2,1)S(1)}, u32[]{:S(2)}, u32[]{:S(2)}) collective-permute-start(bf16[2,1,192,1536]{3,2,1,0:T(8,128)(2,1)} %collective-permute-done.19.refs_1_), channel_id=1, source_target_pairs={{0,8},{8,16},{16,24},{24,28},{28,20},{20,12},{12,4},{4,0},{1,9},{9... | collective-permute-start | bytes 3538952 | tf_op jit(solution)/shard_map/ppermute | solution.py:96
  210.9 45.4 %collective-permute-start.31 = (bf16[2,296,1536]{2,1,0:T(8,128)(2,1)}, bf16[2,296,1536]{2,1,0:T(8,128)(2,1)}, u32[]{:S(2)}, u32[]{:S(2)}) collective-permute-start(bf16[2,296,1536]{2,1,0:T(8,128)(2,1)} %get-tuple-element.595), channel_id=1, source_target_pairs={{0,1},{1,0},{2,3},{3,2},{4,5},{5,4},{6,7},{7,6},{8,9},{9,8},{10,11... | collective-permute-start | bytes 5455880 | tf_op jit(solution)/shard_map/ppermute | solution.py:21
  214.6 41.9 %collective-permute-start.32 = (bf16[2,296,1536]{2,1,0:T(8,128)(2,1)S(1)}, bf16[2,296,1536]{2,1,0:T(8,128)(2,1)}, u32[]{:S(2)}, u32[]{:S(2)}) collective-permute-start(bf16[2,296,1536]{2,1,0:T(8,128)(2,1)S(1)} %add_convert_fusion.3), channel_id=1, source_target_pairs={{0,2},{1,3},{2,0},{3,1},{4,6},{5,7},{6,4},{7,5},{8,10},{9,11},{10,... | collective-permute-start | bytes 5455880 | tf_op jit(solution)/shard_map/ppermute | solution.py:21
  262.8 44.3 %collective-permute-start.37 = (bf16[2,296,1536]{2,1,0:T(8,128)(2,1)}, bf16[2,296,1536]{2,1,0:T(8,128)(2,1)}, u32[]{:S(2)}, u32[]{:S(2)}) collective-permute-start(bf16[2,296,1536]{2,1,0:T(8,128)(2,1)} %get-tuple-element.702.refs_0_.a), channel_id=1, source_target_pairs={{0,2},{1,3},{2,0},{3,1},{4,6},{5,7},{6,4},{7,5},{8,10},{9,11},{10,... | collective-permute-start | bytes 5455880 | tf_op jit(solution)/shard_map/ppermute | solution.py:21
  282.5 33.0 %collective-permute-start.38 = (bf16[2,296,1536]{2,1,0:T(8,128)(2,1)}, bf16[2,296,1536]{2,1,0:T(8,128)(2,1)}, u32[]{:S(2)}, u32[]{:S(2)}) collective-permute-start(bf16[2,296,1536]{2,1,0:T(8,128)(2,1)} %get-tuple-element.702.refs_0_.a), channel_id=1, source_target_pairs={{0,1},{1,0},{2,3},{3,2},{4,5},{5,4},{6,7},{7,6},{8,9},{9,8},{10,11... | collective-permute-start | bytes 5455880 | tf_op jit(solution)/shard_map/ppermute | solution.py:21
  307.1 33.9 %collective-permute-start.40 = (bf16[2,1,192,1536]{3,2,1,0:T(8,128)(2,1)}, bf16[2,1,192,1536]{3,2,1,0:T(8,128)(2,1)S(1)}, u32[]{:S(2)}, u32[]{:S(2)}) collective-permute-start(bf16[2,1,192,1536]{3,2,1,0:T(8,128)(2,1)} %collective-permute-done.35.refs_3_), channel_id=1, source_target_pairs={{0,8},{8,16},{16,24},{24,28},{28,20},{20,12},{12,4},{4,0},{1,9},{9... | collective-permute-start | bytes 3538952 | tf_op jit(solution)/shard_map/ppermute | solution.py:96
  307.8 33.3 %collective-permute-start.41 = (bf16[2,1,192,1536]{3,2,1,0:T(8,128)(2,1)}, bf16[2,1,192,1536]{3,2,1,0:T(8,128)(2,1)}, u32[]{:S(2)}, u32[]{:S(2)}) collective-permute-start(bf16[2,1,192,1536]{3,2,1,0:T(8,128)(2,1)} %collective-permute-done.36.refs_4_), channel_id=1, source_target_pairs={{8,0},{16,8},{24,16},{28,24},{20,28},{12,20},{4,12},{0,4},{9,1},{1... | collective-permute-start | bytes 3538952 | tf_op jit(solution)/shard_map/ppermute | solution.py:99
  424.5 44.0 %collective-permute-start.47 = (bf16[2,192,1536]{2,1,0:T(8,128)(2,1)}, bf16[2,192,1536]{2,1,0:T(8,128)(2,1)}, u32[]{:S(2)}, u32[]{:S(2)}) collective-permute-start(bf16[2,192,1536]{2,1,0:T(8,128)(2,1)} %get-tuple-element.723), channel_id=1, source_target_pairs={{0,8},{8,16},{16,24},{24,28},{28,20},{20,12},{12,4},{4,0},{1,9},{9... | collective-permute-start | bytes 3538952 | tf_op jit(solution)/shard_map/ppermute | solution.py:96
  425.2 43.2 %collective-permute-start.48 = (bf16[2,192,1536]{2,1,0:T(8,128)(2,1)}, bf16[2,192,1536]{2,1,0:T(8,128)(2,1)}, u32[]{:S(2)}, u32[]{:S(2)}) collective-permute-start(bf16[2,192,1536]{2,1,0:T(8,128)(2,1)} %get-tuple-element.724), channel_id=1, source_target_pairs={{8,0},{16,8},{24,16},{28,24},{20,28},{12,20},{4,12},{0,4},{9,1},{1... | collective-permute-start | bytes 3538952 | tf_op jit(solution)/shard_map/ppermute | solution.py:99
  426.7 47.0 %collective-permute-start.49 = (bf16[2,296,1536]{2,1,0:T(8,128)(2,1)}, bf16[2,296,1536]{2,1,0:T(8,128)(2,1)S(1)}, u32[]{:S(2)}, u32[]{:S(2)}) collective-permute-start(bf16[2,296,1536]{2,1,0:T(8,128)(2,1)} %get-tuple-element.731), channel_id=1, source_target_pairs={{0,1},{1,0},{2,3},{3,2},{4,5},{5,4},{6,7},{7,6},{8,9},{9,8},{10,11... | collective-permute-start | bytes 5455880 | tf_op jit(solution)/shard_map/ppermute | solution.py:21
  430.5 43.3 %collective-permute-start.50 = (bf16[2,296,1536]{2,1,0:T(8,128)(2,1)}, bf16[2,296,1536]{2,1,0:T(8,128)(2,1)}, u32[]{:S(2)}, u32[]{:S(2)}) collective-permute-start(bf16[2,296,1536]{2,1,0:T(8,128)(2,1)} %add_convert_fusion.2), channel_id=1, source_target_pairs={{0,2},{1,3},{2,0},{3,1},{4,6},{5,7},{6,4},{7,5},{8,10},{9,11},{10,... | collective-permute-start | bytes 5455880 | tf_op jit(solution)/shard_map/ppermute | solution.py:21
  484.0 47.7 %collective-permute-start.55 = (bf16[2,296,1536]{2,1,0:T(8,128)(2,1)}, bf16[2,296,1536]{2,1,0:T(8,128)(2,1)}, u32[]{:S(2)}, u32[]{:S(2)}) collective-permute-start(bf16[2,296,1536]{2,1,0:T(8,128)(2,1)} %get-tuple-element.793.refs_0_.a), channel_id=1, source_target_pairs={{0,2},{1,3},{2,0},{3,1},{4,6},{5,7},{6,4},{7,5},{8,10},{9,11},{10,... | collective-permute-start | bytes 5455880 | tf_op jit(solution)/shard_map/ppermute | solution.py:21
  489.5 36.8 %collective-permute-start.53 = (bf16[1,192,1536]{2,1,0:T(8,128)(2,1)}, bf16[1,192,1536]{2,1,0:T(8,128)(2,1)}, u32[]{:S(2)}, u32[]{:S(2)}) collective-permute-start(bf16[1,192,1536]{2,1,0:T(8,128)(2,1)} %constant_dynamic-slice_fusion.18), channel_id=1, source_target_pairs={{0,8},{8,16},{16,24},{24,28},{28,20},{20,12},{12,4},{4,0},{1,9},{9... | collective-permute-start | bytes 1769480 | tf_op jit(solution)/shard_map/ppermute | solution.py:96
  492.2 34.6 %collective-permute-start.54 = (bf16[1,192,1536]{2,1,0:T(8,128)(2,1)}, bf16[1,192,1536]{2,1,0:T(8,128)(2,1)}, u32[]{:S(2)}, u32[]{:S(2)}) collective-permute-start(bf16[1,192,1536]{2,1,0:T(8,128)(2,1)} %constant_dynamic-slice_fusion.17), channel_id=1, source_target_pairs={{8,0},{16,8},{24,16},{28,24},{20,28},{12,20},{4,12},{0,4},{9,1},{1... | collective-permute-start | bytes 1769480 | tf_op jit(solution)/shard_map/ppermute | solution.py:99
  547.0 57.7 %collective-permute-start.61 = (bf16[2,192,1536]{2,1,0:T(8,128)(2,1)}, bf16[2,192,1536]{2,1,0:T(8,128)(2,1)}, u32[]{:S(2)}, u32[]{:S(2)}) collective-permute-start(bf16[2,192,1536]{2,1,0:T(8,128)(2,1)} %get-tuple-element.815), channel_id=1, source_target_pairs={{0,8},{8,16},{16,24},{24,28},{28,20},{20,12},{12,4},{4,0},{1,9},{9... | collective-permute-start | bytes 3538952 | tf_op jit(solution)/shard_map/ppermute | solution.py:96
  547.4 57.4 %collective-permute-start.62 = (bf16[2,192,1536]{2,1,0:T(8,128)(2,1)}, bf16[2,192,1536]{2,1,0:T(8,128)(2,1)}, u32[]{:S(2)}, u32[]{:S(2)}) collective-permute-start(bf16[2,192,1536]{2,1,0:T(8,128)(2,1)} %get-tuple-element.816), channel_id=1, source_target_pairs={{8,0},{16,8},{24,16},{28,24},{20,28},{12,20},{4,12},{0,4},{9,1},{1... | collective-permute-start | bytes 3538952 | tf_op jit(solution)/shard_map/ppermute | solution.py:99
  549.1 92.4 %collective-permute-start.63 = (bf16[2,296,1536]{2,1,0:T(8,128)(2,1)}, bf16[2,296,1536]{2,1,0:T(8,128)(2,1)S(1)}, u32[]{:S(2)}, u32[]{:S(2)}) collective-permute-start(bf16[2,296,1536]{2,1,0:T(8,128)(2,1)} %get-tuple-element.831), channel_id=1, source_target_pairs={{0,1},{1,0},{2,3},{3,2},{4,5},{5,4},{6,7},{7,6},{8,9},{9,8},{10,11... | collective-permute-start | bytes 5455880 | tf_op jit(solution)/shard_map/ppermute | solution.py:21
  574.5 67.0 %collective-permute-start.64 = (bf16[2,296,1536]{2,1,0:T(8,128)(2,1)}, bf16[2,296,1536]{2,1,0:T(8,128)(2,1)}, u32[]{:S(2)}, u32[]{:S(2)}) collective-permute-start(bf16[2,296,1536]{2,1,0:T(8,128)(2,1)} %add_convert_fusion.1), channel_id=1, source_target_pairs={{0,2},{1,3},{2,0},{3,1},{4,6},{5,7},{6,4},{7,5},{8,10},{9,11},{10,... | collective-permute-start | bytes 5455880 | tf_op jit(solution)/shard_map/ppermute | solution.py:21
  685.1 36.2 %collective-permute-start.70 = (bf16[1,192,1152]{2,1,0:T(8,128)(2,1)S(1)}, bf16[1,192,1152]{2,1,0:T(8,128)(2,1)}, u32[]{:S(2)}, u32[]{:S(2)}) collective-permute-start(bf16[1,192,1152]{2,1,0:T(8,128)(2,1)S(1)} %constant_dynamic-slice_fusion.16), channel_id=1, source_target_pairs={{0,8},{8,16},{16,24},{24,28},{28,20},{20,12},{12,4},{4,0},{1,9},{9... | collective-permute-start | bytes 1327112 | tf_op jit(solution)/shard_map/ppermute | solution.py:96
  687.8 33.5 %collective-permute-start.71 = (bf16[1,192,1152]{2,1,0:T(8,128)(2,1)}, bf16[1,192,1152]{2,1,0:T(8,128)(2,1)}, u32[]{:S(2)}, u32[]{:S(2)}) collective-permute-start(bf16[1,192,1152]{2,1,0:T(8,128)(2,1)} %constant_dynamic-slice_fusion.15), channel_id=1, source_target_pairs={{8,0},{16,8},{24,16},{28,24},{20,28},{12,20},{4,12},{0,4},{9,1},{1... | collective-permute-start | bytes 1327112 | tf_op jit(solution)/shard_map/ppermute | solution.py:99
  710.3 100.3 %collective-permute-start.77 = (bf16[2,296,1536]{2,1,0:T(8,128)(2,1)}, bf16[2,296,1536]{2,1,0:T(8,128)(2,1)}, u32[]{:S(2)}, u32[]{:S(2)}) collective-permute-start(bf16[2,296,1536]{2,1,0:T(8,128)(2,1)} %get-tuple-element.914), channel_id=1, source_target_pairs={{0,1},{1,0},{2,3},{3,2},{4,5},{5,4},{6,7},{7,6},{8,9},{9,8},{10,11... | collective-permute-start | bytes 5455880 | tf_op jit(solution)/shard_map/ppermute | solution.py:21
  715.1 95.5 %collective-permute-start.78 = (bf16[2,296,1536]{2,1,0:T(8,128)(2,1)}, bf16[2,296,1536]{2,1,0:T(8,128)(2,1)}, u32[]{:S(2)}, u32[]{:S(2)}) collective-permute-start(bf16[2,296,1536]{2,1,0:T(8,128)(2,1)} %add_convert_fusion), channel_id=1, source_target_pairs={{0,2},{1,3},{2,0},{3,1},{4,6},{5,7},{6,4},{7,5},{8,10},{9,11},{10,... | collective-permute-start | bytes 5455880 | tf_op jit(solution)/shard_map/ppermute | solution.py:21
  726.2 66.6 %collective-permute-start.75 = (bf16[2,192,1152]{2,1,0:T(8,128)(2,1)}, bf16[2,192,1152]{2,1,0:T(8,128)(2,1)S(1)}, u32[]{:S(2)}, u32[]{:S(2)}) collective-permute-start(bf16[2,192,1152]{2,1,0:T(8,128)(2,1)} %get-tuple-element.906), channel_id=1, source_target_pairs={{0,8},{8,16},{16,24},{24,28},{28,20},{20,12},{12,4},{4,0},{1,9},{9... | collective-permute-start | bytes 2654216 | tf_op jit(solution)/shard_map/ppermute | solution.py:96
  728.0 64.8 %collective-permute-start.76 = (bf16[2,192,1152]{2,1,0:T(8,128)(2,1)}, bf16[2,192,1152]{2,1,0:T(8,128)(2,1)S(1)}, u32[]{:S(2)}, u32[]{:S(2)}) collective-permute-start(bf16[2,192,1152]{2,1,0:T(8,128)(2,1)} %get-tuple-element.907), channel_id=1, source_target_pairs={{8,0},{16,8},{24,16},{28,24},{20,28},{12,20},{4,12},{0,4},{9,1},{1... | collective-permute-start | bytes 2654216 | tf_op jit(solution)/shard_map/ppermute | solution.py:99
  799.6 54.6 %collective-permute-start.79 = (bf16[2,192,1152]{2,1,0:T(8,128)(2,1)}, bf16[2,192,1152]{2,1,0:T(8,128)(2,1)S(1)}, u32[]{:S(2)}, u32[]{:S(2)}) collective-permute-start(bf16[2,192,1152]{2,1,0:T(8,128)(2,1)} %get-tuple-element.935), channel_id=1, source_target_pairs={{0,8},{8,16},{16,24},{24,28},{28,20},{20,12},{12,4},{4,0},{1,9},{9... | collective-permute-start | bytes 2654216 | tf_op jit(solution)/shard_map/ppermute | solution.py:96
  800.2 54.1 %collective-permute-start.80 = (bf16[2,192,1152]{2,1,0:T(8,128)(2,1)}, bf16[2,192,1152]{2,1,0:T(8,128)(2,1)}, u32[]{:S(2)}, u32[]{:S(2)}) collective-permute-start(bf16[2,192,1152]{2,1,0:T(8,128)(2,1)} %get-tuple-element.936), channel_id=1, source_target_pairs={{8,0},{16,8},{24,16},{28,24},{20,28},{12,20},{4,12},{0,4},{9,1},{1... | collective-permute-start | bytes 2654216 | tf_op jit(solution)/shard_map/ppermute | solution.py:99
  819.0 35.3 %collective-permute-start.81 = (f32[2,2,2,6,384]{4,2,3,1,0:T(2,128)S(1)}, f32[2,2,2,6,384]{4,2,3,1,0:T(2,128)S(1)}, u32[]{:S(2)}, u32[]{:S(2)}) collective-permute-start(f32[2,2,2,6,384]{4,2,3,1,0:T(2,128)S(1)} %pad_maximum_fusion.6), channel_id=1, source_target_pairs={{0,2},{1,3},{2,0},{3,1},{4,6},{5,7},{6,4},{7,5},{8,10},{9,11},{10,... | collective-permute-start | bytes 221192 | tf_op jit(solution)/shard_map/ppermute | solution.py:21
  (111 other events, 1906.5 us)
Sparse Core Ops, SparseCore 0:
  718.4 134.1 all-reduce.2

commit v4 on v3

--- a/solution.py
+++ b/solution.py
@@ -56,12 +56,10 @@
     return held[0] + sum(hop(held[mask], axis, mask, size) for mask in range(1, low))
 
 
-def add_all(value, axis, size):
-    mask = 1
-    while mask < size:
-        value = value + hop(value, axis, mask, size)
-        mask *= 2
-    return value
+def by_column(block, shape):
+    return jnp.moveaxis(block.reshape((4,) + shape), 0, -2).reshape(
+        shape[:-1] + (4 * shape[-1],)
+    )
 
 
 class Order:
@@ -260,38 +258,41 @@
 
 def ring_total(image, text, ahead, back, places, form):
     size, rows, width = image.shape
-    turned = form == "turned"
-    block = rows if turned or rows % 64 else rows // 4
-    part = width // 3
-
-    def kernel(place, image_a, text_a, image_b, text_b, ahead, back, total):
+    block = rows // 4 if form == "plain" and rows % 64 == 0 else rows
+    part = width // 4
+
+    def kernel(place, image_a, text_a, image_b, text_b, ahead, back, total, *more):
         for s, mine in enumerate((image_a, text_a)):
             value = mine[0].astype(F32) + ahead[s].astype(F32) + back[s].astype(F32)
             if form == "parts":
                 for j in range(3):
                     total[s, j] = value[:, j * part : (j + 1) * part]
+                more[0][s] = jnp.transpose(value[:, 3 * part :])
             else:
-                total[s] = jnp.transpose(value) if turned else value
-
-    if form == "parts":
-        out = pl.BlockSpec((2, 3, block, part), lambda i, place: (0, 0, i, 0))
-        shape = (2, 3, rows, part)
-    elif turned:
-        out = pl.BlockSpec((2, width, rows), lambda i, place: (0, 0, 0))
-        shape = (2, width, rows)
+                total[s] = jnp.transpose(value) if form == "turned" else value
+
+    shapes = {
+        "plain": [(2, rows, width)],
+        "turned": [(2, width, rows)],
+        "parts": [(2, 3, rows, part), (2, part, rows)],
+    }[form]
+    if form == "plain":
+        outs = [pl.BlockSpec((2, block, width), lambda i, place: (0, i, 0))]
     else:
-        out = pl.BlockSpec((2, block, width), lambda i, place: (0, i, 0))
-        shape = (2, rows, width)
-    return kernel_call(
+        outs = [
+            pl.BlockSpec(shape, lambda i, place, n=len(shape): (0,) * n) for shape in shapes
+        ]
+    total = kernel_call(
         kernel,
         "ring_total",
         1 + 7e-6 * image.shape[1] * image.shape[2] * 2,
         (rows // block,),
         ring_specs(image, ahead, back, block),
-        out,
-        jax.ShapeDtypeStruct(shape, F32),
+        outs,
+        [jax.ShapeDtypeStruct(shape, F32) for shape in shapes],
         scalars=1,
     )(places, image, text, image, text, ahead, back)
+    return total if form == "parts" else total[0]
 
 
 class Spread:
@@ -301,12 +302,11 @@
         self.beside = hop(part, "tensor", 1, 4)
 
     def arrive(self, order):
-        self.across = order(self.across)
+        self.across, self.beside = order(self.across, self.beside)
         self.corner = hop(self.across, "tensor", 1, 4)
 
     def finish(self, order):
-        beside, corner = order(self.beside, self.corner)
-        return [self.part, beside, self.across, corner]
+        return [self.part, self.beside, self.across, order(self.corner)]
 
 
 class Collect:
@@ -319,9 +319,10 @@
         corner = order(self.corner)
         send = (self.kept.astype(F32) + corner.astype(F32)).astype(BF16)
         self.across = hop(order(send), "tensor", 2, 4)
+        self.beside = order(self.beside)
 
     def finish(self, order):
-        return [self.own, *order(self.beside, self.across)]
+        return [self.own, self.beside, order(self.across)]
 
 
 def piece_specs(pieces, block=None):
@@ -401,15 +402,16 @@
     )(*arrays, *weights, *extras)
 
 
-def weight_grad(pieces, grads, image, size):
+def weight_grad(pieces, grads, image, size, first=0, total=None, earlier=()):
     specs, arrays, (slots, tokens, depth) = piece_specs(pieces)
     width = grads.shape[3]
-    block = column_block(width)
+    block = column_block(math.gcd(first, width))
     text = tokens - image
     spots = [(k, c) for k in range(4) for c in range(slots)]
 
-    def kernel(a, b, c, d, grad, image_out, text_out, sums, image_turned, text_turned):
+    def kernel(a, b, c, d, grad, *refs):
         rows = (a, b, c, d)
+        image_out, text_out, sums, image_turned, text_turned = refs[-5:]
 
         @pl.when(pl.program_id(0) == 0)
         def _():
@@ -430,21 +432,24 @@
         sums[0:1] = jnp.sum(image_grads.astype(F32), 0, keepdims=True)
         sums[1:2] = jnp.sum(text_grads.astype(F32), 0, keepdims=True)
 
-    out = pl.BlockSpec((size, depth // size, block), lambda j: (0, 0, j))
-    shape = jax.ShapeDtypeStruct((size, depth // size, width), BF16)
+    out = pl.BlockSpec((size, depth // size, block), lambda j: (0, 0, first // block + j))
+    shape = jax.ShapeDtypeStruct((size, depth // size, total or width), BF16)
     return kernel_call(
         kernel,
         "weight_grad",
         1 + 3.4e-9 * 4 * slots * tokens * depth * width,
         (width // block,),
-        specs + [pl.BlockSpec((4, slots, tokens, block), lambda j: (0, 0, 0, j))],
+        specs
+        + [pl.BlockSpec((4, slots, tokens, block), lambda j: (0, 0, 0, j))]
+        + [pl.BlockSpec(memory_space=pl.ANY)] * len(earlier),
         [out, out, pl.BlockSpec((2, block), lambda j: (0, j))],
         [shape, shape, jax.ShapeDtypeStruct((2, width), F32)],
         scratch=[
             pltpu.VMEM((depth, len(spots) * image), BF16),
             pltpu.VMEM((depth, len(spots) * text), BF16),
         ],
-    )(*arrays, grads)
+        input_output_aliases={5: 0, 6: 1} if earlier else {},
+    )(*arrays, grads, *earlier)
 
 
 def mul(a, b, dims):
@@ -970,11 +975,9 @@
     mlp_back = Collect(*order(*mlp_parts))
     mlp_back.arrive(order)
     *proj_grad, _ = order.run(
-        lambda *a: weight_grad(a[:4], a[4], image, groups), *branch_full, mixed
-    )
-    fc2_sums.arrive(order)
-    proj_sum = lax.psum_scatter(
-        jnp.stack(order(*proj_grad), 1), "dp", scatter_dimension=0, tiled=False
+        lambda *a: weight_grad(a[:4], a[4], image, groups, 3 * col_width, 4 * col_width),
+        *branch_full,
+        mixed,
     )
     qkv_grads = None
     for slot in range(slots):
@@ -986,43 +989,34 @@
             *given,
         )
         if slot == 0:
+            fc2_sums.arrive(order)
             fc1_sums.arrive(order)
     mlp_terms = mlp_back.finish(order)
     fc1_sums.arrive(order)
     *qkv_grad, qv_sums = order.run(
-        lambda *a: weight_grad(a[:4], a[4], image, groups), *first_full, qkv_grads
-    )
+        lambda *a: weight_grad(
+            a[:4], a[4], image, groups, 0, 4 * col_width, a[5:]
+        ),
+        *first_full,
+        qkv_grads,
+        *proj_grad,
+    )
+    fc1_sums.arrive(order)
     qkv_sums = Scatter(ring, *order(*qkv_grad), "parts")
     first_parts = order.run(
         lambda *a: rows_times(a[0], a[1:], image, True, "split", columns=qkv_part),
         qkv_grads,
         *qkv_full,
     )
-    fc1_sums.arrive(order)
-    first_back = Collect(*first_parts)
+    qkv_sums.arrive(order)
+    first_back = Collect(*order(*first_parts))
     first_back.arrive(order)
-    qkv_sums.arrive(order)
     qv_bias_local = qv_sums.reshape(2, 3, col_width)[:, 0::2]
     proj_bias_local = jnp.sum(middle_vecs[:, :, 3], 0)
     fc2_bias_local = jnp.sum(fc2_bias_local, 0)
     split_sums = jnp.concatenate([qv_bias_local.reshape(-1), fc1_bias_local.reshape(-1)])
     token_sums = jnp.concatenate([proj_bias_local.reshape(-1), fc2_bias_local.reshape(-1)])
-    bias_local = add_all(jnp.concatenate([split_sums, token_sums]), "dp", groups)
-    bias_all = order(lax.all_gather(order(bias_local), "tensor"))
-    cut_a = qv_bias_local.size
-    cut_b = cut_a + fc1_bias_local.size
-    cut_c = cut_b + proj_bias_local.size
-    cut_d = cut_c + fc2_bias_local.size
-
-    def by_column(block, shape):
-        return jnp.moveaxis(block.reshape((4,) + shape), 0, -2).reshape(
-            shape[:-1] + (4 * shape[-1],)
-        )
-
-    qv_bias_grad = by_column(bias_all[:, :cut_a], qv_bias_local.shape)
-    fc1_bias_grad = by_column(bias_all[:, cut_a:cut_b], fc1_bias_local.shape)
-    proj_bias_grad = jnp.sum(bias_all[:, cut_b:cut_c], 0).reshape(proj_bias_local.shape)
-    fc2_bias_grad = jnp.sum(bias_all[:, cut_c:cut_d], 0).reshape(fc2_bias_local.shape)
+    bias_local = jnp.concatenate([split_sums, token_sums])
     image_out, text_out, gate_two = order.run(
         lambda *a: per_slot(
             leave,
@@ -1062,7 +1056,6 @@
         vecs,
         residual,
     )
-    qkv_sums.arrive(order)
     modul_grad = jnp.concatenate(
         [
             enter_vecs,
@@ -1078,11 +1071,15 @@
         ]
     )
     modul_round = order(collect(modul_blocks, "tensor", 4).astype(BF16))
-    modul_all = order(spread(modul_round, "dp", groups))
+    qkv_sums.arrive(order)
+    shared = jnp.concatenate([modul_round.astype(F32).reshape(-1), bias_local])
+    shared = order(spread(order(shared), "dp", groups))
+    modul_all = shared[:, : modul_round.size].astype(BF16)
     modul_all = modul_all.reshape((groups * slots,) + modul_round.shape[1:])
+    bias_local = jnp.sum(shared[:, modul_round.size :], 0)
     cond_part = dot("csjn,sjdn->cd", modul_all, ada_weight)
     ada_bias_part = jnp.sum(modul_all.astype(F32), 0)
-    last = jnp.concatenate([cond_part.reshape(-1), ada_bias_part.reshape(-1)])
+    last = jnp.concatenate([cond_part.reshape(-1), ada_bias_part.reshape(-1), bias_local])
     last = order(spread(order(last), "tensor", 4))
     cond_part = jnp.sum(last[:, : cond_part.size], 0).reshape(groups, slots, rows)
     cond_terms = order(exchange(cond_part, "dp", groups))
@@ -1096,19 +1093,26 @@
     cond_grad = lax.dynamic_slice_in_dim(
         silu_back(cond_term)[0], column * col_width, col_width, 1
     )
-    ada_bias_grad = jnp.stack(
+    last = jnp.stack(
         [
-            lax.dynamic_index_in_dim(
-                last[:, cond_part.size :], column ^ place, 0, keepdims=False
-            ).reshape(ada_bias_part.shape)
+            lax.dynamic_index_in_dim(last[:, cond_part.size :], column ^ place, 0, keepdims=False)
             for place in range(4)
-        ],
-        2,
-    ).reshape(ada_bias.shape)
+        ]
+    )
+    ada_bias_grad = by_column(last[:, : ada_bias_part.size], ada_bias_part.shape)
+    bias_all = last[:, ada_bias_part.size :]
+    cut_a = qv_bias_local.size
+    cut_b = cut_a + fc1_bias_local.size
+    cut_c = cut_b + proj_bias_local.size
+    cut_d = cut_c + fc2_bias_local.size
+
+    qv_bias_grad = by_column(bias_all[:, :cut_a], qv_bias_local.shape)
+    fc1_bias_grad = by_column(bias_all[:, cut_a:cut_b], fc1_bias_local.shape)
+    proj_bias_grad = jnp.sum(bias_all[:, cut_b:cut_c], 0).reshape(proj_bias_local.shape)
+    fc2_bias_grad = jnp.sum(bias_all[:, cut_c:cut_d], 0).reshape(fc2_bias_local.shape)
     ada_grad = dot("cd,csjn->sjdn", cond_rows, modul_all)
     fc2_sum, fc1_sum = fc2_sums.finish(order), fc1_sums.finish(order)
-    proj_sum = jnp.swapaxes(order(proj_sum).astype(F32), 1, 2)
-    qkv_sum = qkv_sums.finish(order)
+    qkv_sum, proj_sum = qkv_sums.finish(order)
     cond_grad = order(cond_grad)
     live = jnp.arange(slots, dtype=jnp.int32) < order.token[0]
     cond_grad = jnp.where(live[:, None], cond_grad, 0.0)

time: 930 us -> 854 us (0.918)
  waiting for transfers between devices: 306 us -> 256 us
  between operations: 20.8 us -> 7.53 us
    unnamed x2 -> x0, waiting for transfers between devices: 32.6 us -> none
    ppermute x47 -> x44, waiting for transfers between devices: 71.2 us -> 52.7 us  [hop(): return lax.ppermute(value, axis, [(i, i ^ mask) for i in range(size)])]
    ppermute x24, waiting for transfers between devices: 12.4 us -> 28.2 us  [backward(): return lax.ppermute(value, 'dp', self.back)]
    ppermute x24, waiting for transfers between devices: 190 us -> 176 us  [forward(): return lax.ppermute(value, 'dp', self.ahead)]
    ppermute x47 -> x44, starting transfers between devices: 38.8 us -> 38.3 us  [hop(): return lax.ppermute(value, axis, [(i, i ^ mask) for i in range(size)])]
  transfers between devices with their start and end apart: 96 -> 92, of which waited for: 43 -> 45; matrix products, arithmetic and copies ran while one was open for 8% -> 7% of each run, Pallas kernels for 34% -> 41%
where the time goes in v4:
time: 854 us; the launch traced here: 844 us
  Pallas kernels  407 us (48%)
  waiting for transfers between devices  256 us (30%)
  starting transfers between devices  88 us (10%)
  local copies, waits for them, and re-layouts  48.2 us (6%)
  other arithmetic  27.3 us (3%)
    ppermute x24, waiting for transfers between devices, forward(): return lax.ppermute(value, 'dp', self.ahead)  176 us
    pallas_call x8, Pallas kernels, rows_times(): kernel_call(kernel, 'rows_times', 1 + 3e-09 * 4 * slots * tokens * depth...  129 us
    pallas_call x4, Pallas kernels, weight_grad(): kernel_call(kernel, 'weight_grad', 1 + 3.4e-09 * 4 * slots * tokens * dep...  68.8 us
    pallas_call x2, Pallas kernels, attend_back(): kernel_call(kernel, 'attend_back', 29, (pairs,), [spec(0), spec(1), spec(...  59 us
    ppermute x44, waiting for transfers between devices, hop(): return lax.ppermute(value, axis, [(i, i ^ mask) for i in range(size)])  52.7 us
    pallas_call x9, Pallas kernels, ring_add(): kernel_call(kernel, 'ring_add', 1 + 7e-06 * image.shape[1] * image.shape[...  46.5 us
    ppermute x44, starting transfers between devices, hop(): return lax.ppermute(value, axis, [(i, i ^ mask) for i in range(size)])  38.3 us
    pallas_call x5, Pallas kernels, per_slot(): kernel_call(kernel, name, 6, (slots,), [spec(value.shape, value.ndim == 2...  33.6 us
  transfers between devices with their start and end apart: 92, of which 45 were waited for; matrix products, arithmetic and copies ran while one was open for 7% of the time, Pallas kernels for 41%

profile of v4, /device:TPU:0, one launch (start us, length us, event | category | flops | bytes accessed | tf_op | source)
XLA Modules:
  0.0 844.1 jit_solution(14024816460043874615)
XLA Ops:
  46.6 9.7 %collective-permute-done.8.refs_1_ = bf16[2,4,192,384]{3,2,1,0:T(8,128)(2,1)} collective-permute-done((bf16[2,4,192,384]{3,2,1,0:T(8,128)(2,1)S(1)}, bf16[2,4,192,384]{3,2,1,0:T(8,128)(2,1)}, u32[]{:S(2)}, u32[]{:S(2)}) %collective-permute-start.8) | collective-permute-done | bytes 1179680 | tf_op jit(solution)/shard_map/ppermute | solution.py:94
  63.6 22.3 %collective-permute-done.10.refs_3_ = bf16[2,4,192,384]{3,2,1,0:T(8,128)(2,1)S(1)} collective-permute-done((bf16[2,4,192,384]{3,2,1,0:T(8,128)(2,1)}, bf16[2,4,192,384]{3,2,1,0:T(8,128)(2,1)S(1)}, u32[]{:S(2)}, u32[]{:S(2)}) %collective-permute-start.10) | collective-permute-done | bytes 1179680 | tf_op jit(solution)/shard_map/ppermute | solution.py:94
  88.5 20.4 %collective-permute-done.12.refs_5_ = bf16[2,4,192,384]{3,2,1,0:T(8,128)(2,1)S(1)} collective-permute-done((bf16[2,4,192,384]{3,2,1,0:T(8,128)(2,1)S(1)}, bf16[2,4,192,384]{3,2,1,0:T(8,128)(2,1)S(1)}, u32[]{:S(2)}, u32[]{:S(2)}) %collective-permute-start.12) | collective-permute-done | bytes 1179680 | tf_op jit(solution)/shard_map/ppermute | solution.py:94
  115.2 12.1 %collective-permute-done.17.refs_7_ = bf16[1,4,192,384]{3,2,1,0:T(8,128)(2,1)S(1)} collective-permute-done((bf16[1,4,192,384]{3,2,1,0:T(8,128)(2,1)S(1)}, bf16[1,4,192,384]{3,2,1,0:T(8,128)(2,1)S(1)}, u32[]{:S(2)}, u32[]{:S(2)}) %collective-permute-start.17) | collective-permute-done | bytes 589856 | tf_op jit(solution)/shard_map/ppermute | solution.py:94
  135.7 8.3 assemble.3
  144.0 17.5 %rows_times.8.q.k.v = bf16[4,2,296,1152]{3,2,1,0:T(8,128)(2,1)} custom-call(bf16[2,296,1536]{2,1,0:T(8,128)(2,1)} %get-tuple-element.852.refs_0_.a, bf16[2,296,1536]{2,1,0:T(8,128)(2,1)} %copy-done.41, bf16[2,296,1536]{2,1,0:T(8,128)(2,1)} %copy-done.40, bf16[2,296,1536]{2,1,0:T(8,128)(2,1)} %copy-done.42, bf16[1536,1536]{1,0:T(8,128)(2,1)} %bitcast.150, ...), custom_call_target="tpu_custom_call" | custom-call | flops 6242351616 | bytes 1 | tf_op jit(solution)/shard_map/rows_times/pallas_call | solution.py:394
  163.7 15.3 %attend.2 = (bf16[4,2,296,384]{3,2,1,0:T(8,128)(2,1)}, f32[2,3,2,1184]{3,2,1,0:T(2,128)}) custom-call(bf16[4,2,296,1152]{3,2,1,0:T(8,128)(2,1)} %rows_times.8.q.k.v, bf16[4,2,296,1152]{3,2,1,0:T(8,128)(2,1)} %rows_times.8.q.k.v, bf16[4,2,296,1152]{3,2,1,0:T(8,128)(2,1)} %rows_times.8.q.k.v), custom_call_target="tpu_custom_call" | custom-call | flops 6899999744 | bytes 1 | tf_op jit(solution)/shard_map/attend/pallas_call | solution.py:522
  179.1 15.3 %attend.3 = (bf16[4,2,296,384]{3,2,1,0:T(8,128)(2,1)}, f32[2,3,2,1184]{3,2,1,0:T(2,128)}) custom-call(bf16[4,2,296,1152]{3,2,1,0:T(8,128)(2,1)} %rows_times.8.q.k.v, bf16[4,2,296,1152]{3,2,1,0:T(8,128)(2,1)} %rows_times.8.q.k.v, bf16[4,2,296,1152]{3,2,1,0:T(8,128)(2,1)} %rows_times.8.q.k.v, ...), custom_call_target="tpu_custom_call", output_to_operand_aliasing={{0}: (3, {}), {1}: (4, {})} | custom-call | flops 6899999744 | bytes 1 | tf_op jit(solution)/shard_map/attend/pallas_call | solution.py:522
  194.6 8.9 %rows_times.9 = (bf16[2,296,1536]{2,1,0:T(8,128)(2,1)}, bf16[2,296,1536]{2,1,0:T(8,128)(2,1)}, bf16[2,296,1536]{2,1,0:T(8,128)(2,1)}, bf16[2,296,1536]{2,1,0:T(8,128)(2,1)}) custom-call(bf16[4,2,296,384]{3,2,1,0:T(8,128)(2,1)} %get-tuple-element.833.refs_0_.refs_1_.refs_2_.refs_3_.grad.mixed, ...), custom_call_target="tpu_custom_call" | custom-call | flops 2387450368 | bytes 1 | tf_op jit(solution)/shard_map/rows_times/pallas_call | solution.py:394
  210.1 22.2 %collective-permute-done.28.refs_5_ = bf16[2,1,192,1536]{3,2,1,0:T(8,128)(2,1)S(1)} collective-permute-done((bf16[2,1,192,1536]{3,2,1,0:T(8,128)(2,1)}, bf16[2,1,192,1536]{3,2,1,0:T(8,128)(2,1)S(1)}, u32[]{:S(2)}, u32[]{:S(2)}) %collective-permute-start.28) | collective-permute-done | bytes 1179680 | tf_op jit(solution)/shard_map/ppermute | solution.py:94
  235.2 11.9 %collective-permute-done.30.refs_7_ = bf16[1,1,192,1536]{3,2,1,0:T(8,128)(2,1)S(1)} collective-permute-done((bf16[1,1,192,1536]{3,2,1,0:T(8,128)(2,1)S(1)}, bf16[1,1,192,1536]{3,2,1,0:T(8,128)(2,1)S(1)}, u32[]{:S(2)}, u32[]{:S(2)}) %collective-permute-start.30) | collective-permute-done | bytes 589856 | tf_op jit(solution)/shard_map/ppermute | solution.py:94
  258.3 7.8 assemble.4
  266.1 8.7 %collective-permute-done.33.refs_1_ = bf16[2,1,192,1536]{3,2,1,0:T(8,128)(2,1)} collective-permute-done((bf16[2,1,192,1536]{3,2,1,0:T(8,128)(2,1)}, bf16[2,1,192,1536]{3,2,1,0:T(8,128)(2,1)}, u32[]{:S(2)}, u32[]{:S(2)}) %collective-permute-start.33) | collective-permute-done | bytes 1179680 | tf_op jit(solution)/shard_map/ppermute | solution.py:94
  277.1 23.2 %collective-permute-done.35.refs_3_ = bf16[2,1,192,1536]{3,2,1,0:T(8,128)(2,1)} collective-permute-done((bf16[2,1,192,1536]{3,2,1,0:T(8,128)(2,1)}, bf16[2,1,192,1536]{3,2,1,0:T(8,128)(2,1)}, u32[]{:S(2)}, u32[]{:S(2)}) %collective-permute-start.35) | collective-permute-done | bytes 1179680 | tf_op jit(solution)/shard_map/ppermute | solution.py:94
  310.1 25.6 %rows_times.10 = (bf16[4,2,296,1536]{3,2,1,0:T(8,128)(2,1)}, bf16[4,2,296,1536]{3,2,1,0:T(8,128)(2,1)}) custom-call(bf16[2,296,1536]{2,1,0:T(8,128)(2,1)} %get-tuple-element.711.refs_0_.a, bf16[2,296,1536]{2,1,0:T(8,128)(2,1)} %collective-permute-done.38.refs_1_.b, bf16[2,296,1536]{2,1,0:T(8,128)(2,1)} %collective-permute-done.37.refs_2_.c, ...), custom_call_target="tpu_custom_call" | custom-call | flops 8169801728 | bytes 1 | tf_op jit(solution)/shard_map/rows_times/pallas_call | solution.py:394
  340.9 20.1 %weight_grad.4 = (bf16[8,192,1536]{2,1,0:T(8,128)(2,1)}, bf16[8,192,1536]{2,1,0:T(8,128)(2,1)}, f32[2,1536]{1,0:T(2,128)}) custom-call(bf16[2,296,1536]{2,1,0:T(8,128)(2,1)} %get-tuple-element.677.a.refs_0_, bf16[2,296,1536]{2,1,0:T(8,128)(2,1)} %collective-permute-done.24.b.refs_1_, bf16[2,296,1536]{2,1,0:T(8,128)(2,1)} %collective-permute-done.23.c.refs_2_, ...), custom_call_target="tpu_custom_call" | custom-call | flops 9197775872 | bytes 1 | tf_op jit(solution)/shard_map/weight_grad/pallas_call | solution.py:437
  361.9 7.8 assemble.5
  374.8 18.5 %rows_times.11.refs_0_.refs_1_.refs_2_.refs_3_.grad = bf16[4,2,296,1536]{3,2,1,0:T(8,128)(2,1)} custom-call(bf16[2,296,1536]{2,1,0:T(8,128)(2,1)} %get-tuple-element.677.a.refs_0_, bf16[2,296,1536]{2,1,0:T(8,128)(2,1)} %collective-permute-done.24.b.refs_1_, bf16[2,296,1536]{2,1,0:T(8,128)(2,1)} %collective-permute-done.23.c.refs_2_, ...), custom_call_target="tpu_custom_call" | custom-call | flops 8169801728 | bytes 1 | tf_op jit(solution)/shard_map/rows_times/pallas_call | solution.py:394
  399.9 17.4 %rows_times.12 = (bf16[2,296,1536]{2,1,0:T(8,128)(2,1)}, bf16[2,296,1536]{2,1,0:T(8,128)(2,1)}, bf16[2,296,1536]{2,1,0:T(8,128)(2,1)}, bf16[2,296,1536]{2,1,0:T(8,128)(2,1)}) custom-call(bf16[4,2,296,1536]{3,2,1,0:T(8,128)(2,1)} %rows_times.11.refs_0_.refs_1_.refs_2_.refs_3_.grad, bf16[4,2,296,1536]{3,2,1,0:T(8,128)(2,1)} %rows_times.11.refs_0_.refs_1_.refs_2_.refs_3_.grad, ...), custom_call_target="tpu_custom_call" | custom-call | flops 8169801728 | bytes 1 | tf_op jit(solution)/shard_map/rows_times/pallas_call | solution.py:394
  426.2 20.1 %weight_grad.5 = (bf16[8,192,1536]{2,1,0:T(8,128)(2,1)}, bf16[8,192,1536]{2,1,0:T(8,128)(2,1)}, f32[2,1536]{1,0:T(2,128)}) custom-call(bf16[2,296,1536]{2,1,0:T(8,128)(2,1)} %get-tuple-element.711.refs_0_.a, bf16[2,296,1536]{2,1,0:T(8,128)(2,1)} %collective-permute-done.38.refs_1_.b, bf16[2,296,1536]{2,1,0:T(8,128)(2,1)} %collective-permute-done.37.refs_2_.c, ...), custom_call_target="tpu_custom_call" | custom-call | flops 9197775872 | bytes 1 | tf_op jit(solution)/shard_map/weight_grad/pallas_call | solution.py:437
  446.2 17.4 %rows_times.13 = (bf16[2,296,1536]{2,1,0:T(8,128)(2,1)}, bf16[2,296,1536]{2,1,0:T(8,128)(2,1)}, bf16[2,296,1536]{2,1,0:T(8,128)(2,1)}, bf16[2,296,1536]{2,1,0:T(8,128)(2,1)}) custom-call(bf16[4,2,296,1536]{3,2,1,0:T(8,128)(2,1)} %get-tuple-element.724.grad.refs_0_.refs_1_.refs_2_.refs_3_, ...), custom_call_target="tpu_custom_call" | custom-call | flops 8169801728 | bytes 1 | tf_op jit(solution)/shard_map/rows_times/pallas_call | solution.py:394
  470.4 9.1 %middle_back.1 = (f32[2,296,1536]{2,1,0:T(8,128)}, bf16[2,296,1536]{2,1,0:T(8,128)(2,1)}, f32[2,2,4,1536]{3,2,1,0:T(4,128)}) custom-call(s32[1]{0:T(128)} %copy.195.seqs, bf16[2,256,1536]{2,1,0:T(8,128)(2,1)} %refs_0_.3, bf16[2,40,1536]{2,1,0:T(8,128)(2,1)} %refs_1_.3, bf16[2,296,1536]{2,1,0:T(8,128)(2,1)} %get-tuple-element.750.refs_2_, ...), custom_call_target="tpu_custom_call" | custom-call | flops 2760000000 | bytes 1 | tf_op jit(solution)/shard_map/middle_back/pallas_call | solution.py:650
  487.0 11.9 %collective-permute-done.51.ahead = bf16[2,192,1536]{2,1,0:T(8,128)(2,1)S(1)} collective-permute-done((bf16[2,192,1536]{2,1,0:T(8,128)(2,1)}, bf16[2,192,1536]{2,1,0:T(8,128)(2,1)S(1)}, u32[]{:S(2)}, u32[]{:S(2)}) %collective-permute-start.51) | collective-permute-done | bytes 1179680 | tf_op jit(solution)/shard_map/ppermute | solution.py:94
  500.9 9.3 %collective-permute-done.52.back = bf16[2,192,1536]{2,1,0:T(8,128)(2,1)} collective-permute-done((bf16[2,192,1536]{2,1,0:T(8,128)(2,1)}, bf16[2,192,1536]{2,1,0:T(8,128)(2,1)}, u32[]{:S(2)}, u32[]{:S(2)}) %collective-permute-start.52) | collective-permute-done | bytes 1179680 | tf_op jit(solution)/shard_map/ppermute | solution.py:97
  531.6 8.9 %rows_times.14.grads = bf16[4,2,296,384]{3,2,1,0:T(8,128)(2,1)} custom-call(bf16[2,296,1536]{2,1,0:T(8,128)(2,1)} %get-tuple-element.803.refs_0_.a, bf16[2,296,1536]{2,1,0:T(8,128)(2,1)} %collective-permute-done.56.refs_1_.b, bf16[2,296,1536]{2,1,0:T(8,128)(2,1)} %collective-permute-done.55.refs_2_.c, ...), custom_call_target="tpu_custom_call" | custom-call | flops 2387450368 | bytes 1 | tf_op jit(solution)/shard_map/rows_times/pallas_call | solution.py:394
  550.3 8.9 %weight_grad.6 = (bf16[8,192,1536]{2,1,0:T(8,128)(2,1)}, bf16[8,192,1536]{2,1,0:T(8,128)(2,1)}, f32[2,384]{1,0:T(2,128)}) custom-call(bf16[2,296,1536]{2,1,0:T(8,128)(2,1)} %get-tuple-element.803.refs_0_.a, bf16[2,296,1536]{2,1,0:T(8,128)(2,1)} %collective-permute-done.56.refs_1_.b, bf16[2,296,1536]{2,1,0:T(8,128)(2,1)} %collective-permute-done.55.refs_2_.c, ...), custom_call_target="tpu_custom_call" | custom-call | flops 2644443904 | bytes 1 | tf_op jit(solution)/shard_map/weight_grad/pallas_call | solution.py:437
  559.8 29.6 %attend_back.2.refs_0_ = bf16[4,2,296,1152]{3,2,1,0:T(8,128)(2,1)} custom-call(bf16[4,2,296,1152]{3,2,1,0:T(8,128)(2,1)} %rows_times.8.q.k.v, bf16[4,2,296,1152]{3,2,1,0:T(8,128)(2,1)} %rows_times.8.q.k.v, bf16[4,2,296,1152]{3,2,1,0:T(8,128)(2,1)} %rows_times.8.q.k.v, bf16[4,2,296,384]{3,2,1,0:T(8,128)(2,1)} %get-tuple-element.833.refs_0_.refs_1_.refs_2_.refs_3_.grad.mixed, ...), custom_call_target="tpu_custom_call" | custom-call | flops 13340000256 | bytes 1 | tf_op jit(solution)/shard_map/attend_back/pallas_call | solution.py:596
  602.8 29.3 %attend_back.3.grad.refs_0_.refs_1_.refs_2_.refs_3_ = bf16[4,2,296,1152]{3,2,1,0:T(8,128)(2,1)} custom-call(bf16[4,2,296,1152]{3,2,1,0:T(8,128)(2,1)} %rows_times.8.q.k.v, bf16[4,2,296,1152]{3,2,1,0:T(8,128)(2,1)} %rows_times.8.q.k.v, bf16[4,2,296,1152]{3,2,1,0:T(8,128)(2,1)} %rows_times.8.q.k.v, ...), custom_call_target="tpu_custom_call", output_to_operand_aliasing={{}: (6, {})} | custom-call | flops 13340000256 | bytes 1 | tf_op jit(solution)/shard_map/attend_back/pallas_call | solution.py:596
  640.5 19.7 %weight_grad.7 = (bf16[8,192,1536]{2,1,0:T(8,128)(2,1)}, bf16[8,192,1536]{2,1,0:T(8,128)(2,1)}, f32[2,1152]{1,0:T(2,128)}) custom-call(bf16[2,296,1536]{2,1,0:T(8,128)(2,1)} %get-tuple-element.852.refs_0_.a, bf16[2,296,1536]{2,1,0:T(8,128)(2,1)} %copy-done.41, bf16[2,296,1536]{2,1,0:T(8,128)(2,1)} %copy-done.40, ...), custom_call_target="tpu_custom_call", output_to_operand_aliasing={{0}: (5, {}), {1}: (6, {})} | custom-call | flops 7013331456 | bytes 1 | tf_op jit(solution)/shard_map/weight_grad/pallas_call | solution.py:437
  671.7 14.8 %rows_times.15 = (bf16[2,296,1536]{2,1,0:T(8,128)(2,1)}, bf16[2,296,1536]{2,1,0:T(8,128)(2,1)}, bf16[2,296,1536]{2,1,0:T(8,128)(2,1)}, bf16[2,296,1536]{2,1,0:T(8,128)(2,1)}) custom-call(bf16[4,2,296,1152]{3,2,1,0:T(8,128)(2,1)} %attend_back.3.grad.refs_0_.refs_1_.refs_2_.refs_3_, bf16[4,2,296,1152]{3,2,1,0:T(8,128)(2,1)} %attend_back.3.grad.refs_0_.refs_1_.refs_2_.refs_3_, ...), custom_call_target="tpu_custom_call" | custom-call | flops 6242351616 | bytes 1 | tf_op jit(solution)/shard_map/rows_times/pallas_call | solution.py:394
  712.5 17.2 %collective-permute-done.73.ahead = bf16[2,192,1536]{2,1,0:T(8,128)(2,1)S(1)} collective-permute-done((bf16[2,192,1536]{2,1,0:T(8,128)(2,1)}, bf16[2,192,1536]{2,1,0:T(8,128)(2,1)S(1)}, u32[]{:S(2)}, u32[]{:S(2)}) %collective-permute-start.73) | collective-permute-done | bytes 1179680 | tf_op jit(solution)/shard_map/ppermute | solution.py:94
  808.8 15.5 %collective-permute-done.86 = f32[4,2,192]{2,1,0:T(2,128)S(1)} collective-permute-done((f32[4,2,192]{2,1,0:T(2,128)S(1)}, f32[4,2,192]{2,1,0:T(2,128)S(1)}, u32[]{:S(2)}, u32[]{:S(2)}) %collective-permute-start.86) | collective-permute-done | bytes 6176 | tf_op jit(solution)/shard_map/ppermute | solution.py:21
  (432 shorter events, 331.6 us)
Async XLA Ops:
  62.2 48.0 %collective-permute-start.14 = (bf16[2,296,1536]{2,1,0:T(8,128)(2,1)}, bf16[2,296,1536]{2,1,0:T(8,128)(2,1)S(1)}, u32[]{:S(2)}, u32[]{:S(2)}) collective-permute-start(bf16[2,296,1536]{2,1,0:T(8,128)(2,1)} %get-tuple-element.852.refs_0_.a), channel_id=1, source_target_pairs={{0,2},{1,3},{2,0},{3,1},{4,6},{5,7},{6,4},{7,5},{8,10},{9,11},{10,... | collective-permute-start | bytes 5455880 | tf_op jit(solution)/shard_map/ppermute | solution.py:21
  63.6 46.5 %collective-permute-start.15 = (bf16[2,296,1536]{2,1,0:T(8,128)(2,1)}, bf16[2,296,1536]{2,1,0:T(8,128)(2,1)S(1)}, u32[]{:S(2)}, u32[]{:S(2)}) collective-permute-start(bf16[2,296,1536]{2,1,0:T(8,128)(2,1)} %get-tuple-element.852.refs_0_.a), channel_id=1, source_target_pairs={{0,1},{1,0},{2,3},{3,2},{4,5},{5,4},{6,7},{7,6},{8,9},{9,8},{10,11... | collective-permute-start | bytes 5455880 | tf_op jit(solution)/shard_map/ppermute | solution.py:21
  129.0 32.5 %collective-permute-start.19 = (bf16[2,1,192,1536]{3,2,1,0:T(8,128)(2,1)}, bf16[2,1,192,1536]{3,2,1,0:T(8,128)(2,1)}, u32[]{:S(2)}, u32[]{:S(2)}) collective-permute-start(bf16[2,1,192,1536]{3,2,1,0:T(8,128)(2,1)} %bitcast.26.refs_0_), channel_id=1, source_target_pairs={{0,8},{8,16},{16,24},{24,28},{28,20},{20,12},{12,4},{4,0},{1,9},{9... | collective-permute-start | bytes 3538952 | tf_op jit(solution)/shard_map/ppermute | solution.py:94
  129.7 31.8 %collective-permute-start.20 = (bf16[2,1,192,1536]{3,2,1,0:T(8,128)(2,1)}, bf16[2,1,192,1536]{3,2,1,0:T(8,128)(2,1)}, u32[]{:S(2)}, u32[]{:S(2)}) collective-permute-start(bf16[2,1,192,1536]{3,2,1,0:T(8,128)(2,1)} %bitcast.26.refs_0_), channel_id=1, source_target_pairs={{8,0},{16,8},{24,16},{28,24},{20,28},{12,20},{4,12},{0,4},{9,1},{1... | collective-permute-start | bytes 3538952 | tf_op jit(solution)/shard_map/ppermute | solution.py:97
  134.2 60.3 %collective-permute-start.23 = (bf16[2,296,1536]{2,1,0:T(8,128)(2,1)}, bf16[2,296,1536]{2,1,0:T(8,128)(2,1)}, u32[]{:S(2)}, u32[]{:S(2)}) collective-permute-start(bf16[2,296,1536]{2,1,0:T(8,128)(2,1)} %get-tuple-element.677.a.refs_0_), channel_id=1, source_target_pairs={{0,2},{1,3},{2,0},{3,1},{4,6},{5,7},{6,4},{7,5},{8,10},{9,11},{10,... | collective-permute-start | bytes 5455880 | tf_op jit(solution)/shard_map/ppermute | solution.py:21
  135.7 58.8 %collective-permute-start.24 = (bf16[2,296,1536]{2,1,0:T(8,128)(2,1)}, bf16[2,296,1536]{2,1,0:T(8,128)(2,1)}, u32[]{:S(2)}, u32[]{:S(2)}) collective-permute-start(bf16[2,296,1536]{2,1,0:T(8,128)(2,1)} %get-tuple-element.677.a.refs_0_), channel_id=1, source_target_pairs={{0,1},{1,0},{2,3},{3,2},{4,5},{5,4},{6,7},{7,6},{8,9},{9,8},{10,11... | collective-permute-start | bytes 5455880 | tf_op jit(solution)/shard_map/ppermute | solution.py:21
  161.5 32.9 %collective-permute-start.21 = (bf16[2,1,192,1536]{3,2,1,0:T(8,128)(2,1)}, bf16[2,1,192,1536]{3,2,1,0:T(8,128)(2,1)S(1)}, u32[]{:S(2)}, u32[]{:S(2)}) collective-permute-start(bf16[2,1,192,1536]{3,2,1,0:T(8,128)(2,1)} %collective-permute-done.19.refs_1_), channel_id=1, source_target_pairs={{0,8},{8,16},{16,24},{24,28},{28,20},{20,12},{12,4},{4,0},{1,9},{9... | collective-permute-start | bytes 3538952 | tf_op jit(solution)/shard_map/ppermute | solution.py:94
  162.2 32.2 %collective-permute-start.22 = (bf16[2,1,192,1536]{3,2,1,0:T(8,128)(2,1)}, bf16[2,1,192,1536]{3,2,1,0:T(8,128)(2,1)}, u32[]{:S(2)}, u32[]{:S(2)}) collective-permute-start(bf16[2,1,192,1536]{3,2,1,0:T(8,128)(2,1)} %collective-permute-done.20.refs_2_), channel_id=1, source_target_pairs={{8,0},{16,8},{24,16},{28,24},{20,28},{12,20},{4,12},{0,4},{9,1},{1... | collective-permute-start | bytes 3538952 | tf_op jit(solution)/shard_map/ppermute | solution.py:97
  204.0 28.3 %collective-permute-start.28 = (bf16[2,1,192,1536]{3,2,1,0:T(8,128)(2,1)}, bf16[2,1,192,1536]{3,2,1,0:T(8,128)(2,1)S(1)}, u32[]{:S(2)}, u32[]{:S(2)}) collective-permute-start(bf16[2,1,192,1536]{3,2,1,0:T(8,128)(2,1)} %copy-done.10), channel_id=1, source_target_pairs={{0,8},{8,16},{16,24},{24,28},{28,20},{20,12},{12,4},{4,0},{1,9},{9... | collective-permute-start | bytes 3538952 | tf_op jit(solution)/shard_map/ppermute | solution.py:94
  209.5 41.9 %collective-permute-start.32 = (bf16[2,296,1536]{2,1,0:T(8,128)(2,1)S(1)}, bf16[2,296,1536]{2,1,0:T(8,128)(2,1)}, u32[]{:S(2)}, u32[]{:S(2)}) collective-permute-start(bf16[2,296,1536]{2,1,0:T(8,128)(2,1)S(1)} %add_convert_fusion.3), channel_id=1, source_target_pairs={{0,2},{1,3},{2,0},{3,1},{4,6},{5,7},{6,4},{7,5},{8,10},{9,11},{10,... | collective-permute-start | bytes 5455880 | tf_op jit(solution)/shard_map/ppermute | solution.py:21
  257.7 44.0 %collective-permute-start.37 = (bf16[2,296,1536]{2,1,0:T(8,128)(2,1)}, bf16[2,296,1536]{2,1,0:T(8,128)(2,1)}, u32[]{:S(2)}, u32[]{:S(2)}) collective-permute-start(bf16[2,296,1536]{2,1,0:T(8,128)(2,1)} %get-tuple-element.711.refs_0_.a), channel_id=1, source_target_pairs={{0,2},{1,3},{2,0},{3,1},{4,6},{5,7},{6,4},{7,5},{8,10},{9,11},{10,... | collective-permute-start | bytes 5455880 | tf_op jit(solution)/shard_map/ppermute | solution.py:21
  258.3 43.4 %collective-permute-start.38 = (bf16[2,296,1536]{2,1,0:T(8,128)(2,1)}, bf16[2,296,1536]{2,1,0:T(8,128)(2,1)}, u32[]{:S(2)}, u32[]{:S(2)}) collective-permute-start(bf16[2,296,1536]{2,1,0:T(8,128)(2,1)} %get-tuple-element.711.refs_0_.a), channel_id=1, source_target_pairs={{0,1},{1,0},{2,3},{3,2},{4,5},{5,4},{6,7},{7,6},{8,9},{9,8},{10,11... | collective-permute-start | bytes 5455880 | tf_op jit(solution)/shard_map/ppermute | solution.py:21
  301.6 34.0 %collective-permute-start.40 = (bf16[2,1,192,1536]{3,2,1,0:T(8,128)(2,1)}, bf16[2,1,192,1536]{3,2,1,0:T(8,128)(2,1)S(1)}, u32[]{:S(2)}, u32[]{:S(2)}) collective-permute-start(bf16[2,1,192,1536]{3,2,1,0:T(8,128)(2,1)} %collective-permute-done.35.refs_3_), channel_id=1, source_target_pairs={{0,8},{8,16},{16,24},{24,28},{28,20},{20,12},{12,4},{4,0},{1,9},{9... | collective-permute-start | bytes 3538952 | tf_op jit(solution)/shard_map/ppermute | solution.py:94
  302.3 33.4 %collective-permute-start.41 = (bf16[2,1,192,1536]{3,2,1,0:T(8,128)(2,1)}, bf16[2,1,192,1536]{3,2,1,0:T(8,128)(2,1)}, u32[]{:S(2)}, u32[]{:S(2)}) collective-permute-start(bf16[2,1,192,1536]{3,2,1,0:T(8,128)(2,1)} %collective-permute-done.36.refs_4_), channel_id=1, source_target_pairs={{8,0},{16,8},{24,16},{28,24},{20,28},{12,20},{4,12},{0,4},{9,1},{1... | collective-permute-start | bytes 3538952 | tf_op jit(solution)/shard_map/ppermute | solution.py:97
  419.6 44.0 %collective-permute-start.48 = (bf16[2,192,1536]{2,1,0:T(8,128)(2,1)}, bf16[2,192,1536]{2,1,0:T(8,128)(2,1)S(1)}, u32[]{:S(2)}, u32[]{:S(2)}) collective-permute-start(bf16[2,192,1536]{2,1,0:T(8,128)(2,1)} %get-tuple-element.732), channel_id=1, source_target_pairs={{0,8},{8,16},{16,24},{24,28},{28,20},{20,12},{12,4},{4,0},{1,9},{9... | collective-permute-start | bytes 3538952 | tf_op jit(solution)/shard_map/ppermute | solution.py:94
  420.2 43.4 %collective-permute-start.49 = (bf16[2,192,1536]{2,1,0:T(8,128)(2,1)}, bf16[2,192,1536]{2,1,0:T(8,128)(2,1)}, u32[]{:S(2)}, u32[]{:S(2)}) collective-permute-start(bf16[2,192,1536]{2,1,0:T(8,128)(2,1)} %get-tuple-element.733), channel_id=1, source_target_pairs={{8,0},{16,8},{24,16},{28,24},{20,28},{12,20},{4,12},{0,4},{9,1},{1... | collective-permute-start | bytes 3538952 | tf_op jit(solution)/shard_map/ppermute | solution.py:97
  425.6 44.8 %collective-permute-start.50 = (bf16[2,296,1536]{2,1,0:T(8,128)(2,1)}, bf16[2,296,1536]{2,1,0:T(8,128)(2,1)}, u32[]{:S(2)}, u32[]{:S(2)}) collective-permute-start(bf16[2,296,1536]{2,1,0:T(8,128)(2,1)} %add_convert_fusion.2), channel_id=1, source_target_pairs={{0,2},{1,3},{2,0},{3,1},{4,6},{5,7},{6,4},{7,5},{8,10},{9,11},{10,... | collective-permute-start | bytes 5455880 | tf_op jit(solution)/shard_map/ppermute | solution.py:21
  469.9 29.1 %collective-permute-start.51 = (bf16[2,192,1536]{2,1,0:T(8,128)(2,1)}, bf16[2,192,1536]{2,1,0:T(8,128)(2,1)S(1)}, u32[]{:S(2)}, u32[]{:S(2)}) collective-permute-start(bf16[2,192,1536]{2,1,0:T(8,128)(2,1)} %get-tuple-element.760), channel_id=1, source_target_pairs={{0,8},{8,16},{16,24},{24,28},{28,20},{20,12},{12,4},{4,0},{1,9},{9... | collective-permute-start | bytes 3538952 | tf_op jit(solution)/shard_map/ppermute | solution.py:94
  479.5 47.9 %collective-permute-start.55 = (bf16[2,296,1536]{2,1,0:T(8,128)(2,1)}, bf16[2,296,1536]{2,1,0:T(8,128)(2,1)}, u32[]{:S(2)}, u32[]{:S(2)}) collective-permute-start(bf16[2,296,1536]{2,1,0:T(8,128)(2,1)} %get-tuple-element.803.refs_0_.a), channel_id=1, source_target_pairs={{0,2},{1,3},{2,0},{3,1},{4,6},{5,7},{6,4},{7,5},{8,10},{9,11},{10,... | collective-permute-start | bytes 5455880 | tf_op jit(solution)/shard_map/ppermute | solution.py:21
  481.2 46.2 %collective-permute-start.56 = (bf16[2,296,1536]{2,1,0:T(8,128)(2,1)}, bf16[2,296,1536]{2,1,0:T(8,128)(2,1)}, u32[]{:S(2)}, u32[]{:S(2)}) collective-permute-start(bf16[2,296,1536]{2,1,0:T(8,128)(2,1)} %get-tuple-element.803.refs_0_.a), channel_id=1, source_target_pairs={{0,1},{1,0},{2,3},{3,2},{4,5},{5,4},{6,7},{7,6},{8,9},{9,8},{10,11... | collective-permute-start | bytes 5455880 | tf_op jit(solution)/shard_map/ppermute | solution.py:21
  481.2 29.1 %collective-permute-start.52 = (bf16[2,192,1536]{2,1,0:T(8,128)(2,1)}, bf16[2,192,1536]{2,1,0:T(8,128)(2,1)}, u32[]{:S(2)}, u32[]{:S(2)}) collective-permute-start(bf16[2,192,1536]{2,1,0:T(8,128)(2,1)} %get-tuple-element.761), channel_id=1, source_target_pairs={{8,0},{16,8},{24,16},{28,24},{20,28},{12,20},{4,12},{0,4},{9,1},{1... | collective-permute-start | bytes 3538952 | tf_op jit(solution)/shard_map/ppermute | solution.py:97
  484.5 31.2 %collective-permute-start.53 = (bf16[1,192,1536]{2,1,0:T(8,128)(2,1)}, bf16[1,192,1536]{2,1,0:T(8,128)(2,1)S(1)}, u32[]{:S(2)}, u32[]{:S(2)}) collective-permute-start(bf16[1,192,1536]{2,1,0:T(8,128)(2,1)} %constant_dynamic-slice_fusion.20), channel_id=1, source_target_pairs={{0,8},{8,16},{16,24},{24,28},{28,20},{20,12},{12,4},{4,0},{1,9},{9... | collective-permute-start | bytes 1769480 | tf_op jit(solution)/shard_map/ppermute | solution.py:94
  541.0 48.3 %collective-permute-start.60 = (bf16[2,192,1536]{2,1,0:T(8,128)(2,1)}, bf16[2,192,1536]{2,1,0:T(8,128)(2,1)}, u32[]{:S(2)}, u32[]{:S(2)}) collective-permute-start(bf16[2,192,1536]{2,1,0:T(8,128)(2,1)} %get-tuple-element.819), channel_id=1, source_target_pairs={{0,8},{8,16},{16,24},{24,28},{28,20},{20,12},{12,4},{4,0},{1,9},{9... | collective-permute-start | bytes 3538952 | tf_op jit(solution)/shard_map/ppermute | solution.py:94
  541.4 47.9 %collective-permute-start.61 = (bf16[2,192,1536]{2,1,0:T(8,128)(2,1)}, bf16[2,192,1536]{2,1,0:T(8,128)(2,1)}, u32[]{:S(2)}, u32[]{:S(2)}) collective-permute-start(bf16[2,192,1536]{2,1,0:T(8,128)(2,1)} %get-tuple-element.820), channel_id=1, source_target_pairs={{8,0},{16,8},{24,16},{28,24},{20,28},{12,20},{4,12},{0,4},{9,1},{1... | collective-permute-start | bytes 3538952 | tf_op jit(solution)/shard_map/ppermute | solution.py:97
  543.1 51.5 %collective-permute-start.62 = (bf16[2,192,1536]{2,1,0:T(8,128)(2,1)}, bf16[2,192,1536]{2,1,0:T(8,128)(2,1)S(1)}, u32[]{:S(2)}, u32[]{:S(2)}) collective-permute-start(bf16[2,192,1536]{2,1,0:T(8,128)(2,1)} %get-tuple-element.822), channel_id=1, source_target_pairs={{0,8},{8,16},{16,24},{24,28},{28,20},{20,12},{12,4},{4,0},{1,9},{9... | collective-permute-start | bytes 3538952 | tf_op jit(solution)/shard_map/ppermute | solution.py:94
  545.7 49.0 %collective-permute-start.63 = (bf16[2,192,1536]{2,1,0:T(8,128)(2,1)}, bf16[2,192,1536]{2,1,0:T(8,128)(2,1)}, u32[]{:S(2)}, u32[]{:S(2)}) collective-permute-start(bf16[2,192,1536]{2,1,0:T(8,128)(2,1)} %get-tuple-element.823), channel_id=1, source_target_pairs={{8,0},{16,8},{24,16},{28,24},{20,28},{12,20},{4,12},{0,4},{9,1},{1... | collective-permute-start | bytes 3538952 | tf_op jit(solution)/shard_map/ppermute | solution.py:97
  559.2 73.0 %collective-permute-start.64 = (bf16[2,296,1536]{2,1,0:T(8,128)(2,1)}, bf16[2,296,1536]{2,1,0:T(8,128)(2,1)}, u32[]{:S(2)}, u32[]{:S(2)}) collective-permute-start(bf16[2,296,1536]{2,1,0:T(8,128)(2,1)} %add_convert_fusion.1), channel_id=1, source_target_pairs={{0,2},{1,3},{2,0},{3,1},{4,6},{5,7},{6,4},{7,5},{8,10},{9,11},{10,... | collective-permute-start | bytes 5455880 | tf_op jit(solution)/shard_map/ppermute | solution.py:21
  600.8 31.4 %collective-permute-start.65 = (bf16[2,192,1536]{2,1,0:T(8,128)(2,1)}, bf16[2,192,1536]{2,1,0:T(8,128)(2,1)S(1)}, u32[]{:S(2)}, u32[]{:S(2)}) collective-permute-start(bf16[2,192,1536]{2,1,0:T(8,128)(2,1)} %get-tuple-element.840), channel_id=1, source_target_pairs={{0,8},{8,16},{16,24},{24,28},{28,20},{20,12},{12,4},{4,0},{1,9},{9... | collective-permute-start | bytes 3538952 | tf_op jit(solution)/shard_map/ppermute | solution.py:94
  601.2 31.0 %collective-permute-start.66 = (bf16[2,192,1536]{2,1,0:T(8,128)(2,1)}, bf16[2,192,1536]{2,1,0:T(8,128)(2,1)}, u32[]{:S(2)}, u32[]{:S(2)}) collective-permute-start(bf16[2,192,1536]{2,1,0:T(8,128)(2,1)} %get-tuple-element.841), channel_id=1, source_target_pairs={{8,0},{16,8},{24,16},{28,24},{20,28},{12,20},{4,12},{0,4},{9,1},{1... | collective-permute-start | bytes 3538952 | tf_op jit(solution)/shard_map/ppermute | solution.py:97
  701.3 42.0 %collective-permute-start.75 = (bf16[2,296,1536]{2,1,0:T(8,128)(2,1)}, bf16[2,296,1536]{2,1,0:T(8,128)(2,1)}, u32[]{:S(2)}, u32[]{:S(2)}) collective-permute-start(bf16[2,296,1536]{2,1,0:T(8,128)(2,1)} %add_convert_fusion), channel_id=1, source_target_pairs={{0,2},{1,3},{2,0},{3,1},{4,6},{5,7},{6,4},{7,5},{8,10},{9,11},{10,... | collective-permute-start | bytes 5455880 | tf_op jit(solution)/shard_map/ppermute | solution.py:21
  797.3 37.6 %collective-permute-start.90 = (bf16[2,192,1536]{2,1,0:T(8,128)(2,1)}, bf16[2,192,1536]{2,1,0:T(8,128)(2,1)S(1)}, u32[]{:S(2)}, u32[]{:S(2)}) collective-permute-start(bf16[2,192,1536]{2,1,0:T(8,128)(2,1)} %get-tuple-element.969), channel_id=1, source_target_pairs={{0,8},{8,16},{16,24},{24,28},{28,20},{20,12},{12,4},{4,0},{1,9},{9... | collective-permute-start | bytes 3538952 | tf_op jit(solution)/shard_map/ppermute | solution.py:94
  798.8 36.0 %collective-permute-start.91 = (bf16[2,192,1536]{2,1,0:T(8,128)(2,1)}, bf16[2,192,1536]{2,1,0:T(8,128)(2,1)}, u32[]{:S(2)}, u32[]{:S(2)}) collective-permute-start(bf16[2,192,1536]{2,1,0:T(8,128)(2,1)} %get-tuple-element.970), channel_id=1, source_target_pairs={{8,0},{16,8},{24,16},{28,24},{20,28},{12,20},{4,12},{0,4},{9,1},{1... | collective-permute-start | bytes 3538952 | tf_op jit(solution)/shard_map/ppermute | solution.py:97
  (107 other events, 1720.2 us)

commit v5 on v4

--- a/solution.py
+++ b/solution.py
@@ -101,6 +101,7 @@
     def __init__(self, ring, shard):
         self.ring, self.step = ring, 0
         self.pieces, self.distances, self.streams = [shard], [0], [0]
+        self.placed, self.full = 0, ()
         self.send(shard, shard)
 
     def send(self, ahead, back):
@@ -122,9 +123,16 @@
     def finish(self, order):
         while len(self.pieces) < self.ring.size + 1:
             self.arrive(order)
-        return assemble(
-            self.pieces, self.streams, self.ring.devices(self.distances), self.ring.size
+        self.place(order)
+        return [f.reshape(-1, f.shape[2]) for f in self.full]
+
+    def place(self, order):
+        new = slice(self.placed, None)
+        places = self.ring.devices(self.distances[new])
+        self.full = order(
+            *assemble(self.pieces[new], self.streams[new], places, self.ring.size, self.full)
         )
+        self.placed = len(self.pieces)
 
 
 class Scatter:
@@ -172,7 +180,7 @@
     )
 
 
-def assemble(pieces, streams, places, size):
+def assemble(pieces, streams, places, size, earlier):
     count = len(pieces)
     parts, rows, width = pieces[0].shape[1:]
     moves = [
@@ -183,8 +191,8 @@
     ]
 
     def kernel(place, *refs):
-        shards, full = refs[:count], refs[count : count + 2]
-        held, sems_in, sems_out = refs[count + 2 : -2], refs[-2], refs[-1]
+        shards, refs = refs[:count], refs[count + len(earlier) :]
+        full, held, sems_in, sems_out = refs[:2], refs[2:-2], refs[-2], refs[-1]
         ins = [pltpu.make_async_copy(shards[i], held[i], sems_in.at[i]) for i in range(count)]
         for copy in ins:
             copy.start()
@@ -201,19 +209,19 @@
 
     whole = pl.BlockSpec(memory_space=pltpu.HBM)
     out = jax.ShapeDtypeStruct((size, rows, parts * width), BF16)
-    full = kernel_call(
+    return kernel_call(
         kernel,
         "assemble",
-        5e-7 * math.prod(out.shape) * 2.5 + 1,
+        1 + 3e-7 * sum(math.prod(p.shape) for p in pieces),
         (1,),
-        [whole] * count,
+        [whole] * (count + len(earlier)),
         [whole] * 2,
         [out] * 2,
         scalars=1,
         scratch=[pltpu.VMEM(p.shape, p.dtype) for p in pieces]
         + [pltpu.SemaphoreType.DMA((count,)), pltpu.SemaphoreType.DMA((len(moves),))],
-    )(places, *pieces)
-    return [f.reshape(size * rows, parts * width) for f in full]
+        input_output_aliases={count + 1: 0, count + 2: 1} if earlier else {},
+    )(places, *pieces, *earlier)
 
 
 def ring_specs(image, ahead, back, block):
@@ -258,7 +266,7 @@
 
 def ring_total(image, text, ahead, back, places, form):
     size, rows, width = image.shape
-    block = rows // 4 if form == "plain" and rows % 64 == 0 else rows
+    block = rows // 4 if rows % 64 == 0 else rows
     part = width // 4
 
     def kernel(place, image_a, text_a, image_b, text_b, ahead, back, total, *more):
@@ -267,21 +275,21 @@
             if form == "parts":
                 for j in range(3):
                     total[s, j] = value[:, j * part : (j + 1) * part]
-                more[0][s] = jnp.transpose(value[:, 3 * part :])
+                more[0][s] = value[:, 3 * part :]
             else:
-                total[s] = jnp.transpose(value) if form == "turned" else value
+                total[s] = value
 
     shapes = {
         "plain": [(2, rows, width)],
-        "turned": [(2, width, rows)],
-        "parts": [(2, 3, rows, part), (2, part, rows)],
+        "parts": [(2, 3, rows, part), (2, rows, part)],
     }[form]
-    if form == "plain":
-        outs = [pl.BlockSpec((2, block, width), lambda i, place: (0, i, 0))]
-    else:
-        outs = [
-            pl.BlockSpec(shape, lambda i, place, n=len(shape): (0,) * n) for shape in shapes
-        ]
+    outs = [
+        pl.BlockSpec(
+            shape[:-2] + (block, shape[-1]),
+            lambda i, place, lead=len(shape) - 2: (0,) * lead + (i, 0),
+        )
+        for shape in shapes
+    ]
     total = kernel_call(
         kernel,
         "ring_total",
@@ -839,10 +847,11 @@
     qkv_ring.arrive(order)
     first_move.arrive(order)
     first_full = first_move.finish(order)
+    qkv_ring.place(order)
     qkv_ring.arrive(order)
     fc1_ring = Gather(ring, order(fc1_shard))
     mlp_move = Spread(order(mlp_round))
-    qkv_full = order(*qkv_ring.finish(order))
+    qkv_full = qkv_ring.finish(order)
 
     qkv = order.run(
         lambda *a: rows_times(
@@ -891,7 +900,7 @@
         proj_add,
     )
     second_move = Spread(second)
-    fc1_full = order(*fc1_ring.finish(order))
+    fc1_full = fc1_ring.finish(order)
     fc2_ring.arrive(order)
     fc2_ring.arrive(order)
     second_move.arrive(order)
@@ -908,8 +917,8 @@
         lambda *a: weight_grad(a[:4], a[4], image, groups), *mlp_full, activated
     )
     fc2_ring.arrive(order)
-    fc2_sums = Scatter(ring, *order(*fc2_grad), "turned")
-    fc2_full = order(*fc2_ring.finish(order))
+    fc2_sums = Scatter(ring, *order(*fc2_grad))
+    fc2_full = fc2_ring.finish(order)
     pre_round = order.run(
         lambda *a: rows_times(
             a[:4],
@@ -993,6 +1002,13 @@
             fc1_sums.arrive(order)
     mlp_terms = mlp_back.finish(order)
     fc1_sums.arrive(order)
+    first_parts = order.run(
+        lambda *a: rows_times(a[0], a[1:], image, True, "split", columns=qkv_part),
+        qkv_grads,
+        *qkv_full,
+    )
+    first_back = Collect(*first_parts)
+    first_back.arrive(order)
     *qkv_grad, qv_sums = order.run(
         lambda *a: weight_grad(
             a[:4], a[4], image, groups, 0, 4 * col_width, a[5:]
@@ -1003,14 +1019,6 @@
     )
     fc1_sums.arrive(order)
     qkv_sums = Scatter(ring, *order(*qkv_grad), "parts")
-    first_parts = order.run(
-        lambda *a: rows_times(a[0], a[1:], image, True, "split", columns=qkv_part),
-        qkv_grads,
-        *qkv_full,
-    )
-    qkv_sums.arrive(order)
-    first_back = Collect(*order(*first_parts))
-    first_back.arrive(order)
     qv_bias_local = qv_sums.reshape(2, 3, col_width)[:, 0::2]
     proj_bias_local = jnp.sum(middle_vecs[:, :, 3], 0)
     fc2_bias_local = jnp.sum(fc2_bias_local, 0)
@@ -1036,6 +1044,8 @@
         after,
         fc2_add,
     )
+    fc2_sum = order(fc2_sums.finish(order))
+    fc1_sum = order(fc1_sums.finish(order))
     qkv_sums.arrive(order)
     first_terms = first_back.finish(order)
     image_grad, text_grad, enter_vecs = order.run(
@@ -1074,6 +1084,8 @@
     qkv_sums.arrive(order)
     shared = jnp.concatenate([modul_round.astype(F32).reshape(-1), bias_local])
     shared = order(spread(order(shared), "dp", groups))
+    qkv_sums.arrive(order)
+    shared = order(shared)
     modul_all = shared[:, : modul_round.size].astype(BF16)
     modul_all = modul_all.reshape((groups * slots,) + modul_round.shape[1:])
     bias_local = jnp.sum(shared[:, modul_round.size :], 0)
@@ -1111,7 +1123,6 @@
     proj_bias_grad = jnp.sum(bias_all[:, cut_b:cut_c], 0).reshape(proj_bias_local.shape)
     fc2_bias_grad = jnp.sum(bias_all[:, cut_c:cut_d], 0).reshape(fc2_bias_local.shape)
     ada_grad = dot("cd,csjn->sjdn", cond_rows, modul_all)
-    fc2_sum, fc1_sum = fc2_sums.finish(order), fc1_sums.finish(order)
     qkv_sum, proj_sum = qkv_sums.finish(order)
     cond_grad = order(cond_grad)
     live = jnp.arange(slots, dtype=jnp.int32) < order.token[0]
@@ -1126,11 +1137,11 @@
         ada_bias_grad,
         qkv_sum,
         qv_bias_grad,
-        proj_sum,
+        jnp.swapaxes(proj_sum, 1, 2),
         proj_bias_grad,
         fc1_sum,
         fc1_bias_grad,
-        fc2_sum,
+        jnp.swapaxes(fc2_sum, 1, 2),
         fc2_bias_grad,
     )
 

time: 854 us -> 855 us (level)
    unnamed x105 -> x97, local copies, waits for them, and re-layouts: 15.5 us -> 6.55 us
    pallas_call x3 -> x4, Pallas kernels: 24 us -> 26.2 us  [assemble(): kernel_call(kernel, 'assemble', 1 + 3e-07 * sum((math.prod(p.shape) for p...]
  transfers between devices with their start and end apart: 92 -> 92, of which waited for: 45 -> 45; matrix products, arithmetic and copies ran while one was open for 7% -> 7% of each run, Pallas kernels for 41% -> 39%
where the time goes in v5:
time: 855 us; the launch traced here: 845 us
  Pallas kernels  409 us (48%)
  waiting for transfers between devices  253 us (30%)
  starting transfers between devices  93.6 us (11%)
  local copies, waits for them, and re-layouts  43.5 us (5%)
  other arithmetic  29.9 us (3%)
    ppermute x24, waiting for transfers between devices, forward(): return lax.ppermute(value, 'dp', self.ahead)  167 us
    pallas_call x8, Pallas kernels, rows_times(): kernel_call(kernel, 'rows_times', 1 + 3e-09 * 4 * slots * tokens * depth...  129 us
    pallas_call x4, Pallas kernels, weight_grad(): kernel_call(kernel, 'weight_grad', 1 + 3.4e-09 * 4 * slots * tokens * dep...  68.8 us
    pallas_call x2, Pallas kernels, attend_back(): kernel_call(kernel, 'attend_back', 29, (pairs,), [spec(0), spec(1), spec(...  58.8 us
    ppermute x44, waiting for transfers between devices, hop(): return lax.ppermute(value, axis, [(i, i ^ mask) for i in range(size)])  56.4 us
    pallas_call x9, Pallas kernels, ring_add(): kernel_call(kernel, 'ring_add', 1 + 7e-06 * image.shape[1] * image.shape[...  46.3 us
    ppermute x44, starting transfers between devices, hop(): return lax.ppermute(value, axis, [(i, i ^ mask) for i in range(size)])  40.3 us
    pallas_call x5, Pallas kernels, per_slot(): kernel_call(kernel, name, 6, (slots,), [spec(value.shape, value.ndim == 2...  33.3 us
  transfers between devices with their start and end apart: 92, of which 45 were waited for; matrix products, arithmetic and copies ran while one was open for 7% of the time, Pallas kernels for 39%

profile of v5, /device:TPU:0, one launch (start us, length us, event | category | flops | bytes accessed | tf_op | source)
XLA Modules:
  0.0 845.1 jit_solution(4505205420239436506)
XLA Ops:
  46.6 9.7 %collective-permute-done.8.refs_1_ = bf16[2,4,192,384]{3,2,1,0:T(8,128)(2,1)} collective-permute-done((bf16[2,4,192,384]{3,2,1,0:T(8,128)(2,1)S(1)}, bf16[2,4,192,384]{3,2,1,0:T(8,128)(2,1)}, u32[]{:S(2)}, u32[]{:S(2)}) %collective-permute-start.8) | collective-permute-done | bytes 1179680 | tf_op jit(solution)/shard_map/ppermute | solution.py:94
  63.6 22.2 %collective-permute-done.10.refs_3_ = bf16[2,4,192,384]{3,2,1,0:T(8,128)(2,1)S(1)} collective-permute-done((bf16[2,4,192,384]{3,2,1,0:T(8,128)(2,1)}, bf16[2,4,192,384]{3,2,1,0:T(8,128)(2,1)S(1)}, u32[]{:S(2)}, u32[]{:S(2)}) %collective-permute-start.10) | collective-permute-done | bytes 1179680 | tf_op jit(solution)/shard_map/ppermute | solution.py:94
  88.4 20.5 %collective-permute-done.12.refs_5_ = bf16[2,4,192,384]{3,2,1,0:T(8,128)(2,1)S(1)} collective-permute-done((bf16[2,4,192,384]{3,2,1,0:T(8,128)(2,1)S(1)}, bf16[2,4,192,384]{3,2,1,0:T(8,128)(2,1)S(1)}, u32[]{:S(2)}, u32[]{:S(2)}) %collective-permute-start.12) | collective-permute-done | bytes 1179680 | tf_op jit(solution)/shard_map/ppermute | solution.py:94
  119.4 7.7 assemble.4
  138.3 17.4 %rows_times.8.q.k.v = bf16[4,2,296,1152]{3,2,1,0:T(8,128)(2,1)} custom-call(bf16[2,296,1536]{2,1,0:T(8,128)(2,1)} %get-tuple-element.879.refs_0_.a, bf16[2,296,1536]{2,1,0:T(8,128)(2,1)} %copy-done.39, bf16[2,296,1536]{2,1,0:T(8,128)(2,1)} %collective-permute-done.14.refs_2_.c, bf16[2,296,1536]{2,1,0:T(8,128)(2,1)} %collective-permute-done.16.refs_3_.d, ...), custom_call_target="tpu_custom_call" | custom-call | flops 6242351616 | bytes 1 | tf_op jit(solution)/shard_map/rows_times/pallas_call | solution.py:402
  160.8 15.3 %attend.2 = (bf16[4,2,296,384]{3,2,1,0:T(8,128)(2,1)}, f32[2,3,2,1184]{3,2,1,0:T(2,128)}) custom-call(bf16[4,2,296,1152]{3,2,1,0:T(8,128)(2,1)} %rows_times.8.q.k.v, bf16[4,2,296,1152]{3,2,1,0:T(8,128)(2,1)} %rows_times.8.q.k.v, bf16[4,2,296,1152]{3,2,1,0:T(8,128)(2,1)} %rows_times.8.q.k.v), custom_call_target="tpu_custom_call" | custom-call | flops 6899999744 | bytes 1 | tf_op jit(solution)/shard_map/attend/pallas_call | solution.py:530
  176.1 15.3 %attend.3 = (bf16[4,2,296,384]{3,2,1,0:T(8,128)(2,1)}, f32[2,3,2,1184]{3,2,1,0:T(2,128)}) custom-call(bf16[4,2,296,1152]{3,2,1,0:T(8,128)(2,1)} %rows_times.8.q.k.v, bf16[4,2,296,1152]{3,2,1,0:T(8,128)(2,1)} %rows_times.8.q.k.v, bf16[4,2,296,1152]{3,2,1,0:T(8,128)(2,1)} %rows_times.8.q.k.v, ...), custom_call_target="tpu_custom_call", output_to_operand_aliasing={{0}: (3, {}), {1}: (4, {})} | custom-call | flops 6899999744 | bytes 1 | tf_op jit(solution)/shard_map/attend/pallas_call | solution.py:530
  191.5 8.6 %rows_times.9 = (bf16[2,296,1536]{2,1,0:T(8,128)(2,1)}, bf16[2,296,1536]{2,1,0:T(8,128)(2,1)}, bf16[2,296,1536]{2,1,0:T(8,128)(2,1)}, bf16[2,296,1536]{2,1,0:T(8,128)(2,1)}) custom-call(bf16[4,2,296,384]{3,2,1,0:T(8,128)(2,1)} %get-tuple-element.844.refs_0_.refs_1_.refs_2_.refs_3_.grad.mixed, ...), custom_call_target="tpu_custom_call" | custom-call | flops 2387450368 | bytes 1 | tf_op jit(solution)/shard_map/rows_times/pallas_call | solution.py:402
  207.7 21.5 %collective-permute-done.28.refs_5_ = bf16[2,1,192,1536]{3,2,1,0:T(8,128)(2,1)S(1)} collective-permute-done((bf16[2,1,192,1536]{3,2,1,0:T(8,128)(2,1)}, bf16[2,1,192,1536]{3,2,1,0:T(8,128)(2,1)S(1)}, u32[]{:S(2)}, u32[]{:S(2)}) %collective-permute-start.28) | collective-permute-done | bytes 1179680 | tf_op jit(solution)/shard_map/ppermute | solution.py:94
  232.1 12.2 %collective-permute-done.30.refs_7_ = bf16[1,1,192,1536]{3,2,1,0:T(8,128)(2,1)S(1)} collective-permute-done((bf16[1,1,192,1536]{3,2,1,0:T(8,128)(2,1)S(1)}, bf16[1,1,192,1536]{3,2,1,0:T(8,128)(2,1)S(1)}, u32[]{:S(2)}, u32[]{:S(2)}) %collective-permute-start.30) | collective-permute-done | bytes 589856 | tf_op jit(solution)/shard_map/ppermute | solution.py:94
  258.3 7.8 assemble.6
  275.7 23.5 %collective-permute-done.35.refs_3_ = bf16[2,1,192,1536]{3,2,1,0:T(8,128)(2,1)} collective-permute-done((bf16[2,1,192,1536]{3,2,1,0:T(8,128)(2,1)}, bf16[2,1,192,1536]{3,2,1,0:T(8,128)(2,1)}, u32[]{:S(2)}, u32[]{:S(2)}) %collective-permute-start.35) | collective-permute-done | bytes 1179680 | tf_op jit(solution)/shard_map/ppermute | solution.py:94
  307.3 25.6 %rows_times.10 = (bf16[4,2,296,1536]{3,2,1,0:T(8,128)(2,1)}, bf16[4,2,296,1536]{3,2,1,0:T(8,128)(2,1)}) custom-call(bf16[2,296,1536]{2,1,0:T(8,128)(2,1)} %get-tuple-element.722.refs_0_.a, bf16[2,296,1536]{2,1,0:T(8,128)(2,1)} %collective-permute-done.38.refs_1_.b, bf16[2,296,1536]{2,1,0:T(8,128)(2,1)} %collective-permute-done.37.refs_2_.c, ...), custom_call_target="tpu_custom_call" | custom-call | flops 8169801728 | bytes 1 | tf_op jit(solution)/shard_map/rows_times/pallas_call | solution.py:402
  337.9 20.1 %weight_grad.4 = (bf16[8,192,1536]{2,1,0:T(8,128)(2,1)}, bf16[8,192,1536]{2,1,0:T(8,128)(2,1)}, f32[2,1536]{1,0:T(2,128)}) custom-call(bf16[2,296,1536]{2,1,0:T(8,128)(2,1)} %get-tuple-element.688.a.refs_0_, bf16[2,296,1536]{2,1,0:T(8,128)(2,1)} %collective-permute-done.24.b.refs_1_, bf16[2,296,1536]{2,1,0:T(8,128)(2,1)} %collective-permute-done.23.c.refs_2_, ...), custom_call_target="tpu_custom_call" | custom-call | flops 9197775872 | bytes 1 | tf_op jit(solution)/shard_map/weight_grad/pallas_call | solution.py:445
  358.8 7.8 assemble.7
  371.8 18.7 %rows_times.11.refs_0_.refs_1_.refs_2_.refs_3_.grad = bf16[4,2,296,1536]{3,2,1,0:T(8,128)(2,1)} custom-call(bf16[2,296,1536]{2,1,0:T(8,128)(2,1)} %get-tuple-element.688.a.refs_0_, bf16[2,296,1536]{2,1,0:T(8,128)(2,1)} %collective-permute-done.24.b.refs_1_, bf16[2,296,1536]{2,1,0:T(8,128)(2,1)} %collective-permute-done.23.c.refs_2_, ...), custom_call_target="tpu_custom_call" | custom-call | flops 8169801728 | bytes 1 | tf_op jit(solution)/shard_map/rows_times/pallas_call | solution.py:402
  397.0 17.4 %rows_times.12 = (bf16[2,296,1536]{2,1,0:T(8,128)(2,1)}, bf16[2,296,1536]{2,1,0:T(8,128)(2,1)}, bf16[2,296,1536]{2,1,0:T(8,128)(2,1)}, bf16[2,296,1536]{2,1,0:T(8,128)(2,1)}) custom-call(bf16[4,2,296,1536]{3,2,1,0:T(8,128)(2,1)} %rows_times.11.refs_0_.refs_1_.refs_2_.refs_3_.grad, bf16[4,2,296,1536]{3,2,1,0:T(8,128)(2,1)} %rows_times.11.refs_0_.refs_1_.refs_2_.refs_3_.grad, ...), custom_call_target="tpu_custom_call" | custom-call | flops 8169801728 | bytes 1 | tf_op jit(solution)/shard_map/rows_times/pallas_call | solution.py:402
  424.4 20.1 %weight_grad.5 = (bf16[8,192,1536]{2,1,0:T(8,128)(2,1)}, bf16[8,192,1536]{2,1,0:T(8,128)(2,1)}, f32[2,1536]{1,0:T(2,128)}) custom-call(bf16[2,296,1536]{2,1,0:T(8,128)(2,1)} %get-tuple-element.722.refs_0_.a, bf16[2,296,1536]{2,1,0:T(8,128)(2,1)} %collective-permute-done.38.refs_1_.b, bf16[2,296,1536]{2,1,0:T(8,128)(2,1)} %collective-permute-done.37.refs_2_.c, ...), custom_call_target="tpu_custom_call" | custom-call | flops 9197775872 | bytes 1 | tf_op jit(solution)/shard_map/weight_grad/pallas_call | solution.py:445
  444.5 17.4 %rows_times.13 = (bf16[2,296,1536]{2,1,0:T(8,128)(2,1)}, bf16[2,296,1536]{2,1,0:T(8,128)(2,1)}, bf16[2,296,1536]{2,1,0:T(8,128)(2,1)}, bf16[2,296,1536]{2,1,0:T(8,128)(2,1)}) custom-call(bf16[4,2,296,1536]{3,2,1,0:T(8,128)(2,1)} %get-tuple-element.735.grad.refs_0_.refs_1_.refs_2_.refs_3_, ...), custom_call_target="tpu_custom_call" | custom-call | flops 8169801728 | bytes 1 | tf_op jit(solution)/shard_map/rows_times/pallas_call | solution.py:402
  468.5 9.1 %middle_back.1 = (f32[2,296,1536]{2,1,0:T(8,128)}, bf16[2,296,1536]{2,1,0:T(8,128)(2,1)}, f32[2,2,4,1536]{3,2,1,0:T(4,128)}) custom-call(s32[1]{0:T(128)} %copy.194.seqs, bf16[2,256,1536]{2,1,0:T(8,128)(2,1)} %refs_0_.3, bf16[2,40,1536]{2,1,0:T(8,128)(2,1)} %refs_1_.3, bf16[2,296,1536]{2,1,0:T(8,128)(2,1)} %get-tuple-element.761.refs_2_, ...), custom_call_target="tpu_custom_call" | custom-call | flops 2760000000 | bytes 1 | tf_op jit(solution)/shard_map/middle_back/pallas_call | solution.py:658
  483.8 13.4 %collective-permute-done.51.ahead = bf16[2,192,1536]{2,1,0:T(8,128)(2,1)S(1)} collective-permute-done((bf16[2,192,1536]{2,1,0:T(8,128)(2,1)}, bf16[2,192,1536]{2,1,0:T(8,128)(2,1)S(1)}, u32[]{:S(2)}, u32[]{:S(2)}) %collective-permute-start.51) | collective-permute-done | bytes 1179680 | tf_op jit(solution)/shard_map/ppermute | solution.py:94
  512.4 6.9 collective-permute-done.54.back
  528.4 8.9 %rows_times.14.grads = bf16[4,2,296,384]{3,2,1,0:T(8,128)(2,1)} custom-call(bf16[2,296,1536]{2,1,0:T(8,128)(2,1)} %get-tuple-element.814.refs_0_.a, bf16[2,296,1536]{2,1,0:T(8,128)(2,1)} %collective-permute-done.56.refs_1_.b, bf16[2,296,1536]{2,1,0:T(8,128)(2,1)} %collective-permute-done.55.refs_2_.c, ...), custom_call_target="tpu_custom_call" | custom-call | flops 2387450368 | bytes 1 | tf_op jit(solution)/shard_map/rows_times/pallas_call | solution.py:402
  547.4 9.0 %weight_grad.6 = (bf16[8,192,1536]{2,1,0:T(8,128)(2,1)}, bf16[8,192,1536]{2,1,0:T(8,128)(2,1)}, f32[2,384]{1,0:T(2,128)}) custom-call(bf16[2,296,1536]{2,1,0:T(8,128)(2,1)} %get-tuple-element.814.refs_0_.a, bf16[2,296,1536]{2,1,0:T(8,128)(2,1)} %collective-permute-done.56.refs_1_.b, bf16[2,296,1536]{2,1,0:T(8,128)(2,1)} %collective-permute-done.55.refs_2_.c, ...), custom_call_target="tpu_custom_call" | custom-call | flops 2644443904 | bytes 1 | tf_op jit(solution)/shard_map/weight_grad/pallas_call | solution.py:445
  558.0 29.4 %attend_back.2.refs_0_ = bf16[4,2,296,1152]{3,2,1,0:T(8,128)(2,1)} custom-call(bf16[4,2,296,1152]{3,2,1,0:T(8,128)(2,1)} %rows_times.8.q.k.v, bf16[4,2,296,1152]{3,2,1,0:T(8,128)(2,1)} %rows_times.8.q.k.v, bf16[4,2,296,1152]{3,2,1,0:T(8,128)(2,1)} %rows_times.8.q.k.v, bf16[4,2,296,384]{3,2,1,0:T(8,128)(2,1)} %get-tuple-element.844.refs_0_.refs_1_.refs_2_.refs_3_.grad.mixed, ...), custom_call_target="tpu_custom_call" | custom-call | flops 13340000256 | bytes 1 | tf_op jit(solution)/shard_map/attend_back/pallas_call | solution.py:604
  599.6 29.4 %attend_back.3.refs_0_.refs_1_.refs_2_.refs_3_.grad = bf16[4,2,296,1152]{3,2,1,0:T(8,128)(2,1)} custom-call(bf16[4,2,296,1152]{3,2,1,0:T(8,128)(2,1)} %rows_times.8.q.k.v, bf16[4,2,296,1152]{3,2,1,0:T(8,128)(2,1)} %rows_times.8.q.k.v, bf16[4,2,296,1152]{3,2,1,0:T(8,128)(2,1)} %rows_times.8.q.k.v, ...), custom_call_target="tpu_custom_call", output_to_operand_aliasing={{}: (6, {})} | custom-call | flops 13340000256 | bytes 1 | tf_op jit(solution)/shard_map/attend_back/pallas_call | solution.py:604
  635.3 14.8 %rows_times.15 = (bf16[2,296,1536]{2,1,0:T(8,128)(2,1)}, bf16[2,296,1536]{2,1,0:T(8,128)(2,1)}, bf16[2,296,1536]{2,1,0:T(8,128)(2,1)}, bf16[2,296,1536]{2,1,0:T(8,128)(2,1)}) custom-call(bf16[4,2,296,1152]{3,2,1,0:T(8,128)(2,1)} %attend_back.3.refs_0_.refs_1_.refs_2_.refs_3_.grad, bf16[4,2,296,1152]{3,2,1,0:T(8,128)(2,1)} %attend_back.3.refs_0_.refs_1_.refs_2_.refs_3_.grad, ...), custom_call_target="tpu_custom_call" | custom-call | flops 6242351616 | bytes 1 | tf_op jit(solution)/shard_map/rows_times/pallas_call | solution.py:402
  662.9 19.6 %weight_grad.7 = (bf16[8,192,1536]{2,1,0:T(8,128)(2,1)}, bf16[8,192,1536]{2,1,0:T(8,128)(2,1)}, f32[2,1152]{1,0:T(2,128)}) custom-call(bf16[2,296,1536]{2,1,0:T(8,128)(2,1)} %get-tuple-element.879.refs_0_.a, bf16[2,296,1536]{2,1,0:T(8,128)(2,1)} %copy-done.39, ...), custom_call_target="tpu_custom_call", output_to_operand_aliasing={{0}: (5, {}), {1}: (6, {})} | custom-call | flops 7013331456 | bytes 1 | tf_op jit(solution)/shard_map/weight_grad/pallas_call | solution.py:445
  715.1 7.2 enter_back.1
  729.2 10.3 %collective-permute-done.76.ahead = bf16[2,192,1536]{2,1,0:T(8,128)(2,1)S(1)} collective-permute-done((bf16[2,192,1536]{2,1,0:T(8,128)(2,1)}, bf16[2,192,1536]{2,1,0:T(8,128)(2,1)S(1)}, u32[]{:S(2)}, u32[]{:S(2)}) %collective-permute-start.76) | collective-permute-done | bytes 1179680 | tf_op jit(solution)/shard_map/ppermute | solution.py:94
  764.2 20.2 %collective-permute-done.82.ahead = bf16[2,192,1536]{2,1,0:T(8,128)(2,1)} collective-permute-done((bf16[2,192,1536]{2,1,0:T(8,128)(2,1)}, bf16[2,192,1536]{2,1,0:T(8,128)(2,1)}, u32[]{:S(2)}, u32[]{:S(2)}) %collective-permute-start.82) | collective-permute-done | bytes 1179680 | tf_op jit(solution)/shard_map/ppermute | solution.py:94
  804.6 23.1 %collective-permute-done.86 = f32[4,2,192]{2,1,0:T(2,128)S(1)} collective-permute-done((f32[4,2,192]{2,1,0:T(2,128)S(1)}, f32[4,2,192]{2,1,0:T(2,128)S(1)}, u32[]{:S(2)}, u32[]{:S(2)}) %collective-permute-start.86) | collective-permute-done | bytes 6176 | tf_op jit(solution)/shard_map/ppermute | solution.py:21
  (430 shorter events, 327.8 us)
Async XLA Ops:
  62.1 48.0 %collective-permute-start.14 = (bf16[2,296,1536]{2,1,0:T(8,128)(2,1)}, bf16[2,296,1536]{2,1,0:T(8,128)(2,1)}, u32[]{:S(2)}, u32[]{:S(2)}) collective-permute-start(bf16[2,296,1536]{2,1,0:T(8,128)(2,1)} %get-tuple-element.879.refs_0_.a), channel_id=1, source_target_pairs={{0,2},{1,3},{2,0},{3,1},{4,6},{5,7},{6,4},{7,5},{8,10},{9,11},{10,... | collective-permute-start | bytes 5455880 | tf_op jit(solution)/shard_map/ppermute | solution.py:21
  63.6 46.5 %collective-permute-start.15 = (bf16[2,296,1536]{2,1,0:T(8,128)(2,1)}, bf16[2,296,1536]{2,1,0:T(8,128)(2,1)S(1)}, u32[]{:S(2)}, u32[]{:S(2)}) collective-permute-start(bf16[2,296,1536]{2,1,0:T(8,128)(2,1)} %get-tuple-element.879.refs_0_.a), channel_id=1, source_target_pairs={{0,1},{1,0},{2,3},{3,2},{4,5},{5,4},{6,7},{7,6},{8,9},{9,8},{10,11... | collective-permute-start | bytes 5455880 | tf_op jit(solution)/shard_map/ppermute | solution.py:21
  134.0 57.5 %collective-permute-start.23 = (bf16[2,296,1536]{2,1,0:T(8,128)(2,1)}, bf16[2,296,1536]{2,1,0:T(8,128)(2,1)}, u32[]{:S(2)}, u32[]{:S(2)}) collective-permute-start(bf16[2,296,1536]{2,1,0:T(8,128)(2,1)} %get-tuple-element.688.a.refs_0_), channel_id=1, source_target_pairs={{0,2},{1,3},{2,0},{3,1},{4,6},{5,7},{6,4},{7,5},{8,10},{9,11},{10,... | collective-permute-start | bytes 5455880 | tf_op jit(solution)/shard_map/ppermute | solution.py:21
  135.4 56.0 %collective-permute-start.24 = (bf16[2,296,1536]{2,1,0:T(8,128)(2,1)}, bf16[2,296,1536]{2,1,0:T(8,128)(2,1)}, u32[]{:S(2)}, u32[]{:S(2)}) collective-permute-start(bf16[2,296,1536]{2,1,0:T(8,128)(2,1)} %get-tuple-element.688.a.refs_0_), channel_id=1, source_target_pairs={{0,1},{1,0},{2,3},{3,2},{4,5},{5,4},{6,7},{7,6},{8,9},{9,8},{10,11... | collective-permute-start | bytes 5455880 | tf_op jit(solution)/shard_map/ppermute | solution.py:21
  158.5 32.9 %collective-permute-start.21 = (bf16[2,1,192,1536]{3,2,1,0:T(8,128)(2,1)S(1)}, bf16[2,1,192,1536]{3,2,1,0:T(8,128)(2,1)}, u32[]{:S(2)}, u32[]{:S(2)}) collective-permute-start(bf16[2,1,192,1536]{3,2,1,0:T(8,128)(2,1)S(1)} %collective-permute-done.19.refs_1_), channel_id=1, source_target_pairs={{0,8},{8,16},{16,24},{24,28},{28,20},{20,12},{12,4},{4,0},{1,9},{9... | collective-permute-start | bytes 3538952 | tf_op jit(solution)/shard_map/ppermute | solution.py:94
  158.8 32.6 %collective-permute-start.22 = (bf16[2,1,192,1536]{3,2,1,0:T(8,128)(2,1)}, bf16[2,1,192,1536]{3,2,1,0:T(8,128)(2,1)}, u32[]{:S(2)}, u32[]{:S(2)}) collective-permute-start(bf16[2,1,192,1536]{3,2,1,0:T(8,128)(2,1)} %collective-permute-done.20.refs_2_), channel_id=1, source_target_pairs={{8,0},{16,8},{24,16},{28,24},{20,28},{12,20},{4,12},{0,4},{9,1},{1... | collective-permute-start | bytes 3538952 | tf_op jit(solution)/shard_map/ppermute | solution.py:97
  200.6 28.5 %collective-permute-start.28 = (bf16[2,1,192,1536]{3,2,1,0:T(8,128)(2,1)}, bf16[2,1,192,1536]{3,2,1,0:T(8,128)(2,1)S(1)}, u32[]{:S(2)}, u32[]{:S(2)}) collective-permute-start(bf16[2,1,192,1536]{3,2,1,0:T(8,128)(2,1)} %collective-permute-done.21.refs_3_), channel_id=1, source_target_pairs={{0,8},{8,16},{16,24},{24,28},{28,20},{20,12},{12,4},{4,0},{1,9},{9... | collective-permute-start | bytes 3538952 | tf_op jit(solution)/shard_map/ppermute | solution.py:94
  200.9 28.3 %collective-permute-start.29 = (bf16[2,1,192,1536]{3,2,1,0:T(8,128)(2,1)}, bf16[2,1,192,1536]{3,2,1,0:T(8,128)(2,1)S(1)}, u32[]{:S(2)}, u32[]{:S(2)}) collective-permute-start(bf16[2,1,192,1536]{3,2,1,0:T(8,128)(2,1)} %collective-permute-done.22.refs_4_), channel_id=1, source_target_pairs={{8,0},{16,8},{24,16},{28,24},{20,28},{12,20},{4,12},{0,4},{9,1},{1... | collective-permute-start | bytes 3538952 | tf_op jit(solution)/shard_map/ppermute | solution.py:97
  206.1 42.6 %collective-permute-start.32 = (bf16[2,296,1536]{2,1,0:T(8,128)(2,1)S(1)}, bf16[2,296,1536]{2,1,0:T(8,128)(2,1)}, u32[]{:S(2)}, u32[]{:S(2)}) collective-permute-start(bf16[2,296,1536]{2,1,0:T(8,128)(2,1)S(1)} %add_convert_fusion.3), channel_id=1, source_target_pairs={{0,2},{1,3},{2,0},{3,1},{4,6},{5,7},{6,4},{7,5},{8,10},{9,11},{10,... | collective-permute-start | bytes 5455880 | tf_op jit(solution)/shard_map/ppermute | solution.py:21
  254.9 44.6 %collective-permute-start.37 = (bf16[2,296,1536]{2,1,0:T(8,128)(2,1)}, bf16[2,296,1536]{2,1,0:T(8,128)(2,1)}, u32[]{:S(2)}, u32[]{:S(2)}) collective-permute-start(bf16[2,296,1536]{2,1,0:T(8,128)(2,1)} %get-tuple-element.722.refs_0_.a), channel_id=1, source_target_pairs={{0,2},{1,3},{2,0},{3,1},{4,6},{5,7},{6,4},{7,5},{8,10},{9,11},{10,... | collective-permute-start | bytes 5455880 | tf_op jit(solution)/shard_map/ppermute | solution.py:21
  256.5 43.0 %collective-permute-start.38 = (bf16[2,296,1536]{2,1,0:T(8,128)(2,1)}, bf16[2,296,1536]{2,1,0:T(8,128)(2,1)}, u32[]{:S(2)}, u32[]{:S(2)}) collective-permute-start(bf16[2,296,1536]{2,1,0:T(8,128)(2,1)} %get-tuple-element.722.refs_0_.a), channel_id=1, source_target_pairs={{0,1},{1,0},{2,3},{3,2},{4,5},{5,4},{6,7},{7,6},{8,9},{9,8},{10,11... | collective-permute-start | bytes 5455880 | tf_op jit(solution)/shard_map/ppermute | solution.py:21
  299.5 33.3 %collective-permute-start.40 = (bf16[2,1,192,1536]{3,2,1,0:T(8,128)(2,1)}, bf16[2,1,192,1536]{3,2,1,0:T(8,128)(2,1)S(1)}, u32[]{:S(2)}, u32[]{:S(2)}) collective-permute-start(bf16[2,1,192,1536]{3,2,1,0:T(8,128)(2,1)} %collective-permute-done.35.refs_3_), channel_id=1, source_target_pairs={{0,8},{8,16},{16,24},{24,28},{28,20},{20,12},{12,4},{4,0},{1,9},{9... | collective-permute-start | bytes 3538952 | tf_op jit(solution)/shard_map/ppermute | solution.py:94
  299.9 32.9 %collective-permute-start.41 = (bf16[2,1,192,1536]{3,2,1,0:T(8,128)(2,1)}, bf16[2,1,192,1536]{3,2,1,0:T(8,128)(2,1)}, u32[]{:S(2)}, u32[]{:S(2)}) collective-permute-start(bf16[2,1,192,1536]{3,2,1,0:T(8,128)(2,1)} %collective-permute-done.36.refs_4_), channel_id=1, source_target_pairs={{8,0},{16,8},{24,16},{28,24},{20,28},{12,20},{4,12},{0,4},{9,1},{1... | collective-permute-start | bytes 3538952 | tf_op jit(solution)/shard_map/ppermute | solution.py:97
  416.7 45.1 %collective-permute-start.48 = (bf16[2,192,1536]{2,1,0:T(8,128)(2,1)}, bf16[2,192,1536]{2,1,0:T(8,128)(2,1)S(1)}, u32[]{:S(2)}, u32[]{:S(2)}) collective-permute-start(bf16[2,192,1536]{2,1,0:T(8,128)(2,1)} %get-tuple-element.743), channel_id=1, source_target_pairs={{0,8},{8,16},{16,24},{24,28},{28,20},{20,12},{12,4},{4,0},{1,9},{9... | collective-permute-start | bytes 3538952 | tf_op jit(solution)/shard_map/ppermute | solution.py:94
  417.1 44.7 %collective-permute-start.49 = (bf16[2,192,1536]{2,1,0:T(8,128)(2,1)}, bf16[2,192,1536]{2,1,0:T(8,128)(2,1)}, u32[]{:S(2)}, u32[]{:S(2)}) collective-permute-start(bf16[2,192,1536]{2,1,0:T(8,128)(2,1)} %get-tuple-element.744), channel_id=1, source_target_pairs={{8,0},{16,8},{24,16},{28,24},{20,28},{12,20},{4,12},{0,4},{9,1},{1... | collective-permute-start | bytes 3538952 | tf_op jit(solution)/shard_map/ppermute | solution.py:97
  422.7 45.7 %collective-permute-start.50 = (bf16[2,296,1536]{2,1,0:T(8,128)(2,1)}, bf16[2,296,1536]{2,1,0:T(8,128)(2,1)}, u32[]{:S(2)}, u32[]{:S(2)}) collective-permute-start(bf16[2,296,1536]{2,1,0:T(8,128)(2,1)} %add_convert_fusion.2), channel_id=1, source_target_pairs={{0,2},{1,3},{2,0},{3,1},{4,6},{5,7},{6,4},{7,5},{8,10},{9,11},{10,... | collective-permute-start | bytes 5455880 | tf_op jit(solution)/shard_map/ppermute | solution.py:21
  468.1 29.1 %collective-permute-start.51 = (bf16[2,192,1536]{2,1,0:T(8,128)(2,1)}, bf16[2,192,1536]{2,1,0:T(8,128)(2,1)S(1)}, u32[]{:S(2)}, u32[]{:S(2)}) collective-permute-start(bf16[2,192,1536]{2,1,0:T(8,128)(2,1)} %get-tuple-element.771), channel_id=1, source_target_pairs={{0,8},{8,16},{16,24},{24,28},{28,20},{20,12},{12,4},{4,0},{1,9},{9... | collective-permute-start | bytes 3538952 | tf_op jit(solution)/shard_map/ppermute | solution.py:94
  477.5 46.7 %collective-permute-start.55 = (bf16[2,296,1536]{2,1,0:T(8,128)(2,1)}, bf16[2,296,1536]{2,1,0:T(8,128)(2,1)}, u32[]{:S(2)}, u32[]{:S(2)}) collective-permute-start(bf16[2,296,1536]{2,1,0:T(8,128)(2,1)} %get-tuple-element.814.refs_0_.a), channel_id=1, source_target_pairs={{0,2},{1,3},{2,0},{3,1},{4,6},{5,7},{6,4},{7,5},{8,10},{9,11},{10,... | collective-permute-start | bytes 5455880 | tf_op jit(solution)/shard_map/ppermute | solution.py:21
  478.0 46.2 %collective-permute-start.56 = (bf16[2,296,1536]{2,1,0:T(8,128)(2,1)}, bf16[2,296,1536]{2,1,0:T(8,128)(2,1)}, u32[]{:S(2)}, u32[]{:S(2)}) collective-permute-start(bf16[2,296,1536]{2,1,0:T(8,128)(2,1)} %get-tuple-element.814.refs_0_.a), channel_id=1, source_target_pairs={{0,1},{1,0},{2,3},{3,2},{4,5},{5,4},{6,7},{7,6},{8,9},{9,8},{10,11... | collective-permute-start | bytes 5455880 | tf_op jit(solution)/shard_map/ppermute | solution.py:21
  478.0 29.1 %collective-permute-start.52 = (bf16[2,192,1536]{2,1,0:T(8,128)(2,1)}, bf16[2,192,1536]{2,1,0:T(8,128)(2,1)}, u32[]{:S(2)}, u32[]{:S(2)}) collective-permute-start(bf16[2,192,1536]{2,1,0:T(8,128)(2,1)} %get-tuple-element.772), channel_id=1, source_target_pairs={{8,0},{16,8},{24,16},{28,24},{20,28},{12,20},{4,12},{0,4},{9,1},{1... | collective-permute-start | bytes 3538952 | tf_op jit(solution)/shard_map/ppermute | solution.py:97
  481.5 30.8 %collective-permute-start.53 = (bf16[1,192,1536]{2,1,0:T(8,128)(2,1)}, bf16[1,192,1536]{2,1,0:T(8,128)(2,1)S(1)}, u32[]{:S(2)}, u32[]{:S(2)}) collective-permute-start(bf16[1,192,1536]{2,1,0:T(8,128)(2,1)} %constant_dynamic-slice_fusion.20), channel_id=1, source_target_pairs={{0,8},{8,16},{16,24},{24,28},{28,20},{20,12},{12,4},{4,0},{1,9},{9... | collective-permute-start | bytes 1769480 | tf_op jit(solution)/shard_map/ppermute | solution.py:94
  537.8 49.6 %collective-permute-start.60 = (bf16[2,192,1536]{2,1,0:T(8,128)(2,1)}, bf16[2,192,1536]{2,1,0:T(8,128)(2,1)S(1)}, u32[]{:S(2)}, u32[]{:S(2)}) collective-permute-start(bf16[2,192,1536]{2,1,0:T(8,128)(2,1)} %get-tuple-element.830), channel_id=1, source_target_pairs={{0,8},{8,16},{16,24},{24,28},{28,20},{20,12},{12,4},{4,0},{1,9},{9... | collective-permute-start | bytes 3538952 | tf_op jit(solution)/shard_map/ppermute | solution.py:94
  539.0 48.4 %collective-permute-start.61 = (bf16[2,192,1536]{2,1,0:T(8,128)(2,1)}, bf16[2,192,1536]{2,1,0:T(8,128)(2,1)}, u32[]{:S(2)}, u32[]{:S(2)}) collective-permute-start(bf16[2,192,1536]{2,1,0:T(8,128)(2,1)} %get-tuple-element.831), channel_id=1, source_target_pairs={{8,0},{16,8},{24,16},{28,24},{20,28},{12,20},{4,12},{0,4},{9,1},{1... | collective-permute-start | bytes 3538952 | tf_op jit(solution)/shard_map/ppermute | solution.py:97
  539.9 51.6 %collective-permute-start.62 = (bf16[2,192,1536]{2,1,0:T(8,128)(2,1)}, bf16[2,192,1536]{2,1,0:T(8,128)(2,1)}, u32[]{:S(2)}, u32[]{:S(2)}) collective-permute-start(bf16[2,192,1536]{2,1,0:T(8,128)(2,1)} %get-tuple-element.833), channel_id=1, source_target_pairs={{0,8},{8,16},{16,24},{24,28},{28,20},{20,12},{12,4},{4,0},{1,9},{9... | collective-permute-start | bytes 3538952 | tf_op jit(solution)/shard_map/ppermute | solution.py:94
  542.5 49.8 %collective-permute-start.63 = (bf16[2,192,1536]{2,1,0:T(8,128)(2,1)}, bf16[2,192,1536]{2,1,0:T(8,128)(2,1)}, u32[]{:S(2)}, u32[]{:S(2)}) collective-permute-start(bf16[2,192,1536]{2,1,0:T(8,128)(2,1)} %get-tuple-element.834), channel_id=1, source_target_pairs={{8,0},{16,8},{24,16},{28,24},{20,28},{12,20},{4,12},{0,4},{9,1},{1... | collective-permute-start | bytes 3538952 | tf_op jit(solution)/shard_map/ppermute | solution.py:97
  556.3 72.7 %collective-permute-start.64 = (bf16[2,296,1536]{2,1,0:T(8,128)(2,1)}, bf16[2,296,1536]{2,1,0:T(8,128)(2,1)}, u32[]{:S(2)}, u32[]{:S(2)}) collective-permute-start(bf16[2,296,1536]{2,1,0:T(8,128)(2,1)} %add_convert_fusion.1), channel_id=1, source_target_pairs={{0,2},{1,3},{2,0},{3,1},{4,6},{5,7},{6,4},{7,5},{8,10},{9,11},{10,... | collective-permute-start | bytes 5455880 | tf_op jit(solution)/shard_map/ppermute | solution.py:21
  597.6 31.5 %collective-permute-start.65 = (bf16[2,192,1536]{2,1,0:T(8,128)(2,1)}, bf16[2,192,1536]{2,1,0:T(8,128)(2,1)S(1)}, u32[]{:S(2)}, u32[]{:S(2)}) collective-permute-start(bf16[2,192,1536]{2,1,0:T(8,128)(2,1)} %get-tuple-element.851), channel_id=1, source_target_pairs={{0,8},{8,16},{16,24},{24,28},{28,20},{20,12},{12,4},{4,0},{1,9},{9... | collective-permute-start | bytes 3538952 | tf_op jit(solution)/shard_map/ppermute | solution.py:94
  599.4 29.7 %collective-permute-start.66 = (bf16[2,192,1536]{2,1,0:T(8,128)(2,1)}, bf16[2,192,1536]{2,1,0:T(8,128)(2,1)}, u32[]{:S(2)}, u32[]{:S(2)}) collective-permute-start(bf16[2,192,1536]{2,1,0:T(8,128)(2,1)} %get-tuple-element.852), channel_id=1, source_target_pairs={{8,0},{16,8},{24,16},{28,24},{20,28},{12,20},{4,12},{0,4},{9,1},{1... | collective-permute-start | bytes 3538952 | tf_op jit(solution)/shard_map/ppermute | solution.py:97
  656.8 28.3 %collective-permute-start.70 = (bf16[2,192,1536]{2,1,0:T(8,128)(2,1)}, bf16[2,192,1536]{2,1,0:T(8,128)(2,1)S(1)}, u32[]{:S(2)}, u32[]{:S(2)}) collective-permute-start(bf16[2,192,1536]{2,1,0:T(8,128)(2,1)} %get-tuple-element.891), channel_id=1, source_target_pairs={{8,0},{16,8},{24,16},{28,24},{20,28},{12,20},{4,12},{0,4},{9,1},{1... | collective-permute-start | bytes 3538952 | tf_op jit(solution)/shard_map/ppermute | solution.py:97
  661.3 53.7 %collective-permute-start.73 = (bf16[2,296,1536]{2,1,0:T(8,128)(2,1)}, bf16[2,296,1536]{2,1,0:T(8,128)(2,1)}, u32[]{:S(2)}, u32[]{:S(2)}) collective-permute-start(bf16[2,296,1536]{2,1,0:T(8,128)(2,1)} %add_convert_fusion), channel_id=1, source_target_pairs={{0,2},{1,3},{2,0},{3,1},{4,6},{5,7},{6,4},{7,5},{8,10},{9,11},{10,... | collective-permute-start | bytes 5455880 | tf_op jit(solution)/shard_map/ppermute | solution.py:21
  797.8 40.5 %collective-permute-start.90 = (bf16[2,192,1536]{2,1,0:T(8,128)(2,1)}, bf16[2,192,1536]{2,1,0:T(8,128)(2,1)S(1)}, u32[]{:S(2)}, u32[]{:S(2)}) collective-permute-start(bf16[2,192,1536]{2,1,0:T(8,128)(2,1)} %get-tuple-element.983), channel_id=1, source_target_pairs={{0,8},{8,16},{16,24},{24,28},{28,20},{20,12},{12,4},{4,0},{1,9},{9... | collective-permute-start | bytes 3538952 | tf_op jit(solution)/shard_map/ppermute | solution.py:94
  798.1 40.2 %collective-permute-start.91 = (bf16[2,192,1536]{2,1,0:T(8,128)(2,1)}, bf16[2,192,1536]{2,1,0:T(8,128)(2,1)}, u32[]{:S(2)}, u32[]{:S(2)}) collective-permute-start(bf16[2,192,1536]{2,1,0:T(8,128)(2,1)} %get-tuple-element.984), channel_id=1, source_target_pairs={{8,0},{16,8},{24,16},{28,24},{20,28},{12,20},{4,12},{0,4},{9,1},{1... | collective-permute-start | bytes 3538952 | tf_op jit(solution)/shard_map/ppermute | solution.py:97
  (104 other events, 1675.3 us)

commit v6 on v5

--- a/solution.py
+++ b/solution.py
@@ -136,12 +136,10 @@
 
 
 class Scatter:
-    def __init__(self, ring, image, text, form="plain"):
+    def __init__(self, ring, image, text, far_image, far_text, form="plain"):
         self.ring, self.image, self.text, self.form = ring, image, text, form
         self.left = ring.size // 2
-        far = ring.devices([self.left])[0]
-        chunk = [lax.dynamic_index_in_dim(g, far, 0) for g in (image, text)]
-        self.moving = (ring.forward(chunk[0]), ring.backward(chunk[1]))
+        self.moving = (ring.forward(far_image), ring.backward(far_text))
 
     def arrive(self, order):
         ahead, back = order(*self.moving)
@@ -336,12 +334,12 @@
 def piece_specs(pieces, block=None):
     if isinstance(pieces, (list, tuple)):
         shape = pieces[0].shape
-        spec = pl.BlockSpec(shape, lambda j: (0, 0, 0), pipeline_mode=pl.Buffered(1))
+        spec = pl.BlockSpec(shape, lambda j, *_: (0, 0, 0), pipeline_mode=pl.Buffered(1))
         return [spec] * 4, list(pieces), shape
     shape = pieces.shape[1:]
     specs = [
         pl.BlockSpec(
-            (None,) + shape, lambda j, k=k: (k, 0, 0, 0), pipeline_mode=pl.Buffered(1)
+            (None,) + shape, lambda j, *_, k=k: (k, 0, 0, 0), pipeline_mode=pl.Buffered(1)
         )
         for k in range(4)
     ]
@@ -410,16 +408,18 @@
     )(*arrays, *weights, *extras)
 
 
-def weight_grad(pieces, grads, image, size, first=0, total=None, earlier=()):
+def weight_grad(pieces, grads, image, ring, first=0, total=None, earlier=()):
+    size = ring.size
+    far = ring.devices([size // 2])
     specs, arrays, (slots, tokens, depth) = piece_specs(pieces)
     width = grads.shape[3]
     block = column_block(math.gcd(first, width))
     text = tokens - image
     spots = [(k, c) for k in range(4) for c in range(slots)]
 
-    def kernel(a, b, c, d, grad, *refs):
+    def kernel(far, a, b, c, d, grad, *refs):
         rows = (a, b, c, d)
-        image_out, text_out, sums, image_turned, text_turned = refs[-5:]
+        image_out, text_out, far_image, far_text, sums, image_turned, text_turned = refs[-7:]
 
         @pl.when(pl.program_id(0) == 0)
         def _():
@@ -437,27 +437,36 @@
         text_out[...] = (
             mul(text_turned[...], text_grads, DOT_NN).astype(BF16).reshape(text_out.shape)
         )
+        far_image[0] = image_out[far[0]]
+        far_text[0] = text_out[far[0]]
         sums[0:1] = jnp.sum(image_grads.astype(F32), 0, keepdims=True)
         sums[1:2] = jnp.sum(text_grads.astype(F32), 0, keepdims=True)
 
-    out = pl.BlockSpec((size, depth // size, block), lambda j: (0, 0, first // block + j))
-    shape = jax.ShapeDtypeStruct((size, depth // size, total or width), BF16)
+    outs, shapes = [], []
+    for count in (size, size, 1, 1):
+        outs.append(
+            pl.BlockSpec(
+                (count, depth // size, block), lambda j, *_: (0, 0, first // block + j)
+            )
+        )
+        shapes.append(jax.ShapeDtypeStruct((count, depth // size, total or width), BF16))
     return kernel_call(
         kernel,
         "weight_grad",
         1 + 3.4e-9 * 4 * slots * tokens * depth * width,
         (width // block,),
         specs
-        + [pl.BlockSpec((4, slots, tokens, block), lambda j: (0, 0, 0, j))]
+        + [pl.BlockSpec((4, slots, tokens, block), lambda j, *_: (0, 0, 0, j))]
         + [pl.BlockSpec(memory_space=pl.ANY)] * len(earlier),
-        [out, out, pl.BlockSpec((2, block), lambda j: (0, j))],
-        [shape, shape, jax.ShapeDtypeStruct((2, width), F32)],
+        outs + [pl.BlockSpec((2, block), lambda j, *_: (0, j))],
+        shapes + [jax.ShapeDtypeStruct((2, width), F32)],
+        scalars=1,
         scratch=[
             pltpu.VMEM((depth, len(spots) * image), BF16),
             pltpu.VMEM((depth, len(spots) * text), BF16),
         ],
-        input_output_aliases={5: 0, 6: 1} if earlier else {},
-    )(*arrays, grads, *earlier)
+        input_output_aliases={6 + i: i for i in range(len(earlier))},
+    )(far, *arrays, grads, *earlier)
 
 
 def mul(a, b, dims):
@@ -902,6 +911,7 @@
     second_move = Spread(second)
     fc1_full = fc1_ring.finish(order)
     fc2_ring.arrive(order)
+    fc2_ring.place(order)
     fc2_ring.arrive(order)
     second_move.arrive(order)
     second_full = second_move.finish(order)
@@ -914,7 +924,7 @@
     )
     fc2_ring.arrive(order)
     *fc2_grad, _ = order.run(
-        lambda *a: weight_grad(a[:4], a[4], image, groups), *mlp_full, activated
+        lambda *a: weight_grad(a[:4], a[4], image, ring), *mlp_full, activated
     )
     fc2_ring.arrive(order)
     fc2_sums = Scatter(ring, *order(*fc2_grad))
@@ -944,7 +954,7 @@
     second_back = Collect(*second_parts)
     second_back.arrive(order)
     *fc1_grad, fc1_bias_local = order.run(
-        lambda *a: weight_grad(a[:4], a[4], image, groups), *second_full, pre_round
+        lambda *a: weight_grad(a[:4], a[4], image, ring), *second_full, pre_round
     )
     fc1_sums = Scatter(ring, *order(*fc1_grad))
     mlp_parts = order.run(
@@ -984,7 +994,7 @@
     mlp_back = Collect(*order(*mlp_parts))
     mlp_back.arrive(order)
     *proj_grad, _ = order.run(
-        lambda *a: weight_grad(a[:4], a[4], image, groups, 3 * col_width, 4 * col_width),
+        lambda *a: weight_grad(a[:4], a[4], image, ring, 3 * col_width, 4 * col_width),
         *branch_full,
         mixed,
     )
@@ -1002,23 +1012,24 @@
             fc1_sums.arrive(order)
     mlp_terms = mlp_back.finish(order)
     fc1_sums.arrive(order)
+    *qkv_grad, qv_sums = order.run(
+        lambda *a: weight_grad(
+            a[:4], a[4], image, ring, 0, 4 * col_width, a[5:]
+        ),
+        *first_full,
+        qkv_grads,
+        *proj_grad,
+    )
+    fc1_sums.arrive(order)
+    qkv_sums = Scatter(ring, *order(*qkv_grad), "parts")
     first_parts = order.run(
         lambda *a: rows_times(a[0], a[1:], image, True, "split", columns=qkv_part),
         qkv_grads,
         *qkv_full,
     )
-    first_back = Collect(*first_parts)
+    qkv_sums.arrive(order)
+    first_back = Collect(*order(*first_parts))
     first_back.arrive(order)
-    *qkv_grad, qv_sums = order.run(
-        lambda *a: weight_grad(
-            a[:4], a[4], image, groups, 0, 4 * col_width, a[5:]
-        ),
-        *first_full,
-        qkv_grads,
-        *proj_grad,
-    )
-    fc1_sums.arrive(order)
-    qkv_sums = Scatter(ring, *order(*qkv_grad), "parts")
     qv_bias_local = qv_sums.reshape(2, 3, col_width)[:, 0::2]
     proj_bias_local = jnp.sum(middle_vecs[:, :, 3], 0)
     fc2_bias_local = jnp.sum(fc2_bias_local, 0)
@@ -1084,8 +1095,6 @@
     qkv_sums.arrive(order)
     shared = jnp.concatenate([modul_round.astype(F32).reshape(-1), bias_local])
     shared = order(spread(order(shared), "dp", groups))
-    qkv_sums.arrive(order)
-    shared = order(shared)
     modul_all = shared[:, : modul_round.size].astype(BF16)
     modul_all = modul_all.reshape((groups * slots,) + modul_round.shape[1:])
     bias_local = jnp.sum(shared[:, modul_round.size :], 0)
@@ -1093,6 +1102,8 @@
     ada_bias_part = jnp.sum(modul_all.astype(F32), 0)
     last = jnp.concatenate([cond_part.reshape(-1), ada_bias_part.reshape(-1), bias_local])
     last = order(spread(order(last), "tensor", 4))
+    qkv_sums.arrive(order)
+    last = order(last)
     cond_part = jnp.sum(last[:, : cond_part.size], 0).reshape(groups, slots, rows)
     cond_terms = order(exchange(cond_part, "dp", groups))
     cond_term = jnp.stack(

time: 855 us -> 828 us (0.968)
  waiting for transfers between devices: 253 us -> 238 us
  local copies, waits for them, and re-layouts: 43.5 us -> 31.8 us
    ppermute x44, waiting for transfers between devices: 56.4 us -> 42.3 us  [hop(): return lax.ppermute(value, axis, [(i, i ^ mask) for i in range(size)])]
    dynamic_slice x6 -> x0, local copies, waits for them, and re-layouts: 11.2 us -> none  [__init__(): chunk = [lax.dynamic_index_in_dim(g, far, 0) for g in (image, text)]]
    pallas_call x4 -> x5, Pallas kernels: 26.2 us -> 28 us  [assemble(): kernel_call(kernel, 'assemble', 1 + 3e-07 * sum((math.prod(p.shape) for p...]
  transfers between devices with their start and end apart: 92 -> 92, of which waited for: 45 -> 48; matrix products, arithmetic and copies ran while one was open for 7% -> 6% of each run, Pallas kernels for 39% -> 44%
where the time goes in v6:
time: 828 us; the launch traced here: 819 us
  Pallas kernels  414 us (50%)
  waiting for transfers between devices  238 us (29%)
  starting transfers between devices  91.9 us (11%)
  local copies, waits for them, and re-layouts  31.8 us (4%)
  other arithmetic  28.7 us (3%)
    ppermute x24, waiting for transfers between devices, forward(): return lax.ppermute(value, 'dp', self.ahead)  164 us
    pallas_call x8, Pallas kernels, rows_times(): kernel_call(kernel, 'rows_times', 1 + 3e-09 * 4 * slots * tokens * depth...  129 us
    pallas_call x4, Pallas kernels, weight_grad(): kernel_call(kernel, 'weight_grad', 1 + 3.4e-09 * 4 * slots * tokens * dep...  71.9 us
    pallas_call x2, Pallas kernels, attend_back(): kernel_call(kernel, 'attend_back', 29, (pairs,), [spec(0), spec(1), spec(...  59 us
    pallas_call x9, Pallas kernels, ring_add(): kernel_call(kernel, 'ring_add', 1 + 7e-06 * image.shape[1] * image.shape[...  46.3 us
    ppermute x44, waiting for transfers between devices, hop(): return lax.ppermute(value, axis, [(i, i ^ mask) for i in range(size)])  42.3 us
    ppermute x44, starting transfers between devices, hop(): return lax.ppermute(value, axis, [(i, i ^ mask) for i in range(size)])  39.8 us
    pallas_call x5, Pallas kernels, per_slot(): kernel_call(kernel, name, 6, (slots,), [spec(value.shape, value.ndim == 2...  33.6 us
  transfers between devices with their start and end apart: 92, of which 48 were waited for; matrix products, arithmetic and copies ran while one was open for 6% of the time, Pallas kernels for 44%

profile of v6, /device:TPU:0, one launch (start us, length us, event | category | flops | bytes accessed | tf_op | source)
XLA Modules:
  0.0 818.7 jit_solution(3390896512378774313)
XLA Ops:
  46.6 9.7 %collective-permute-done.8.refs_1_ = bf16[2,4,192,384]{3,2,1,0:T(8,128)(2,1)} collective-permute-done((bf16[2,4,192,384]{3,2,1,0:T(8,128)(2,1)S(1)}, bf16[2,4,192,384]{3,2,1,0:T(8,128)(2,1)}, u32[]{:S(2)}, u32[]{:S(2)}) %collective-permute-start.8) | collective-permute-done | bytes 1179680 | tf_op jit(solution)/shard_map/ppermute | solution.py:94
  63.6 22.2 %collective-permute-done.10.refs_3_ = bf16[2,4,192,384]{3,2,1,0:T(8,128)(2,1)S(1)} collective-permute-done((bf16[2,4,192,384]{3,2,1,0:T(8,128)(2,1)}, bf16[2,4,192,384]{3,2,1,0:T(8,128)(2,1)S(1)}, u32[]{:S(2)}, u32[]{:S(2)}) %collective-permute-start.10) | collective-permute-done | bytes 1179680 | tf_op jit(solution)/shard_map/ppermute | solution.py:94
  88.4 20.5 %collective-permute-done.12.refs_5_ = bf16[2,4,192,384]{3,2,1,0:T(8,128)(2,1)S(1)} collective-permute-done((bf16[2,4,192,384]{3,2,1,0:T(8,128)(2,1)S(1)}, bf16[2,4,192,384]{3,2,1,0:T(8,128)(2,1)S(1)}, u32[]{:S(2)}, u32[]{:S(2)}) %collective-permute-start.12) | collective-permute-done | bytes 1179680 | tf_op jit(solution)/shard_map/ppermute | solution.py:94
  119.4 7.7 assemble.5
  138.3 17.4 %rows_times.8.q.k.v = bf16[4,2,296,1152]{3,2,1,0:T(8,128)(2,1)} custom-call(bf16[2,296,1536]{2,1,0:T(8,128)(2,1)} %get-tuple-element.918.refs_0_.a, bf16[2,296,1536]{2,1,0:T(8,128)(2,1)} %copy-done.40, bf16[2,296,1536]{2,1,0:T(8,128)(2,1)} %collective-permute-done.14.refs_2_.c, bf16[2,296,1536]{2,1,0:T(8,128)(2,1)} %collective-permute-done.16.refs_3_.d, ...), custom_call_target="tpu_custom_call" | custom-call | flops 6242351616 | bytes 1 | tf_op jit(solution)/shard_map/rows_times/pallas_call | solution.py:400
  160.7 15.3 %attend.2 = (bf16[4,2,296,384]{3,2,1,0:T(8,128)(2,1)}, f32[2,3,2,1184]{3,2,1,0:T(2,128)}) custom-call(bf16[4,2,296,1152]{3,2,1,0:T(8,128)(2,1)} %rows_times.8.q.k.v, bf16[4,2,296,1152]{3,2,1,0:T(8,128)(2,1)} %rows_times.8.q.k.v, bf16[4,2,296,1152]{3,2,1,0:T(8,128)(2,1)} %rows_times.8.q.k.v), custom_call_target="tpu_custom_call" | custom-call | flops 6899999744 | bytes 1 | tf_op jit(solution)/shard_map/attend/pallas_call | solution.py:539
  176.0 15.3 %attend.3 = (bf16[4,2,296,384]{3,2,1,0:T(8,128)(2,1)}, f32[2,3,2,1184]{3,2,1,0:T(2,128)}) custom-call(bf16[4,2,296,1152]{3,2,1,0:T(8,128)(2,1)} %rows_times.8.q.k.v, bf16[4,2,296,1152]{3,2,1,0:T(8,128)(2,1)} %rows_times.8.q.k.v, bf16[4,2,296,1152]{3,2,1,0:T(8,128)(2,1)} %rows_times.8.q.k.v, ...), custom_call_target="tpu_custom_call", output_to_operand_aliasing={{0}: (3, {}), {1}: (4, {})} | custom-call | flops 6899999744 | bytes 1 | tf_op jit(solution)/shard_map/attend/pallas_call | solution.py:539
  191.4 8.6 %rows_times.9 = (bf16[2,296,1536]{2,1,0:T(8,128)(2,1)}, bf16[2,296,1536]{2,1,0:T(8,128)(2,1)}, bf16[2,296,1536]{2,1,0:T(8,128)(2,1)}, bf16[2,296,1536]{2,1,0:T(8,128)(2,1)}) custom-call(bf16[4,2,296,384]{3,2,1,0:T(8,128)(2,1)} %get-tuple-element.897.refs_0_.refs_1_.refs_2_.refs_3_.grad.mixed, ...), custom_call_target="tpu_custom_call" | custom-call | flops 2387450368 | bytes 1 | tf_op jit(solution)/shard_map/rows_times/pallas_call | solution.py:400
  207.6 21.4 %collective-permute-done.28.refs_5_ = bf16[2,1,192,1536]{3,2,1,0:T(8,128)(2,1)S(1)} collective-permute-done((bf16[2,1,192,1536]{3,2,1,0:T(8,128)(2,1)}, bf16[2,1,192,1536]{3,2,1,0:T(8,128)(2,1)S(1)}, u32[]{:S(2)}, u32[]{:S(2)}) %collective-permute-start.28) | collective-permute-done | bytes 1179680 | tf_op jit(solution)/shard_map/ppermute | solution.py:94
  232.0 12.2 %collective-permute-done.30.refs_7_ = bf16[1,1,192,1536]{3,2,1,0:T(8,128)(2,1)S(1)} collective-permute-done((bf16[1,1,192,1536]{3,2,1,0:T(8,128)(2,1)S(1)}, bf16[1,1,192,1536]{3,2,1,0:T(8,128)(2,1)S(1)}, u32[]{:S(2)}, u32[]{:S(2)}) %collective-permute-start.30) | collective-permute-done | bytes 589856 | tf_op jit(solution)/shard_map/ppermute | solution.py:94
  248.2 6.2 middle.1
  257.9 8.0 assemble.7
  281.0 17.6 %collective-permute-done.35.refs_0_ = bf16[2,1,192,1536]{3,2,1,0:T(8,128)(2,1)S(1)} collective-permute-done((bf16[2,1,192,1536]{3,2,1,0:T(8,128)(2,1)}, bf16[2,1,192,1536]{3,2,1,0:T(8,128)(2,1)S(1)}, u32[]{:S(2)}, u32[]{:S(2)}) %collective-permute-start.35) | collective-permute-done | bytes 1179680 | tf_op jit(solution)/shard_map/ppermute | solution.py:94
  306.6 25.6 %rows_times.10 = (bf16[4,2,296,1536]{3,2,1,0:T(8,128)(2,1)}, bf16[4,2,296,1536]{3,2,1,0:T(8,128)(2,1)}) custom-call(bf16[2,296,1536]{2,1,0:T(8,128)(2,1)} %get-tuple-element.767.refs_0_.a, bf16[2,296,1536]{2,1,0:T(8,128)(2,1)} %collective-permute-done.38.refs_1_.b, bf16[2,296,1536]{2,1,0:T(8,128)(2,1)} %collective-permute-done.37.refs_2_.c, ...), custom_call_target="tpu_custom_call" | custom-call | flops 8169801728 | bytes 1 | tf_op jit(solution)/shard_map/rows_times/pallas_call | solution.py:400
  337.5 21.0 %weight_grad.4 = (bf16[8,192,1536]{2,1,0:T(8,128)(2,1)}, bf16[8,192,1536]{2,1,0:T(8,128)(2,1)}, bf16[1,192,1536]{2,1,0:T(8,128)(2,1)}, bf16[1,192,1536]{2,1,0:T(8,128)(2,1)}, f32[2,1536]{1,0:T(2,128)}) custom-call(s32[1]{0:T(128)} %dynamic-slice.4.far, bf16[2,296,1536]{2,1,0:T(8,128)(2,1)} %get-tuple-element.731.a.refs_0_, ...), custom_call_target="tpu_custom_call" | custom-call | flops 9197775872 | bytes 1 | tf_op jit(solution)/shard_map/weight_grad/pallas_call | solution.py:453
  366.9 18.5 %rows_times.11.refs_0_.refs_1_.refs_2_.refs_3_.grad = bf16[4,2,296,1536]{3,2,1,0:T(8,128)(2,1)} custom-call(bf16[2,296,1536]{2,1,0:T(8,128)(2,1)} %get-tuple-element.731.a.refs_0_, bf16[2,296,1536]{2,1,0:T(8,128)(2,1)} %collective-permute-done.24.b.refs_1_, bf16[2,296,1536]{2,1,0:T(8,128)(2,1)} %collective-permute-done.23.c.refs_2_, ...), custom_call_target="tpu_custom_call" | custom-call | flops 8169801728 | bytes 1 | tf_op jit(solution)/shard_map/rows_times/pallas_call | solution.py:400
  392.0 17.4 %rows_times.12 = (bf16[2,296,1536]{2,1,0:T(8,128)(2,1)}, bf16[2,296,1536]{2,1,0:T(8,128)(2,1)}, bf16[2,296,1536]{2,1,0:T(8,128)(2,1)}, bf16[2,296,1536]{2,1,0:T(8,128)(2,1)}) custom-call(bf16[4,2,296,1536]{3,2,1,0:T(8,128)(2,1)} %rows_times.11.refs_0_.refs_1_.refs_2_.refs_3_.grad, bf16[4,2,296,1536]{3,2,1,0:T(8,128)(2,1)} %rows_times.11.refs_0_.refs_1_.refs_2_.refs_3_.grad, ...), custom_call_target="tpu_custom_call" | custom-call | flops 8169801728 | bytes 1 | tf_op jit(solution)/shard_map/rows_times/pallas_call | solution.py:400
  419.5 20.9 %weight_grad.5 = (bf16[8,192,1536]{2,1,0:T(8,128)(2,1)}, bf16[8,192,1536]{2,1,0:T(8,128)(2,1)}, bf16[1,192,1536]{2,1,0:T(8,128)(2,1)}, bf16[1,192,1536]{2,1,0:T(8,128)(2,1)}, f32[2,1536]{1,0:T(2,128)}) custom-call(s32[1]{0:T(128)} %dynamic-slice.4.far, bf16[2,296,1536]{2,1,0:T(8,128)(2,1)} %get-tuple-element.767.refs_0_.a, ...), custom_call_target="tpu_custom_call" | custom-call | flops 9197775872 | bytes 1 | tf_op jit(solution)/shard_map/weight_grad/pallas_call | solution.py:453
  440.3 17.4 %rows_times.13 = (bf16[2,296,1536]{2,1,0:T(8,128)(2,1)}, bf16[2,296,1536]{2,1,0:T(8,128)(2,1)}, bf16[2,296,1536]{2,1,0:T(8,128)(2,1)}, bf16[2,296,1536]{2,1,0:T(8,128)(2,1)}) custom-call(bf16[4,2,296,1536]{3,2,1,0:T(8,128)(2,1)} %get-tuple-element.784.grad.refs_0_.refs_1_.refs_2_.refs_3_, ...), custom_call_target="tpu_custom_call" | custom-call | flops 8169801728 | bytes 1 | tf_op jit(solution)/shard_map/rows_times/pallas_call | solution.py:400
  464.4 9.1 %middle_back.1 = (f32[2,296,1536]{2,1,0:T(8,128)}, bf16[2,296,1536]{2,1,0:T(8,128)(2,1)}, f32[2,2,4,1536]{3,2,1,0:T(4,128)}) custom-call(s32[1]{0:T(128)} %copy.204.seqs, bf16[2,256,1536]{2,1,0:T(8,128)(2,1)} %refs_0_.3, bf16[2,40,1536]{2,1,0:T(8,128)(2,1)} %refs_1_.3, bf16[2,296,1536]{2,1,0:T(8,128)(2,1)} %get-tuple-element.810.refs_2_, ...), custom_call_target="tpu_custom_call" | custom-call | flops 2760000000 | bytes 1 | tf_op jit(solution)/shard_map/middle_back/pallas_call | solution.py:667
  476.0 17.1 %collective-permute-done.51.ahead = bf16[2,192,1536]{2,1,0:T(8,128)(2,1)S(1)} collective-permute-done((bf16[2,192,1536]{2,1,0:T(8,128)(2,1)}, bf16[2,192,1536]{2,1,0:T(8,128)(2,1)S(1)}, u32[]{:S(2)}, u32[]{:S(2)}) %collective-permute-start.51) | collective-permute-done | bytes 1179680 | tf_op jit(solution)/shard_map/ppermute | solution.py:94
  495.8 7.2 collective-permute-done.52.back
  508.3 7.0 collective-permute-done.54.back
  524.4 9.0 %rows_times.14.grads = bf16[4,2,296,384]{3,2,1,0:T(8,128)(2,1)} custom-call(bf16[2,296,1536]{2,1,0:T(8,128)(2,1)} %get-tuple-element.865.refs_0_.a, bf16[2,296,1536]{2,1,0:T(8,128)(2,1)} %collective-permute-done.56.refs_1_.b, bf16[2,296,1536]{2,1,0:T(8,128)(2,1)} %collective-permute-done.55.refs_2_.c, ...), custom_call_target="tpu_custom_call" | custom-call | flops 2387450368 | bytes 1 | tf_op jit(solution)/shard_map/rows_times/pallas_call | solution.py:400
  543.3 9.6 %weight_grad.6 = (bf16[8,192,1536]{2,1,0:T(8,128)(2,1)}, bf16[8,192,1536]{2,1,0:T(8,128)(2,1)}, bf16[1,192,1536]{2,1,0:T(8,128)(2,1)}, bf16[1,192,1536]{2,1,0:T(8,128)(2,1)}, f32[2,384]{1,0:T(2,128)}) custom-call(s32[1]{0:T(128)} %dynamic-slice.4.far, bf16[2,296,1536]{2,1,0:T(8,128)(2,1)} %get-tuple-element.865.refs_0_.a, ...), custom_call_target="tpu_custom_call" | custom-call | flops 2644443904 | bytes 1 | tf_op jit(solution)/shard_map/weight_grad/pallas_call | solution.py:453
  554.6 29.6 %attend_back.2.refs_0_ = bf16[4,2,296,1152]{3,2,1,0:T(8,128)(2,1)} custom-call(bf16[4,2,296,1152]{3,2,1,0:T(8,128)(2,1)} %rows_times.8.q.k.v, bf16[4,2,296,1152]{3,2,1,0:T(8,128)(2,1)} %rows_times.8.q.k.v, bf16[4,2,296,1152]{3,2,1,0:T(8,128)(2,1)} %rows_times.8.q.k.v, bf16[4,2,296,384]{3,2,1,0:T(8,128)(2,1)} %get-tuple-element.897.refs_0_.refs_1_.refs_2_.refs_3_.grad.mixed, ...), custom_call_target="tpu_custom_call" | custom-call | flops 13340000256 | bytes 1 | tf_op jit(solution)/shard_map/attend_back/pallas_call | solution.py:613
  595.5 29.4 %attend_back.3.grad.refs_0_.refs_1_.refs_2_.refs_3_ = bf16[4,2,296,1152]{3,2,1,0:T(8,128)(2,1)} custom-call(bf16[4,2,296,1152]{3,2,1,0:T(8,128)(2,1)} %rows_times.8.q.k.v, bf16[4,2,296,1152]{3,2,1,0:T(8,128)(2,1)} %rows_times.8.q.k.v, bf16[4,2,296,1152]{3,2,1,0:T(8,128)(2,1)} %rows_times.8.q.k.v, ...), custom_call_target="tpu_custom_call", output_to_operand_aliasing={{}: (6, {})} | custom-call | flops 13340000256 | bytes 1 | tf_op jit(solution)/shard_map/attend_back/pallas_call | solution.py:613
  633.2 20.4 %weight_grad.7 = (bf16[8,192,1536]{2,1,0:T(8,128)(2,1)}, bf16[8,192,1536]{2,1,0:T(8,128)(2,1)}, bf16[1,192,1536]{2,1,0:T(8,128)(2,1)}, bf16[1,192,1536]{2,1,0:T(8,128)(2,1)}, f32[2,1152]{1,0:T(2,128)}) custom-call(s32[1]{0:T(128)} %dynamic-slice.4.far, ...), custom_call_target="tpu_custom_call", output_to_operand_aliasing={{0}: (6, {}), {1}: (7, {}), {2}: (8, {}), {3}: (9, {})} | custom-call | flops 7013331456 | bytes 1 | tf_op jit(solution)/shard_map/weight_grad/pallas_call | solution.py:453
  661.3 14.7 %rows_times.15 = (bf16[2,296,1536]{2,1,0:T(8,128)(2,1)}, bf16[2,296,1536]{2,1,0:T(8,128)(2,1)}, bf16[2,296,1536]{2,1,0:T(8,128)(2,1)}, bf16[2,296,1536]{2,1,0:T(8,128)(2,1)}) custom-call(bf16[4,2,296,1152]{3,2,1,0:T(8,128)(2,1)} %attend_back.3.grad.refs_0_.refs_1_.refs_2_.refs_3_, bf16[4,2,296,1152]{3,2,1,0:T(8,128)(2,1)} %attend_back.3.grad.refs_0_.refs_1_.refs_2_.refs_3_, ...), custom_call_target="tpu_custom_call" | custom-call | flops 6242351616 | bytes 1 | tf_op jit(solution)/shard_map/rows_times/pallas_call | solution.py:400
  732.8 7.4 enter_back.1
  747.2 6.8 collective-permute-done.78.ahead
  786.7 14.3 %collective-permute-done.86.ahead = bf16[2,192,1536]{2,1,0:T(8,128)(2,1)S(1)} collective-permute-done((bf16[2,192,1536]{2,1,0:T(8,128)(2,1)}, bf16[2,192,1536]{2,1,0:T(8,128)(2,1)S(1)}, u32[]{:S(2)}, u32[]{:S(2)}) %collective-permute-start.86) | collective-permute-done | bytes 1179680 | tf_op jit(solution)/shard_map/ppermute | solution.py:94
  (437 shorter events, 328.4 us)
Async XLA Ops:
  62.1 48.0 %collective-permute-start.14 = (bf16[2,296,1536]{2,1,0:T(8,128)(2,1)}, bf16[2,296,1536]{2,1,0:T(8,128)(2,1)}, u32[]{:S(2)}, u32[]{:S(2)}) collective-permute-start(bf16[2,296,1536]{2,1,0:T(8,128)(2,1)} %get-tuple-element.918.refs_0_.a), channel_id=1, source_target_pairs={{0,2},{1,3},{2,0},{3,1},{4,6},{5,7},{6,4},{7,5},{8,10},{9,11},{10,... | collective-permute-start | bytes 5455880 | tf_op jit(solution)/shard_map/ppermute | solution.py:21
  63.6 46.5 %collective-permute-start.15 = (bf16[2,296,1536]{2,1,0:T(8,128)(2,1)}, bf16[2,296,1536]{2,1,0:T(8,128)(2,1)S(1)}, u32[]{:S(2)}, u32[]{:S(2)}) collective-permute-start(bf16[2,296,1536]{2,1,0:T(8,128)(2,1)} %get-tuple-element.918.refs_0_.a), channel_id=1, source_target_pairs={{0,1},{1,0},{2,3},{3,2},{4,5},{5,4},{6,7},{7,6},{8,9},{9,8},{10,11... | collective-permute-start | bytes 5455880 | tf_op jit(solution)/shard_map/ppermute | solution.py:21
  130.6 27.5 %collective-permute-start.19 = (bf16[2,1,192,1536]{3,2,1,0:T(8,128)(2,1)}, bf16[2,1,192,1536]{3,2,1,0:T(8,128)(2,1)S(1)}, u32[]{:S(2)}, u32[]{:S(2)}) collective-permute-start(bf16[2,1,192,1536]{3,2,1,0:T(8,128)(2,1)} %bitcast.168), channel_id=1, source_target_pairs={{0,8},{8,16},{16,24},{24,28},{28,20},{20,12},{12,4},{4,0},{1,9},{9... | collective-permute-start | bytes 3538952 | tf_op jit(solution)/shard_map/ppermute | solution.py:94
  134.0 57.3 %collective-permute-start.23 = (bf16[2,296,1536]{2,1,0:T(8,128)(2,1)}, bf16[2,296,1536]{2,1,0:T(8,128)(2,1)}, u32[]{:S(2)}, u32[]{:S(2)}) collective-permute-start(bf16[2,296,1536]{2,1,0:T(8,128)(2,1)} %get-tuple-element.731.a.refs_0_), channel_id=1, source_target_pairs={{0,2},{1,3},{2,0},{3,1},{4,6},{5,7},{6,4},{7,5},{8,10},{9,11},{10,... | collective-permute-start | bytes 5455880 | tf_op jit(solution)/shard_map/ppermute | solution.py:21
  135.4 55.9 %collective-permute-start.24 = (bf16[2,296,1536]{2,1,0:T(8,128)(2,1)}, bf16[2,296,1536]{2,1,0:T(8,128)(2,1)}, u32[]{:S(2)}, u32[]{:S(2)}) collective-permute-start(bf16[2,296,1536]{2,1,0:T(8,128)(2,1)} %get-tuple-element.731.a.refs_0_), channel_id=1, source_target_pairs={{0,1},{1,0},{2,3},{3,2},{4,5},{5,4},{6,7},{7,6},{8,9},{9,8},{10,11... | collective-permute-start | bytes 5455880 | tf_op jit(solution)/shard_map/ppermute | solution.py:21
  158.5 32.8 %collective-permute-start.21 = (bf16[2,1,192,1536]{3,2,1,0:T(8,128)(2,1)S(1)}, bf16[2,1,192,1536]{3,2,1,0:T(8,128)(2,1)}, u32[]{:S(2)}, u32[]{:S(2)}) collective-permute-start(bf16[2,1,192,1536]{3,2,1,0:T(8,128)(2,1)S(1)} %collective-permute-done.19.refs_1_), channel_id=1, source_target_pairs={{0,8},{8,16},{16,24},{24,28},{28,20},{20,12},{12,4},{4,0},{1,9},{9... | collective-permute-start | bytes 3538952 | tf_op jit(solution)/shard_map/ppermute | solution.py:94
  158.8 32.5 %collective-permute-start.22 = (bf16[2,1,192,1536]{3,2,1,0:T(8,128)(2,1)}, bf16[2,1,192,1536]{3,2,1,0:T(8,128)(2,1)}, u32[]{:S(2)}, u32[]{:S(2)}) collective-permute-start(bf16[2,1,192,1536]{3,2,1,0:T(8,128)(2,1)} %collective-permute-done.20.refs_2_), channel_id=1, source_target_pairs={{8,0},{16,8},{24,16},{28,24},{20,28},{12,20},{4,12},{0,4},{9,1},{1... | collective-permute-start | bytes 3538952 | tf_op jit(solution)/shard_map/ppermute | solution.py:97
  200.5 28.5 %collective-permute-start.28 = (bf16[2,1,192,1536]{3,2,1,0:T(8,128)(2,1)}, bf16[2,1,192,1536]{3,2,1,0:T(8,128)(2,1)S(1)}, u32[]{:S(2)}, u32[]{:S(2)}) collective-permute-start(bf16[2,1,192,1536]{3,2,1,0:T(8,128)(2,1)} %collective-permute-done.21.refs_3_), channel_id=1, source_target_pairs={{0,8},{8,16},{16,24},{24,28},{28,20},{20,12},{12,4},{4,0},{1,9},{9... | collective-permute-start | bytes 3538952 | tf_op jit(solution)/shard_map/ppermute | solution.py:94
  200.8 28.2 %collective-permute-start.29 = (bf16[2,1,192,1536]{3,2,1,0:T(8,128)(2,1)}, bf16[2,1,192,1536]{3,2,1,0:T(8,128)(2,1)S(1)}, u32[]{:S(2)}, u32[]{:S(2)}) collective-permute-start(bf16[2,1,192,1536]{3,2,1,0:T(8,128)(2,1)} %collective-permute-done.22.refs_4_), channel_id=1, source_target_pairs={{8,0},{16,8},{24,16},{28,24},{20,28},{12,20},{4,12},{0,4},{9,1},{1... | collective-permute-start | bytes 3538952 | tf_op jit(solution)/shard_map/ppermute | solution.py:97
  206.0 42.2 %collective-permute-start.32 = (bf16[2,296,1536]{2,1,0:T(8,128)(2,1)S(1)}, bf16[2,296,1536]{2,1,0:T(8,128)(2,1)}, u32[]{:S(2)}, u32[]{:S(2)}) collective-permute-start(bf16[2,296,1536]{2,1,0:T(8,128)(2,1)S(1)} %add_convert_fusion.3), channel_id=1, source_target_pairs={{0,2},{1,3},{2,0},{3,1},{4,6},{5,7},{6,4},{7,5},{8,10},{9,11},{10,... | collective-permute-start | bytes 5455880 | tf_op jit(solution)/shard_map/ppermute | solution.py:21
  254.5 44.5 %collective-permute-start.37 = (bf16[2,296,1536]{2,1,0:T(8,128)(2,1)}, bf16[2,296,1536]{2,1,0:T(8,128)(2,1)}, u32[]{:S(2)}, u32[]{:S(2)}) collective-permute-start(bf16[2,296,1536]{2,1,0:T(8,128)(2,1)} %get-tuple-element.767.refs_0_.a), channel_id=1, source_target_pairs={{0,2},{1,3},{2,0},{3,1},{4,6},{5,7},{6,4},{7,5},{8,10},{9,11},{10,... | collective-permute-start | bytes 5455880 | tf_op jit(solution)/shard_map/ppermute | solution.py:21
  256.1 42.9 %collective-permute-start.38 = (bf16[2,296,1536]{2,1,0:T(8,128)(2,1)}, bf16[2,296,1536]{2,1,0:T(8,128)(2,1)}, u32[]{:S(2)}, u32[]{:S(2)}) collective-permute-start(bf16[2,296,1536]{2,1,0:T(8,128)(2,1)} %get-tuple-element.767.refs_0_.a), channel_id=1, source_target_pairs={{0,1},{1,0},{2,3},{3,2},{4,5},{5,4},{6,7},{7,6},{8,9},{9,8},{10,11... | collective-permute-start | bytes 5455880 | tf_op jit(solution)/shard_map/ppermute | solution.py:21
  301.0 31.3 %collective-permute-start.40 = (bf16[2,1,192,1536]{3,2,1,0:T(8,128)(2,1)}, bf16[2,1,192,1536]{3,2,1,0:T(8,128)(2,1)S(1)}, u32[]{:S(2)}, u32[]{:S(2)}) collective-permute-start(bf16[2,1,192,1536]{3,2,1,0:T(8,128)(2,1)} %copy-done.11), channel_id=1, source_target_pairs={{0,8},{8,16},{16,24},{24,28},{28,20},{20,12},{12,4},{4,0},{1,9},{9... | collective-permute-start | bytes 3538952 | tf_op jit(solution)/shard_map/ppermute | solution.py:94
  301.4 30.9 %collective-permute-start.41 = (bf16[2,1,192,1536]{3,2,1,0:T(8,128)(2,1)}, bf16[2,1,192,1536]{3,2,1,0:T(8,128)(2,1)}, u32[]{:S(2)}, u32[]{:S(2)}) collective-permute-start(bf16[2,1,192,1536]{3,2,1,0:T(8,128)(2,1)} %collective-permute-done.36.refs_1_), channel_id=1, source_target_pairs={{8,0},{16,8},{24,16},{28,24},{20,28},{12,20},{4,12},{0,4},{9,1},{1... | collective-permute-start | bytes 3538952 | tf_op jit(solution)/shard_map/ppermute | solution.py:97
  411.8 45.9 %collective-permute-start.48 = (bf16[2,192,1536]{2,1,0:T(8,128)(2,1)}, bf16[2,192,1536]{2,1,0:T(8,128)(2,1)S(1)}, u32[]{:S(2)}, u32[]{:S(2)}) collective-permute-start(bf16[2,192,1536]{2,1,0:T(8,128)(2,1)} %get-tuple-element.792), channel_id=1, source_target_pairs={{0,8},{8,16},{16,24},{24,28},{28,20},{20,12},{12,4},{4,0},{1,9},{9... | collective-permute-start | bytes 3538952 | tf_op jit(solution)/shard_map/ppermute | solution.py:94
  412.3 45.4 %collective-permute-start.49 = (bf16[2,192,1536]{2,1,0:T(8,128)(2,1)}, bf16[2,192,1536]{2,1,0:T(8,128)(2,1)}, u32[]{:S(2)}, u32[]{:S(2)}) collective-permute-start(bf16[2,192,1536]{2,1,0:T(8,128)(2,1)} %get-tuple-element.793), channel_id=1, source_target_pairs={{8,0},{16,8},{24,16},{28,24},{20,28},{12,20},{4,12},{0,4},{9,1},{1... | collective-permute-start | bytes 3538952 | tf_op jit(solution)/shard_map/ppermute | solution.py:97
  417.8 46.6 %collective-permute-start.50 = (bf16[2,296,1536]{2,1,0:T(8,128)(2,1)}, bf16[2,296,1536]{2,1,0:T(8,128)(2,1)}, u32[]{:S(2)}, u32[]{:S(2)}) collective-permute-start(bf16[2,296,1536]{2,1,0:T(8,128)(2,1)} %add_convert_fusion.2), channel_id=1, source_target_pairs={{0,2},{1,3},{2,0},{3,1},{4,6},{5,7},{6,4},{7,5},{8,10},{9,11},{10,... | collective-permute-start | bytes 5455880 | tf_op jit(solution)/shard_map/ppermute | solution.py:21
  464.0 29.1 %collective-permute-start.51 = (bf16[2,192,1536]{2,1,0:T(8,128)(2,1)}, bf16[2,192,1536]{2,1,0:T(8,128)(2,1)S(1)}, u32[]{:S(2)}, u32[]{:S(2)}) collective-permute-start(bf16[2,192,1536]{2,1,0:T(8,128)(2,1)} %get-tuple-element.820), channel_id=1, source_target_pairs={{0,8},{8,16},{16,24},{24,28},{28,20},{20,12},{12,4},{4,0},{1,9},{9... | collective-permute-start | bytes 3538952 | tf_op jit(solution)/shard_map/ppermute | solution.py:94
  473.5 46.7 %collective-permute-start.55 = (bf16[2,296,1536]{2,1,0:T(8,128)(2,1)}, bf16[2,296,1536]{2,1,0:T(8,128)(2,1)}, u32[]{:S(2)}, u32[]{:S(2)}) collective-permute-start(bf16[2,296,1536]{2,1,0:T(8,128)(2,1)} %get-tuple-element.865.refs_0_.a), channel_id=1, source_target_pairs={{0,2},{1,3},{2,0},{3,1},{4,6},{5,7},{6,4},{7,5},{8,10},{9,11},{10,... | collective-permute-start | bytes 5455880 | tf_op jit(solution)/shard_map/ppermute | solution.py:21
  473.9 46.2 %collective-permute-start.56 = (bf16[2,296,1536]{2,1,0:T(8,128)(2,1)}, bf16[2,296,1536]{2,1,0:T(8,128)(2,1)}, u32[]{:S(2)}, u32[]{:S(2)}) collective-permute-start(bf16[2,296,1536]{2,1,0:T(8,128)(2,1)} %get-tuple-element.865.refs_0_.a), channel_id=1, source_target_pairs={{0,1},{1,0},{2,3},{3,2},{4,5},{5,4},{6,7},{7,6},{8,9},{9,8},{10,11... | collective-permute-start | bytes 5455880 | tf_op jit(solution)/shard_map/ppermute | solution.py:21
  473.9 29.1 %collective-permute-start.52 = (bf16[2,192,1536]{2,1,0:T(8,128)(2,1)}, bf16[2,192,1536]{2,1,0:T(8,128)(2,1)}, u32[]{:S(2)}, u32[]{:S(2)}) collective-permute-start(bf16[2,192,1536]{2,1,0:T(8,128)(2,1)} %get-tuple-element.821), channel_id=1, source_target_pairs={{8,0},{16,8},{24,16},{28,24},{20,28},{12,20},{4,12},{0,4},{9,1},{1... | collective-permute-start | bytes 3538952 | tf_op jit(solution)/shard_map/ppermute | solution.py:97
  475.5 32.8 %collective-permute-start.53 = (bf16[1,192,1536]{2,1,0:T(8,128)(2,1)}, bf16[1,192,1536]{2,1,0:T(8,128)(2,1)S(1)}, u32[]{:S(2)}, u32[]{:S(2)}) collective-permute-start(bf16[1,192,1536]{2,1,0:T(8,128)(2,1)} %get-tuple-element.828), channel_id=1, source_target_pairs={{0,8},{8,16},{16,24},{24,28},{28,20},{20,12},{12,4},{4,0},{1,9},{9... | collective-permute-start | bytes 1769480 | tf_op jit(solution)/shard_map/ppermute | solution.py:94
  533.8 50.4 %collective-permute-start.60 = (bf16[2,192,1536]{2,1,0:T(8,128)(2,1)}, bf16[2,192,1536]{2,1,0:T(8,128)(2,1)S(1)}, u32[]{:S(2)}, u32[]{:S(2)}) collective-permute-start(bf16[2,192,1536]{2,1,0:T(8,128)(2,1)} %get-tuple-element.883), channel_id=1, source_target_pairs={{0,8},{8,16},{16,24},{24,28},{28,20},{20,12},{12,4},{4,0},{1,9},{9... | collective-permute-start | bytes 3538952 | tf_op jit(solution)/shard_map/ppermute | solution.py:94
  534.9 49.4 %collective-permute-start.61 = (bf16[2,192,1536]{2,1,0:T(8,128)(2,1)}, bf16[2,192,1536]{2,1,0:T(8,128)(2,1)}, u32[]{:S(2)}, u32[]{:S(2)}) collective-permute-start(bf16[2,192,1536]{2,1,0:T(8,128)(2,1)} %get-tuple-element.884), channel_id=1, source_target_pairs={{8,0},{16,8},{24,16},{28,24},{20,28},{12,20},{4,12},{0,4},{9,1},{1... | collective-permute-start | bytes 3538952 | tf_op jit(solution)/shard_map/ppermute | solution.py:97
  535.9 51.6 %collective-permute-start.62 = (bf16[2,192,1536]{2,1,0:T(8,128)(2,1)}, bf16[2,192,1536]{2,1,0:T(8,128)(2,1)}, u32[]{:S(2)}, u32[]{:S(2)}) collective-permute-start(bf16[2,192,1536]{2,1,0:T(8,128)(2,1)} %get-tuple-element.886), channel_id=1, source_target_pairs={{0,8},{8,16},{16,24},{24,28},{28,20},{20,12},{12,4},{4,0},{1,9},{9... | collective-permute-start | bytes 3538952 | tf_op jit(solution)/shard_map/ppermute | solution.py:94
  538.5 49.7 %collective-permute-start.63 = (bf16[2,192,1536]{2,1,0:T(8,128)(2,1)}, bf16[2,192,1536]{2,1,0:T(8,128)(2,1)}, u32[]{:S(2)}, u32[]{:S(2)}) collective-permute-start(bf16[2,192,1536]{2,1,0:T(8,128)(2,1)} %get-tuple-element.887), channel_id=1, source_target_pairs={{8,0},{16,8},{24,16},{28,24},{20,28},{12,20},{4,12},{0,4},{9,1},{1... | collective-permute-start | bytes 3538952 | tf_op jit(solution)/shard_map/ppermute | solution.py:97
  552.9 72.0 %collective-permute-start.64 = (bf16[2,296,1536]{2,1,0:T(8,128)(2,1)}, bf16[2,296,1536]{2,1,0:T(8,128)(2,1)}, u32[]{:S(2)}, u32[]{:S(2)}) collective-permute-start(bf16[2,296,1536]{2,1,0:T(8,128)(2,1)} %add_convert_fusion.1), channel_id=1, source_target_pairs={{0,2},{1,3},{2,0},{3,1},{4,6},{5,7},{6,4},{7,5},{8,10},{9,11},{10,... | collective-permute-start | bytes 5455880 | tf_op jit(solution)/shard_map/ppermute | solution.py:21
  593.5 31.4 %collective-permute-start.65 = (bf16[2,192,1536]{2,1,0:T(8,128)(2,1)}, bf16[2,192,1536]{2,1,0:T(8,128)(2,1)S(1)}, u32[]{:S(2)}, u32[]{:S(2)}) collective-permute-start(bf16[2,192,1536]{2,1,0:T(8,128)(2,1)} %get-tuple-element.904), channel_id=1, source_target_pairs={{0,8},{8,16},{16,24},{24,28},{28,20},{20,12},{12,4},{4,0},{1,9},{9... | collective-permute-start | bytes 3538952 | tf_op jit(solution)/shard_map/ppermute | solution.py:94
  595.3 29.7 %collective-permute-start.66 = (bf16[2,192,1536]{2,1,0:T(8,128)(2,1)}, bf16[2,192,1536]{2,1,0:T(8,128)(2,1)}, u32[]{:S(2)}, u32[]{:S(2)}) collective-permute-start(bf16[2,192,1536]{2,1,0:T(8,128)(2,1)} %get-tuple-element.905), channel_id=1, source_target_pairs={{8,0},{16,8},{24,16},{28,24},{20,28},{12,20},{4,12},{0,4},{9,1},{1... | collective-permute-start | bytes 3538952 | tf_op jit(solution)/shard_map/ppermute | solution.py:97
  690.8 42.0 %collective-permute-start.75 = (bf16[2,296,1536]{2,1,0:T(8,128)(2,1)}, bf16[2,296,1536]{2,1,0:T(8,128)(2,1)}, u32[]{:S(2)}, u32[]{:S(2)}) collective-permute-start(bf16[2,296,1536]{2,1,0:T(8,128)(2,1)} %add_convert_fusion), channel_id=1, source_target_pairs={{0,2},{1,3},{2,0},{3,1},{4,6},{5,7},{6,4},{7,5},{8,10},{9,11},{10,... | collective-permute-start | bytes 5455880 | tf_op jit(solution)/shard_map/ppermute | solution.py:21
  692.4 27.9 %collective-permute-start.73 = (bf16[2,192,1536]{2,1,0:T(8,128)(2,1)}, bf16[2,192,1536]{2,1,0:T(8,128)(2,1)S(1)}, u32[]{:S(2)}, u32[]{:S(2)}) collective-permute-start(bf16[2,192,1536]{2,1,0:T(8,128)(2,1)} %get-tuple-element.996), channel_id=1, source_target_pairs={{0,8},{8,16},{16,24},{24,28},{28,20},{20,12},{12,4},{4,0},{1,9},{9... | collective-permute-start | bytes 3538952 | tf_op jit(solution)/shard_map/ppermute | solution.py:94
  694.1 27.8 %collective-permute-start.74 = (bf16[2,192,1536]{2,1,0:T(8,128)(2,1)}, bf16[2,192,1536]{2,1,0:T(8,128)(2,1)}, u32[]{:S(2)}, u32[]{:S(2)}) collective-permute-start(bf16[2,192,1536]{2,1,0:T(8,128)(2,1)} %get-tuple-element.997), channel_id=1, source_target_pairs={{8,0},{16,8},{24,16},{28,24},{20,28},{12,20},{4,12},{0,4},{9,1},{1... | collective-permute-start | bytes 3538952 | tf_op jit(solution)/shard_map/ppermute | solution.py:97
  (107 other events, 1680.0 us)

commit v7 on v6

--- a/solution.py
+++ b/solution.py
@@ -142,15 +142,21 @@
         self.moving = (ring.forward(far_image), ring.backward(far_text))
 
     def arrive(self, order):
-        ahead, back = order(*self.moving)
+        self.take(order)
+        self.add(order)
+
+    def take(self, order):
+        self.taken = order(*self.moving)
         self.left -= 1
+
+    def add(self, order):
+        ahead, back = order(*self.taken)
         places = self.ring.devices([self.left, -self.left])
         if self.left == 0:
             self.total = ring_total(self.image, self.text, ahead, back, places, self.form)
-            return True
+            return
         ahead, back = order(*ring_add(self.image, self.text, ahead, back, places))
         self.moving = (self.ring.forward(ahead), self.ring.backward(back))
-        return False
 
     def finish(self, order):
         while self.left:
@@ -947,11 +953,12 @@
         *mlp_full,
         *fc2_full,
     )
-    fc2_sums.arrive(order)
+    fc2_sums.take(order)
     second_parts = order.run(
         lambda *a: rows_times(a[0], a[1:], image, True, "split"), pre_round, *fc1_full
     )
     second_back = Collect(*second_parts)
+    fc2_sums.add(order)
     second_back.arrive(order)
     *fc1_grad, fc1_bias_local = order.run(
         lambda *a: weight_grad(a[:4], a[4], image, ring), *second_full, pre_round
@@ -960,7 +967,7 @@
     mlp_parts = order.run(
         lambda *a: rows_times(a[0], a[1:], image, True, "split"), activated, *fc2_full
     )
-    fc2_sums.arrive(order)
+    fc2_sums.take(order)
     second_terms = second_back.finish(order)
     residual, branch_round, middle_vecs = order.run(
         lambda *a: per_slot(
@@ -982,6 +989,7 @@
         branch,
     )
     branch_back = Spread(branch_round)
+    fc2_sums.add(order)
     fc2_sums.arrive(order)
     fc1_sums.arrive(order)
     branch_back.arrive(order)
@@ -1027,8 +1035,9 @@
         qkv_grads,
         *qkv_full,
     )
-    qkv_sums.arrive(order)
+    qkv_sums.take(order)
     first_back = Collect(*order(*first_parts))
+    qkv_sums.add(order)
     first_back.arrive(order)
     qv_bias_local = qv_sums.reshape(2, 3, col_width)[:, 0::2]
     proj_bias_local = jnp.sum(middle_vecs[:, :, 3], 0)
@@ -1092,9 +1101,11 @@
         ]
     )
     modul_round = order(collect(modul_blocks, "tensor", 4).astype(BF16))
-    qkv_sums.arrive(order)
+    qkv_sums.take(order)
     shared = jnp.concatenate([modul_round.astype(F32).reshape(-1), bias_local])
-    shared = order(spread(order(shared), "dp", groups))
+    shared = order(shared)
+    qkv_sums.add(order)
+    shared = order(spread(shared, "dp", groups))
     modul_all = shared[:, : modul_round.size].astype(BF16)
     modul_all = modul_all.reshape((groups * slots,) + modul_round.shape[1:])
     bias_local = jnp.sum(shared[:, modul_round.size :], 0)

time: 828 us -> 818 us (0.988)
    ppermute x24, waiting for transfers between devices: 164 us -> 177 us  [forward(): return lax.ppermute(value, 'dp', self.ahead)]
    ppermute x24, waiting for transfers between devices: 31.6 us -> 18.2 us  [backward(): return lax.ppermute(value, 'dp', self.back)]
  transfers between devices with their start and end apart: 92 -> 92, of which waited for: 48 -> 45; matrix products, arithmetic and copies ran while one was open for 6% -> 6% of each run, Pallas kernels for 44% -> 45%
where the time goes in v7:
time: 818 us; the launch traced here: 809 us
  Pallas kernels  414 us (51%)
  waiting for transfers between devices  230 us (28%)
  starting transfers between devices  90.3 us (11%)
  local copies, waits for them, and re-layouts  29.8 us (4%)
  other arithmetic  29.2 us (4%)
    ppermute x24, waiting for transfers between devices, forward(): return lax.ppermute(value, 'dp', self.ahead)  177 us
    pallas_call x8, Pallas kernels, rows_times(): kernel_call(kernel, 'rows_times', 1 + 3e-09 * 4 * slots * tokens * depth...  129 us
    pallas_call x4, Pallas kernels, weight_grad(): kernel_call(kernel, 'weight_grad', 1 + 3.4e-09 * 4 * slots * tokens * dep...  71.9 us
    pallas_call x2, Pallas kernels, attend_back(): kernel_call(kernel, 'attend_back', 29, (pairs,), [spec(0), spec(1), spec(...  59 us
    pallas_call x9, Pallas kernels, ring_add(): kernel_call(kernel, 'ring_add', 1 + 7e-06 * image.shape[1] * image.shape[...  46.3 us
    ppermute x44, starting transfers between devices, hop(): return lax.ppermute(value, axis, [(i, i ^ mask) for i in range(size)])  38.6 us
    ppermute x44, waiting for transfers between devices, hop(): return lax.ppermute(value, axis, [(i, i ^ mask) for i in range(size)])  34.4 us
    pallas_call x5, Pallas kernels, per_slot(): kernel_call(kernel, name, 6, (slots,), [spec(value.shape, value.ndim == 2...  34 us
  transfers between devices with their start and end apart: 92, of which 45 were waited for; matrix products, arithmetic and copies ran while one was open for 6% of the time, Pallas kernels for 45%

profile of v7, /device:TPU:0, one launch (start us, length us, event | category | flops | bytes accessed | tf_op | source)
XLA Modules:
  0.0 808.9 jit_solution(1066525046267538491)
XLA Ops:
  35.6 6.1 all_gather.3.refs_4_.refs_5_
  46.6 9.7 %collective-permute-done.8.refs_1_ = bf16[2,4,192,384]{3,2,1,0:T(8,128)(2,1)} collective-permute-done((bf16[2,4,192,384]{3,2,1,0:T(8,128)(2,1)S(1)}, bf16[2,4,192,384]{3,2,1,0:T(8,128)(2,1)}, u32[]{:S(2)}, u32[]{:S(2)}) %collective-permute-start.8) | collective-permute-done | bytes 1179680 | tf_op jit(solution)/shard_map/ppermute | solution.py:94
  63.6 22.2 %collective-permute-done.10.refs_3_ = bf16[2,4,192,384]{3,2,1,0:T(8,128)(2,1)S(1)} collective-permute-done((bf16[2,4,192,384]{3,2,1,0:T(8,128)(2,1)}, bf16[2,4,192,384]{3,2,1,0:T(8,128)(2,1)S(1)}, u32[]{:S(2)}, u32[]{:S(2)}) %collective-permute-start.10) | collective-permute-done | bytes 1179680 | tf_op jit(solution)/shard_map/ppermute | solution.py:94
  88.4 20.5 %collective-permute-done.12.refs_5_ = bf16[2,4,192,384]{3,2,1,0:T(8,128)(2,1)S(1)} collective-permute-done((bf16[2,4,192,384]{3,2,1,0:T(8,128)(2,1)S(1)}, bf16[2,4,192,384]{3,2,1,0:T(8,128)(2,1)S(1)}, u32[]{:S(2)}, u32[]{:S(2)}) %collective-permute-start.12) | collective-permute-done | bytes 1179680 | tf_op jit(solution)/shard_map/ppermute | solution.py:94
  119.4 7.7 assemble.5
  138.3 17.4 %rows_times.8.q.k.v = bf16[4,2,296,1152]{3,2,1,0:T(8,128)(2,1)} custom-call(bf16[2,296,1536]{2,1,0:T(8,128)(2,1)} %get-tuple-element.936.refs_0_.a, bf16[2,296,1536]{2,1,0:T(8,128)(2,1)} %copy-done.40, bf16[2,296,1536]{2,1,0:T(8,128)(2,1)} %collective-permute-done.14.refs_2_.c, bf16[2,296,1536]{2,1,0:T(8,128)(2,1)} %collective-permute-done.16.refs_3_.d, ...), custom_call_target="tpu_custom_call" | custom-call | flops 6242351616 | bytes 1 | tf_op jit(solution)/shard_map/rows_times/pallas_call | solution.py:406
  160.7 15.3 %attend.2 = (bf16[4,2,296,384]{3,2,1,0:T(8,128)(2,1)}, f32[2,3,2,1184]{3,2,1,0:T(2,128)}) custom-call(bf16[4,2,296,1152]{3,2,1,0:T(8,128)(2,1)} %rows_times.8.q.k.v, bf16[4,2,296,1152]{3,2,1,0:T(8,128)(2,1)} %rows_times.8.q.k.v, bf16[4,2,296,1152]{3,2,1,0:T(8,128)(2,1)} %rows_times.8.q.k.v), custom_call_target="tpu_custom_call" | custom-call | flops 6899999744 | bytes 1 | tf_op jit(solution)/shard_map/attend/pallas_call | solution.py:545
  176.0 15.3 %attend.3 = (bf16[4,2,296,384]{3,2,1,0:T(8,128)(2,1)}, f32[2,3,2,1184]{3,2,1,0:T(2,128)}) custom-call(bf16[4,2,296,1152]{3,2,1,0:T(8,128)(2,1)} %rows_times.8.q.k.v, bf16[4,2,296,1152]{3,2,1,0:T(8,128)(2,1)} %rows_times.8.q.k.v, bf16[4,2,296,1152]{3,2,1,0:T(8,128)(2,1)} %rows_times.8.q.k.v, ...), custom_call_target="tpu_custom_call", output_to_operand_aliasing={{0}: (3, {}), {1}: (4, {})} | custom-call | flops 6899999744 | bytes 1 | tf_op jit(solution)/shard_map/attend/pallas_call | solution.py:545
  191.4 8.6 %rows_times.9 = (bf16[2,296,1536]{2,1,0:T(8,128)(2,1)}, bf16[2,296,1536]{2,1,0:T(8,128)(2,1)}, bf16[2,296,1536]{2,1,0:T(8,128)(2,1)}, bf16[2,296,1536]{2,1,0:T(8,128)(2,1)}) custom-call(bf16[4,2,296,384]{3,2,1,0:T(8,128)(2,1)} %get-tuple-element.915.refs_0_.refs_1_.refs_2_.refs_3_.grad.mixed, ...), custom_call_target="tpu_custom_call" | custom-call | flops 2387450368 | bytes 1 | tf_op jit(solution)/shard_map/rows_times/pallas_call | solution.py:406
  207.6 21.4 %collective-permute-done.28.refs_5_ = bf16[2,1,192,1536]{3,2,1,0:T(8,128)(2,1)S(1)} collective-permute-done((bf16[2,1,192,1536]{3,2,1,0:T(8,128)(2,1)}, bf16[2,1,192,1536]{3,2,1,0:T(8,128)(2,1)S(1)}, u32[]{:S(2)}, u32[]{:S(2)}) %collective-permute-start.28) | collective-permute-done | bytes 1179680 | tf_op jit(solution)/shard_map/ppermute | solution.py:94
  232.0 12.2 %collective-permute-done.30.refs_7_ = bf16[1,1,192,1536]{3,2,1,0:T(8,128)(2,1)S(1)} collective-permute-done((bf16[1,1,192,1536]{3,2,1,0:T(8,128)(2,1)S(1)}, bf16[1,1,192,1536]{3,2,1,0:T(8,128)(2,1)S(1)}, u32[]{:S(2)}, u32[]{:S(2)}) %collective-permute-start.30) | collective-permute-done | bytes 589856 | tf_op jit(solution)/shard_map/ppermute | solution.py:94
  248.3 6.2 middle.1
  258.0 8.0 assemble.7
  281.1 17.6 %collective-permute-done.35.refs_0_ = bf16[2,1,192,1536]{3,2,1,0:T(8,128)(2,1)S(1)} collective-permute-done((bf16[2,1,192,1536]{3,2,1,0:T(8,128)(2,1)}, bf16[2,1,192,1536]{3,2,1,0:T(8,128)(2,1)S(1)}, u32[]{:S(2)}, u32[]{:S(2)}) %collective-permute-start.35) | collective-permute-done | bytes 1179680 | tf_op jit(solution)/shard_map/ppermute | solution.py:94
  306.1 25.6 %rows_times.10 = (bf16[4,2,296,1536]{3,2,1,0:T(8,128)(2,1)}, bf16[4,2,296,1536]{3,2,1,0:T(8,128)(2,1)}) custom-call(bf16[2,296,1536]{2,1,0:T(8,128)(2,1)} %get-tuple-element.782.refs_0_.a, bf16[2,296,1536]{2,1,0:T(8,128)(2,1)} %collective-permute-done.38.refs_1_.b, bf16[2,296,1536]{2,1,0:T(8,128)(2,1)} %collective-permute-done.37.refs_2_.c, ...), custom_call_target="tpu_custom_call" | custom-call | flops 8169801728 | bytes 1 | tf_op jit(solution)/shard_map/rows_times/pallas_call | solution.py:406
  337.0 21.0 %weight_grad.4 = (bf16[8,192,1536]{2,1,0:T(8,128)(2,1)}, bf16[8,192,1536]{2,1,0:T(8,128)(2,1)}, bf16[1,192,1536]{2,1,0:T(8,128)(2,1)}, bf16[1,192,1536]{2,1,0:T(8,128)(2,1)}, f32[2,1536]{1,0:T(2,128)}) custom-call(s32[1]{0:T(128)} %dynamic-slice.4.far, bf16[2,296,1536]{2,1,0:T(8,128)(2,1)} %get-tuple-element.743.a.refs_0_, ...), custom_call_target="tpu_custom_call" | custom-call | flops 9197775872 | bytes 1 | tf_op jit(solution)/shard_map/weight_grad/pallas_call | solution.py:459
  366.5 18.5 %rows_times.11.refs_0_.refs_1_.refs_2_.refs_3_.grad = bf16[4,2,296,1536]{3,2,1,0:T(8,128)(2,1)} custom-call(bf16[2,296,1536]{2,1,0:T(8,128)(2,1)} %get-tuple-element.743.a.refs_0_, bf16[2,296,1536]{2,1,0:T(8,128)(2,1)} %collective-permute-done.24.b.refs_1_, bf16[2,296,1536]{2,1,0:T(8,128)(2,1)} %collective-permute-done.23.c.refs_2_, ...), custom_call_target="tpu_custom_call" | custom-call | flops 8169801728 | bytes 1 | tf_op jit(solution)/shard_map/rows_times/pallas_call | solution.py:406
  385.0 17.8 %rows_times.12 = (bf16[2,296,1536]{2,1,0:T(8,128)(2,1)}, bf16[2,296,1536]{2,1,0:T(8,128)(2,1)}, bf16[2,296,1536]{2,1,0:T(8,128)(2,1)}, bf16[2,296,1536]{2,1,0:T(8,128)(2,1)}) custom-call(bf16[4,2,296,1536]{3,2,1,0:T(8,128)(2,1)} %rows_times.11.refs_0_.refs_1_.refs_2_.refs_3_.grad, bf16[4,2,296,1536]{3,2,1,0:T(8,128)(2,1)} %rows_times.11.refs_0_.refs_1_.refs_2_.refs_3_.grad, ...), custom_call_target="tpu_custom_call" | custom-call | flops 8169801728 | bytes 1 | tf_op jit(solution)/shard_map/rows_times/pallas_call | solution.py:406
  418.7 20.9 %weight_grad.5 = (bf16[8,192,1536]{2,1,0:T(8,128)(2,1)}, bf16[8,192,1536]{2,1,0:T(8,128)(2,1)}, bf16[1,192,1536]{2,1,0:T(8,128)(2,1)}, bf16[1,192,1536]{2,1,0:T(8,128)(2,1)}, f32[2,1536]{1,0:T(2,128)}) custom-call(s32[1]{0:T(128)} %dynamic-slice.4.far, bf16[2,296,1536]{2,1,0:T(8,128)(2,1)} %get-tuple-element.782.refs_0_.a, ...), custom_call_target="tpu_custom_call" | custom-call | flops 9197775872 | bytes 1 | tf_op jit(solution)/shard_map/weight_grad/pallas_call | solution.py:459
  439.5 17.4 %rows_times.13 = (bf16[2,296,1536]{2,1,0:T(8,128)(2,1)}, bf16[2,296,1536]{2,1,0:T(8,128)(2,1)}, bf16[2,296,1536]{2,1,0:T(8,128)(2,1)}, bf16[2,296,1536]{2,1,0:T(8,128)(2,1)}) custom-call(bf16[4,2,296,1536]{3,2,1,0:T(8,128)(2,1)} %get-tuple-element.799.grad.refs_0_.refs_1_.refs_2_.refs_3_, ...), custom_call_target="tpu_custom_call" | custom-call | flops 8169801728 | bytes 1 | tf_op jit(solution)/shard_map/rows_times/pallas_call | solution.py:406
  456.9 9.5 %middle_back.1 = (f32[2,296,1536]{2,1,0:T(8,128)}, bf16[2,296,1536]{2,1,0:T(8,128)(2,1)}, f32[2,2,4,1536]{3,2,1,0:T(4,128)}) custom-call(s32[1]{0:T(128)} %copy.204.seqs, bf16[2,256,1536]{2,1,0:T(8,128)(2,1)} %refs_0_.3, bf16[2,40,1536]{2,1,0:T(8,128)(2,1)} %refs_1_.3, bf16[2,296,1536]{2,1,0:T(8,128)(2,1)} %get-tuple-element.820.refs_2_, ...), custom_call_target="tpu_custom_call" | custom-call | flops 2760000000 | bytes 1 | tf_op jit(solution)/shard_map/middle_back/pallas_call | solution.py:673
  474.8 26.0 %collective-permute-done.51.ahead = bf16[2,192,1536]{2,1,0:T(8,128)(2,1)S(1)} collective-permute-done((bf16[2,192,1536]{2,1,0:T(8,128)(2,1)}, bf16[2,192,1536]{2,1,0:T(8,128)(2,1)S(1)}, u32[]{:S(2)}, u32[]{:S(2)}) %collective-permute-start.51) | collective-permute-done | bytes 1179680 | tf_op jit(solution)/shard_map/ppermute | solution.py:94
  523.2 9.0 %rows_times.14.grads = bf16[4,2,296,384]{3,2,1,0:T(8,128)(2,1)} custom-call(bf16[2,296,1536]{2,1,0:T(8,128)(2,1)} %get-tuple-element.883.refs_0_.a, bf16[2,296,1536]{2,1,0:T(8,128)(2,1)} %collective-permute-done.56.refs_1_.b, bf16[2,296,1536]{2,1,0:T(8,128)(2,1)} %collective-permute-done.55.refs_2_.c, ...), custom_call_target="tpu_custom_call" | custom-call | flops 2387450368 | bytes 1 | tf_op jit(solution)/shard_map/rows_times/pallas_call | solution.py:406
  542.1 9.6 %weight_grad.6 = (bf16[8,192,1536]{2,1,0:T(8,128)(2,1)}, bf16[8,192,1536]{2,1,0:T(8,128)(2,1)}, bf16[1,192,1536]{2,1,0:T(8,128)(2,1)}, bf16[1,192,1536]{2,1,0:T(8,128)(2,1)}, f32[2,384]{1,0:T(2,128)}) custom-call(s32[1]{0:T(128)} %dynamic-slice.4.far, bf16[2,296,1536]{2,1,0:T(8,128)(2,1)} %get-tuple-element.883.refs_0_.a, ...), custom_call_target="tpu_custom_call" | custom-call | flops 2644443904 | bytes 1 | tf_op jit(solution)/shard_map/weight_grad/pallas_call | solution.py:459
  553.2 29.6 %attend_back.2.refs_0_ = bf16[4,2,296,1152]{3,2,1,0:T(8,128)(2,1)} custom-call(bf16[4,2,296,1152]{3,2,1,0:T(8,128)(2,1)} %rows_times.8.q.k.v, bf16[4,2,296,1152]{3,2,1,0:T(8,128)(2,1)} %rows_times.8.q.k.v, bf16[4,2,296,1152]{3,2,1,0:T(8,128)(2,1)} %rows_times.8.q.k.v, bf16[4,2,296,384]{3,2,1,0:T(8,128)(2,1)} %get-tuple-element.915.refs_0_.refs_1_.refs_2_.refs_3_.grad.mixed, ...), custom_call_target="tpu_custom_call" | custom-call | flops 13340000256 | bytes 1 | tf_op jit(solution)/shard_map/attend_back/pallas_call | solution.py:619
  593.8 29.4 %attend_back.3.grad.refs_0_.refs_1_.refs_2_.refs_3_ = bf16[4,2,296,1152]{3,2,1,0:T(8,128)(2,1)} custom-call(bf16[4,2,296,1152]{3,2,1,0:T(8,128)(2,1)} %rows_times.8.q.k.v, bf16[4,2,296,1152]{3,2,1,0:T(8,128)(2,1)} %rows_times.8.q.k.v, bf16[4,2,296,1152]{3,2,1,0:T(8,128)(2,1)} %rows_times.8.q.k.v, ...), custom_call_target="tpu_custom_call", output_to_operand_aliasing={{}: (6, {})} | custom-call | flops 13340000256 | bytes 1 | tf_op jit(solution)/shard_map/attend_back/pallas_call | solution.py:619
  631.5 20.4 %weight_grad.7 = (bf16[8,192,1536]{2,1,0:T(8,128)(2,1)}, bf16[8,192,1536]{2,1,0:T(8,128)(2,1)}, bf16[1,192,1536]{2,1,0:T(8,128)(2,1)}, bf16[1,192,1536]{2,1,0:T(8,128)(2,1)}, f32[2,1152]{1,0:T(2,128)}) custom-call(s32[1]{0:T(128)} %dynamic-slice.4.far, ...), custom_call_target="tpu_custom_call", output_to_operand_aliasing={{0}: (6, {}), {1}: (7, {}), {2}: (8, {}), {3}: (9, {})} | custom-call | flops 7013331456 | bytes 1 | tf_op jit(solution)/shard_map/weight_grad/pallas_call | solution.py:459
  659.5 14.7 %rows_times.15 = (bf16[2,296,1536]{2,1,0:T(8,128)(2,1)}, bf16[2,296,1536]{2,1,0:T(8,128)(2,1)}, bf16[2,296,1536]{2,1,0:T(8,128)(2,1)}, bf16[2,296,1536]{2,1,0:T(8,128)(2,1)}) custom-call(bf16[4,2,296,1152]{3,2,1,0:T(8,128)(2,1)} %attend_back.3.grad.refs_0_.refs_1_.refs_2_.refs_3_, bf16[4,2,296,1152]{3,2,1,0:T(8,128)(2,1)} %attend_back.3.grad.refs_0_.refs_1_.refs_2_.refs_3_, ...), custom_call_target="tpu_custom_call" | custom-call | flops 6242351616 | bytes 1 | tf_op jit(solution)/shard_map/rows_times/pallas_call | solution.py:406
  701.6 6.0 leave.1
  726.2 7.4 enter_back.1
  740.6 7.1 collective-permute-done.78.ahead
  776.9 15.0 %collective-permute-done.86.ahead = bf16[2,192,1536]{2,1,0:T(8,128)(2,1)S(1)} collective-permute-done((bf16[2,192,1536]{2,1,0:T(8,128)(2,1)}, bf16[2,192,1536]{2,1,0:T(8,128)(2,1)S(1)}, u32[]{:S(2)}, u32[]{:S(2)}) %collective-permute-start.86) | collective-permute-done | bytes 1179680 | tf_op jit(solution)/shard_map/ppermute | solution.py:94
  (437 shorter events, 310.0 us)
Async XLA Ops:
  62.1 48.0 %collective-permute-start.14 = (bf16[2,296,1536]{2,1,0:T(8,128)(2,1)}, bf16[2,296,1536]{2,1,0:T(8,128)(2,1)}, u32[]{:S(2)}, u32[]{:S(2)}) collective-permute-start(bf16[2,296,1536]{2,1,0:T(8,128)(2,1)} %get-tuple-element.936.refs_0_.a), channel_id=1, source_target_pairs={{0,2},{1,3},{2,0},{3,1},{4,6},{5,7},{6,4},{7,5},{8,10},{9,11},{10,... | collective-permute-start | bytes 5455880 | tf_op jit(solution)/shard_map/ppermute | solution.py:21
  63.6 46.5 %collective-permute-start.15 = (bf16[2,296,1536]{2,1,0:T(8,128)(2,1)}, bf16[2,296,1536]{2,1,0:T(8,128)(2,1)S(1)}, u32[]{:S(2)}, u32[]{:S(2)}) collective-permute-start(bf16[2,296,1536]{2,1,0:T(8,128)(2,1)} %get-tuple-element.936.refs_0_.a), channel_id=1, source_target_pairs={{0,1},{1,0},{2,3},{3,2},{4,5},{5,4},{6,7},{7,6},{8,9},{9,8},{10,11... | collective-permute-start | bytes 5455880 | tf_op jit(solution)/shard_map/ppermute | solution.py:21
  130.6 27.5 %collective-permute-start.19 = (bf16[2,1,192,1536]{3,2,1,0:T(8,128)(2,1)}, bf16[2,1,192,1536]{3,2,1,0:T(8,128)(2,1)S(1)}, u32[]{:S(2)}, u32[]{:S(2)}) collective-permute-start(bf16[2,1,192,1536]{3,2,1,0:T(8,128)(2,1)} %bitcast.168), channel_id=1, source_target_pairs={{0,8},{8,16},{16,24},{24,28},{28,20},{20,12},{12,4},{4,0},{1,9},{9... | collective-permute-start | bytes 3538952 | tf_op jit(solution)/shard_map/ppermute | solution.py:94
  134.0 57.3 %collective-permute-start.23 = (bf16[2,296,1536]{2,1,0:T(8,128)(2,1)}, bf16[2,296,1536]{2,1,0:T(8,128)(2,1)}, u32[]{:S(2)}, u32[]{:S(2)}) collective-permute-start(bf16[2,296,1536]{2,1,0:T(8,128)(2,1)} %get-tuple-element.743.a.refs_0_), channel_id=1, source_target_pairs={{0,2},{1,3},{2,0},{3,1},{4,6},{5,7},{6,4},{7,5},{8,10},{9,11},{10,... | collective-permute-start | bytes 5455880 | tf_op jit(solution)/shard_map/ppermute | solution.py:21
  135.4 55.9 %collective-permute-start.24 = (bf16[2,296,1536]{2,1,0:T(8,128)(2,1)}, bf16[2,296,1536]{2,1,0:T(8,128)(2,1)}, u32[]{:S(2)}, u32[]{:S(2)}) collective-permute-start(bf16[2,296,1536]{2,1,0:T(8,128)(2,1)} %get-tuple-element.743.a.refs_0_), channel_id=1, source_target_pairs={{0,1},{1,0},{2,3},{3,2},{4,5},{5,4},{6,7},{7,6},{8,9},{9,8},{10,11... | collective-permute-start | bytes 5455880 | tf_op jit(solution)/shard_map/ppermute | solution.py:21
  158.5 32.8 %collective-permute-start.21 = (bf16[2,1,192,1536]{3,2,1,0:T(8,128)(2,1)S(1)}, bf16[2,1,192,1536]{3,2,1,0:T(8,128)(2,1)}, u32[]{:S(2)}, u32[]{:S(2)}) collective-permute-start(bf16[2,1,192,1536]{3,2,1,0:T(8,128)(2,1)S(1)} %collective-permute-done.19.refs_1_), channel_id=1, source_target_pairs={{0,8},{8,16},{16,24},{24,28},{28,20},{20,12},{12,4},{4,0},{1,9},{9... | collective-permute-start | bytes 3538952 | tf_op jit(solution)/shard_map/ppermute | solution.py:94
  158.8 32.5 %collective-permute-start.22 = (bf16[2,1,192,1536]{3,2,1,0:T(8,128)(2,1)}, bf16[2,1,192,1536]{3,2,1,0:T(8,128)(2,1)}, u32[]{:S(2)}, u32[]{:S(2)}) collective-permute-start(bf16[2,1,192,1536]{3,2,1,0:T(8,128)(2,1)} %collective-permute-done.20.refs_2_), channel_id=1, source_target_pairs={{8,0},{16,8},{24,16},{28,24},{20,28},{12,20},{4,12},{0,4},{9,1},{1... | collective-permute-start | bytes 3538952 | tf_op jit(solution)/shard_map/ppermute | solution.py:97
  200.6 28.5 %collective-permute-start.28 = (bf16[2,1,192,1536]{3,2,1,0:T(8,128)(2,1)}, bf16[2,1,192,1536]{3,2,1,0:T(8,128)(2,1)S(1)}, u32[]{:S(2)}, u32[]{:S(2)}) collective-permute-start(bf16[2,1,192,1536]{3,2,1,0:T(8,128)(2,1)} %collective-permute-done.21.refs_3_), channel_id=1, source_target_pairs={{0,8},{8,16},{16,24},{24,28},{28,20},{20,12},{12,4},{4,0},{1,9},{9... | collective-permute-start | bytes 3538952 | tf_op jit(solution)/shard_map/ppermute | solution.py:94
  200.9 28.2 %collective-permute-start.29 = (bf16[2,1,192,1536]{3,2,1,0:T(8,128)(2,1)}, bf16[2,1,192,1536]{3,2,1,0:T(8,128)(2,1)S(1)}, u32[]{:S(2)}, u32[]{:S(2)}) collective-permute-start(bf16[2,1,192,1536]{3,2,1,0:T(8,128)(2,1)} %collective-permute-done.22.refs_4_), channel_id=1, source_target_pairs={{8,0},{16,8},{24,16},{28,24},{20,28},{12,20},{4,12},{0,4},{9,1},{1... | collective-permute-start | bytes 3538952 | tf_op jit(solution)/shard_map/ppermute | solution.py:97
  206.1 42.2 %collective-permute-start.32 = (bf16[2,296,1536]{2,1,0:T(8,128)(2,1)S(1)}, bf16[2,296,1536]{2,1,0:T(8,128)(2,1)}, u32[]{:S(2)}, u32[]{:S(2)}) collective-permute-start(bf16[2,296,1536]{2,1,0:T(8,128)(2,1)S(1)} %add_convert_fusion.3), channel_id=1, source_target_pairs={{0,2},{1,3},{2,0},{3,1},{4,6},{5,7},{6,4},{7,5},{8,10},{9,11},{10,... | collective-permute-start | bytes 5455880 | tf_op jit(solution)/shard_map/ppermute | solution.py:21
  254.5 44.5 %collective-permute-start.37 = (bf16[2,296,1536]{2,1,0:T(8,128)(2,1)}, bf16[2,296,1536]{2,1,0:T(8,128)(2,1)}, u32[]{:S(2)}, u32[]{:S(2)}) collective-permute-start(bf16[2,296,1536]{2,1,0:T(8,128)(2,1)} %get-tuple-element.782.refs_0_.a), channel_id=1, source_target_pairs={{0,2},{1,3},{2,0},{3,1},{4,6},{5,7},{6,4},{7,5},{8,10},{9,11},{10,... | collective-permute-start | bytes 5455880 | tf_op jit(solution)/shard_map/ppermute | solution.py:21
  256.1 42.9 %collective-permute-start.38 = (bf16[2,296,1536]{2,1,0:T(8,128)(2,1)}, bf16[2,296,1536]{2,1,0:T(8,128)(2,1)}, u32[]{:S(2)}, u32[]{:S(2)}) collective-permute-start(bf16[2,296,1536]{2,1,0:T(8,128)(2,1)} %get-tuple-element.782.refs_0_.a), channel_id=1, source_target_pairs={{0,1},{1,0},{2,3},{3,2},{4,5},{5,4},{6,7},{7,6},{8,9},{9,8},{10,11... | collective-permute-start | bytes 5455880 | tf_op jit(solution)/shard_map/ppermute | solution.py:21
  299.7 32.0 %collective-permute-start.40 = (bf16[2,1,192,1536]{3,2,1,0:T(8,128)(2,1)}, bf16[2,1,192,1536]{3,2,1,0:T(8,128)(2,1)S(1)}, u32[]{:S(2)}, u32[]{:S(2)}) collective-permute-start(bf16[2,1,192,1536]{3,2,1,0:T(8,128)(2,1)} %copy-done.12), channel_id=1, source_target_pairs={{0,8},{8,16},{16,24},{24,28},{28,20},{20,12},{12,4},{4,0},{1,9},{9... | collective-permute-start | bytes 3538952 | tf_op jit(solution)/shard_map/ppermute | solution.py:94
  300.2 31.5 %collective-permute-start.41 = (bf16[2,1,192,1536]{3,2,1,0:T(8,128)(2,1)}, bf16[2,1,192,1536]{3,2,1,0:T(8,128)(2,1)}, u32[]{:S(2)}, u32[]{:S(2)}) collective-permute-start(bf16[2,1,192,1536]{3,2,1,0:T(8,128)(2,1)} %collective-permute-done.36.refs_1_), channel_id=1, source_target_pairs={{8,0},{16,8},{24,16},{28,24},{20,28},{12,20},{4,12},{0,4},{9,1},{1... | collective-permute-start | bytes 3538952 | tf_op jit(solution)/shard_map/ppermute | solution.py:97
  413.2 43.8 %collective-permute-start.50 = (bf16[2,296,1536]{2,1,0:T(8,128)(2,1)}, bf16[2,296,1536]{2,1,0:T(8,128)(2,1)}, u32[]{:S(2)}, u32[]{:S(2)}) collective-permute-start(bf16[2,296,1536]{2,1,0:T(8,128)(2,1)} %add_convert_fusion.2), channel_id=1, source_target_pairs={{0,2},{1,3},{2,0},{3,1},{4,6},{5,7},{6,4},{7,5},{8,10},{9,11},{10,... | collective-permute-start | bytes 5455880 | tf_op jit(solution)/shard_map/ppermute | solution.py:21
  416.5 40.4 %collective-permute-start.48 = (bf16[2,192,1536]{2,1,0:T(8,128)(2,1)}, bf16[2,192,1536]{2,1,0:T(8,128)(2,1)S(1)}, u32[]{:S(2)}, u32[]{:S(2)}) collective-permute-start(bf16[2,192,1536]{2,1,0:T(8,128)(2,1)} %get-tuple-element.807), channel_id=1, source_target_pairs={{0,8},{8,16},{16,24},{24,28},{28,20},{20,12},{12,4},{4,0},{1,9},{9... | collective-permute-start | bytes 3538952 | tf_op jit(solution)/shard_map/ppermute | solution.py:94
  417.3 39.6 %collective-permute-start.49 = (bf16[2,192,1536]{2,1,0:T(8,128)(2,1)}, bf16[2,192,1536]{2,1,0:T(8,128)(2,1)}, u32[]{:S(2)}, u32[]{:S(2)}) collective-permute-start(bf16[2,192,1536]{2,1,0:T(8,128)(2,1)} %get-tuple-element.808), channel_id=1, source_target_pairs={{8,0},{16,8},{24,16},{28,24},{20,28},{12,20},{4,12},{0,4},{9,1},{1... | collective-permute-start | bytes 3538952 | tf_op jit(solution)/shard_map/ppermute | solution.py:97
  471.7 29.1 %collective-permute-start.51 = (bf16[2,192,1536]{2,1,0:T(8,128)(2,1)}, bf16[2,192,1536]{2,1,0:T(8,128)(2,1)S(1)}, u32[]{:S(2)}, u32[]{:S(2)}) collective-permute-start(bf16[2,192,1536]{2,1,0:T(8,128)(2,1)} %get-tuple-element.838), channel_id=1, source_target_pairs={{0,8},{8,16},{16,24},{24,28},{28,20},{20,12},{12,4},{4,0},{1,9},{9... | collective-permute-start | bytes 3538952 | tf_op jit(solution)/shard_map/ppermute | solution.py:94
  472.5 46.5 %collective-permute-start.55 = (bf16[2,296,1536]{2,1,0:T(8,128)(2,1)}, bf16[2,296,1536]{2,1,0:T(8,128)(2,1)}, u32[]{:S(2)}, u32[]{:S(2)}) collective-permute-start(bf16[2,296,1536]{2,1,0:T(8,128)(2,1)} %get-tuple-element.883.refs_0_.a), channel_id=1, source_target_pairs={{0,2},{1,3},{2,0},{3,1},{4,6},{5,7},{6,4},{7,5},{8,10},{9,11},{10,... | collective-permute-start | bytes 5455880 | tf_op jit(solution)/shard_map/ppermute | solution.py:21
  472.8 46.2 %collective-permute-start.56 = (bf16[2,296,1536]{2,1,0:T(8,128)(2,1)}, bf16[2,296,1536]{2,1,0:T(8,128)(2,1)}, u32[]{:S(2)}, u32[]{:S(2)}) collective-permute-start(bf16[2,296,1536]{2,1,0:T(8,128)(2,1)} %get-tuple-element.883.refs_0_.a), channel_id=1, source_target_pairs={{0,1},{1,0},{2,3},{3,2},{4,5},{5,4},{6,7},{7,6},{8,9},{9,8},{10,11... | collective-permute-start | bytes 5455880 | tf_op jit(solution)/shard_map/ppermute | solution.py:21
  472.8 30.4 %collective-permute-start.52 = (bf16[2,192,1536]{2,1,0:T(8,128)(2,1)}, bf16[2,192,1536]{2,1,0:T(8,128)(2,1)}, u32[]{:S(2)}, u32[]{:S(2)}) collective-permute-start(bf16[2,192,1536]{2,1,0:T(8,128)(2,1)} %get-tuple-element.839), channel_id=1, source_target_pairs={{8,0},{16,8},{24,16},{28,24},{20,28},{12,20},{4,12},{0,4},{9,1},{1... | collective-permute-start | bytes 3538952 | tf_op jit(solution)/shard_map/ppermute | solution.py:97
  474.3 37.3 %collective-permute-start.53 = (bf16[1,192,1536]{2,1,0:T(8,128)(2,1)}, bf16[1,192,1536]{2,1,0:T(8,128)(2,1)S(1)}, u32[]{:S(2)}, u32[]{:S(2)}) collective-permute-start(bf16[1,192,1536]{2,1,0:T(8,128)(2,1)} %get-tuple-element.846), channel_id=1, source_target_pairs={{0,8},{8,16},{16,24},{24,28},{28,20},{20,12},{12,4},{4,0},{1,9},{9... | collective-permute-start | bytes 1769480 | tf_op jit(solution)/shard_map/ppermute | solution.py:94
  532.7 50.1 %collective-permute-start.60 = (bf16[2,192,1536]{2,1,0:T(8,128)(2,1)}, bf16[2,192,1536]{2,1,0:T(8,128)(2,1)S(1)}, u32[]{:S(2)}, u32[]{:S(2)}) collective-permute-start(bf16[2,192,1536]{2,1,0:T(8,128)(2,1)} %get-tuple-element.901), channel_id=1, source_target_pairs={{0,8},{8,16},{16,24},{24,28},{28,20},{20,12},{12,4},{4,0},{1,9},{9... | collective-permute-start | bytes 3538952 | tf_op jit(solution)/shard_map/ppermute | solution.py:94
  533.2 49.7 %collective-permute-start.61 = (bf16[2,192,1536]{2,1,0:T(8,128)(2,1)}, bf16[2,192,1536]{2,1,0:T(8,128)(2,1)}, u32[]{:S(2)}, u32[]{:S(2)}) collective-permute-start(bf16[2,192,1536]{2,1,0:T(8,128)(2,1)} %get-tuple-element.902), channel_id=1, source_target_pairs={{8,0},{16,8},{24,16},{28,24},{20,28},{12,20},{4,12},{0,4},{9,1},{1... | collective-permute-start | bytes 3538952 | tf_op jit(solution)/shard_map/ppermute | solution.py:97
  534.7 51.6 %collective-permute-start.62 = (bf16[2,192,1536]{2,1,0:T(8,128)(2,1)}, bf16[2,192,1536]{2,1,0:T(8,128)(2,1)}, u32[]{:S(2)}, u32[]{:S(2)}) collective-permute-start(bf16[2,192,1536]{2,1,0:T(8,128)(2,1)} %get-tuple-element.904), channel_id=1, source_target_pairs={{0,8},{8,16},{16,24},{24,28},{28,20},{20,12},{12,4},{4,0},{1,9},{9... | collective-permute-start | bytes 3538952 | tf_op jit(solution)/shard_map/ppermute | solution.py:94
  537.4 49.1 %collective-permute-start.63 = (bf16[2,192,1536]{2,1,0:T(8,128)(2,1)}, bf16[2,192,1536]{2,1,0:T(8,128)(2,1)}, u32[]{:S(2)}, u32[]{:S(2)}) collective-permute-start(bf16[2,192,1536]{2,1,0:T(8,128)(2,1)} %get-tuple-element.905), channel_id=1, source_target_pairs={{8,0},{16,8},{24,16},{28,24},{20,28},{12,20},{4,12},{0,4},{9,1},{1... | collective-permute-start | bytes 3538952 | tf_op jit(solution)/shard_map/ppermute | solution.py:97
  551.7 71.4 %collective-permute-start.64 = (bf16[2,296,1536]{2,1,0:T(8,128)(2,1)}, bf16[2,296,1536]{2,1,0:T(8,128)(2,1)}, u32[]{:S(2)}, u32[]{:S(2)}) collective-permute-start(bf16[2,296,1536]{2,1,0:T(8,128)(2,1)} %add_convert_fusion.1), channel_id=1, source_target_pairs={{0,2},{1,3},{2,0},{3,1},{4,6},{5,7},{6,4},{7,5},{8,10},{9,11},{10,... | collective-permute-start | bytes 5455880 | tf_op jit(solution)/shard_map/ppermute | solution.py:21
  591.7 31.4 %collective-permute-start.65 = (bf16[2,192,1536]{2,1,0:T(8,128)(2,1)}, bf16[2,192,1536]{2,1,0:T(8,128)(2,1)S(1)}, u32[]{:S(2)}, u32[]{:S(2)}) collective-permute-start(bf16[2,192,1536]{2,1,0:T(8,128)(2,1)} %get-tuple-element.922), channel_id=1, source_target_pairs={{0,8},{8,16},{16,24},{24,28},{28,20},{20,12},{12,4},{4,0},{1,9},{9... | collective-permute-start | bytes 3538952 | tf_op jit(solution)/shard_map/ppermute | solution.py:94
  593.5 29.7 %collective-permute-start.66 = (bf16[2,192,1536]{2,1,0:T(8,128)(2,1)}, bf16[2,192,1536]{2,1,0:T(8,128)(2,1)}, u32[]{:S(2)}, u32[]{:S(2)}) collective-permute-start(bf16[2,192,1536]{2,1,0:T(8,128)(2,1)} %get-tuple-element.923), channel_id=1, source_target_pairs={{8,0},{16,8},{24,16},{28,24},{20,28},{12,20},{4,12},{0,4},{9,1},{1... | collective-permute-start | bytes 3538952 | tf_op jit(solution)/shard_map/ppermute | solution.py:97
  683.8 42.4 %collective-permute-start.75 = (bf16[2,296,1536]{2,1,0:T(8,128)(2,1)}, bf16[2,296,1536]{2,1,0:T(8,128)(2,1)}, u32[]{:S(2)}, u32[]{:S(2)}) collective-permute-start(bf16[2,296,1536]{2,1,0:T(8,128)(2,1)} %add_convert_fusion), channel_id=1, source_target_pairs={{0,2},{1,3},{2,0},{3,1},{4,6},{5,7},{6,4},{7,5},{8,10},{9,11},{10,... | collective-permute-start | bytes 5455880 | tf_op jit(solution)/shard_map/ppermute | solution.py:21
  685.3 28.3 %collective-permute-start.73 = (bf16[2,192,1536]{2,1,0:T(8,128)(2,1)}, bf16[2,192,1536]{2,1,0:T(8,128)(2,1)S(1)}, u32[]{:S(2)}, u32[]{:S(2)}) collective-permute-start(bf16[2,192,1536]{2,1,0:T(8,128)(2,1)} %get-tuple-element.1017), channel_id=1, source_target_pairs={{0,8},{8,16},{16,24},{24,28},{28,20},{20,12},{12,4},{4,0},{1,9},{9... | collective-permute-start | bytes 3538952 | tf_op jit(solution)/shard_map/ppermute | solution.py:94
  687.0 28.1 %collective-permute-start.74 = (bf16[2,192,1536]{2,1,0:T(8,128)(2,1)}, bf16[2,192,1536]{2,1,0:T(8,128)(2,1)}, u32[]{:S(2)}, u32[]{:S(2)}) collective-permute-start(bf16[2,192,1536]{2,1,0:T(8,128)(2,1)} %get-tuple-element.1018), channel_id=1, source_target_pairs={{8,0},{16,8},{24,16},{28,24},{20,28},{12,20},{4,12},{0,4},{9,1},{1... | collective-permute-start | bytes 3538952 | tf_op jit(solution)/shard_map/ppermute | solution.py:97
  (107 other events, 1682.3 us)

commit v8 on v7

--- a/solution.py
+++ b/solution.py
@@ -1112,9 +1112,10 @@
     cond_part = dot("csjn,sjdn->cd", modul_all, ada_weight)
     ada_bias_part = jnp.sum(modul_all.astype(F32), 0)
     last = jnp.concatenate([cond_part.reshape(-1), ada_bias_part.reshape(-1), bias_local])
+    last = order(last)
+    qkv_sums.take(order)
     last = order(spread(order(last), "tensor", 4))
-    qkv_sums.arrive(order)
-    last = order(last)
+    qkv_sums.add(order)
     cond_part = jnp.sum(last[:, : cond_part.size], 0).reshape(groups, slots, rows)
     cond_terms = order(exchange(cond_part, "dp", groups))
     cond_term = jnp.stack(

time: 818 us -> 823 us (level)
  transfers between devices with their start and end apart: 92 -> 92, of which waited for: 45 -> 44; matrix products, arithmetic and copies ran while one was open for 6% -> 6% of each run, Pallas kernels for 45% -> 44%
where the time goes in v8:
time: 823 us; the launch traced here: 813 us
  Pallas kernels  414 us (50%)
  waiting for transfers between devices  237 us (29%)
  starting transfers between devices  89.9 us (11%)
  local copies, waits for them, and re-layouts  28.7 us (3%)
  other arithmetic  28.5 us (3%)
    ppermute x24, waiting for transfers between devices, forward(): return lax.ppermute(value, 'dp', self.ahead)  183 us
    pallas_call x8, Pallas kernels, rows_times(): kernel_call(kernel, 'rows_times', 1 + 3e-09 * 4 * slots * tokens * depth...  129 us
    pallas_call x4, Pallas kernels, weight_grad(): kernel_call(kernel, 'weight_grad', 1 + 3.4e-09 * 4 * slots * tokens * dep...  71.9 us
    pallas_call x2, Pallas kernels, attend_back(): kernel_call(kernel, 'attend_back', 29, (pairs,), [spec(0), spec(1), spec(...  58.9 us
    pallas_call x9, Pallas kernels, ring_add(): kernel_call(kernel, 'ring_add', 1 + 7e-06 * image.shape[1] * image.shape[...  46.2 us
    ppermute x44, starting transfers between devices, hop(): return lax.ppermute(value, axis, [(i, i ^ mask) for i in range(size)])  38.7 us
    ppermute x44, waiting for transfers between devices, hop(): return lax.ppermute(value, axis, [(i, i ^ mask) for i in range(size)])  36.5 us
    pallas_call x5, Pallas kernels, per_slot(): kernel_call(kernel, name, 6, (slots,), [spec(value.shape, value.ndim == 2...  34 us
  transfers between devices with their start and end apart: 92, of which 44 were waited for; matrix products, arithmetic and copies ran while one was open for 6% of the time, Pallas kernels for 44%

profile of v8, /device:TPU:0, one launch (start us, length us, event | category | flops | bytes accessed | tf_op | source)
XLA Modules:
  0.0 813.5 jit_solution(1788018723423091753)
XLA Ops:
  35.6 6.1 all_gather.3.refs_4_.refs_5_
  46.6 9.7 %collective-permute-done.8.refs_1_ = bf16[2,4,192,384]{3,2,1,0:T(8,128)(2,1)} collective-permute-done((bf16[2,4,192,384]{3,2,1,0:T(8,128)(2,1)S(1)}, bf16[2,4,192,384]{3,2,1,0:T(8,128)(2,1)}, u32[]{:S(2)}, u32[]{:S(2)}) %collective-permute-start.8) | collective-permute-done | bytes 1179680 | tf_op jit(solution)/shard_map/ppermute | solution.py:94
  63.6 22.2 %collective-permute-done.10.refs_3_ = bf16[2,4,192,384]{3,2,1,0:T(8,128)(2,1)S(1)} collective-permute-done((bf16[2,4,192,384]{3,2,1,0:T(8,128)(2,1)}, bf16[2,4,192,384]{3,2,1,0:T(8,128)(2,1)S(1)}, u32[]{:S(2)}, u32[]{:S(2)}) %collective-permute-start.10) | collective-permute-done | bytes 1179680 | tf_op jit(solution)/shard_map/ppermute | solution.py:94
  88.4 20.5 %collective-permute-done.12.refs_5_ = bf16[2,4,192,384]{3,2,1,0:T(8,128)(2,1)S(1)} collective-permute-done((bf16[2,4,192,384]{3,2,1,0:T(8,128)(2,1)S(1)}, bf16[2,4,192,384]{3,2,1,0:T(8,128)(2,1)S(1)}, u32[]{:S(2)}, u32[]{:S(2)}) %collective-permute-start.12) | collective-permute-done | bytes 1179680 | tf_op jit(solution)/shard_map/ppermute | solution.py:94
  119.4 7.7 assemble.5
  138.3 17.5 %rows_times.8.q.k.v = bf16[4,2,296,1152]{3,2,1,0:T(8,128)(2,1)} custom-call(bf16[2,296,1536]{2,1,0:T(8,128)(2,1)} %get-tuple-element.939.refs_0_.a, bf16[2,296,1536]{2,1,0:T(8,128)(2,1)} %copy-done.39, bf16[2,296,1536]{2,1,0:T(8,128)(2,1)} %collective-permute-done.14.refs_2_.c, bf16[2,296,1536]{2,1,0:T(8,128)(2,1)} %collective-permute-done.16.refs_3_.d, ...), custom_call_target="tpu_custom_call" | custom-call | flops 6242351616 | bytes 1 | tf_op jit(solution)/shard_map/rows_times/pallas_call | solution.py:406
  160.7 15.3 %attend.2 = (bf16[4,2,296,384]{3,2,1,0:T(8,128)(2,1)}, f32[2,3,2,1184]{3,2,1,0:T(2,128)}) custom-call(bf16[4,2,296,1152]{3,2,1,0:T(8,128)(2,1)} %rows_times.8.q.k.v, bf16[4,2,296,1152]{3,2,1,0:T(8,128)(2,1)} %rows_times.8.q.k.v, bf16[4,2,296,1152]{3,2,1,0:T(8,128)(2,1)} %rows_times.8.q.k.v), custom_call_target="tpu_custom_call" | custom-call | flops 6899999744 | bytes 1 | tf_op jit(solution)/shard_map/attend/pallas_call | solution.py:545
  176.0 15.3 %attend.3 = (bf16[4,2,296,384]{3,2,1,0:T(8,128)(2,1)}, f32[2,3,2,1184]{3,2,1,0:T(2,128)}) custom-call(bf16[4,2,296,1152]{3,2,1,0:T(8,128)(2,1)} %rows_times.8.q.k.v, bf16[4,2,296,1152]{3,2,1,0:T(8,128)(2,1)} %rows_times.8.q.k.v, bf16[4,2,296,1152]{3,2,1,0:T(8,128)(2,1)} %rows_times.8.q.k.v, ...), custom_call_target="tpu_custom_call", output_to_operand_aliasing={{0}: (3, {}), {1}: (4, {})} | custom-call | flops 6899999744 | bytes 1 | tf_op jit(solution)/shard_map/attend/pallas_call | solution.py:545
  191.4 8.6 %rows_times.9 = (bf16[2,296,1536]{2,1,0:T(8,128)(2,1)}, bf16[2,296,1536]{2,1,0:T(8,128)(2,1)}, bf16[2,296,1536]{2,1,0:T(8,128)(2,1)}, bf16[2,296,1536]{2,1,0:T(8,128)(2,1)}) custom-call(bf16[4,2,296,384]{3,2,1,0:T(8,128)(2,1)} %get-tuple-element.918.refs_0_.refs_1_.refs_2_.refs_3_.grad.mixed, ...), custom_call_target="tpu_custom_call" | custom-call | flops 2387450368 | bytes 1 | tf_op jit(solution)/shard_map/rows_times/pallas_call | solution.py:406
  207.6 21.5 %collective-permute-done.28.refs_5_ = bf16[2,1,192,1536]{3,2,1,0:T(8,128)(2,1)S(1)} collective-permute-done((bf16[2,1,192,1536]{3,2,1,0:T(8,128)(2,1)}, bf16[2,1,192,1536]{3,2,1,0:T(8,128)(2,1)S(1)}, u32[]{:S(2)}, u32[]{:S(2)}) %collective-permute-start.28) | collective-permute-done | bytes 1179680 | tf_op jit(solution)/shard_map/ppermute | solution.py:94
  231.9 12.2 %collective-permute-done.30.refs_7_ = bf16[1,1,192,1536]{3,2,1,0:T(8,128)(2,1)S(1)} collective-permute-done((bf16[1,1,192,1536]{3,2,1,0:T(8,128)(2,1)S(1)}, bf16[1,1,192,1536]{3,2,1,0:T(8,128)(2,1)S(1)}, u32[]{:S(2)}, u32[]{:S(2)}) %collective-permute-start.30) | collective-permute-done | bytes 589856 | tf_op jit(solution)/shard_map/ppermute | solution.py:94
  248.2 6.2 middle.1
  257.9 8.0 assemble.7
  281.0 17.6 %collective-permute-done.35.refs_0_ = bf16[2,1,192,1536]{3,2,1,0:T(8,128)(2,1)S(1)} collective-permute-done((bf16[2,1,192,1536]{3,2,1,0:T(8,128)(2,1)}, bf16[2,1,192,1536]{3,2,1,0:T(8,128)(2,1)S(1)}, u32[]{:S(2)}, u32[]{:S(2)}) %collective-permute-start.35) | collective-permute-done | bytes 1179680 | tf_op jit(solution)/shard_map/ppermute | solution.py:94
  306.0 25.6 %rows_times.10 = (bf16[4,2,296,1536]{3,2,1,0:T(8,128)(2,1)}, bf16[4,2,296,1536]{3,2,1,0:T(8,128)(2,1)}) custom-call(bf16[2,296,1536]{2,1,0:T(8,128)(2,1)} %get-tuple-element.785.refs_0_.a, bf16[2,296,1536]{2,1,0:T(8,128)(2,1)} %collective-permute-done.38.refs_1_.b, bf16[2,296,1536]{2,1,0:T(8,128)(2,1)} %collective-permute-done.37.refs_2_.c, ...), custom_call_target="tpu_custom_call" | custom-call | flops 8169801728 | bytes 1 | tf_op jit(solution)/shard_map/rows_times/pallas_call | solution.py:406
  336.9 20.9 %weight_grad.4 = (bf16[8,192,1536]{2,1,0:T(8,128)(2,1)}, bf16[8,192,1536]{2,1,0:T(8,128)(2,1)}, bf16[1,192,1536]{2,1,0:T(8,128)(2,1)}, bf16[1,192,1536]{2,1,0:T(8,128)(2,1)}, f32[2,1536]{1,0:T(2,128)}) custom-call(s32[1]{0:T(128)} %dynamic-slice.4.far, bf16[2,296,1536]{2,1,0:T(8,128)(2,1)} %get-tuple-element.746.a.refs_0_, ...), custom_call_target="tpu_custom_call" | custom-call | flops 9197775872 | bytes 1 | tf_op jit(solution)/shard_map/weight_grad/pallas_call | solution.py:459
  366.3 18.5 %rows_times.11.refs_0_.refs_1_.refs_2_.refs_3_.grad = bf16[4,2,296,1536]{3,2,1,0:T(8,128)(2,1)} custom-call(bf16[2,296,1536]{2,1,0:T(8,128)(2,1)} %get-tuple-element.746.a.refs_0_, bf16[2,296,1536]{2,1,0:T(8,128)(2,1)} %collective-permute-done.24.b.refs_1_, bf16[2,296,1536]{2,1,0:T(8,128)(2,1)} %collective-permute-done.23.c.refs_2_, ...), custom_call_target="tpu_custom_call" | custom-call | flops 8169801728 | bytes 1 | tf_op jit(solution)/shard_map/rows_times/pallas_call | solution.py:406
  384.8 17.8 %rows_times.12 = (bf16[2,296,1536]{2,1,0:T(8,128)(2,1)}, bf16[2,296,1536]{2,1,0:T(8,128)(2,1)}, bf16[2,296,1536]{2,1,0:T(8,128)(2,1)}, bf16[2,296,1536]{2,1,0:T(8,128)(2,1)}) custom-call(bf16[4,2,296,1536]{3,2,1,0:T(8,128)(2,1)} %rows_times.11.refs_0_.refs_1_.refs_2_.refs_3_.grad, bf16[4,2,296,1536]{3,2,1,0:T(8,128)(2,1)} %rows_times.11.refs_0_.refs_1_.refs_2_.refs_3_.grad, ...), custom_call_target="tpu_custom_call" | custom-call | flops 8169801728 | bytes 1 | tf_op jit(solution)/shard_map/rows_times/pallas_call | solution.py:406
  418.5 20.8 %weight_grad.5 = (bf16[8,192,1536]{2,1,0:T(8,128)(2,1)}, bf16[8,192,1536]{2,1,0:T(8,128)(2,1)}, bf16[1,192,1536]{2,1,0:T(8,128)(2,1)}, bf16[1,192,1536]{2,1,0:T(8,128)(2,1)}, f32[2,1536]{1,0:T(2,128)}) custom-call(s32[1]{0:T(128)} %dynamic-slice.4.far, bf16[2,296,1536]{2,1,0:T(8,128)(2,1)} %get-tuple-element.785.refs_0_.a, ...), custom_call_target="tpu_custom_call" | custom-call | flops 9197775872 | bytes 1 | tf_op jit(solution)/shard_map/weight_grad/pallas_call | solution.py:459
  439.3 17.4 %rows_times.13 = (bf16[2,296,1536]{2,1,0:T(8,128)(2,1)}, bf16[2,296,1536]{2,1,0:T(8,128)(2,1)}, bf16[2,296,1536]{2,1,0:T(8,128)(2,1)}, bf16[2,296,1536]{2,1,0:T(8,128)(2,1)}) custom-call(bf16[4,2,296,1536]{3,2,1,0:T(8,128)(2,1)} %get-tuple-element.802.grad.refs_0_.refs_1_.refs_2_.refs_3_, ...), custom_call_target="tpu_custom_call" | custom-call | flops 8169801728 | bytes 1 | tf_op jit(solution)/shard_map/rows_times/pallas_call | solution.py:406
  456.8 9.5 %middle_back.1 = (f32[2,296,1536]{2,1,0:T(8,128)}, bf16[2,296,1536]{2,1,0:T(8,128)(2,1)}, f32[2,2,4,1536]{3,2,1,0:T(4,128)}) custom-call(s32[1]{0:T(128)} %copy.204.seqs, bf16[2,256,1536]{2,1,0:T(8,128)(2,1)} %refs_0_.3, bf16[2,40,1536]{2,1,0:T(8,128)(2,1)} %refs_1_.3, bf16[2,296,1536]{2,1,0:T(8,128)(2,1)} %get-tuple-element.823.refs_2_, ...), custom_call_target="tpu_custom_call" | custom-call | flops 2760000000 | bytes 1 | tf_op jit(solution)/shard_map/middle_back/pallas_call | solution.py:673
  474.7 25.9 %collective-permute-done.51.ahead = bf16[2,192,1536]{2,1,0:T(8,128)(2,1)S(1)} collective-permute-done((bf16[2,192,1536]{2,1,0:T(8,128)(2,1)}, bf16[2,192,1536]{2,1,0:T(8,128)(2,1)S(1)}, u32[]{:S(2)}, u32[]{:S(2)}) %collective-permute-start.51) | collective-permute-done | bytes 1179680 | tf_op jit(solution)/shard_map/ppermute | solution.py:94
  523.1 9.0 %rows_times.14.grads = bf16[4,2,296,384]{3,2,1,0:T(8,128)(2,1)} custom-call(bf16[2,296,1536]{2,1,0:T(8,128)(2,1)} %get-tuple-element.886.refs_0_.a, bf16[2,296,1536]{2,1,0:T(8,128)(2,1)} %collective-permute-done.56.refs_1_.b, bf16[2,296,1536]{2,1,0:T(8,128)(2,1)} %collective-permute-done.55.refs_2_.c, ...), custom_call_target="tpu_custom_call" | custom-call | flops 2387450368 | bytes 1 | tf_op jit(solution)/shard_map/rows_times/pallas_call | solution.py:406
  541.9 9.6 %weight_grad.6 = (bf16[8,192,1536]{2,1,0:T(8,128)(2,1)}, bf16[8,192,1536]{2,1,0:T(8,128)(2,1)}, bf16[1,192,1536]{2,1,0:T(8,128)(2,1)}, bf16[1,192,1536]{2,1,0:T(8,128)(2,1)}, f32[2,384]{1,0:T(2,128)}) custom-call(s32[1]{0:T(128)} %dynamic-slice.4.far, bf16[2,296,1536]{2,1,0:T(8,128)(2,1)} %get-tuple-element.886.refs_0_.a, ...), custom_call_target="tpu_custom_call" | custom-call | flops 2644443904 | bytes 1 | tf_op jit(solution)/shard_map/weight_grad/pallas_call | solution.py:459
  553.0 29.6 %attend_back.2.refs_0_ = bf16[4,2,296,1152]{3,2,1,0:T(8,128)(2,1)} custom-call(bf16[4,2,296,1152]{3,2,1,0:T(8,128)(2,1)} %rows_times.8.q.k.v, bf16[4,2,296,1152]{3,2,1,0:T(8,128)(2,1)} %rows_times.8.q.k.v, bf16[4,2,296,1152]{3,2,1,0:T(8,128)(2,1)} %rows_times.8.q.k.v, bf16[4,2,296,384]{3,2,1,0:T(8,128)(2,1)} %get-tuple-element.918.refs_0_.refs_1_.refs_2_.refs_3_.grad.mixed, ...), custom_call_target="tpu_custom_call" | custom-call | flops 13340000256 | bytes 1 | tf_op jit(solution)/shard_map/attend_back/pallas_call | solution.py:619
  593.7 29.3 %attend_back.3.grad.refs_0_.refs_1_.refs_2_.refs_3_ = bf16[4,2,296,1152]{3,2,1,0:T(8,128)(2,1)} custom-call(bf16[4,2,296,1152]{3,2,1,0:T(8,128)(2,1)} %rows_times.8.q.k.v, bf16[4,2,296,1152]{3,2,1,0:T(8,128)(2,1)} %rows_times.8.q.k.v, bf16[4,2,296,1152]{3,2,1,0:T(8,128)(2,1)} %rows_times.8.q.k.v, ...), custom_call_target="tpu_custom_call", output_to_operand_aliasing={{}: (6, {})} | custom-call | flops 13340000256 | bytes 1 | tf_op jit(solution)/shard_map/attend_back/pallas_call | solution.py:619
  631.3 20.5 %weight_grad.7 = (bf16[8,192,1536]{2,1,0:T(8,128)(2,1)}, bf16[8,192,1536]{2,1,0:T(8,128)(2,1)}, bf16[1,192,1536]{2,1,0:T(8,128)(2,1)}, bf16[1,192,1536]{2,1,0:T(8,128)(2,1)}, f32[2,1152]{1,0:T(2,128)}) custom-call(s32[1]{0:T(128)} %dynamic-slice.4.far, ...), custom_call_target="tpu_custom_call", output_to_operand_aliasing={{0}: (6, {}), {1}: (7, {}), {2}: (8, {}), {3}: (9, {})} | custom-call | flops 7013331456 | bytes 1 | tf_op jit(solution)/shard_map/weight_grad/pallas_call | solution.py:459
  659.4 14.7 %rows_times.15 = (bf16[2,296,1536]{2,1,0:T(8,128)(2,1)}, bf16[2,296,1536]{2,1,0:T(8,128)(2,1)}, bf16[2,296,1536]{2,1,0:T(8,128)(2,1)}, bf16[2,296,1536]{2,1,0:T(8,128)(2,1)}) custom-call(bf16[4,2,296,1152]{3,2,1,0:T(8,128)(2,1)} %attend_back.3.grad.refs_0_.refs_1_.refs_2_.refs_3_, bf16[4,2,296,1152]{3,2,1,0:T(8,128)(2,1)} %attend_back.3.grad.refs_0_.refs_1_.refs_2_.refs_3_, ...), custom_call_target="tpu_custom_call" | custom-call | flops 6242351616 | bytes 1 | tf_op jit(solution)/shard_map/rows_times/pallas_call | solution.py:406
  707.4 6.1 collective-permute-done.73.ahead
  726.0 7.4 enter_back.1
  740.4 7.1 collective-permute-done.78.ahead
  769.2 19.9 %collective-permute-done.84.ahead = bf16[2,192,1536]{2,1,0:T(8,128)(2,1)} collective-permute-done((bf16[2,192,1536]{2,1,0:T(8,128)(2,1)}, bf16[2,192,1536]{2,1,0:T(8,128)(2,1)}, u32[]{:S(2)}, u32[]{:S(2)}) %collective-permute-start.84) | collective-permute-done | bytes 1179680 | tf_op jit(solution)/shard_map/ppermute | solution.py:94
  (435 shorter events, 309.6 us)
Async XLA Ops:
  62.1 48.0 %collective-permute-start.14 = (bf16[2,296,1536]{2,1,0:T(8,128)(2,1)}, bf16[2,296,1536]{2,1,0:T(8,128)(2,1)}, u32[]{:S(2)}, u32[]{:S(2)}) collective-permute-start(bf16[2,296,1536]{2,1,0:T(8,128)(2,1)} %get-tuple-element.939.refs_0_.a), channel_id=1, source_target_pairs={{0,2},{1,3},{2,0},{3,1},{4,6},{5,7},{6,4},{7,5},{8,10},{9,11},{10,... | collective-permute-start | bytes 5455880 | tf_op jit(solution)/shard_map/ppermute | solution.py:21
  63.6 46.5 %collective-permute-start.15 = (bf16[2,296,1536]{2,1,0:T(8,128)(2,1)}, bf16[2,296,1536]{2,1,0:T(8,128)(2,1)S(1)}, u32[]{:S(2)}, u32[]{:S(2)}) collective-permute-start(bf16[2,296,1536]{2,1,0:T(8,128)(2,1)} %get-tuple-element.939.refs_0_.a), channel_id=1, source_target_pairs={{0,1},{1,0},{2,3},{3,2},{4,5},{5,4},{6,7},{7,6},{8,9},{9,8},{10,11... | collective-permute-start | bytes 5455880 | tf_op jit(solution)/shard_map/ppermute | solution.py:21
  130.5 27.5 %collective-permute-start.19 = (bf16[2,1,192,1536]{3,2,1,0:T(8,128)(2,1)}, bf16[2,1,192,1536]{3,2,1,0:T(8,128)(2,1)S(1)}, u32[]{:S(2)}, u32[]{:S(2)}) collective-permute-start(bf16[2,1,192,1536]{3,2,1,0:T(8,128)(2,1)} %bitcast.168), channel_id=1, source_target_pairs={{0,8},{8,16},{16,24},{24,28},{28,20},{20,12},{12,4},{4,0},{1,9},{9... | collective-permute-start | bytes 3538952 | tf_op jit(solution)/shard_map/ppermute | solution.py:94
  133.9 57.4 %collective-permute-start.23 = (bf16[2,296,1536]{2,1,0:T(8,128)(2,1)}, bf16[2,296,1536]{2,1,0:T(8,128)(2,1)}, u32[]{:S(2)}, u32[]{:S(2)}) collective-permute-start(bf16[2,296,1536]{2,1,0:T(8,128)(2,1)} %get-tuple-element.746.a.refs_0_), channel_id=1, source_target_pairs={{0,2},{1,3},{2,0},{3,1},{4,6},{5,7},{6,4},{7,5},{8,10},{9,11},{10,... | collective-permute-start | bytes 5455880 | tf_op jit(solution)/shard_map/ppermute | solution.py:21
  135.4 55.9 %collective-permute-start.24 = (bf16[2,296,1536]{2,1,0:T(8,128)(2,1)}, bf16[2,296,1536]{2,1,0:T(8,128)(2,1)}, u32[]{:S(2)}, u32[]{:S(2)}) collective-permute-start(bf16[2,296,1536]{2,1,0:T(8,128)(2,1)} %get-tuple-element.746.a.refs_0_), channel_id=1, source_target_pairs={{0,1},{1,0},{2,3},{3,2},{4,5},{5,4},{6,7},{7,6},{8,9},{9,8},{10,11... | collective-permute-start | bytes 5455880 | tf_op jit(solution)/shard_map/ppermute | solution.py:21
  158.5 32.8 %collective-permute-start.21 = (bf16[2,1,192,1536]{3,2,1,0:T(8,128)(2,1)S(1)}, bf16[2,1,192,1536]{3,2,1,0:T(8,128)(2,1)}, u32[]{:S(2)}, u32[]{:S(2)}) collective-permute-start(bf16[2,1,192,1536]{3,2,1,0:T(8,128)(2,1)S(1)} %collective-permute-done.19.refs_1_), channel_id=1, source_target_pairs={{0,8},{8,16},{16,24},{24,28},{28,20},{20,12},{12,4},{4,0},{1,9},{9... | collective-permute-start | bytes 3538952 | tf_op jit(solution)/shard_map/ppermute | solution.py:94
  158.8 32.5 %collective-permute-start.22 = (bf16[2,1,192,1536]{3,2,1,0:T(8,128)(2,1)}, bf16[2,1,192,1536]{3,2,1,0:T(8,128)(2,1)}, u32[]{:S(2)}, u32[]{:S(2)}) collective-permute-start(bf16[2,1,192,1536]{3,2,1,0:T(8,128)(2,1)} %collective-permute-done.20.refs_2_), channel_id=1, source_target_pairs={{8,0},{16,8},{24,16},{28,24},{20,28},{12,20},{4,12},{0,4},{9,1},{1... | collective-permute-start | bytes 3538952 | tf_op jit(solution)/shard_map/ppermute | solution.py:97
  200.5 28.5 %collective-permute-start.28 = (bf16[2,1,192,1536]{3,2,1,0:T(8,128)(2,1)}, bf16[2,1,192,1536]{3,2,1,0:T(8,128)(2,1)S(1)}, u32[]{:S(2)}, u32[]{:S(2)}) collective-permute-start(bf16[2,1,192,1536]{3,2,1,0:T(8,128)(2,1)} %collective-permute-done.21.refs_3_), channel_id=1, source_target_pairs={{0,8},{8,16},{16,24},{24,28},{28,20},{20,12},{12,4},{4,0},{1,9},{9... | collective-permute-start | bytes 3538952 | tf_op jit(solution)/shard_map/ppermute | solution.py:94
  200.8 28.2 %collective-permute-start.29 = (bf16[2,1,192,1536]{3,2,1,0:T(8,128)(2,1)}, bf16[2,1,192,1536]{3,2,1,0:T(8,128)(2,1)S(1)}, u32[]{:S(2)}, u32[]{:S(2)}) collective-permute-start(bf16[2,1,192,1536]{3,2,1,0:T(8,128)(2,1)} %collective-permute-done.22.refs_4_), channel_id=1, source_target_pairs={{8,0},{16,8},{24,16},{28,24},{20,28},{12,20},{4,12},{0,4},{9,1},{1... | collective-permute-start | bytes 3538952 | tf_op jit(solution)/shard_map/ppermute | solution.py:97
  206.0 42.2 %collective-permute-start.32 = (bf16[2,296,1536]{2,1,0:T(8,128)(2,1)S(1)}, bf16[2,296,1536]{2,1,0:T(8,128)(2,1)}, u32[]{:S(2)}, u32[]{:S(2)}) collective-permute-start(bf16[2,296,1536]{2,1,0:T(8,128)(2,1)S(1)} %add_convert_fusion.3), channel_id=1, source_target_pairs={{0,2},{1,3},{2,0},{3,1},{4,6},{5,7},{6,4},{7,5},{8,10},{9,11},{10,... | collective-permute-start | bytes 5455880 | tf_op jit(solution)/shard_map/ppermute | solution.py:21
  254.5 44.5 %collective-permute-start.37 = (bf16[2,296,1536]{2,1,0:T(8,128)(2,1)}, bf16[2,296,1536]{2,1,0:T(8,128)(2,1)}, u32[]{:S(2)}, u32[]{:S(2)}) collective-permute-start(bf16[2,296,1536]{2,1,0:T(8,128)(2,1)} %get-tuple-element.785.refs_0_.a), channel_id=1, source_target_pairs={{0,2},{1,3},{2,0},{3,1},{4,6},{5,7},{6,4},{7,5},{8,10},{9,11},{10,... | collective-permute-start | bytes 5455880 | tf_op jit(solution)/shard_map/ppermute | solution.py:21
  256.1 42.9 %collective-permute-start.38 = (bf16[2,296,1536]{2,1,0:T(8,128)(2,1)}, bf16[2,296,1536]{2,1,0:T(8,128)(2,1)}, u32[]{:S(2)}, u32[]{:S(2)}) collective-permute-start(bf16[2,296,1536]{2,1,0:T(8,128)(2,1)} %get-tuple-element.785.refs_0_.a), channel_id=1, source_target_pairs={{0,1},{1,0},{2,3},{3,2},{4,5},{5,4},{6,7},{7,6},{8,9},{9,8},{10,11... | collective-permute-start | bytes 5455880 | tf_op jit(solution)/shard_map/ppermute | solution.py:21
  299.6 32.0 %collective-permute-start.40 = (bf16[2,1,192,1536]{3,2,1,0:T(8,128)(2,1)}, bf16[2,1,192,1536]{3,2,1,0:T(8,128)(2,1)S(1)}, u32[]{:S(2)}, u32[]{:S(2)}) collective-permute-start(bf16[2,1,192,1536]{3,2,1,0:T(8,128)(2,1)} %copy-done.12), channel_id=1, source_target_pairs={{0,8},{8,16},{16,24},{24,28},{28,20},{20,12},{12,4},{4,0},{1,9},{9... | collective-permute-start | bytes 3538952 | tf_op jit(solution)/shard_map/ppermute | solution.py:94
  300.2 31.4 %collective-permute-start.41 = (bf16[2,1,192,1536]{3,2,1,0:T(8,128)(2,1)}, bf16[2,1,192,1536]{3,2,1,0:T(8,128)(2,1)}, u32[]{:S(2)}, u32[]{:S(2)}) collective-permute-start(bf16[2,1,192,1536]{3,2,1,0:T(8,128)(2,1)} %collective-permute-done.36.refs_1_), channel_id=1, source_target_pairs={{8,0},{16,8},{24,16},{28,24},{20,28},{12,20},{4,12},{0,4},{9,1},{1... | collective-permute-start | bytes 3538952 | tf_op jit(solution)/shard_map/ppermute | solution.py:97
  413.0 43.8 %collective-permute-start.50 = (bf16[2,296,1536]{2,1,0:T(8,128)(2,1)}, bf16[2,296,1536]{2,1,0:T(8,128)(2,1)}, u32[]{:S(2)}, u32[]{:S(2)}) collective-permute-start(bf16[2,296,1536]{2,1,0:T(8,128)(2,1)} %add_convert_fusion.2), channel_id=1, source_target_pairs={{0,2},{1,3},{2,0},{3,1},{4,6},{5,7},{6,4},{7,5},{8,10},{9,11},{10,... | collective-permute-start | bytes 5455880 | tf_op jit(solution)/shard_map/ppermute | solution.py:21
  416.3 40.5 %collective-permute-start.48 = (bf16[2,192,1536]{2,1,0:T(8,128)(2,1)}, bf16[2,192,1536]{2,1,0:T(8,128)(2,1)S(1)}, u32[]{:S(2)}, u32[]{:S(2)}) collective-permute-start(bf16[2,192,1536]{2,1,0:T(8,128)(2,1)} %get-tuple-element.810), channel_id=1, source_target_pairs={{0,8},{8,16},{16,24},{24,28},{28,20},{20,12},{12,4},{4,0},{1,9},{9... | collective-permute-start | bytes 3538952 | tf_op jit(solution)/shard_map/ppermute | solution.py:94
  416.9 39.8 %collective-permute-start.49 = (bf16[2,192,1536]{2,1,0:T(8,128)(2,1)}, bf16[2,192,1536]{2,1,0:T(8,128)(2,1)}, u32[]{:S(2)}, u32[]{:S(2)}) collective-permute-start(bf16[2,192,1536]{2,1,0:T(8,128)(2,1)} %get-tuple-element.811), channel_id=1, source_target_pairs={{8,0},{16,8},{24,16},{28,24},{20,28},{12,20},{4,12},{0,4},{9,1},{1... | collective-permute-start | bytes 3538952 | tf_op jit(solution)/shard_map/ppermute | solution.py:97
  471.5 29.1 %collective-permute-start.51 = (bf16[2,192,1536]{2,1,0:T(8,128)(2,1)}, bf16[2,192,1536]{2,1,0:T(8,128)(2,1)S(1)}, u32[]{:S(2)}, u32[]{:S(2)}) collective-permute-start(bf16[2,192,1536]{2,1,0:T(8,128)(2,1)} %get-tuple-element.841), channel_id=1, source_target_pairs={{0,8},{8,16},{16,24},{24,28},{28,20},{20,12},{12,4},{4,0},{1,9},{9... | collective-permute-start | bytes 3538952 | tf_op jit(solution)/shard_map/ppermute | solution.py:94
  472.2 46.8 %collective-permute-start.55 = (bf16[2,296,1536]{2,1,0:T(8,128)(2,1)}, bf16[2,296,1536]{2,1,0:T(8,128)(2,1)}, u32[]{:S(2)}, u32[]{:S(2)}) collective-permute-start(bf16[2,296,1536]{2,1,0:T(8,128)(2,1)} %get-tuple-element.886.refs_0_.a), channel_id=1, source_target_pairs={{0,2},{1,3},{2,0},{3,1},{4,6},{5,7},{6,4},{7,5},{8,10},{9,11},{10,... | collective-permute-start | bytes 5455880 | tf_op jit(solution)/shard_map/ppermute | solution.py:21
  472.7 46.2 %collective-permute-start.56 = (bf16[2,296,1536]{2,1,0:T(8,128)(2,1)}, bf16[2,296,1536]{2,1,0:T(8,128)(2,1)}, u32[]{:S(2)}, u32[]{:S(2)}) collective-permute-start(bf16[2,296,1536]{2,1,0:T(8,128)(2,1)} %get-tuple-element.886.refs_0_.a), channel_id=1, source_target_pairs={{0,1},{1,0},{2,3},{3,2},{4,5},{5,4},{6,7},{7,6},{8,9},{9,8},{10,11... | collective-permute-start | bytes 5455880 | tf_op jit(solution)/shard_map/ppermute | solution.py:21
  472.7 30.4 %collective-permute-start.52 = (bf16[2,192,1536]{2,1,0:T(8,128)(2,1)}, bf16[2,192,1536]{2,1,0:T(8,128)(2,1)}, u32[]{:S(2)}, u32[]{:S(2)}) collective-permute-start(bf16[2,192,1536]{2,1,0:T(8,128)(2,1)} %get-tuple-element.842), channel_id=1, source_target_pairs={{8,0},{16,8},{24,16},{28,24},{20,28},{12,20},{4,12},{0,4},{9,1},{1... | collective-permute-start | bytes 3538952 | tf_op jit(solution)/shard_map/ppermute | solution.py:97
  474.1 37.4 %collective-permute-start.53 = (bf16[1,192,1536]{2,1,0:T(8,128)(2,1)}, bf16[1,192,1536]{2,1,0:T(8,128)(2,1)S(1)}, u32[]{:S(2)}, u32[]{:S(2)}) collective-permute-start(bf16[1,192,1536]{2,1,0:T(8,128)(2,1)} %get-tuple-element.849), channel_id=1, source_target_pairs={{0,8},{8,16},{16,24},{24,28},{28,20},{20,12},{12,4},{4,0},{1,9},{9... | collective-permute-start | bytes 1769480 | tf_op jit(solution)/shard_map/ppermute | solution.py:94
  532.6 50.0 %collective-permute-start.60 = (bf16[2,192,1536]{2,1,0:T(8,128)(2,1)}, bf16[2,192,1536]{2,1,0:T(8,128)(2,1)S(1)}, u32[]{:S(2)}, u32[]{:S(2)}) collective-permute-start(bf16[2,192,1536]{2,1,0:T(8,128)(2,1)} %get-tuple-element.904), channel_id=1, source_target_pairs={{0,8},{8,16},{16,24},{24,28},{28,20},{20,12},{12,4},{4,0},{1,9},{9... | collective-permute-start | bytes 3538952 | tf_op jit(solution)/shard_map/ppermute | solution.py:94
  533.0 49.6 %collective-permute-start.61 = (bf16[2,192,1536]{2,1,0:T(8,128)(2,1)}, bf16[2,192,1536]{2,1,0:T(8,128)(2,1)}, u32[]{:S(2)}, u32[]{:S(2)}) collective-permute-start(bf16[2,192,1536]{2,1,0:T(8,128)(2,1)} %get-tuple-element.905), channel_id=1, source_target_pairs={{8,0},{16,8},{24,16},{28,24},{20,28},{12,20},{4,12},{0,4},{9,1},{1... | collective-permute-start | bytes 3538952 | tf_op jit(solution)/shard_map/ppermute | solution.py:97
  534.6 51.6 %collective-permute-start.62 = (bf16[2,192,1536]{2,1,0:T(8,128)(2,1)}, bf16[2,192,1536]{2,1,0:T(8,128)(2,1)}, u32[]{:S(2)}, u32[]{:S(2)}) collective-permute-start(bf16[2,192,1536]{2,1,0:T(8,128)(2,1)} %get-tuple-element.907), channel_id=1, source_target_pairs={{0,8},{8,16},{16,24},{24,28},{28,20},{20,12},{12,4},{4,0},{1,9},{9... | collective-permute-start | bytes 3538952 | tf_op jit(solution)/shard_map/ppermute | solution.py:94
  537.3 49.1 %collective-permute-start.63 = (bf16[2,192,1536]{2,1,0:T(8,128)(2,1)}, bf16[2,192,1536]{2,1,0:T(8,128)(2,1)}, u32[]{:S(2)}, u32[]{:S(2)}) collective-permute-start(bf16[2,192,1536]{2,1,0:T(8,128)(2,1)} %get-tuple-element.908), channel_id=1, source_target_pairs={{8,0},{16,8},{24,16},{28,24},{20,28},{12,20},{4,12},{0,4},{9,1},{1... | collective-permute-start | bytes 3538952 | tf_op jit(solution)/shard_map/ppermute | solution.py:97
  551.5 71.5 %collective-permute-start.64 = (bf16[2,296,1536]{2,1,0:T(8,128)(2,1)}, bf16[2,296,1536]{2,1,0:T(8,128)(2,1)}, u32[]{:S(2)}, u32[]{:S(2)}) collective-permute-start(bf16[2,296,1536]{2,1,0:T(8,128)(2,1)} %add_convert_fusion.1), channel_id=1, source_target_pairs={{0,2},{1,3},{2,0},{3,1},{4,6},{5,7},{6,4},{7,5},{8,10},{9,11},{10,... | collective-permute-start | bytes 5455880 | tf_op jit(solution)/shard_map/ppermute | solution.py:21
  591.6 31.4 %collective-permute-start.65 = (bf16[2,192,1536]{2,1,0:T(8,128)(2,1)}, bf16[2,192,1536]{2,1,0:T(8,128)(2,1)S(1)}, u32[]{:S(2)}, u32[]{:S(2)}) collective-permute-start(bf16[2,192,1536]{2,1,0:T(8,128)(2,1)} %get-tuple-element.925), channel_id=1, source_target_pairs={{0,8},{8,16},{16,24},{24,28},{28,20},{20,12},{12,4},{4,0},{1,9},{9... | collective-permute-start | bytes 3538952 | tf_op jit(solution)/shard_map/ppermute | solution.py:94
  593.4 29.6 %collective-permute-start.66 = (bf16[2,192,1536]{2,1,0:T(8,128)(2,1)}, bf16[2,192,1536]{2,1,0:T(8,128)(2,1)}, u32[]{:S(2)}, u32[]{:S(2)}) collective-permute-start(bf16[2,192,1536]{2,1,0:T(8,128)(2,1)} %get-tuple-element.926), channel_id=1, source_target_pairs={{8,0},{16,8},{24,16},{28,24},{20,28},{12,20},{4,12},{0,4},{9,1},{1... | collective-permute-start | bytes 3538952 | tf_op jit(solution)/shard_map/ppermute | solution.py:97
  683.7 42.4 %collective-permute-start.75 = (bf16[2,296,1536]{2,1,0:T(8,128)(2,1)}, bf16[2,296,1536]{2,1,0:T(8,128)(2,1)}, u32[]{:S(2)}, u32[]{:S(2)}) collective-permute-start(bf16[2,296,1536]{2,1,0:T(8,128)(2,1)} %add_convert_fusion), channel_id=1, source_target_pairs={{0,2},{1,3},{2,0},{3,1},{4,6},{5,7},{6,4},{7,5},{8,10},{9,11},{10,... | collective-permute-start | bytes 5455880 | tf_op jit(solution)/shard_map/ppermute | solution.py:21
  685.2 28.3 %collective-permute-start.73 = (bf16[2,192,1536]{2,1,0:T(8,128)(2,1)}, bf16[2,192,1536]{2,1,0:T(8,128)(2,1)S(1)}, u32[]{:S(2)}, u32[]{:S(2)}) collective-permute-start(bf16[2,192,1536]{2,1,0:T(8,128)(2,1)} %get-tuple-element.1020), channel_id=1, source_target_pairs={{0,8},{8,16},{16,24},{24,28},{28,20},{20,12},{12,4},{4,0},{1,9},{9... | collective-permute-start | bytes 3538952 | tf_op jit(solution)/shard_map/ppermute | solution.py:94
  686.9 28.1 %collective-permute-start.74 = (bf16[2,192,1536]{2,1,0:T(8,128)(2,1)}, bf16[2,192,1536]{2,1,0:T(8,128)(2,1)}, u32[]{:S(2)}, u32[]{:S(2)}) collective-permute-start(bf16[2,192,1536]{2,1,0:T(8,128)(2,1)} %get-tuple-element.1021), channel_id=1, source_target_pairs={{8,0},{16,8},{24,16},{28,24},{20,28},{12,20},{4,12},{0,4},{9,1},{1... | collective-permute-start | bytes 3538952 | tf_op jit(solution)/shard_map/ppermute | solution.py:97
  (106 other events, 1706.3 us)

commit v9 on v7

--- a/solution.py
+++ b/solution.py
@@ -11,7 +11,7 @@
 PAIR = 2 * HEAD_DIM
 FACTOR = 1.0 / math.sqrt(HEAD_DIM)
 VMEM = 60 << 20
-FLOPS_PER_US = 460000000
+FLOPS_PER_US = 345000000
 EPSILON = 1e-06
 F32 = jnp.float32
 BF16 = jnp.bfloat16

time: 818 us -> 815 us (level)
  transfers between devices with their start and end apart: 92 -> 92, of which waited for: 45 -> 46; matrix products, arithmetic and copies ran while one was open for 6% -> 6% of each run, Pallas kernels for 45% -> 46%
where the time goes in v9:
time: 815 us; the launch traced here: 806 us
  Pallas kernels  414 us (51%)
  waiting for transfers between devices  230 us (28%)
  starting transfers between devices  90.2 us (11%)
  other arithmetic  28.6 us (4%)
  local copies, waits for them, and re-layouts  27 us (3%)
    ppermute x24, waiting for transfers between devices, forward(): return lax.ppermute(value, 'dp', self.ahead)  177 us
    pallas_call x8, Pallas kernels, rows_times(): kernel_call(kernel, 'rows_times', 1 + 3e-09 * 4 * slots * tokens * depth...  129 us
    pallas_call x4, Pallas kernels, weight_grad(): kernel_call(kernel, 'weight_grad', 1 + 3.4e-09 * 4 * slots * tokens * dep...  71.8 us
    pallas_call x2, Pallas kernels, attend_back(): kernel_call(kernel, 'attend_back', 29, (pairs,), [spec(0), spec(1), spec(...  59 us
    pallas_call x9, Pallas kernels, ring_add(): kernel_call(kernel, 'ring_add', 1 + 7e-06 * image.shape[1] * image.shape[...  46.4 us
    ppermute x44, starting transfers between devices, hop(): return lax.ppermute(value, axis, [(i, i ^ mask) for i in range(size)])  39.4 us
    pallas_call x5, Pallas kernels, per_slot(): kernel_call(kernel, name, 6, (slots,), [spec(value.shape, value.ndim == 2...  34 us
    ppermute x44, waiting for transfers between devices, hop(): return lax.ppermute(value, axis, [(i, i ^ mask) for i in range(size)])  33.8 us
  transfers between devices with their start and end apart: 92, of which 46 were waited for; matrix products, arithmetic and copies ran while one was open for 6% of the time, Pallas kernels for 46%

profile of v9, /device:TPU:0, one launch (start us, length us, event | category | flops | bytes accessed | tf_op | source)
XLA Modules:
  0.0 805.8 jit_solution(10305546632870279367)
XLA Ops:
  35.6 6.1 all_gather.3.refs_4_.refs_5_
  46.6 9.7 %collective-permute-done.8.refs_1_ = bf16[2,4,192,384]{3,2,1,0:T(8,128)(2,1)} collective-permute-done((bf16[2,4,192,384]{3,2,1,0:T(8,128)(2,1)S(1)}, bf16[2,4,192,384]{3,2,1,0:T(8,128)(2,1)}, u32[]{:S(2)}, u32[]{:S(2)}) %collective-permute-start.8) | collective-permute-done | bytes 1179680 | tf_op jit(solution)/shard_map/ppermute | solution.py:94
  63.6 22.2 %collective-permute-done.10.refs_3_ = bf16[2,4,192,384]{3,2,1,0:T(8,128)(2,1)S(1)} collective-permute-done((bf16[2,4,192,384]{3,2,1,0:T(8,128)(2,1)}, bf16[2,4,192,384]{3,2,1,0:T(8,128)(2,1)S(1)}, u32[]{:S(2)}, u32[]{:S(2)}) %collective-permute-start.10) | collective-permute-done | bytes 1179680 | tf_op jit(solution)/shard_map/ppermute | solution.py:94
  88.4 20.5 %collective-permute-done.12.refs_5_ = bf16[2,4,192,384]{3,2,1,0:T(8,128)(2,1)S(1)} collective-permute-done((bf16[2,4,192,384]{3,2,1,0:T(8,128)(2,1)S(1)}, bf16[2,4,192,384]{3,2,1,0:T(8,128)(2,1)S(1)}, u32[]{:S(2)}, u32[]{:S(2)}) %collective-permute-start.12) | collective-permute-done | bytes 1179680 | tf_op jit(solution)/shard_map/ppermute | solution.py:94
  115.7 7.9 assemble.5
  138.5 17.4 %rows_times.8.q.k.v = bf16[4,2,296,1152]{3,2,1,0:T(8,128)(2,1)} custom-call(bf16[2,296,1536]{2,1,0:T(8,128)(2,1)} %get-tuple-element.936.refs_0_.a, bf16[2,296,1536]{2,1,0:T(8,128)(2,1)} %collective-permute-done.15.refs_1_.b, bf16[2,296,1536]{2,1,0:T(8,128)(2,1)} %collective-permute-done.14.refs_2_.c, ...), custom_call_target="tpu_custom_call" | custom-call | flops 4681763328 | bytes 1 | tf_op jit(solution)/shard_map/rows_times/pallas_call | solution.py:406
  158.5 15.3 %attend.2 = (bf16[4,2,296,384]{3,2,1,0:T(8,128)(2,1)}, f32[2,3,2,1184]{3,2,1,0:T(2,128)}) custom-call(bf16[4,2,296,1152]{3,2,1,0:T(8,128)(2,1)} %rows_times.8.q.k.v, bf16[4,2,296,1152]{3,2,1,0:T(8,128)(2,1)} %rows_times.8.q.k.v, bf16[4,2,296,1152]{3,2,1,0:T(8,128)(2,1)} %rows_times.8.q.k.v), custom_call_target="tpu_custom_call" | custom-call | flops 5175000064 | bytes 1 | tf_op jit(solution)/shard_map/attend/pallas_call | solution.py:545
  173.8 15.3 %attend.3 = (bf16[4,2,296,384]{3,2,1,0:T(8,128)(2,1)}, f32[2,3,2,1184]{3,2,1,0:T(2,128)}) custom-call(bf16[4,2,296,1152]{3,2,1,0:T(8,128)(2,1)} %rows_times.8.q.k.v, bf16[4,2,296,1152]{3,2,1,0:T(8,128)(2,1)} %rows_times.8.q.k.v, bf16[4,2,296,1152]{3,2,1,0:T(8,128)(2,1)} %rows_times.8.q.k.v, ...), custom_call_target="tpu_custom_call", output_to_operand_aliasing={{0}: (3, {}), {1}: (4, {})} | custom-call | flops 5175000064 | bytes 1 | tf_op jit(solution)/shard_map/attend/pallas_call | solution.py:545
  189.2 8.5 %rows_times.9 = (bf16[2,296,1536]{2,1,0:T(8,128)(2,1)}, bf16[2,296,1536]{2,1,0:T(8,128)(2,1)}, bf16[2,296,1536]{2,1,0:T(8,128)(2,1)}, bf16[2,296,1536]{2,1,0:T(8,128)(2,1)}) custom-call(bf16[4,2,296,384]{3,2,1,0:T(8,128)(2,1)} %get-tuple-element.915.refs_0_.refs_1_.refs_2_.refs_3_.grad.mixed, ...), custom_call_target="tpu_custom_call" | custom-call | flops 1790587904 | bytes 1 | tf_op jit(solution)/shard_map/rows_times/pallas_call | solution.py:406
  205.4 21.5 %collective-permute-done.28.refs_5_ = bf16[2,1,192,1536]{3,2,1,0:T(8,128)(2,1)S(1)} collective-permute-done((bf16[2,1,192,1536]{3,2,1,0:T(8,128)(2,1)}, bf16[2,1,192,1536]{3,2,1,0:T(8,128)(2,1)S(1)}, u32[]{:S(2)}, u32[]{:S(2)}) %collective-permute-start.28) | collective-permute-done | bytes 1179680 | tf_op jit(solution)/shard_map/ppermute | solution.py:94
  229.7 12.2 %collective-permute-done.30.refs_7_ = bf16[1,1,192,1536]{3,2,1,0:T(8,128)(2,1)S(1)} collective-permute-done((bf16[1,1,192,1536]{3,2,1,0:T(8,128)(2,1)S(1)}, bf16[1,1,192,1536]{3,2,1,0:T(8,128)(2,1)S(1)}, u32[]{:S(2)}, u32[]{:S(2)}) %collective-permute-start.30) | collective-permute-done | bytes 589856 | tf_op jit(solution)/shard_map/ppermute | solution.py:94
  246.4 6.3 middle.1
  256.1 8.0 assemble.7
  264.0 6.1 collective-permute-done.33.refs_1_
  279.2 17.6 %collective-permute-done.35.refs_0_ = bf16[2,1,192,1536]{3,2,1,0:T(8,128)(2,1)S(1)} collective-permute-done((bf16[2,1,192,1536]{3,2,1,0:T(8,128)(2,1)}, bf16[2,1,192,1536]{3,2,1,0:T(8,128)(2,1)S(1)}, u32[]{:S(2)}, u32[]{:S(2)}) %collective-permute-start.35) | collective-permute-done | bytes 1179680 | tf_op jit(solution)/shard_map/ppermute | solution.py:94
  304.5 25.6 %rows_times.10 = (bf16[4,2,296,1536]{3,2,1,0:T(8,128)(2,1)}, bf16[4,2,296,1536]{3,2,1,0:T(8,128)(2,1)}) custom-call(bf16[2,296,1536]{2,1,0:T(8,128)(2,1)} %get-tuple-element.782.refs_0_.a, bf16[2,296,1536]{2,1,0:T(8,128)(2,1)} %collective-permute-done.38.refs_1_.b, bf16[2,296,1536]{2,1,0:T(8,128)(2,1)} %collective-permute-done.37.refs_2_.c, ...), custom_call_target="tpu_custom_call" | custom-call | flops 6127351296 | bytes 1 | tf_op jit(solution)/shard_map/rows_times/pallas_call | solution.py:406
  335.3 20.9 %weight_grad.4 = (bf16[8,192,1536]{2,1,0:T(8,128)(2,1)}, bf16[8,192,1536]{2,1,0:T(8,128)(2,1)}, bf16[1,192,1536]{2,1,0:T(8,128)(2,1)}, bf16[1,192,1536]{2,1,0:T(8,128)(2,1)}, f32[2,1536]{1,0:T(2,128)}) custom-call(s32[1]{0:T(128)} %dynamic-slice.4.far, bf16[2,296,1536]{2,1,0:T(8,128)(2,1)} %get-tuple-element.743.a.refs_0_, ...), custom_call_target="tpu_custom_call" | custom-call | flops 6898331648 | bytes 1 | tf_op jit(solution)/shard_map/weight_grad/pallas_call | solution.py:459
  363.8 18.5 %rows_times.11.refs_0_.refs_1_.refs_2_.refs_3_.grad = bf16[4,2,296,1536]{3,2,1,0:T(8,128)(2,1)} custom-call(bf16[2,296,1536]{2,1,0:T(8,128)(2,1)} %get-tuple-element.743.a.refs_0_, bf16[2,296,1536]{2,1,0:T(8,128)(2,1)} %collective-permute-done.24.b.refs_1_, bf16[2,296,1536]{2,1,0:T(8,128)(2,1)} %collective-permute-done.23.c.refs_2_, ...), custom_call_target="tpu_custom_call" | custom-call | flops 6127351296 | bytes 1 | tf_op jit(solution)/shard_map/rows_times/pallas_call | solution.py:406
  382.4 17.8 %rows_times.12 = (bf16[2,296,1536]{2,1,0:T(8,128)(2,1)}, bf16[2,296,1536]{2,1,0:T(8,128)(2,1)}, bf16[2,296,1536]{2,1,0:T(8,128)(2,1)}, bf16[2,296,1536]{2,1,0:T(8,128)(2,1)}) custom-call(bf16[4,2,296,1536]{3,2,1,0:T(8,128)(2,1)} %rows_times.11.refs_0_.refs_1_.refs_2_.refs_3_.grad, bf16[4,2,296,1536]{3,2,1,0:T(8,128)(2,1)} %rows_times.11.refs_0_.refs_1_.refs_2_.refs_3_.grad, ...), custom_call_target="tpu_custom_call" | custom-call | flops 6127351296 | bytes 1 | tf_op jit(solution)/shard_map/rows_times/pallas_call | solution.py:406
  416.1 20.8 %weight_grad.5 = (bf16[8,192,1536]{2,1,0:T(8,128)(2,1)}, bf16[8,192,1536]{2,1,0:T(8,128)(2,1)}, bf16[1,192,1536]{2,1,0:T(8,128)(2,1)}, bf16[1,192,1536]{2,1,0:T(8,128)(2,1)}, f32[2,1536]{1,0:T(2,128)}) custom-call(s32[1]{0:T(128)} %dynamic-slice.4.far, bf16[2,296,1536]{2,1,0:T(8,128)(2,1)} %get-tuple-element.782.refs_0_.a, ...), custom_call_target="tpu_custom_call" | custom-call | flops 6898331648 | bytes 1 | tf_op jit(solution)/shard_map/weight_grad/pallas_call | solution.py:459
  436.9 17.4 %rows_times.13 = (bf16[2,296,1536]{2,1,0:T(8,128)(2,1)}, bf16[2,296,1536]{2,1,0:T(8,128)(2,1)}, bf16[2,296,1536]{2,1,0:T(8,128)(2,1)}, bf16[2,296,1536]{2,1,0:T(8,128)(2,1)}) custom-call(bf16[4,2,296,1536]{3,2,1,0:T(8,128)(2,1)} %get-tuple-element.799.grad.refs_0_.refs_1_.refs_2_.refs_3_, ...), custom_call_target="tpu_custom_call" | custom-call | flops 6127351296 | bytes 1 | tf_op jit(solution)/shard_map/rows_times/pallas_call | solution.py:406
  454.4 9.5 %middle_back.1 = (f32[2,296,1536]{2,1,0:T(8,128)}, bf16[2,296,1536]{2,1,0:T(8,128)(2,1)}, f32[2,2,4,1536]{3,2,1,0:T(4,128)}) custom-call(s32[1]{0:T(128)} %copy.204.seqs, bf16[2,256,1536]{2,1,0:T(8,128)(2,1)} %refs_0_.3, bf16[2,40,1536]{2,1,0:T(8,128)(2,1)} %refs_1_.3, bf16[2,296,1536]{2,1,0:T(8,128)(2,1)} %get-tuple-element.820.refs_2_, ...), custom_call_target="tpu_custom_call" | custom-call | flops 2070000000 | bytes 1 | tf_op jit(solution)/shard_map/middle_back/pallas_call | solution.py:673
  472.9 25.4 %collective-permute-done.51.ahead = bf16[2,192,1536]{2,1,0:T(8,128)(2,1)S(1)} collective-permute-done((bf16[2,192,1536]{2,1,0:T(8,128)(2,1)}, bf16[2,192,1536]{2,1,0:T(8,128)(2,1)S(1)}, u32[]{:S(2)}, u32[]{:S(2)}) %collective-permute-start.51) | collective-permute-done | bytes 1179680 | tf_op jit(solution)/shard_map/ppermute | solution.py:94
  521.3 8.9 %rows_times.14.grads = bf16[4,2,296,384]{3,2,1,0:T(8,128)(2,1)} custom-call(bf16[2,296,1536]{2,1,0:T(8,128)(2,1)} %get-tuple-element.883.refs_0_.a, bf16[2,296,1536]{2,1,0:T(8,128)(2,1)} %collective-permute-done.56.refs_1_.b, bf16[2,296,1536]{2,1,0:T(8,128)(2,1)} %collective-permute-done.55.refs_2_.c, ...), custom_call_target="tpu_custom_call" | custom-call | flops 1790587904 | bytes 1 | tf_op jit(solution)/shard_map/rows_times/pallas_call | solution.py:406
  539.6 9.6 %weight_grad.6 = (bf16[8,192,1536]{2,1,0:T(8,128)(2,1)}, bf16[8,192,1536]{2,1,0:T(8,128)(2,1)}, bf16[1,192,1536]{2,1,0:T(8,128)(2,1)}, bf16[1,192,1536]{2,1,0:T(8,128)(2,1)}, f32[2,384]{1,0:T(2,128)}) custom-call(s32[1]{0:T(128)} %dynamic-slice.4.far, bf16[2,296,1536]{2,1,0:T(8,128)(2,1)} %get-tuple-element.883.refs_0_.a, ...), custom_call_target="tpu_custom_call" | custom-call | flops 1983332864 | bytes 1 | tf_op jit(solution)/shard_map/weight_grad/pallas_call | solution.py:459
  550.6 29.6 %attend_back.2.refs_0_ = bf16[4,2,296,1152]{3,2,1,0:T(8,128)(2,1)} custom-call(bf16[4,2,296,1152]{3,2,1,0:T(8,128)(2,1)} %rows_times.8.q.k.v, bf16[4,2,296,1152]{3,2,1,0:T(8,128)(2,1)} %rows_times.8.q.k.v, bf16[4,2,296,1152]{3,2,1,0:T(8,128)(2,1)} %rows_times.8.q.k.v, bf16[4,2,296,384]{3,2,1,0:T(8,128)(2,1)} %get-tuple-element.915.refs_0_.refs_1_.refs_2_.refs_3_.grad.mixed, ...), custom_call_target="tpu_custom_call" | custom-call | flops 10005000192 | bytes 1 | tf_op jit(solution)/shard_map/attend_back/pallas_call | solution.py:619
  591.8 29.4 %attend_back.3.grad.refs_0_.refs_1_.refs_2_.refs_3_ = bf16[4,2,296,1152]{3,2,1,0:T(8,128)(2,1)} custom-call(bf16[4,2,296,1152]{3,2,1,0:T(8,128)(2,1)} %rows_times.8.q.k.v, bf16[4,2,296,1152]{3,2,1,0:T(8,128)(2,1)} %rows_times.8.q.k.v, bf16[4,2,296,1152]{3,2,1,0:T(8,128)(2,1)} %rows_times.8.q.k.v, ...), custom_call_target="tpu_custom_call", output_to_operand_aliasing={{}: (6, {})} | custom-call | flops 10005000192 | bytes 1 | tf_op jit(solution)/shard_map/attend_back/pallas_call | solution.py:619
  629.4 20.4 %weight_grad.7 = (bf16[8,192,1536]{2,1,0:T(8,128)(2,1)}, bf16[8,192,1536]{2,1,0:T(8,128)(2,1)}, bf16[1,192,1536]{2,1,0:T(8,128)(2,1)}, bf16[1,192,1536]{2,1,0:T(8,128)(2,1)}, f32[2,1152]{1,0:T(2,128)}) custom-call(s32[1]{0:T(128)} %dynamic-slice.4.far, ...), custom_call_target="tpu_custom_call", output_to_operand_aliasing={{0}: (6, {}), {1}: (7, {}), {2}: (8, {}), {3}: (9, {})} | custom-call | flops 5259998720 | bytes 1 | tf_op jit(solution)/shard_map/weight_grad/pallas_call | solution.py:459
  656.8 14.7 %rows_times.15 = (bf16[2,296,1536]{2,1,0:T(8,128)(2,1)}, bf16[2,296,1536]{2,1,0:T(8,128)(2,1)}, bf16[2,296,1536]{2,1,0:T(8,128)(2,1)}, bf16[2,296,1536]{2,1,0:T(8,128)(2,1)}) custom-call(bf16[4,2,296,1152]{3,2,1,0:T(8,128)(2,1)} %attend_back.3.grad.refs_0_.refs_1_.refs_2_.refs_3_, bf16[4,2,296,1152]{3,2,1,0:T(8,128)(2,1)} %attend_back.3.grad.refs_0_.refs_1_.refs_2_.refs_3_, ...), custom_call_target="tpu_custom_call" | custom-call | flops 4681763328 | bytes 1 | tf_op jit(solution)/shard_map/rows_times/pallas_call | solution.py:406
  723.4 7.4 enter_back.1
  737.8 7.1 collective-permute-done.78.ahead
  774.1 14.0 %collective-permute-done.86.ahead = bf16[2,192,1536]{2,1,0:T(8,128)(2,1)S(1)} collective-permute-done((bf16[2,192,1536]{2,1,0:T(8,128)(2,1)}, bf16[2,192,1536]{2,1,0:T(8,128)(2,1)S(1)}, u32[]{:S(2)}, u32[]{:S(2)}) %collective-permute-start.86) | collective-permute-done | bytes 1179680 | tf_op jit(solution)/shard_map/ppermute | solution.py:94
  (437 shorter events, 308.5 us)
Async XLA Ops:
  62.1 48.0 %collective-permute-start.14 = (bf16[2,296,1536]{2,1,0:T(8,128)(2,1)}, bf16[2,296,1536]{2,1,0:T(8,128)(2,1)}, u32[]{:S(2)}, u32[]{:S(2)}) collective-permute-start(bf16[2,296,1536]{2,1,0:T(8,128)(2,1)} %get-tuple-element.936.refs_0_.a), channel_id=1, source_target_pairs={{0,2},{1,3},{2,0},{3,1},{4,6},{5,7},{6,4},{7,5},{8,10},{9,11},{10,... | collective-permute-start | bytes 5455880 | tf_op jit(solution)/shard_map/ppermute | solution.py:21
  63.6 46.5 %collective-permute-start.15 = (bf16[2,296,1536]{2,1,0:T(8,128)(2,1)}, bf16[2,296,1536]{2,1,0:T(8,128)(2,1)}, u32[]{:S(2)}, u32[]{:S(2)}) collective-permute-start(bf16[2,296,1536]{2,1,0:T(8,128)(2,1)} %get-tuple-element.936.refs_0_.a), channel_id=1, source_target_pairs={{0,1},{1,0},{2,3},{3,2},{4,5},{5,4},{6,7},{7,6},{8,9},{9,8},{10,11... | collective-permute-start | bytes 5455880 | tf_op jit(solution)/shard_map/ppermute | solution.py:21
  128.8 27.5 %collective-permute-start.19 = (bf16[2,1,192,1536]{3,2,1,0:T(8,128)(2,1)}, bf16[2,1,192,1536]{3,2,1,0:T(8,128)(2,1)S(1)}, u32[]{:S(2)}, u32[]{:S(2)}) collective-permute-start(bf16[2,1,192,1536]{3,2,1,0:T(8,128)(2,1)} %bitcast.168), channel_id=1, source_target_pairs={{0,8},{8,16},{16,24},{24,28},{28,20},{20,12},{12,4},{4,0},{1,9},{9... | collective-permute-start | bytes 3538952 | tf_op jit(solution)/shard_map/ppermute | solution.py:94
  133.4 55.7 %collective-permute-start.23 = (bf16[2,296,1536]{2,1,0:T(8,128)(2,1)}, bf16[2,296,1536]{2,1,0:T(8,128)(2,1)}, u32[]{:S(2)}, u32[]{:S(2)}) collective-permute-start(bf16[2,296,1536]{2,1,0:T(8,128)(2,1)} %get-tuple-element.743.a.refs_0_), channel_id=1, source_target_pairs={{0,2},{1,3},{2,0},{3,1},{4,6},{5,7},{6,4},{7,5},{8,10},{9,11},{10,... | collective-permute-start | bytes 5455880 | tf_op jit(solution)/shard_map/ppermute | solution.py:21
  134.9 54.2 %collective-permute-start.24 = (bf16[2,296,1536]{2,1,0:T(8,128)(2,1)}, bf16[2,296,1536]{2,1,0:T(8,128)(2,1)}, u32[]{:S(2)}, u32[]{:S(2)}) collective-permute-start(bf16[2,296,1536]{2,1,0:T(8,128)(2,1)} %get-tuple-element.743.a.refs_0_), channel_id=1, source_target_pairs={{0,1},{1,0},{2,3},{3,2},{4,5},{5,4},{6,7},{7,6},{8,9},{9,8},{10,11... | collective-permute-start | bytes 5455880 | tf_op jit(solution)/shard_map/ppermute | solution.py:21
  156.3 32.8 %collective-permute-start.21 = (bf16[2,1,192,1536]{3,2,1,0:T(8,128)(2,1)S(1)}, bf16[2,1,192,1536]{3,2,1,0:T(8,128)(2,1)}, u32[]{:S(2)}, u32[]{:S(2)}) collective-permute-start(bf16[2,1,192,1536]{3,2,1,0:T(8,128)(2,1)S(1)} %collective-permute-done.19.refs_1_), channel_id=1, source_target_pairs={{0,8},{8,16},{16,24},{24,28},{28,20},{20,12},{12,4},{4,0},{1,9},{9... | collective-permute-start | bytes 3538952 | tf_op jit(solution)/shard_map/ppermute | solution.py:94
  157.0 32.2 %collective-permute-start.22 = (bf16[2,1,192,1536]{3,2,1,0:T(8,128)(2,1)}, bf16[2,1,192,1536]{3,2,1,0:T(8,128)(2,1)}, u32[]{:S(2)}, u32[]{:S(2)}) collective-permute-start(bf16[2,1,192,1536]{3,2,1,0:T(8,128)(2,1)} %collective-permute-done.20.refs_2_), channel_id=1, source_target_pairs={{8,0},{16,8},{24,16},{28,24},{20,28},{12,20},{4,12},{0,4},{9,1},{1... | collective-permute-start | bytes 3538952 | tf_op jit(solution)/shard_map/ppermute | solution.py:97
  198.3 28.5 %collective-permute-start.28 = (bf16[2,1,192,1536]{3,2,1,0:T(8,128)(2,1)}, bf16[2,1,192,1536]{3,2,1,0:T(8,128)(2,1)S(1)}, u32[]{:S(2)}, u32[]{:S(2)}) collective-permute-start(bf16[2,1,192,1536]{3,2,1,0:T(8,128)(2,1)} %collective-permute-done.21.refs_3_), channel_id=1, source_target_pairs={{0,8},{8,16},{16,24},{24,28},{28,20},{20,12},{12,4},{4,0},{1,9},{9... | collective-permute-start | bytes 3538952 | tf_op jit(solution)/shard_map/ppermute | solution.py:94
  198.9 28.2 %collective-permute-start.29 = (bf16[2,1,192,1536]{3,2,1,0:T(8,128)(2,1)}, bf16[2,1,192,1536]{3,2,1,0:T(8,128)(2,1)S(1)}, u32[]{:S(2)}, u32[]{:S(2)}) collective-permute-start(bf16[2,1,192,1536]{3,2,1,0:T(8,128)(2,1)} %collective-permute-done.22.refs_4_), channel_id=1, source_target_pairs={{8,0},{16,8},{24,16},{28,24},{20,28},{12,20},{4,12},{0,4},{9,1},{1... | collective-permute-start | bytes 3538952 | tf_op jit(solution)/shard_map/ppermute | solution.py:97
  203.8 42.6 %collective-permute-start.32 = (bf16[2,296,1536]{2,1,0:T(8,128)(2,1)S(1)}, bf16[2,296,1536]{2,1,0:T(8,128)(2,1)}, u32[]{:S(2)}, u32[]{:S(2)}) collective-permute-start(bf16[2,296,1536]{2,1,0:T(8,128)(2,1)S(1)} %add_convert_fusion.3), channel_id=1, source_target_pairs={{0,2},{1,3},{2,0},{3,1},{4,6},{5,7},{6,4},{7,5},{8,10},{9,11},{10,... | collective-permute-start | bytes 5455880 | tf_op jit(solution)/shard_map/ppermute | solution.py:21
  252.6 45.3 %collective-permute-start.37 = (bf16[2,296,1536]{2,1,0:T(8,128)(2,1)}, bf16[2,296,1536]{2,1,0:T(8,128)(2,1)}, u32[]{:S(2)}, u32[]{:S(2)}) collective-permute-start(bf16[2,296,1536]{2,1,0:T(8,128)(2,1)} %get-tuple-element.782.refs_0_.a), channel_id=1, source_target_pairs={{0,2},{1,3},{2,0},{3,1},{4,6},{5,7},{6,4},{7,5},{8,10},{9,11},{10,... | collective-permute-start | bytes 5455880 | tf_op jit(solution)/shard_map/ppermute | solution.py:21
  254.2 43.7 %collective-permute-start.38 = (bf16[2,296,1536]{2,1,0:T(8,128)(2,1)}, bf16[2,296,1536]{2,1,0:T(8,128)(2,1)}, u32[]{:S(2)}, u32[]{:S(2)}) collective-permute-start(bf16[2,296,1536]{2,1,0:T(8,128)(2,1)} %get-tuple-element.782.refs_0_.a), channel_id=1, source_target_pairs={{0,1},{1,0},{2,3},{3,2},{4,5},{5,4},{6,7},{7,6},{8,9},{9,8},{10,11... | collective-permute-start | bytes 5455880 | tf_op jit(solution)/shard_map/ppermute | solution.py:21
  298.0 32.1 %collective-permute-start.40 = (bf16[2,1,192,1536]{3,2,1,0:T(8,128)(2,1)}, bf16[2,1,192,1536]{3,2,1,0:T(8,128)(2,1)S(1)}, u32[]{:S(2)}, u32[]{:S(2)}) collective-permute-start(bf16[2,1,192,1536]{3,2,1,0:T(8,128)(2,1)} %copy-done.11), channel_id=1, source_target_pairs={{0,8},{8,16},{16,24},{24,28},{28,20},{20,12},{12,4},{4,0},{1,9},{9... | collective-permute-start | bytes 3538952 | tf_op jit(solution)/shard_map/ppermute | solution.py:94
  299.1 31.0 %collective-permute-start.41 = (bf16[2,1,192,1536]{3,2,1,0:T(8,128)(2,1)}, bf16[2,1,192,1536]{3,2,1,0:T(8,128)(2,1)}, u32[]{:S(2)}, u32[]{:S(2)}) collective-permute-start(bf16[2,1,192,1536]{3,2,1,0:T(8,128)(2,1)} %collective-permute-done.36.refs_1_), channel_id=1, source_target_pairs={{8,0},{16,8},{24,16},{28,24},{20,28},{12,20},{4,12},{0,4},{9,1},{1... | collective-permute-start | bytes 3538952 | tf_op jit(solution)/shard_map/ppermute | solution.py:97
  410.7 43.7 %collective-permute-start.50 = (bf16[2,296,1536]{2,1,0:T(8,128)(2,1)}, bf16[2,296,1536]{2,1,0:T(8,128)(2,1)}, u32[]{:S(2)}, u32[]{:S(2)}) collective-permute-start(bf16[2,296,1536]{2,1,0:T(8,128)(2,1)} %add_convert_fusion.2), channel_id=1, source_target_pairs={{0,2},{1,3},{2,0},{3,1},{4,6},{5,7},{6,4},{7,5},{8,10},{9,11},{10,... | collective-permute-start | bytes 5455880 | tf_op jit(solution)/shard_map/ppermute | solution.py:21
  413.9 40.4 %collective-permute-start.48 = (bf16[2,192,1536]{2,1,0:T(8,128)(2,1)}, bf16[2,192,1536]{2,1,0:T(8,128)(2,1)S(1)}, u32[]{:S(2)}, u32[]{:S(2)}) collective-permute-start(bf16[2,192,1536]{2,1,0:T(8,128)(2,1)} %get-tuple-element.807), channel_id=1, source_target_pairs={{0,8},{8,16},{16,24},{24,28},{28,20},{20,12},{12,4},{4,0},{1,9},{9... | collective-permute-start | bytes 3538952 | tf_op jit(solution)/shard_map/ppermute | solution.py:94
  415.0 39.3 %collective-permute-start.49 = (bf16[2,192,1536]{2,1,0:T(8,128)(2,1)}, bf16[2,192,1536]{2,1,0:T(8,128)(2,1)}, u32[]{:S(2)}, u32[]{:S(2)}) collective-permute-start(bf16[2,192,1536]{2,1,0:T(8,128)(2,1)} %get-tuple-element.808), channel_id=1, source_target_pairs={{8,0},{16,8},{24,16},{28,24},{20,28},{12,20},{4,12},{0,4},{9,1},{1... | collective-permute-start | bytes 3538952 | tf_op jit(solution)/shard_map/ppermute | solution.py:97
  469.1 29.1 %collective-permute-start.51 = (bf16[2,192,1536]{2,1,0:T(8,128)(2,1)}, bf16[2,192,1536]{2,1,0:T(8,128)(2,1)S(1)}, u32[]{:S(2)}, u32[]{:S(2)}) collective-permute-start(bf16[2,192,1536]{2,1,0:T(8,128)(2,1)} %get-tuple-element.838), channel_id=1, source_target_pairs={{0,8},{8,16},{16,24},{24,28},{28,20},{20,12},{12,4},{4,0},{1,9},{9... | collective-permute-start | bytes 3538952 | tf_op jit(solution)/shard_map/ppermute | solution.py:94
  470.2 46.9 %collective-permute-start.55 = (bf16[2,296,1536]{2,1,0:T(8,128)(2,1)}, bf16[2,296,1536]{2,1,0:T(8,128)(2,1)}, u32[]{:S(2)}, u32[]{:S(2)}) collective-permute-start(bf16[2,296,1536]{2,1,0:T(8,128)(2,1)} %get-tuple-element.883.refs_0_.a), channel_id=1, source_target_pairs={{0,2},{1,3},{2,0},{3,1},{4,6},{5,7},{6,4},{7,5},{8,10},{9,11},{10,... | collective-permute-start | bytes 5455880 | tf_op jit(solution)/shard_map/ppermute | solution.py:21
  470.9 46.2 %collective-permute-start.56 = (bf16[2,296,1536]{2,1,0:T(8,128)(2,1)}, bf16[2,296,1536]{2,1,0:T(8,128)(2,1)}, u32[]{:S(2)}, u32[]{:S(2)}) collective-permute-start(bf16[2,296,1536]{2,1,0:T(8,128)(2,1)} %get-tuple-element.883.refs_0_.a), channel_id=1, source_target_pairs={{0,1},{1,0},{2,3},{3,2},{4,5},{5,4},{6,7},{7,6},{8,9},{9,8},{10,11... | collective-permute-start | bytes 5455880 | tf_op jit(solution)/shard_map/ppermute | solution.py:21
  470.9 29.7 %collective-permute-start.52 = (bf16[2,192,1536]{2,1,0:T(8,128)(2,1)}, bf16[2,192,1536]{2,1,0:T(8,128)(2,1)}, u32[]{:S(2)}, u32[]{:S(2)}) collective-permute-start(bf16[2,192,1536]{2,1,0:T(8,128)(2,1)} %get-tuple-element.839), channel_id=1, source_target_pairs={{8,0},{16,8},{24,16},{28,24},{20,28},{12,20},{4,12},{0,4},{9,1},{1... | collective-permute-start | bytes 3538952 | tf_op jit(solution)/shard_map/ppermute | solution.py:97
  471.8 37.3 %collective-permute-start.53 = (bf16[1,192,1536]{2,1,0:T(8,128)(2,1)}, bf16[1,192,1536]{2,1,0:T(8,128)(2,1)S(1)}, u32[]{:S(2)}, u32[]{:S(2)}) collective-permute-start(bf16[1,192,1536]{2,1,0:T(8,128)(2,1)} %get-tuple-element.846), channel_id=1, source_target_pairs={{0,8},{8,16},{16,24},{24,28},{28,20},{20,12},{12,4},{4,0},{1,9},{9... | collective-permute-start | bytes 1769480 | tf_op jit(solution)/shard_map/ppermute | solution.py:94
  530.7 49.5 %collective-permute-start.60 = (bf16[2,192,1536]{2,1,0:T(8,128)(2,1)}, bf16[2,192,1536]{2,1,0:T(8,128)(2,1)S(1)}, u32[]{:S(2)}, u32[]{:S(2)}) collective-permute-start(bf16[2,192,1536]{2,1,0:T(8,128)(2,1)} %get-tuple-element.901), channel_id=1, source_target_pairs={{0,8},{8,16},{16,24},{24,28},{28,20},{20,12},{12,4},{4,0},{1,9},{9... | collective-permute-start | bytes 3538952 | tf_op jit(solution)/shard_map/ppermute | solution.py:94
  531.1 49.1 %collective-permute-start.61 = (bf16[2,192,1536]{2,1,0:T(8,128)(2,1)}, bf16[2,192,1536]{2,1,0:T(8,128)(2,1)}, u32[]{:S(2)}, u32[]{:S(2)}) collective-permute-start(bf16[2,192,1536]{2,1,0:T(8,128)(2,1)} %get-tuple-element.902), channel_id=1, source_target_pairs={{8,0},{16,8},{24,16},{28,24},{20,28},{12,20},{4,12},{0,4},{9,1},{1... | collective-permute-start | bytes 3538952 | tf_op jit(solution)/shard_map/ppermute | solution.py:97
  532.8 51.6 %collective-permute-start.62 = (bf16[2,192,1536]{2,1,0:T(8,128)(2,1)}, bf16[2,192,1536]{2,1,0:T(8,128)(2,1)}, u32[]{:S(2)}, u32[]{:S(2)}) collective-permute-start(bf16[2,192,1536]{2,1,0:T(8,128)(2,1)} %get-tuple-element.904), channel_id=1, source_target_pairs={{0,8},{8,16},{16,24},{24,28},{28,20},{20,12},{12,4},{4,0},{1,9},{9... | collective-permute-start | bytes 3538952 | tf_op jit(solution)/shard_map/ppermute | solution.py:94
  535.4 49.0 %collective-permute-start.63 = (bf16[2,192,1536]{2,1,0:T(8,128)(2,1)}, bf16[2,192,1536]{2,1,0:T(8,128)(2,1)}, u32[]{:S(2)}, u32[]{:S(2)}) collective-permute-start(bf16[2,192,1536]{2,1,0:T(8,128)(2,1)} %get-tuple-element.905), channel_id=1, source_target_pairs={{8,0},{16,8},{24,16},{28,24},{20,28},{12,20},{4,12},{0,4},{9,1},{1... | collective-permute-start | bytes 3538952 | tf_op jit(solution)/shard_map/ppermute | solution.py:97
  549.2 71.9 %collective-permute-start.64 = (bf16[2,296,1536]{2,1,0:T(8,128)(2,1)}, bf16[2,296,1536]{2,1,0:T(8,128)(2,1)}, u32[]{:S(2)}, u32[]{:S(2)}) collective-permute-start(bf16[2,296,1536]{2,1,0:T(8,128)(2,1)} %add_convert_fusion.1), channel_id=1, source_target_pairs={{0,2},{1,3},{2,0},{3,1},{4,6},{5,7},{6,4},{7,5},{8,10},{9,11},{10,... | collective-permute-start | bytes 5455880 | tf_op jit(solution)/shard_map/ppermute | solution.py:21
  589.7 31.4 %collective-permute-start.65 = (bf16[2,192,1536]{2,1,0:T(8,128)(2,1)}, bf16[2,192,1536]{2,1,0:T(8,128)(2,1)S(1)}, u32[]{:S(2)}, u32[]{:S(2)}) collective-permute-start(bf16[2,192,1536]{2,1,0:T(8,128)(2,1)} %get-tuple-element.922), channel_id=1, source_target_pairs={{0,8},{8,16},{16,24},{24,28},{28,20},{20,12},{12,4},{4,0},{1,9},{9... | collective-permute-start | bytes 3538952 | tf_op jit(solution)/shard_map/ppermute | solution.py:94
  590.7 30.4 %collective-permute-start.66 = (bf16[2,192,1536]{2,1,0:T(8,128)(2,1)}, bf16[2,192,1536]{2,1,0:T(8,128)(2,1)}, u32[]{:S(2)}, u32[]{:S(2)}) collective-permute-start(bf16[2,192,1536]{2,1,0:T(8,128)(2,1)} %get-tuple-element.923), channel_id=1, source_target_pairs={{8,0},{16,8},{24,16},{28,24},{20,28},{12,20},{4,12},{0,4},{9,1},{1... | collective-permute-start | bytes 3538952 | tf_op jit(solution)/shard_map/ppermute | solution.py:97
  681.1 42.4 %collective-permute-start.75 = (bf16[2,296,1536]{2,1,0:T(8,128)(2,1)}, bf16[2,296,1536]{2,1,0:T(8,128)(2,1)}, u32[]{:S(2)}, u32[]{:S(2)}) collective-permute-start(bf16[2,296,1536]{2,1,0:T(8,128)(2,1)} %add_convert_fusion), channel_id=1, source_target_pairs={{0,2},{1,3},{2,0},{3,1},{4,6},{5,7},{6,4},{7,5},{8,10},{9,11},{10,... | collective-permute-start | bytes 5455880 | tf_op jit(solution)/shard_map/ppermute | solution.py:21
  682.6 28.3 %collective-permute-start.73 = (bf16[2,192,1536]{2,1,0:T(8,128)(2,1)}, bf16[2,192,1536]{2,1,0:T(8,128)(2,1)S(1)}, u32[]{:S(2)}, u32[]{:S(2)}) collective-permute-start(bf16[2,192,1536]{2,1,0:T(8,128)(2,1)} %get-tuple-element.1017), channel_id=1, source_target_pairs={{0,8},{8,16},{16,24},{24,28},{28,20},{20,12},{12,4},{4,0},{1,9},{9... | collective-permute-start | bytes 3538952 | tf_op jit(solution)/shard_map/ppermute | solution.py:94
  684.3 28.1 %collective-permute-start.74 = (bf16[2,192,1536]{2,1,0:T(8,128)(2,1)}, bf16[2,192,1536]{2,1,0:T(8,128)(2,1)}, u32[]{:S(2)}, u32[]{:S(2)}) collective-permute-start(bf16[2,192,1536]{2,1,0:T(8,128)(2,1)} %get-tuple-element.1018), channel_id=1, source_target_pairs={{8,0},{16,8},{24,16},{28,24},{20,28},{12,20},{4,12},{0,4},{9,1},{1... | collective-permute-start | bytes 3538952 | tf_op jit(solution)/shard_map/ppermute | solution.py:97
  (107 other events, 1640.4 us)

commit v10 on v9

--- a/solution.py
+++ b/solution.py
@@ -11,7 +11,7 @@
 PAIR = 2 * HEAD_DIM
 FACTOR = 1.0 / math.sqrt(HEAD_DIM)
 VMEM = 60 << 20
-FLOPS_PER_US = 345000000
+FLOPS_PER_US = 253000000
 EPSILON = 1e-06
 F32 = jnp.float32
 BF16 = jnp.bfloat16

time: 815 us -> 816 us (level)
  no operation moved by 1% of the time
where the time goes in v10:
time: 816 us; the launch traced here: 807 us
  Pallas kernels  414 us (51%)
  waiting for transfers between devices  231 us (28%)
  starting transfers between devices  90.1 us (11%)
  other arithmetic  28.6 us (4%)
  local copies, waits for them, and re-layouts  27 us (3%)
    ppermute x24, waiting for transfers between devices, forward(): return lax.ppermute(value, 'dp', self.ahead)  178 us
    pallas_call x8, Pallas kernels, rows_times(): kernel_call(kernel, 'rows_times', 1 + 3e-09 * 4 * slots * tokens * depth...  129 us
    pallas_call x4, Pallas kernels, weight_grad(): kernel_call(kernel, 'weight_grad', 1 + 3.4e-09 * 4 * slots * tokens * dep...  71.8 us
    pallas_call x2, Pallas kernels, attend_back(): kernel_call(kernel, 'attend_back', 29, (pairs,), [spec(0), spec(1), spec(...  59 us
    pallas_call x9, Pallas kernels, ring_add(): kernel_call(kernel, 'ring_add', 1 + 7e-06 * image.shape[1] * image.shape[...  46.4 us
    ppermute x44, starting transfers between devices, hop(): return lax.ppermute(value, axis, [(i, i ^ mask) for i in range(size)])  39.2 us
    ppermute x44, waiting for transfers between devices, hop(): return lax.ppermute(value, axis, [(i, i ^ mask) for i in range(size)])  34.7 us
    pallas_call x5, Pallas kernels, per_slot(): kernel_call(kernel, name, 6, (slots,), [spec(value.shape, value.ndim == 2...  34 us
  transfers between devices with their start and end apart: 92, of which 46 were waited for; matrix products, arithmetic and copies ran while one was open for 6% of the time, Pallas kernels for 46%

profile of v10, /device:TPU:0, one launch (start us, length us, event | category | flops | bytes accessed | tf_op | source)
XLA Modules:
  0.0 806.5 jit_solution(13299809932643401538)
XLA Ops:
  35.6 6.1 all_gather.3.refs_4_.refs_5_
  46.6 9.7 %collective-permute-done.8.refs_1_ = bf16[2,4,192,384]{3,2,1,0:T(8,128)(2,1)} collective-permute-done((bf16[2,4,192,384]{3,2,1,0:T(8,128)(2,1)S(1)}, bf16[2,4,192,384]{3,2,1,0:T(8,128)(2,1)}, u32[]{:S(2)}, u32[]{:S(2)}) %collective-permute-start.8) | collective-permute-done | bytes 1179680 | tf_op jit(solution)/shard_map/ppermute | solution.py:94
  63.6 22.2 %collective-permute-done.10.refs_3_ = bf16[2,4,192,384]{3,2,1,0:T(8,128)(2,1)S(1)} collective-permute-done((bf16[2,4,192,384]{3,2,1,0:T(8,128)(2,1)}, bf16[2,4,192,384]{3,2,1,0:T(8,128)(2,1)S(1)}, u32[]{:S(2)}, u32[]{:S(2)}) %collective-permute-start.10) | collective-permute-done | bytes 1179680 | tf_op jit(solution)/shard_map/ppermute | solution.py:94
  88.4 20.5 %collective-permute-done.12.refs_5_ = bf16[2,4,192,384]{3,2,1,0:T(8,128)(2,1)S(1)} collective-permute-done((bf16[2,4,192,384]{3,2,1,0:T(8,128)(2,1)S(1)}, bf16[2,4,192,384]{3,2,1,0:T(8,128)(2,1)S(1)}, u32[]{:S(2)}, u32[]{:S(2)}) %collective-permute-start.12) | collective-permute-done | bytes 1179680 | tf_op jit(solution)/shard_map/ppermute | solution.py:94
  115.7 7.9 assemble.5
  138.5 17.4 %rows_times.8.q.k.v = bf16[4,2,296,1152]{3,2,1,0:T(8,128)(2,1)} custom-call(bf16[2,296,1536]{2,1,0:T(8,128)(2,1)} %get-tuple-element.936.refs_0_.a, bf16[2,296,1536]{2,1,0:T(8,128)(2,1)} %collective-permute-done.15.refs_1_.b, bf16[2,296,1536]{2,1,0:T(8,128)(2,1)} %collective-permute-done.14.refs_2_.c, ...), custom_call_target="tpu_custom_call" | custom-call | flops 3433293312 | bytes 1 | tf_op jit(solution)/shard_map/rows_times/pallas_call | solution.py:406
  158.5 15.3 %attend.2 = (bf16[4,2,296,384]{3,2,1,0:T(8,128)(2,1)}, f32[2,3,2,1184]{3,2,1,0:T(2,128)}) custom-call(bf16[4,2,296,1152]{3,2,1,0:T(8,128)(2,1)} %rows_times.8.q.k.v, bf16[4,2,296,1152]{3,2,1,0:T(8,128)(2,1)} %rows_times.8.q.k.v, bf16[4,2,296,1152]{3,2,1,0:T(8,128)(2,1)} %rows_times.8.q.k.v), custom_call_target="tpu_custom_call" | custom-call | flops 3795000064 | bytes 1 | tf_op jit(solution)/shard_map/attend/pallas_call | solution.py:545
  173.8 15.3 %attend.3 = (bf16[4,2,296,384]{3,2,1,0:T(8,128)(2,1)}, f32[2,3,2,1184]{3,2,1,0:T(2,128)}) custom-call(bf16[4,2,296,1152]{3,2,1,0:T(8,128)(2,1)} %rows_times.8.q.k.v, bf16[4,2,296,1152]{3,2,1,0:T(8,128)(2,1)} %rows_times.8.q.k.v, bf16[4,2,296,1152]{3,2,1,0:T(8,128)(2,1)} %rows_times.8.q.k.v, ...), custom_call_target="tpu_custom_call", output_to_operand_aliasing={{0}: (3, {}), {1}: (4, {})} | custom-call | flops 3795000064 | bytes 1 | tf_op jit(solution)/shard_map/attend/pallas_call | solution.py:545
  189.2 8.5 %rows_times.9 = (bf16[2,296,1536]{2,1,0:T(8,128)(2,1)}, bf16[2,296,1536]{2,1,0:T(8,128)(2,1)}, bf16[2,296,1536]{2,1,0:T(8,128)(2,1)}, bf16[2,296,1536]{2,1,0:T(8,128)(2,1)}) custom-call(bf16[4,2,296,384]{3,2,1,0:T(8,128)(2,1)} %get-tuple-element.915.refs_0_.refs_1_.refs_2_.refs_3_.grad.mixed, ...), custom_call_target="tpu_custom_call" | custom-call | flops 1313097728 | bytes 1 | tf_op jit(solution)/shard_map/rows_times/pallas_call | solution.py:406
  205.4 21.5 %collective-permute-done.28.refs_5_ = bf16[2,1,192,1536]{3,2,1,0:T(8,128)(2,1)S(1)} collective-permute-done((bf16[2,1,192,1536]{3,2,1,0:T(8,128)(2,1)}, bf16[2,1,192,1536]{3,2,1,0:T(8,128)(2,1)S(1)}, u32[]{:S(2)}, u32[]{:S(2)}) %collective-permute-start.28) | collective-permute-done | bytes 1179680 | tf_op jit(solution)/shard_map/ppermute | solution.py:94
  229.7 12.2 %collective-permute-done.30.refs_7_ = bf16[1,1,192,1536]{3,2,1,0:T(8,128)(2,1)S(1)} collective-permute-done((bf16[1,1,192,1536]{3,2,1,0:T(8,128)(2,1)S(1)}, bf16[1,1,192,1536]{3,2,1,0:T(8,128)(2,1)S(1)}, u32[]{:S(2)}, u32[]{:S(2)}) %collective-permute-start.30) | collective-permute-done | bytes 589856 | tf_op jit(solution)/shard_map/ppermute | solution.py:94
  246.4 6.3 middle.1
  256.1 8.0 assemble.7
  264.0 6.1 collective-permute-done.33.refs_1_
  279.0 17.7 %collective-permute-done.35.refs_0_ = bf16[2,1,192,1536]{3,2,1,0:T(8,128)(2,1)S(1)} collective-permute-done((bf16[2,1,192,1536]{3,2,1,0:T(8,128)(2,1)}, bf16[2,1,192,1536]{3,2,1,0:T(8,128)(2,1)S(1)}, u32[]{:S(2)}, u32[]{:S(2)}) %collective-permute-start.35) | collective-permute-done | bytes 1179680 | tf_op jit(solution)/shard_map/ppermute | solution.py:94
  302.1 25.6 %rows_times.10 = (bf16[4,2,296,1536]{3,2,1,0:T(8,128)(2,1)}, bf16[4,2,296,1536]{3,2,1,0:T(8,128)(2,1)}) custom-call(bf16[2,296,1536]{2,1,0:T(8,128)(2,1)} %get-tuple-element.782.refs_0_.a, bf16[2,296,1536]{2,1,0:T(8,128)(2,1)} %collective-permute-done.38.refs_1_.b, bf16[2,296,1536]{2,1,0:T(8,128)(2,1)} %collective-permute-done.37.refs_2_.c, ...), custom_call_target="tpu_custom_call" | custom-call | flops 4493390848 | bytes 1 | tf_op jit(solution)/shard_map/rows_times/pallas_call | solution.py:406
  334.2 20.9 %weight_grad.4 = (bf16[8,192,1536]{2,1,0:T(8,128)(2,1)}, bf16[8,192,1536]{2,1,0:T(8,128)(2,1)}, bf16[1,192,1536]{2,1,0:T(8,128)(2,1)}, bf16[1,192,1536]{2,1,0:T(8,128)(2,1)}, f32[2,1536]{1,0:T(2,128)}) custom-call(s32[1]{0:T(128)} %dynamic-slice.4.far, bf16[2,296,1536]{2,1,0:T(8,128)(2,1)} %get-tuple-element.743.a.refs_0_, ...), custom_call_target="tpu_custom_call" | custom-call | flops 5058776576 | bytes 1 | tf_op jit(solution)/shard_map/weight_grad/pallas_call | solution.py:459
  364.6 18.5 %rows_times.11.refs_0_.refs_1_.refs_2_.refs_3_.grad = bf16[4,2,296,1536]{3,2,1,0:T(8,128)(2,1)} custom-call(bf16[2,296,1536]{2,1,0:T(8,128)(2,1)} %get-tuple-element.743.a.refs_0_, bf16[2,296,1536]{2,1,0:T(8,128)(2,1)} %collective-permute-done.24.b.refs_1_, bf16[2,296,1536]{2,1,0:T(8,128)(2,1)} %collective-permute-done.23.c.refs_2_, ...), custom_call_target="tpu_custom_call" | custom-call | flops 4493390848 | bytes 1 | tf_op jit(solution)/shard_map/rows_times/pallas_call | solution.py:406
  383.2 17.8 %rows_times.12 = (bf16[2,296,1536]{2,1,0:T(8,128)(2,1)}, bf16[2,296,1536]{2,1,0:T(8,128)(2,1)}, bf16[2,296,1536]{2,1,0:T(8,128)(2,1)}, bf16[2,296,1536]{2,1,0:T(8,128)(2,1)}) custom-call(bf16[4,2,296,1536]{3,2,1,0:T(8,128)(2,1)} %rows_times.11.refs_0_.refs_1_.refs_2_.refs_3_.grad, bf16[4,2,296,1536]{3,2,1,0:T(8,128)(2,1)} %rows_times.11.refs_0_.refs_1_.refs_2_.refs_3_.grad, ...), custom_call_target="tpu_custom_call" | custom-call | flops 4493390848 | bytes 1 | tf_op jit(solution)/shard_map/rows_times/pallas_call | solution.py:406
  416.9 20.8 %weight_grad.5 = (bf16[8,192,1536]{2,1,0:T(8,128)(2,1)}, bf16[8,192,1536]{2,1,0:T(8,128)(2,1)}, bf16[1,192,1536]{2,1,0:T(8,128)(2,1)}, bf16[1,192,1536]{2,1,0:T(8,128)(2,1)}, f32[2,1536]{1,0:T(2,128)}) custom-call(s32[1]{0:T(128)} %dynamic-slice.4.far, bf16[2,296,1536]{2,1,0:T(8,128)(2,1)} %get-tuple-element.782.refs_0_.a, ...), custom_call_target="tpu_custom_call" | custom-call | flops 5058776576 | bytes 1 | tf_op jit(solution)/shard_map/weight_grad/pallas_call | solution.py:459
  437.7 17.4 %rows_times.13 = (bf16[2,296,1536]{2,1,0:T(8,128)(2,1)}, bf16[2,296,1536]{2,1,0:T(8,128)(2,1)}, bf16[2,296,1536]{2,1,0:T(8,128)(2,1)}, bf16[2,296,1536]{2,1,0:T(8,128)(2,1)}) custom-call(bf16[4,2,296,1536]{3,2,1,0:T(8,128)(2,1)} %get-tuple-element.799.grad.refs_0_.refs_1_.refs_2_.refs_3_, ...), custom_call_target="tpu_custom_call" | custom-call | flops 4493390848 | bytes 1 | tf_op jit(solution)/shard_map/rows_times/pallas_call | solution.py:406
  455.1 9.5 %middle_back.1 = (f32[2,296,1536]{2,1,0:T(8,128)}, bf16[2,296,1536]{2,1,0:T(8,128)(2,1)}, f32[2,2,4,1536]{3,2,1,0:T(4,128)}) custom-call(s32[1]{0:T(128)} %copy.204.seqs, bf16[2,256,1536]{2,1,0:T(8,128)(2,1)} %refs_0_.3, bf16[2,40,1536]{2,1,0:T(8,128)(2,1)} %refs_1_.3, bf16[2,296,1536]{2,1,0:T(8,128)(2,1)} %get-tuple-element.820.refs_2_, ...), custom_call_target="tpu_custom_call" | custom-call | flops 1518000000 | bytes 1 | tf_op jit(solution)/shard_map/middle_back/pallas_call | solution.py:673
  473.7 25.3 %collective-permute-done.51.ahead = bf16[2,192,1536]{2,1,0:T(8,128)(2,1)S(1)} collective-permute-done((bf16[2,192,1536]{2,1,0:T(8,128)(2,1)}, bf16[2,192,1536]{2,1,0:T(8,128)(2,1)S(1)}, u32[]{:S(2)}, u32[]{:S(2)}) %collective-permute-start.51) | collective-permute-done | bytes 1179680 | tf_op jit(solution)/shard_map/ppermute | solution.py:94
  522.1 8.9 %rows_times.14.grads = bf16[4,2,296,384]{3,2,1,0:T(8,128)(2,1)} custom-call(bf16[2,296,1536]{2,1,0:T(8,128)(2,1)} %get-tuple-element.883.refs_0_.a, bf16[2,296,1536]{2,1,0:T(8,128)(2,1)} %collective-permute-done.56.refs_1_.b, bf16[2,296,1536]{2,1,0:T(8,128)(2,1)} %collective-permute-done.55.refs_2_.c, ...), custom_call_target="tpu_custom_call" | custom-call | flops 1313097728 | bytes 1 | tf_op jit(solution)/shard_map/rows_times/pallas_call | solution.py:406
  540.3 9.6 %weight_grad.6 = (bf16[8,192,1536]{2,1,0:T(8,128)(2,1)}, bf16[8,192,1536]{2,1,0:T(8,128)(2,1)}, bf16[1,192,1536]{2,1,0:T(8,128)(2,1)}, bf16[1,192,1536]{2,1,0:T(8,128)(2,1)}, f32[2,384]{1,0:T(2,128)}) custom-call(s32[1]{0:T(128)} %dynamic-slice.4.far, bf16[2,296,1536]{2,1,0:T(8,128)(2,1)} %get-tuple-element.883.refs_0_.a, ...), custom_call_target="tpu_custom_call" | custom-call | flops 1454444160 | bytes 1 | tf_op jit(solution)/shard_map/weight_grad/pallas_call | solution.py:459
  551.3 29.6 %attend_back.2.refs_0_ = bf16[4,2,296,1152]{3,2,1,0:T(8,128)(2,1)} custom-call(bf16[4,2,296,1152]{3,2,1,0:T(8,128)(2,1)} %rows_times.8.q.k.v, bf16[4,2,296,1152]{3,2,1,0:T(8,128)(2,1)} %rows_times.8.q.k.v, bf16[4,2,296,1152]{3,2,1,0:T(8,128)(2,1)} %rows_times.8.q.k.v, bf16[4,2,296,384]{3,2,1,0:T(8,128)(2,1)} %get-tuple-element.915.refs_0_.refs_1_.refs_2_.refs_3_.grad.mixed, ...), custom_call_target="tpu_custom_call" | custom-call | flops 7336999936 | bytes 1 | tf_op jit(solution)/shard_map/attend_back/pallas_call | solution.py:619
  592.5 29.4 %attend_back.3.grad.refs_0_.refs_1_.refs_2_.refs_3_ = bf16[4,2,296,1152]{3,2,1,0:T(8,128)(2,1)} custom-call(bf16[4,2,296,1152]{3,2,1,0:T(8,128)(2,1)} %rows_times.8.q.k.v, bf16[4,2,296,1152]{3,2,1,0:T(8,128)(2,1)} %rows_times.8.q.k.v, bf16[4,2,296,1152]{3,2,1,0:T(8,128)(2,1)} %rows_times.8.q.k.v, ...), custom_call_target="tpu_custom_call", output_to_operand_aliasing={{}: (6, {})} | custom-call | flops 7336999936 | bytes 1 | tf_op jit(solution)/shard_map/attend_back/pallas_call | solution.py:619
  630.2 20.4 %weight_grad.7 = (bf16[8,192,1536]{2,1,0:T(8,128)(2,1)}, bf16[8,192,1536]{2,1,0:T(8,128)(2,1)}, bf16[1,192,1536]{2,1,0:T(8,128)(2,1)}, bf16[1,192,1536]{2,1,0:T(8,128)(2,1)}, f32[2,1152]{1,0:T(2,128)}) custom-call(s32[1]{0:T(128)} %dynamic-slice.4.far, ...), custom_call_target="tpu_custom_call", output_to_operand_aliasing={{0}: (6, {}), {1}: (7, {}), {2}: (8, {}), {3}: (9, {})} | custom-call | flops 3857332480 | bytes 1 | tf_op jit(solution)/shard_map/weight_grad/pallas_call | solution.py:459
  657.9 14.7 %rows_times.15 = (bf16[2,296,1536]{2,1,0:T(8,128)(2,1)}, bf16[2,296,1536]{2,1,0:T(8,128)(2,1)}, bf16[2,296,1536]{2,1,0:T(8,128)(2,1)}, bf16[2,296,1536]{2,1,0:T(8,128)(2,1)}) custom-call(bf16[4,2,296,1152]{3,2,1,0:T(8,128)(2,1)} %attend_back.3.grad.refs_0_.refs_1_.refs_2_.refs_3_, bf16[4,2,296,1152]{3,2,1,0:T(8,128)(2,1)} %attend_back.3.grad.refs_0_.refs_1_.refs_2_.refs_3_, ...), custom_call_target="tpu_custom_call" | custom-call | flops 3433293312 | bytes 1 | tf_op jit(solution)/shard_map/rows_times/pallas_call | solution.py:406
  724.5 7.4 enter_back.1
  738.9 7.0 collective-permute-done.78.ahead
  774.9 15.1 %collective-permute-done.86.ahead = bf16[2,192,1536]{2,1,0:T(8,128)(2,1)S(1)} collective-permute-done((bf16[2,192,1536]{2,1,0:T(8,128)(2,1)}, bf16[2,192,1536]{2,1,0:T(8,128)(2,1)S(1)}, u32[]{:S(2)}, u32[]{:S(2)}) %collective-permute-start.86) | collective-permute-done | bytes 1179680 | tf_op jit(solution)/shard_map/ppermute | solution.py:94
  (437 shorter events, 308.1 us)
Async XLA Ops:
  62.1 48.0 %collective-permute-start.14 = (bf16[2,296,1536]{2,1,0:T(8,128)(2,1)}, bf16[2,296,1536]{2,1,0:T(8,128)(2,1)}, u32[]{:S(2)}, u32[]{:S(2)}) collective-permute-start(bf16[2,296,1536]{2,1,0:T(8,128)(2,1)} %get-tuple-element.936.refs_0_.a), channel_id=1, source_target_pairs={{0,2},{1,3},{2,0},{3,1},{4,6},{5,7},{6,4},{7,5},{8,10},{9,11},{10,... | collective-permute-start | bytes 5455880 | tf_op jit(solution)/shard_map/ppermute | solution.py:21
  63.6 46.5 %collective-permute-start.15 = (bf16[2,296,1536]{2,1,0:T(8,128)(2,1)}, bf16[2,296,1536]{2,1,0:T(8,128)(2,1)}, u32[]{:S(2)}, u32[]{:S(2)}) collective-permute-start(bf16[2,296,1536]{2,1,0:T(8,128)(2,1)} %get-tuple-element.936.refs_0_.a), channel_id=1, source_target_pairs={{0,1},{1,0},{2,3},{3,2},{4,5},{5,4},{6,7},{7,6},{8,9},{9,8},{10,11... | collective-permute-start | bytes 5455880 | tf_op jit(solution)/shard_map/ppermute | solution.py:21
  132.2 57.0 %collective-permute-start.23 = (bf16[2,296,1536]{2,1,0:T(8,128)(2,1)}, bf16[2,296,1536]{2,1,0:T(8,128)(2,1)}, u32[]{:S(2)}, u32[]{:S(2)}) collective-permute-start(bf16[2,296,1536]{2,1,0:T(8,128)(2,1)} %get-tuple-element.743.a.refs_0_), channel_id=1, source_target_pairs={{0,2},{1,3},{2,0},{3,1},{4,6},{5,7},{6,4},{7,5},{8,10},{9,11},{10,... | collective-permute-start | bytes 5455880 | tf_op jit(solution)/shard_map/ppermute | solution.py:21
  133.7 55.4 %collective-permute-start.24 = (bf16[2,296,1536]{2,1,0:T(8,128)(2,1)}, bf16[2,296,1536]{2,1,0:T(8,128)(2,1)}, u32[]{:S(2)}, u32[]{:S(2)}) collective-permute-start(bf16[2,296,1536]{2,1,0:T(8,128)(2,1)} %get-tuple-element.743.a.refs_0_), channel_id=1, source_target_pairs={{0,1},{1,0},{2,3},{3,2},{4,5},{5,4},{6,7},{7,6},{8,9},{9,8},{10,11... | collective-permute-start | bytes 5455880 | tf_op jit(solution)/shard_map/ppermute | solution.py:21
  156.3 32.8 %collective-permute-start.21 = (bf16[2,1,192,1536]{3,2,1,0:T(8,128)(2,1)S(1)}, bf16[2,1,192,1536]{3,2,1,0:T(8,128)(2,1)}, u32[]{:S(2)}, u32[]{:S(2)}) collective-permute-start(bf16[2,1,192,1536]{3,2,1,0:T(8,128)(2,1)S(1)} %collective-permute-done.19.refs_1_), channel_id=1, source_target_pairs={{0,8},{8,16},{16,24},{24,28},{28,20},{20,12},{12,4},{4,0},{1,9},{9... | collective-permute-start | bytes 3538952 | tf_op jit(solution)/shard_map/ppermute | solution.py:94
  157.0 32.2 %collective-permute-start.22 = (bf16[2,1,192,1536]{3,2,1,0:T(8,128)(2,1)}, bf16[2,1,192,1536]{3,2,1,0:T(8,128)(2,1)}, u32[]{:S(2)}, u32[]{:S(2)}) collective-permute-start(bf16[2,1,192,1536]{3,2,1,0:T(8,128)(2,1)} %collective-permute-done.20.refs_2_), channel_id=1, source_target_pairs={{8,0},{16,8},{24,16},{28,24},{20,28},{12,20},{4,12},{0,4},{9,1},{1... | collective-permute-start | bytes 3538952 | tf_op jit(solution)/shard_map/ppermute | solution.py:97
  198.3 28.5 %collective-permute-start.28 = (bf16[2,1,192,1536]{3,2,1,0:T(8,128)(2,1)}, bf16[2,1,192,1536]{3,2,1,0:T(8,128)(2,1)S(1)}, u32[]{:S(2)}, u32[]{:S(2)}) collective-permute-start(bf16[2,1,192,1536]{3,2,1,0:T(8,128)(2,1)} %collective-permute-done.21.refs_3_), channel_id=1, source_target_pairs={{0,8},{8,16},{16,24},{24,28},{28,20},{20,12},{12,4},{4,0},{1,9},{9... | collective-permute-start | bytes 3538952 | tf_op jit(solution)/shard_map/ppermute | solution.py:94
  198.9 28.2 %collective-permute-start.29 = (bf16[2,1,192,1536]{3,2,1,0:T(8,128)(2,1)}, bf16[2,1,192,1536]{3,2,1,0:T(8,128)(2,1)S(1)}, u32[]{:S(2)}, u32[]{:S(2)}) collective-permute-start(bf16[2,1,192,1536]{3,2,1,0:T(8,128)(2,1)} %collective-permute-done.22.refs_4_), channel_id=1, source_target_pairs={{8,0},{16,8},{24,16},{28,24},{20,28},{12,20},{4,12},{0,4},{9,1},{1... | collective-permute-start | bytes 3538952 | tf_op jit(solution)/shard_map/ppermute | solution.py:97
  203.8 42.6 %collective-permute-start.32 = (bf16[2,296,1536]{2,1,0:T(8,128)(2,1)S(1)}, bf16[2,296,1536]{2,1,0:T(8,128)(2,1)}, u32[]{:S(2)}, u32[]{:S(2)}) collective-permute-start(bf16[2,296,1536]{2,1,0:T(8,128)(2,1)S(1)} %add_convert_fusion.3), channel_id=1, source_target_pairs={{0,2},{1,3},{2,0},{3,1},{4,6},{5,7},{6,4},{7,5},{8,10},{9,11},{10,... | collective-permute-start | bytes 5455880 | tf_op jit(solution)/shard_map/ppermute | solution.py:21
  252.6 45.3 %collective-permute-start.37 = (bf16[2,296,1536]{2,1,0:T(8,128)(2,1)}, bf16[2,296,1536]{2,1,0:T(8,128)(2,1)}, u32[]{:S(2)}, u32[]{:S(2)}) collective-permute-start(bf16[2,296,1536]{2,1,0:T(8,128)(2,1)} %get-tuple-element.782.refs_0_.a), channel_id=1, source_target_pairs={{0,2},{1,3},{2,0},{3,1},{4,6},{5,7},{6,4},{7,5},{8,10},{9,11},{10,... | collective-permute-start | bytes 5455880 | tf_op jit(solution)/shard_map/ppermute | solution.py:21
  254.2 43.7 %collective-permute-start.38 = (bf16[2,296,1536]{2,1,0:T(8,128)(2,1)}, bf16[2,296,1536]{2,1,0:T(8,128)(2,1)}, u32[]{:S(2)}, u32[]{:S(2)}) collective-permute-start(bf16[2,296,1536]{2,1,0:T(8,128)(2,1)} %get-tuple-element.782.refs_0_.a), channel_id=1, source_target_pairs={{0,1},{1,0},{2,3},{3,2},{4,5},{5,4},{6,7},{7,6},{8,9},{9,8},{10,11... | collective-permute-start | bytes 5455880 | tf_op jit(solution)/shard_map/ppermute | solution.py:21
  298.0 29.7 %collective-permute-start.40 = (bf16[2,1,192,1536]{3,2,1,0:T(8,128)(2,1)}, bf16[2,1,192,1536]{3,2,1,0:T(8,128)(2,1)S(1)}, u32[]{:S(2)}, u32[]{:S(2)}) collective-permute-start(bf16[2,1,192,1536]{3,2,1,0:T(8,128)(2,1)} %copy-done.12), channel_id=1, source_target_pairs={{0,8},{8,16},{16,24},{24,28},{28,20},{20,12},{12,4},{4,0},{1,9},{9... | collective-permute-start | bytes 3538952 | tf_op jit(solution)/shard_map/ppermute | solution.py:94
  299.1 28.6 %collective-permute-start.41 = (bf16[2,1,192,1536]{3,2,1,0:T(8,128)(2,1)}, bf16[2,1,192,1536]{3,2,1,0:T(8,128)(2,1)}, u32[]{:S(2)}, u32[]{:S(2)}) collective-permute-start(bf16[2,1,192,1536]{3,2,1,0:T(8,128)(2,1)} %collective-permute-done.36.refs_1_), channel_id=1, source_target_pairs={{8,0},{16,8},{24,16},{28,24},{20,28},{12,20},{4,12},{0,4},{9,1},{1... | collective-permute-start | bytes 3538952 | tf_op jit(solution)/shard_map/ppermute | solution.py:97
  355.2 28.0 %collective-permute-start.44 = (bf16[1,192,1536]{2,1,0:T(8,128)(2,1)}, bf16[1,192,1536]{2,1,0:T(8,128)(2,1)S(1)}, u32[]{:S(2)}, u32[]{:S(2)}) collective-permute-start(bf16[1,192,1536]{2,1,0:T(8,128)(2,1)} %get-tuple-element.751), channel_id=1, source_target_pairs={{0,8},{8,16},{16,24},{24,28},{28,20},{20,12},{12,4},{4,0},{1,9},{9... | collective-permute-start | bytes 1769480 | tf_op jit(solution)/shard_map/ppermute | solution.py:94
  411.4 43.7 %collective-permute-start.50 = (bf16[2,296,1536]{2,1,0:T(8,128)(2,1)}, bf16[2,296,1536]{2,1,0:T(8,128)(2,1)}, u32[]{:S(2)}, u32[]{:S(2)}) collective-permute-start(bf16[2,296,1536]{2,1,0:T(8,128)(2,1)} %add_convert_fusion.2), channel_id=1, source_target_pairs={{0,2},{1,3},{2,0},{3,1},{4,6},{5,7},{6,4},{7,5},{8,10},{9,11},{10,... | collective-permute-start | bytes 5455880 | tf_op jit(solution)/shard_map/ppermute | solution.py:21
  412.8 42.3 %collective-permute-start.48 = (bf16[2,192,1536]{2,1,0:T(8,128)(2,1)}, bf16[2,192,1536]{2,1,0:T(8,128)(2,1)S(1)}, u32[]{:S(2)}, u32[]{:S(2)}) collective-permute-start(bf16[2,192,1536]{2,1,0:T(8,128)(2,1)} %get-tuple-element.807), channel_id=1, source_target_pairs={{0,8},{8,16},{16,24},{24,28},{28,20},{20,12},{12,4},{4,0},{1,9},{9... | collective-permute-start | bytes 3538952 | tf_op jit(solution)/shard_map/ppermute | solution.py:94
  414.0 41.1 %collective-permute-start.49 = (bf16[2,192,1536]{2,1,0:T(8,128)(2,1)}, bf16[2,192,1536]{2,1,0:T(8,128)(2,1)}, u32[]{:S(2)}, u32[]{:S(2)}) collective-permute-start(bf16[2,192,1536]{2,1,0:T(8,128)(2,1)} %get-tuple-element.808), channel_id=1, source_target_pairs={{8,0},{16,8},{24,16},{28,24},{20,28},{12,20},{4,12},{0,4},{9,1},{1... | collective-permute-start | bytes 3538952 | tf_op jit(solution)/shard_map/ppermute | solution.py:97
  469.9 29.1 %collective-permute-start.51 = (bf16[2,192,1536]{2,1,0:T(8,128)(2,1)}, bf16[2,192,1536]{2,1,0:T(8,128)(2,1)S(1)}, u32[]{:S(2)}, u32[]{:S(2)}) collective-permute-start(bf16[2,192,1536]{2,1,0:T(8,128)(2,1)} %get-tuple-element.838), channel_id=1, source_target_pairs={{0,8},{8,16},{16,24},{24,28},{28,20},{20,12},{12,4},{4,0},{1,9},{9... | collective-permute-start | bytes 3538952 | tf_op jit(solution)/shard_map/ppermute | solution.py:94
  471.1 46.8 %collective-permute-start.55 = (bf16[2,296,1536]{2,1,0:T(8,128)(2,1)}, bf16[2,296,1536]{2,1,0:T(8,128)(2,1)}, u32[]{:S(2)}, u32[]{:S(2)}) collective-permute-start(bf16[2,296,1536]{2,1,0:T(8,128)(2,1)} %get-tuple-element.883.refs_0_.a), channel_id=1, source_target_pairs={{0,2},{1,3},{2,0},{3,1},{4,6},{5,7},{6,4},{7,5},{8,10},{9,11},{10,... | collective-permute-start | bytes 5455880 | tf_op jit(solution)/shard_map/ppermute | solution.py:21
  471.7 46.2 %collective-permute-start.56 = (bf16[2,296,1536]{2,1,0:T(8,128)(2,1)}, bf16[2,296,1536]{2,1,0:T(8,128)(2,1)}, u32[]{:S(2)}, u32[]{:S(2)}) collective-permute-start(bf16[2,296,1536]{2,1,0:T(8,128)(2,1)} %get-tuple-element.883.refs_0_.a), channel_id=1, source_target_pairs={{0,1},{1,0},{2,3},{3,2},{4,5},{5,4},{6,7},{7,6},{8,9},{9,8},{10,11... | collective-permute-start | bytes 5455880 | tf_op jit(solution)/shard_map/ppermute | solution.py:21
  471.7 29.8 %collective-permute-start.52 = (bf16[2,192,1536]{2,1,0:T(8,128)(2,1)}, bf16[2,192,1536]{2,1,0:T(8,128)(2,1)}, u32[]{:S(2)}, u32[]{:S(2)}) collective-permute-start(bf16[2,192,1536]{2,1,0:T(8,128)(2,1)} %get-tuple-element.839), channel_id=1, source_target_pairs={{8,0},{16,8},{24,16},{28,24},{20,28},{12,20},{4,12},{0,4},{9,1},{1... | collective-permute-start | bytes 3538952 | tf_op jit(solution)/shard_map/ppermute | solution.py:97
  472.5 37.3 %collective-permute-start.53 = (bf16[1,192,1536]{2,1,0:T(8,128)(2,1)}, bf16[1,192,1536]{2,1,0:T(8,128)(2,1)S(1)}, u32[]{:S(2)}, u32[]{:S(2)}) collective-permute-start(bf16[1,192,1536]{2,1,0:T(8,128)(2,1)} %get-tuple-element.846), channel_id=1, source_target_pairs={{0,8},{8,16},{16,24},{24,28},{28,20},{20,12},{12,4},{4,0},{1,9},{9... | collective-permute-start | bytes 1769480 | tf_op jit(solution)/shard_map/ppermute | solution.py:94
  531.5 49.4 %collective-permute-start.60 = (bf16[2,192,1536]{2,1,0:T(8,128)(2,1)}, bf16[2,192,1536]{2,1,0:T(8,128)(2,1)S(1)}, u32[]{:S(2)}, u32[]{:S(2)}) collective-permute-start(bf16[2,192,1536]{2,1,0:T(8,128)(2,1)} %get-tuple-element.901), channel_id=1, source_target_pairs={{0,8},{8,16},{16,24},{24,28},{28,20},{20,12},{12,4},{4,0},{1,9},{9... | collective-permute-start | bytes 3538952 | tf_op jit(solution)/shard_map/ppermute | solution.py:94
  531.9 49.1 %collective-permute-start.61 = (bf16[2,192,1536]{2,1,0:T(8,128)(2,1)}, bf16[2,192,1536]{2,1,0:T(8,128)(2,1)}, u32[]{:S(2)}, u32[]{:S(2)}) collective-permute-start(bf16[2,192,1536]{2,1,0:T(8,128)(2,1)} %get-tuple-element.902), channel_id=1, source_target_pairs={{8,0},{16,8},{24,16},{28,24},{20,28},{12,20},{4,12},{0,4},{9,1},{1... | collective-permute-start | bytes 3538952 | tf_op jit(solution)/shard_map/ppermute | solution.py:97
  533.6 51.6 %collective-permute-start.62 = (bf16[2,192,1536]{2,1,0:T(8,128)(2,1)}, bf16[2,192,1536]{2,1,0:T(8,128)(2,1)}, u32[]{:S(2)}, u32[]{:S(2)}) collective-permute-start(bf16[2,192,1536]{2,1,0:T(8,128)(2,1)} %get-tuple-element.904), channel_id=1, source_target_pairs={{0,8},{8,16},{16,24},{24,28},{28,20},{20,12},{12,4},{4,0},{1,9},{9... | collective-permute-start | bytes 3538952 | tf_op jit(solution)/shard_map/ppermute | solution.py:94
  536.2 48.9 %collective-permute-start.63 = (bf16[2,192,1536]{2,1,0:T(8,128)(2,1)}, bf16[2,192,1536]{2,1,0:T(8,128)(2,1)}, u32[]{:S(2)}, u32[]{:S(2)}) collective-permute-start(bf16[2,192,1536]{2,1,0:T(8,128)(2,1)} %get-tuple-element.905), channel_id=1, source_target_pairs={{8,0},{16,8},{24,16},{28,24},{20,28},{12,20},{4,12},{0,4},{9,1},{1... | collective-permute-start | bytes 3538952 | tf_op jit(solution)/shard_map/ppermute | solution.py:97
  550.0 71.9 %collective-permute-start.64 = (bf16[2,296,1536]{2,1,0:T(8,128)(2,1)}, bf16[2,296,1536]{2,1,0:T(8,128)(2,1)}, u32[]{:S(2)}, u32[]{:S(2)}) collective-permute-start(bf16[2,296,1536]{2,1,0:T(8,128)(2,1)} %add_convert_fusion.1), channel_id=1, source_target_pairs={{0,2},{1,3},{2,0},{3,1},{4,6},{5,7},{6,4},{7,5},{8,10},{9,11},{10,... | collective-permute-start | bytes 5455880 | tf_op jit(solution)/shard_map/ppermute | solution.py:21
  590.4 31.4 %collective-permute-start.65 = (bf16[2,192,1536]{2,1,0:T(8,128)(2,1)}, bf16[2,192,1536]{2,1,0:T(8,128)(2,1)S(1)}, u32[]{:S(2)}, u32[]{:S(2)}) collective-permute-start(bf16[2,192,1536]{2,1,0:T(8,128)(2,1)} %get-tuple-element.922), channel_id=1, source_target_pairs={{0,8},{8,16},{16,24},{24,28},{28,20},{20,12},{12,4},{4,0},{1,9},{9... | collective-permute-start | bytes 3538952 | tf_op jit(solution)/shard_map/ppermute | solution.py:94
  591.8 30.1 %collective-permute-start.66 = (bf16[2,192,1536]{2,1,0:T(8,128)(2,1)}, bf16[2,192,1536]{2,1,0:T(8,128)(2,1)}, u32[]{:S(2)}, u32[]{:S(2)}) collective-permute-start(bf16[2,192,1536]{2,1,0:T(8,128)(2,1)} %get-tuple-element.923), channel_id=1, source_target_pairs={{8,0},{16,8},{24,16},{28,24},{20,28},{12,20},{4,12},{0,4},{9,1},{1... | collective-permute-start | bytes 3538952 | tf_op jit(solution)/shard_map/ppermute | solution.py:97
  682.2 42.4 %collective-permute-start.75 = (bf16[2,296,1536]{2,1,0:T(8,128)(2,1)}, bf16[2,296,1536]{2,1,0:T(8,128)(2,1)}, u32[]{:S(2)}, u32[]{:S(2)}) collective-permute-start(bf16[2,296,1536]{2,1,0:T(8,128)(2,1)} %add_convert_fusion), channel_id=1, source_target_pairs={{0,2},{1,3},{2,0},{3,1},{4,6},{5,7},{6,4},{7,5},{8,10},{9,11},{10,... | collective-permute-start | bytes 5455880 | tf_op jit(solution)/shard_map/ppermute | solution.py:21
  683.7 28.3 %collective-permute-start.73 = (bf16[2,192,1536]{2,1,0:T(8,128)(2,1)}, bf16[2,192,1536]{2,1,0:T(8,128)(2,1)S(1)}, u32[]{:S(2)}, u32[]{:S(2)}) collective-permute-start(bf16[2,192,1536]{2,1,0:T(8,128)(2,1)} %get-tuple-element.1017), channel_id=1, source_target_pairs={{0,8},{8,16},{16,24},{24,28},{28,20},{20,12},{12,4},{4,0},{1,9},{9... | collective-permute-start | bytes 3538952 | tf_op jit(solution)/shard_map/ppermute | solution.py:94
  685.1 28.1 %collective-permute-start.74 = (bf16[2,192,1536]{2,1,0:T(8,128)(2,1)}, bf16[2,192,1536]{2,1,0:T(8,128)(2,1)}, u32[]{:S(2)}, u32[]{:S(2)}) collective-permute-start(bf16[2,192,1536]{2,1,0:T(8,128)(2,1)} %get-tuple-element.1018), channel_id=1, source_target_pairs={{8,0},{16,8},{24,16},{28,24},{20,28},{12,20},{4,12},{0,4},{9,1},{1... | collective-permute-start | bytes 3538952 | tf_op jit(solution)/shard_map/ppermute | solution.py:97
  (107 other events, 1641.4 us)
